TPU v7x, 32 devices: a whole 2x2x4 slice. The times are simulated.
32 devices in a mesh: ctx: 8 (over y, x, core), head: 4 (over z).
Axes of the slice: x: 2, y: 2, z: 4, core: 2. Of those that a mesh axis runs over, the one named last changes fastest.
Arguments:
- token_ids: int32 [2048], P('ctx'), may hold values from 0 to 31999
- labels: int32 [2048], P('ctx'), may hold values from 0 to 31999
- answer_mask: int32 [2048], P('ctx'), may hold values 0 or 1
- pair_map: int32 [8], replicated, may hold values from 0 to 7, each once
- w_layer: float32 [2048, 21504], P('ctx', 'head')
- w_vocab: float32 [2048, 64000], P('ctx', 'head')
- gains: float32 [2048, 3], P('ctx'), may hold values from 0.5 to 1.5
- mom_layer: float32 [2048, 21504], P('ctx', 'head'), may hold values from -1.1444092e-05 to 1.1444092e-05
- mom_vocab: float32 [2048, 64000], P('ctx', 'head'), may hold values from -1.1444092e-05 to 1.1444092e-05
- mom_gains: float32 [2048, 3], P('ctx'), may hold values from -1.1444092e-05 to 1.1444092e-05
- avg_layer: float32 [2048, 21504], P('ctx', 'head')
- avg_vocab: float32 [2048, 64000], P('ctx', 'head')
- avg_gains: float32 [2048, 3], P('ctx'), may hold values from 0.5 to 1.5
Outputs:
- layer_new: float32 [2048, 21504], P('ctx', 'head')
- layer_moment: float32 [2048, 21504], P('ctx', 'head')
- layer_average: float32 [2048, 21504], P('ctx', 'head')
- layer_copy: bfloat16 [2048, 21504], P('ctx', 'head')
- vocab_new: float32 [2048, 64000], P('ctx', 'head')
- vocab_moment: float32 [2048, 64000], P('ctx', 'head')
- vocab_average: float32 [2048, 64000], P('ctx', 'head')
- vocab_copy: bfloat16 [2048, 64000], P('ctx', 'head')
- gains_new: float32 [2048, 3], P('ctx')
- gains_moment: float32 [2048, 3], P('ctx')
- gains_average: float32 [2048, 3], P('ctx')
- gains_copy: bfloat16 [2048, 3], P('ctx')
- loss: float32 [], replicated
- grad_norm: float32 [], replicated
Inputs may be any that keep to these rules, and one draw needn't show every extreme that they name: `pair_map`: each index of ctx appears once.
All inputs are finite; a program needn't handle non-finite values. No bound on the sum of `answer_mask` on one device may be relied on, other than what follows from the above.
Results may differ from a plain program's by a relative error of at most 0.015.
The roundings to bfloat16 on the way count: a program that leaves them out, or rounds other values in their place, can miss the bound.
Values may be sent and summed in bfloat16 or wider, within the bound.
No kernel may reach another device: no remote copies, remote signals or barrier semaphores. Data moves between devices by JAX's collectives and lax.ppermute only.
A program may use at most 832 MiB of HBM per device.

v0:
```python
import math

import jax
import jax.numpy as jnp
from jax import lax
from jax.sharding import PartitionSpec as P

D = 2048
HEADS = 32
KV = 4
HD = 64
FF = 5632
V = 32000
SEQS = 2


eps = 1e-05
z_weight = 0.0001
momentum_rate = 0.5
average_rate = 0.5
clip_level = 0.01


def merged(value, axis, join):
    pieces = jax.tree.map(lambda part: lax.all_gather(part, axis), value)
    head = jax.tree.map(lambda part: part[0], pieces)
    tail = jax.tree.map(lambda part: part[1:], pieces)
    subtotal, _ = lax.scan(lambda subtotal, share: (join(subtotal, share), None), head, tail)
    return subtotal


def widths():
    group = HEADS // KV
    return (group, group * HD, FF // KV, V // KV)


def layer_spread(length):
    group, qg, ffg, vg = widths()
    attn_in = qg + 2 * HD
    column = jnp.arange(attn_in + qg + 3 * ffg)
    return jnp.where(
        column < attn_in,
        D ** (-0.5),
        jnp.where(
            column < attn_in + qg,
            (length / (4.0 * HEADS * HD)) ** 0.5,
            jnp.where(column < attn_in + qg + 2 * ffg, D ** (-0.5), FF ** (-0.5)),
        ),
    ).astype(jnp.float32)


def vocab_spread():
    vg = V // KV
    column = jnp.arange(2 * vg)
    return jnp.where(column < vg, 2.0 * D ** (-0.5), 1.0).astype(jnp.float32)


def total_params():
    return D * (2 * HEADS * HD + 2 * KV * HD + 3 * FF + 2 * V + 3)


def yarn_tables(positions, head_dim):
    half = head_dim // 2
    index = jnp.arange(half, dtype=jnp.float32)
    inverse = 10000.0 ** (-2.0 * index / head_dim)
    ratio = 2048.0 * inverse / (2.0 * math.pi)
    ramp = jnp.clip((ratio - 1.0) / 31.0, 0.0, 1.0)
    freq = (1.0 - ramp) * inverse / 4.0 + ramp * inverse
    angle = positions[:, None] * freq[None, :]
    mscale = 0.1 * math.log(4.0) + 1.0
    return (jnp.cos(angle) * mscale, jnp.sin(angle) * mscale)


def rope(x, cosine, sine):
    half = x.shape[-1] // 2
    first = x[..., :half]
    second = x[..., half:]
    return jnp.concatenate(
        [first * cosine - second * sine, second * cosine + first * sine], axis=-1
    )


def norm(x, gain):
    return x * lax.rsqrt(jnp.mean(x * x, axis=-1, keepdims=True) + eps) * gain


def update(weight, moment, average, grad, rate):
    moment_new = momentum_rate * moment + grad
    weight_new = weight - rate * (grad + momentum_rate * moment_new)
    average_new = average_rate * average + (1.0 - average_rate) * weight_new
    return (weight_new, moment_new, average_new)


def merge_stats(first, second):
    top = jnp.maximum(first[0], second[0])
    total = first[1] * jnp.exp(first[0] - top) + second[1] * jnp.exp(second[0] - top)
    return (top, total, first[2] + second[2])


def keep_same(args):
    return args


def contract_first(left, right):
    return lax.dot_general(
        left, right, (((1,), (1,)), ((), ())), preferred_element_type=jnp.float32
    )


def masked_scores(q_part, keys, q_index, k_index, span):
    scores = jnp.einsum(
        "qhd,kd->hqk", q_part, keys, preferred_element_type=jnp.float32
    ) * keys.shape[-1] ** (-0.5)
    offset = jnp.arange(span, dtype=jnp.int32)
    allowed = (k_index * span + offset)[None, :] <= (q_index * span + offset)[:, None]
    return jnp.where(allowed[None], scores, -jnp.inf)


def local(
    token_ids,
    labels,
    answer_mask,
    pair_map,
    w_layer,
    w_vocab,
    gains,
    mom_layer,
    mom_vocab,
    mom_gains,
    avg_layer,
    avg_vocab,
    avg_gains,
):
    f32 = jnp.float32
    bf16 = jnp.bfloat16
    group, qg, ffg, vg = widths()
    attn_in = qg + 2 * HD
    layer_width = attn_in + qg + 3 * ffg
    n_ctx = lax.axis_size("ctx")
    n_head = lax.axis_size("head")
    place = lax.axis_index("ctx")
    shard = lax.axis_index("head")
    tok = token_ids.shape[0]
    nblk = 2 * SEQS
    span = tok // nblk
    length = n_ctx * tok // SEQS
    scale = HD ** (-0.5)
    first = pair_map[place]
    mirror = 2 * n_ctx - 1 - first
    local_rows = jnp.arange(tok, dtype=jnp.int32)
    positions = jnp.where(local_rows // span % 2 == 0, first, mirror) * span + local_rows % span
    cosine, sine = yarn_tables(positions.astype(f32), HD)
    vocab_send = w_vocab.astype(bf16)
    layer_full, vocab_full, gain_full = (
        lax.all_gather(w_layer.astype(bf16), "ctx", axis=0, tiled=True),
        lax.all_gather(vocab_send, "ctx", axis=0, tiled=True),
        lax.all_gather(gains.astype(bf16), "ctx", axis=0, tiled=True),
    )
    gain_f = gain_full.astype(f32)
    w_in = layer_full[:, :attn_in]
    w_out = layer_full[:, attn_in : attn_in + qg]
    w_gu = layer_full[:, attn_in + qg : attn_in + qg + 2 * ffg]
    w_down = layer_full[:, attn_in + qg + 2 * ffg :]
    w_head = vocab_full[:, :vg]
    offset_id = shard * vg
    local_ids = token_ids - offset_id
    inside = (local_ids >= 0) & (local_ids < vg)
    picked = jnp.take(vocab_full[:, vg:], jnp.where(inside, local_ids, 0), axis=1).T
    embedded = jnp.where(inside[:, None], picked, jnp.zeros_like(picked))
    x0 = lax.psum(embedded.astype(f32).astype(jnp.bfloat16), "head").astype(jnp.float32)
    a1 = norm(x0, gain_f[:, 0]).astype(bf16)
    raw = jnp.dot(a1, w_in, preferred_element_type=f32)

    def rotate(values):
        queries = rope(values[:, :qg].reshape(tok, group, HD), cosine[:, None, :], sine[:, None, :])
        keys = rope(values[:, qg : qg + HD], cosine, sine)
        return (queries, keys, values[:, qg + HD :])

    (q_f, k_f, v_f), rotate_back = jax.vjp(rotate, raw)
    q_blocks = q_f.astype(bf16).reshape(nblk, span, group, HD)
    kv_local = jnp.concatenate([k_f, v_f], axis=1).astype(bf16)
    kv_every, mask_every = (
        lax.all_gather(kv_local, "ctx", axis=0, tiled=True),
        lax.all_gather(answer_mask.astype(bf16), "ctx", axis=0, tiled=True),
    )
    count = jnp.sum(mask_every.astype(f32))
    kv_blocks = kv_every.reshape(n_ctx, nblk, span, 2 * HD)
    key_index = jnp.stack([pair_map, 2 * n_ctx - 1 - pair_map], axis=1)
    q_index = jnp.stack([first, mirror] * SEQS)

    def stat_step(carry, item):
        top, total = carry
        keys_dev, k_index = item
        for b in range(nblk):
            for half in range(2):
                kb = 2 * (b // 2) + half

                def stat_live(args):
                    top_b, total_b = args
                    s = masked_scores(
                        q_blocks[b], keys_dev[kb, :, :HD], q_index[b], k_index[half], span
                    )
                    new_top = jnp.maximum(top_b, jnp.max(s, axis=-1))
                    return (
                        new_top,
                        total_b * jnp.exp(top_b - new_top)
                        + jnp.sum(jnp.exp(s - new_top[..., None]), axis=-1),
                    )

                new = lax.cond(
                    k_index[half] <= q_index[b], stat_live, keep_same, (top[b], total[b])
                )
                top = top.at[b].set(new[0])
                total = total.at[b].set(new[1])
        return ((top, total), None)

    start_top = jnp.full((nblk, group, span), -jnp.inf, f32)
    start_total = jnp.zeros((nblk, group, span), f32)
    (top, total), _ = lax.scan(stat_step, (start_top, start_total), (kv_blocks, key_index))
    lse_attn = top + jnp.log(total)

    def out_step(acc, item):
        keys_dev, k_index = item
        for b in range(nblk):
            for half in range(2):
                kb = 2 * (b // 2) + half

                def out_live(acc_b):
                    s = masked_scores(
                        q_blocks[b], keys_dev[kb, :, :HD], q_index[b], k_index[half], span
                    )
                    probs = jnp.exp(s - lse_attn[b][..., None])
                    return acc_b + jnp.einsum(
                        "hqk,kd->hqd",
                        probs.astype(bf16),
                        keys_dev[kb, :, HD:],
                        preferred_element_type=f32,
                    )

                acc = acc.at[b].set(
                    lax.cond(k_index[half] <= q_index[b], out_live, keep_same, acc[b])
                )
        return (acc, None)

    acc, _ = lax.scan(out_step, jnp.zeros((nblk, group, span, HD), f32), (kv_blocks, key_index))
    attn_f = acc.transpose(0, 2, 1, 3).reshape(tok, qg)
    attn_b = attn_f.astype(bf16)
    y_attn = lax.psum(contract_first(attn_b, w_out).astype(jnp.bfloat16), "head").astype(
        jnp.float32
    )
    x1 = x0 + y_attn
    a2 = norm(x1, gain_f[:, 1]).astype(bf16)
    gate_up = jnp.dot(a2, w_gu, preferred_element_type=f32)

    def glu(values):
        return jax.nn.silu(values[:, :ffg]) * values[:, ffg:]

    hidden_f, glu_back = jax.vjp(glu, gate_up)
    hidden_b = hidden_f.astype(bf16)
    y_ffn = lax.psum(contract_first(hidden_b, w_down).astype(jnp.bfloat16), "head").astype(
        jnp.float32
    )
    x2 = x1 + y_ffn
    final_b = norm(x2, gain_f[:, 2]).astype(bf16)
    logits = jnp.dot(final_b, w_head, preferred_element_type=f32)
    row_top = jnp.max(logits, axis=-1)
    row_total = jnp.sum(jnp.exp(logits - row_top[:, None]), axis=-1)
    local_labels = labels - offset_id
    label_in = (local_labels >= 0) & (local_labels < vg)
    hit = (jnp.arange(vg, dtype=jnp.int32)[None, :] == local_labels[:, None]) & label_in[:, None]
    label_logit = jnp.sum(jnp.where(hit, logits, 0.0), axis=-1)
    top_all, total_all, label_all = merged((row_top, row_total, label_logit), "head", merge_stats)
    lse = top_all + jnp.log(total_all)
    valid = answer_mask.astype(f32)
    loss_part = jnp.sum(valid * (lse - label_all + z_weight * lse * lse)) / count
    soft = jnp.exp(logits - lse[:, None])
    dlog_b = (
        (valid / count)[:, None] * ((1.0 + 2.0 * z_weight * lse)[:, None] * soft - hit.astype(f32))
    ).astype(bf16)
    d_final = lax.psum(contract_first(dlog_b, w_head).astype(jnp.bfloat16), "head").astype(
        jnp.float32
    )
    _, final_back = jax.vjp(norm, x2, gain_f[:, 2])
    dx2, d_gain2 = final_back(d_final)
    dyf_b = dx2.astype(bf16)
    d_hidden = jnp.dot(dyf_b, w_down, preferred_element_type=f32)
    d_gate_up_b = glu_back(d_hidden)[0].astype(bf16)
    d_second = lax.psum(contract_first(d_gate_up_b, w_gu).astype(jnp.bfloat16), "head").astype(
        jnp.float32
    )
    _, second_back = jax.vjp(norm, x1, gain_f[:, 1])
    dx1_norm, d_gain1 = second_back(d_second)
    dx1 = dx2 + dx1_norm
    dya_b = dx1.astype(bf16)
    d_attn_b = jnp.dot(dya_b, w_out, preferred_element_type=f32).astype(bf16)
    d_blocks = d_attn_b.reshape(nblk, span, group, HD)
    delta = jnp.einsum(
        "bqhd,bqhd->bhq", d_blocks.astype(f32), attn_f.reshape(nblk, span, group, HD)
    )

    def back_step(dq, item):
        keys_dev, k_index = item
        dkv = jnp.zeros((nblk, span, 2 * HD), f32)
        for b in range(nblk):
            for half in range(2):
                kb = 2 * (b // 2) + half

                def back_live(args):
                    dq_b, dkv_b = args
                    keys = keys_dev[kb, :, :HD]
                    values = keys_dev[kb, :, HD:]
                    s = masked_scores(q_blocks[b], keys, q_index[b], k_index[half], span)
                    probs = jnp.exp(s - lse_attn[b][..., None])
                    grad_v = jnp.einsum(
                        "hqk,qhd->kd", probs.astype(bf16), d_blocks[b], preferred_element_type=f32
                    )
                    grad_p = jnp.einsum(
                        "qhd,kd->hqk", d_blocks[b], values, preferred_element_type=f32
                    )
                    grad_s = (probs * (grad_p - delta[b][..., None])).astype(bf16)
                    dq_new = dq_b + scale * jnp.einsum(
                        "hqk,kd->qhd", grad_s, keys, preferred_element_type=f32
                    )
                    grad_k = scale * jnp.einsum(
                        "hqk,qhd->kd", grad_s, q_blocks[b], preferred_element_type=f32
                    )
                    return (dq_new, dkv_b + jnp.concatenate([grad_k, grad_v], axis=-1))

                new = lax.cond(k_index[half] <= q_index[b], back_live, keep_same, (dq[b], dkv[kb]))
                dq = dq.at[b].set(new[0])
                dkv = dkv.at[kb].set(new[1])
        return (dq, dkv)

    dq, dkv_every = lax.scan(
        back_step, jnp.zeros((nblk, span, group, HD), f32), (kv_blocks, key_index)
    )
    dkv_own = lax.psum_scatter(
        dkv_every.reshape(n_ctx * tok, 2 * HD).astype(jnp.bfloat16),
        "ctx",
        scatter_dimension=0,
        tiled=True,
    ).astype(jnp.float32)
    d_raw_b = rotate_back((dq.reshape(tok, group, HD), dkv_own[:, :HD], dkv_own[:, HD:]))[0].astype(
        bf16
    )
    d_first = lax.psum(contract_first(d_raw_b, w_in).astype(jnp.bfloat16), "head").astype(
        jnp.float32
    )
    _, first_back = jax.vjp(norm, x0, gain_f[:, 0])
    dx0_norm, d_gain0 = first_back(d_first)
    dx0 = dx1 + dx0_norm
    embed_slot = jnp.where(inside, local_ids, vg)

    def outer(left, right):
        return lax.dot_general(
            left, right, (((0,), (0,)), ((), ())), preferred_element_type=jnp.float32
        )

    gain_term = jnp.stack([d_gain0, d_gain1, d_gain2], axis=1)
    parts = [
        outer(a1, d_raw_b),
        outer(dya_b, attn_b),
        outer(a2, d_gate_up_b),
        outer(dyf_b, hidden_b),
        outer(final_b, dlog_b),
    ]
    parts.append(jax.ops.segment_sum(dx0, embed_slot, vg + 1)[:vg].T)
    parts.append(gain_term)
    grads = lax.psum_scatter(
        jnp.concatenate(parts, axis=1).astype(jnp.bfloat16), "ctx", scatter_dimension=0, tiled=True
    ).astype(jnp.float32)
    grad_layer = grads[:, :layer_width]
    grad_vocab = grads[:, layer_width : layer_width + 2 * vg]
    grad_gain = grads[:, layer_width + 2 * vg :]
    squares = (
        jnp.sum(grad_layer * grad_layer)
        + jnp.sum(grad_vocab * grad_vocab)
        + jnp.sum(grad_gain * grad_gain) / n_head
    )
    total_sq, loss = lax.psum((squares, loss_part / n_head), ("ctx", "head"))
    grad_norm = jnp.sqrt(total_sq)
    factor = jnp.minimum(1.0, clip_level / grad_norm)
    base = 1.5 * math.sqrt(total_params()) / clip_level
    layer_new, layer_moment, layer_average = update(
        w_layer, mom_layer, avg_layer, factor * grad_layer, base * layer_spread(length)
    )
    vocab_new, vocab_moment, vocab_average = update(
        w_vocab, mom_vocab, avg_vocab, factor * grad_vocab, base * vocab_spread()
    )
    gains_new, gains_moment, gains_average = update(
        gains, mom_gains, avg_gains, factor * grad_gain, base * 0.1
    )
    return (
        layer_new,
        layer_moment,
        layer_average,
        layer_new.astype(bf16),
        vocab_new,
        vocab_moment,
        vocab_average,
        vocab_new.astype(bf16),
        gains_new,
        gains_moment,
        gains_average,
        gains_new.astype(bf16),
        loss,
        grad_norm,
    )


def solution(mesh):
    in_specs = (
        P("ctx"),
        P("ctx"),
        P("ctx"),
        P(),
        P("ctx", "head"),
        P("ctx", "head"),
        P("ctx", None),
        P("ctx", "head"),
        P("ctx", "head"),
        P("ctx", None),
        P("ctx", "head"),
        P("ctx", "head"),
        P("ctx", None),
    )
    out_specs = (
        P("ctx", "head"),
        P("ctx", "head"),
        P("ctx", "head"),
        P("ctx", "head"),
        P("ctx", "head"),
        P("ctx", "head"),
        P("ctx", "head"),
        P("ctx", "head"),
        P("ctx", None),
        P("ctx", None),
        P("ctx", None),
        P("ctx", None),
        P(),
        P(),
    )
    return jax.shard_map(local, mesh=mesh, in_specs=in_specs, out_specs=out_specs, check_vma=False)
```

profile of v0, /device:TPU:0, one launch (start us, length us, event | category | flops | bytes accessed | tf_op | source)
XLA Modules:
  0.0 3085.3 jit_solution(16151892121469663935)
XLA Ops:
  7.2 16.9 copy.201
  24.1 8.7 convert_element_type.296
  33.5 311.4 %all-gather.10.cloned.1.call-done = bf16[2048,16000]{0,1:T(8,128)(2,1)} async-done(((bf16[256,16000]{0,1:T(8,128)(2,1)}), bf16[2048,16000]{0,1:T(8,128)(2,1)}) %all-gather.10.cloned.1.call-update) | async-done | bytes 65536016 | tf_op jit(solution)/shard_map/all_gather | solution.py:156
  344.9 22.7 slice.1746
  367.5 10.5 gather_fusion
  379.3 4.4 convert_element_type.301
  385.7 8.8 all_gather.34
  395.1 35.6 %all-reduce.18.cloned.1.call-done = bf16[256,2048]{1,0:T(8,128)(2,1)} async-done(((bf16[256,2048]{1,0:T(8,128)(2,1)}), bf16[256,2048]{1,0:T(8,128)(2,1)}) %all-reduce.18.cloned.1.call-update) | async-done | bytes 1048592 | tf_op jit(solution)/shard_map/psum | solution.py:170
  432.2 112.1 %all-gather.12.cloned.1.call-done = bf16[2048,5376]{1,0:T(8,128)(2,1)} async-done(((bf16[256,5376]{1,0:T(8,128)(2,1)}), bf16[2048,5376]{1,0:T(8,128)(2,1)}) %all-gather.12.cloned.1.call-update) | async-done | bytes 22020112 | tf_op jit(solution)/shard_map/all_gather | solution.py:155
  550.4 10.0 all_gather.36
  560.5 125.8 %while.97 = (s32[]{:T(128)}, f32[4,8,64]{2,1,0:T(8,128)S(1)}, f32[4,8,64]{2,1,0:T(8,128)S(1)}, s32[8,2]{1,0:T(8,128)S(1)}, s32[1]{0:T(128)}, /*index=5*/bf16[8,4...) while((s32[]{:T(128)}, f32[4,8,64]{2,1,0:T(8,128)S(1)}, ...), condition=%wide.region_35.36_spmd, body=%wide.region_2.35_spmd.sunk | while | flops 34907160 | bytes 3867729 | solution.py:219
  686.4 77.1 %while.98 = (s32[]{:T(128)}, f32[4,8,64,64]{3,2,1,0:T(8,128)S(1)}, s32[8,2]{1,0:T(8,128)S(1)}, s32[1]{0:T(128)}, bf16[8,4,64,128]{3,2,1,0:T(8,128)(2,1)S(1)}, /*...) while((s32[]{:T(128)}, f32[4,8,64,64]{3,2,1,0:T(8,128)S(1)}, ...), condition=%wide.region_54.55_spmd, body=%wide.region_37.54_spmd.sunk | while | flops 68453392 | bytes 10003377 | solution.py:245
  768.3 66.1 %all-reduce.20.cloned.1.call-done = bf16[256,2048]{1,0:T(8,128)(2,1)} async-done(((bf16[256,2048]{1,0:T(8,128)(2,1)}), bf16[256,2048]{1,0:T(8,128)(2,1)}) %all-reduce.20.cloned.1.call-update) | async-done | bytes 1048592 | tf_op jit(solution)/shard_map/psum | solution.py:248
  836.2 6.4 fusion.438
  844.7 5.7 fusion.451
  850.5 9.1 all-gather.3
  860.2 41.4 %all-reduce.22.cloned.1.call-done = bf16[256,2048]{1,0:T(8,128)(2,1)} async-done(((bf16[256,2048]{1,0:T(8,128)(2,1)}), bf16[256,2048]{1,0:T(8,128)(2,1)}) %all-reduce.22.cloned.1.call-update) | async-done | bytes 1048592 | tf_op jit(solution)/shard_map/psum | solution.py:260
  903.5 18.5 fusion.534
  921.9 5.1 select_reduce_fusion
  927.0 9.3 all-gather.5
  936.3 7.9 all-gather.6
  944.2 9.2 all-gather.4
  955.0 17.9 fusion.448
  973.4 6.1 copy.219
  979.5 16.9 copy.221
  996.4 17.0 copy.223
  1013.4 6.1 copy.218
  1028.4 5.0 fusion.487
  1035.0 8.4 fusion.445
  1043.7 18.0 convolution_convert_fusion
  1063.0 31.7 %all-reduce.26.cloned.1.call-done = bf16[256,2048]{1,0:T(8,128)(2,1)} async-done(((bf16[256,2048]{1,0:T(8,128)(2,1)}), bf16[256,2048]{1,0:T(8,128)(2,1)}) %all-reduce.26.cloned.1.call-update) | async-done | bytes 1048592 | tf_op jit(solution)/shard_map/psum | solution.py:288
  1107.2 350.8 %while.100 = (s32[]{:T(128)}, f32[4,64,8,64]{3,1,2,0:T(8,128)}, bf16[8,4,64,128]{3,2,1,0:T(8,128)(2,1)}, s32[8,2]{1,0:T(8,128)S(1)}, s32[1]{0:T(128)}, /*index=5...) while((s32[]{:T(128)}, f32[4,64,8,64]{3,1,2,0:T(8,128)}, ...), condition=%wide.region_85.86_spmd, body=%wide.region_68.85_spmd.sunk | while | flops 170320912 | bytes 24750540 | solution.py:334
  1148.7 4.0 conditional.71
  1161.5 3.9 conditional.64
  1234.5 4.0 conditional.71
  1278.0 4.0 conditional.71
  1321.6 4.0 conditional.71
  1365.2 4.0 conditional.71
  1378.0 3.9 conditional.64
  1460.2 8.3 convolution_convert_fusion.1
  1468.5 15.2 copy.217
  1487.1 9.0 reduce-scatter.4.cloned.1.call-done
  1501.9 4.2 convolution_convert_fusion.2
  1510.8 43.1 %all-reduce.28.cloned.1.call-done = bf16[256,2048]{1,0:T(8,128)(2,1)} async-done(((bf16[256,2048]{1,0:T(8,128)(2,1)}), bf16[256,2048]{1,0:T(8,128)(2,1)}) %all-reduce.28.cloned.1.call-update) | async-done | bytes 1048592 | tf_op jit(solution)/shard_map/psum | solution.py:346
  1559.5 20.7 broadcast_in_dim.409
  1580.2 50.8 %scatter_fusion = f32[8001,2048]{1,0:T(8,128)} fusion(f32[8001,2048]{1,0:T(8,128)} %broadcast_in_dim.409, s32[256]{0:T(256)S(1)} %copy-done.51, f32[256,2048]{1,0:T(8,128)S(1)} %copy-done.16), kind=kCustom, calls=%fused_computation.1 | custom fusion | flops 524288 | bytes 6292480 | tf_op jit(solution)/shard_map/scatter-add | solution.py:367
  1631.0 31.9 %fusion.431 = bf16[2048,8000]{0,1:T(8,128)(2,1)} fusion(f32[8001,2048]{1,0:T(8,128)} %scatter_fusion), kind=kLoop, calls=%fused_computation.658 | loop fusion | bytes 65536000 | tf_op jit(solution)/shard_map/transpose | solution.py:367
  1662.9 352.5 %concatenate.149 = bf16[2048,21379]{0,1:T(8,128)(2,1)} concatenate(bf16[2048,640]{0,1:T(8,128)(2,1)S(1)} %copy-done.13, bf16[2048,512]{0,1:T(8,128)(2,1)} %convolution_convert_fusion.4, bf16[2048,2816]{0,1:T(8,128)(2,1)} %copy.217, bf16[2048,1408]{0,1:T(8,128)(2,1)} %convolution_convert_fusion.2, bf16[2048,8000]{0,1:T(8,128)(2,1)} %convolution_convert_fusion, ...), dimensions={1} | concatenate | bytes 175136768 | tf_op jit(solution)/shard_map/concatenate | solution.py:370
  2015.4 850.0 %reduce_scatter.22 = bf16[256,21379]{0,1:T(8,128)(2,1)} reduce-scatter(bf16[2048,21379]{0,1:T(8,128)(2,1)} %concatenate.149), channel_id=1, replica_groups=mesh['ctx'=8,'head'=4] {'ctx'}, use_global_device_ids=true, dimensions={0}, to_apply=%region_93.94 | reduce-scatter | bytes 98514432 | tf_op jit(solution)/shard_map/reduce_scatter | solution.py:369
  2865.4 6.1 convert_element_type.331
  2871.5 5.5 multiply_reduce_fusion
  2881.8 6.2 copy.220
  2888.0 38.6 %all-reduce.10 = (f32[]{:T(128)}, f32[]{:T(128)}) all-reduce(f32[]{:T(128)S(6)} %add.903, f32[]{:T(128)S(6)} %div.118), channel_id=1, replica_groups=mesh['ctx'=8,'head'=4] {'ctx','head'}, use_global_device_ids=true, to_apply=%region_97.98 | all-reduce | flops 2 | bytes 16 | tf_op jit(solution)/shard_map/psum | solution.py:380
  2928.7 29.8 fusion.519
  2958.5 16.9 copy.228
  2975.4 17.5 add_multiply_fusion
  2992.9 16.9 copy.230
  3009.8 16.9 copy.229
  3026.6 11.6 copy.231
  3038.3 9.9 fusion.520
  3048.2 6.1 copy.224
  3054.2 7.3 add_multiply_fusion.1
  3061.6 6.1 copy.226
  3067.7 6.1 copy.225
  (1847 shorter events, 677.3 us)
Async XLA Ops:
  7.2 337.7 %all-gather.10.cloned.1.call-start = ((), (), s32[]{:S(2)}) async-start(), calls=%async_computation.2 | async-start | bytes 73728000 | tf_op jit(solution)/shard_map/all_gather | solution.py:156
  32.8 397.9 %all-reduce.18.cloned.1.call-start = ((), (), s32[]{:S(2)}) async-start(), calls=%async_computation.3 | async-start | bytes 2097152 | tf_op jit(solution)/shard_map/psum | solution.py:170
  379.2 165.1 %all-gather.12.cloned.1.call-start = ((), (), s32[]{:S(2)}) async-start(), calls=%async_computation.4 | async-start | bytes 24772608 | tf_op jit(solution)/shard_map/all_gather | solution.py:155
  383.7 450.8 %all-reduce.20.cloned.1.call-start = ((), (), s32[]{:S(2)}) async-start(), calls=%async_computation.5 | async-start | bytes 2097152 | tf_op jit(solution)/shard_map/psum | solution.py:248
  394.4 153.7 %copy-start.57 = (f32[32]{0:T(128)}, f32[32]{0:T(128)S(1)}, u32[]{:S(2)}) copy-start(f32[32]{0:T(128)S(1)} %multiply_add_fusion.14) | copy-start | bytes 388
  395.1 153.0 %copy-start.47 = (f32[256]{0:T(256)}, f32[256]{0:T(256)S(1)}, u32[]{:S(2)}) copy-start(f32[256]{0:T(256)S(1)} %fusion.509) | copy-start | bytes 3076
  395.1 149.2 %copy-start.36 = (f32[2048,1]{0,1:T(1,128)}, f32[2048,1]{0,1:T(1,128)S(1)}, u32[]{:S(2)}) copy-start(f32[2048,1]{0,1:T(1,128)S(1)} %get-tuple-element.2405) | copy-start | bytes 24580
  395.1 702.5 %copy-start.34 = (f32[2048,1]{0,1:T(1,128)}, f32[2048,1]{0,1:T(1,128)S(1)}, u32[]{:S(2)}) copy-start(f32[2048,1]{0,1:T(1,128)S(1)} %get-tuple-element.2403) | copy-start | bytes 24580
  432.2 112.2 %copy-start.49 = (f32[256]{0:T(256)}, f32[256]{0:T(256)S(1)}, u32[]{:S(2)}) copy-start(f32[256]{0:T(256)S(1)} %fusion.471) | copy-start | bytes 3076
  432.2 112.1 %copy-start.40 = (f32[256]{0:T(256)}, f32[256]{0:T(256)S(1)}, u32[]{:S(2)}) copy-start(f32[256]{0:T(256)S(1)} %fusion.513) | copy-start | bytes 3076
  763.5 4.7 copy-start.20
  764.8 3.5 copy-start.28
  764.8 69.7 %copy-start.1 = (bf16[256,2048]{1,0:T(8,128)(2,1)S(1)}, bf16[256,2048]{1,0:T(8,128)(2,1)}, u32[]{:S(2)}) copy-start(bf16[256,2048]{1,0:T(8,128)(2,1)} %all-reduce.18.cloned.1.call-done) | copy-start | bytes 3145732
  768.3 133.4 %all-reduce.22.cloned.1.call-start = ((), (), s32[]{:S(2)}) async-start(), calls=%async_computation.6 | async-start | bytes 2097152 | tf_op jit(solution)/shard_map/psum | solution.py:260
  836.2 261.5 %copy-start.39 = (f32[256]{0:T(256)}, f32[256]{0:T(256)S(1)}, u32[]{:S(2)}) copy-start(f32[256]{0:T(256)S(1)} %fusion.514) | copy-start | bytes 3076
  844.6 5.7 copy-start.24
  844.6 5.8 copy-start.60
  844.6 15.6 copy-start.59
  850.4 172.7 %all-reduce.24.cloned.1.call-start = ((), (), s32[]{:S(2)}) async-start(), calls=%async_computation.7 | async-start | bytes 2097152 | tf_op jit(solution)/shard_map/psum | solution.py:280
  972.9 121.8 %all-reduce.26.cloned.1.call-start = ((), (), s32[]{:S(2)}) async-start(), calls=%async_computation.8 | async-start | bytes 2097152 | tf_op jit(solution)/shard_map/psum | solution.py:288
  1023.1 3.4 copy-start.9
  1023.1 3.4 copy-start.14
  1028.4 5.1 copy-start.17
  1043.4 452.6 %reduce-scatter.4.cloned.1.call-start = ((), (), s32[]{:S(2)}) async-start(), calls=%async_computation.9 | async-start | bytes 589824 | tf_op jit(solution)/shard_map/reduce_scatter | solution.py:337
  1094.7 3.0 copy-start.15
  1094.7 3.0 copy-start.21
  1107.2 8.1 copy-start.53
  1147.4 10.0 copy-start.54
  1157.3 8.2 copy-start.53
  1193.6 5.9 copy-start.54
  1199.5 4.9 copy-start.53
  1233.1 10.0 copy-start.54
  1243.0 4.9 copy-start.53
  1276.7 10.0 copy-start.54
  1286.6 4.9 copy-start.53
  1320.2 10.0 copy-start.54
  1330.2 4.9 copy-start.53
  1363.8 10.0 copy-start.54
  1373.8 8.2 copy-start.53
  1410.0 5.9 copy-start.54
  1415.9 8.2 copy-start.53
  1452.1 5.9 copy-start.54
  1460.1 93.8 %all-reduce.28.cloned.1.call-start = ((), (), s32[]{:S(2)}) async-start(), calls=%async_computation.10 | async-start | bytes 2097152 | tf_op jit(solution)/shard_map/psum | solution.py:346
  1468.5 15.3 copy-start.43
  1468.5 15.3 copy-start.5
  1483.7 3.2 copy-start.31
  1483.7 3.2 copy-start.33
  1485.1 11.9 copy-start.48
  1485.1 11.9 copy-start.58
  1497.9 3.9 copy-start.18
  1497.9 3.9 copy-start.25
  1501.9 4.3 copy-start.42
  1501.9 4.3 copy-start.7
  1501.9 4.3 copy-start.29
  1510.8 45.6 %copy-start.50 = (f32[256]{0:T(256)S(1)}, f32[256]{0:T(256)}, u32[]{:S(2)}) copy-start(f32[256]{0:T(256)} %copy-done.49) | copy-start | bytes 3076
  1559.5 20.7 copy-start.16
  1559.5 20.7 copy-start.51
  1631.0 31.9 %copy-start.13 = (bf16[2048,640]{0,1:T(8,128)(2,1)S(1)}, bf16[2048,640]{0,1:T(8,128)(2,1)}, u32[]{:S(2)}) copy-start(bf16[2048,640]{0,1:T(8,128)(2,1)} %convolution_convert_fusion.3) | copy-start | bytes 7864324
  2871.5 7.7 copy-start
  2881.8 45.6 %copy-start.46 = (f32[256,3]{0,1:T(4,128)S(1)}, f32[256,3]{0,1:T(4,128)}, u32[]{:S(2)}) copy-start(f32[256,3]{0,1:T(4,128)} %param.155) | copy-start | bytes 9220
  2881.8 45.6 %copy-start.56 = (f32[256,3]{0,1:T(4,128)S(1)}, f32[256,3]{0,1:T(4,128)}, u32[]{:S(2)}) copy-start(f32[256,3]{0,1:T(4,128)} %param.158) | copy-start | bytes 9220
  2881.8 46.9 %copy-start.35 = (f32[16000]{0:T(1024)S(1)}, f32[16000]{0:T(1024)}, u32[]{:S(2)}) copy-start(f32[16000]{0:T(1024)} %select_multiply_fusion) | copy-start | bytes 192004
  2928.7 147.9 %copy-start.44 = (f32[256,3]{0,1:T(4,128)}, f32[256,3]{0,1:T(4,128)S(1)}, u32[]{:S(2)}) copy-start(f32[256,3]{0,1:T(4,128)S(1)} %get-tuple-element.2287) | copy-start | bytes 9220
  3026.6 11.6 copy-start.38
  (35 other events, 50.6 us)
Sparse Core Ops, SparseCore 0:
  32.9 311.8 all-gather.9
  379.3 51.3 all-reduce.17
  433.2 111.1 all-gather.11
  768.4 66.0 all-reduce.19
  850.5 51.1 all-reduce.21
  973.0 50.0 all-reduce.23
  1043.6 51.1 all-reduce.25
  1460.3 35.7 reduce-scatter.3
  1502.0 51.8 all-reduce.27
where the time goes:
time: 3120 us; the launch traced here: 3090 us
  blocking collectives  943 us (30%)
  local copies, waits for them, and re-layouts  931 us (30%)
  waiting for transfers between devices  652 us (21%)
  other arithmetic  211 us (7%)
  matrix products  175 us (6%)
  loops' own time  151 us (5%)
    reduce_scatter x1, blocking collectives, local(): lax.psum_scatter(jnp.concatenate(parts, axis=1).astype(jnp.bfloat16), 'ct...  850 us
    concatenate x1, local copies, waits for them, and re-layouts, local(): jnp.concatenate(parts, axis=1).astype(jnp.bfloat16)  353 us
    all_gather x1, waiting for transfers between devices, local(): lax.all_gather(vocab_send, 'ctx', axis=0, tiled=True)  311 us
    unnamed x136, local copies, waits for them, and re-layouts  161 us
    all_gather x1, waiting for transfers between devices, local(): lax.all_gather(w_layer.astype(bf16), 'ctx', axis=0, tiled=True)  112 us
    scatter x64, local copies, waits for them, and re-layouts, back_step(): dq = dq.at[b].set(new[0])  68.9 us
    psum x1, waiting for transfers between devices, local(): lax.psum(contract_first(attn_b, w_out).astype(jnp.bfloat16), 'head')  66.1 us
  transfers between devices with their start and end apart: 9, of which 9 were waited for; matrix products, arithmetic and copies ran while one was open for 4% of the time, Pallas kernels for 0%

commit v1 on v0

v1 whole, which is shorter than its diff:
```python
import functools
import math

import jax
import jax.numpy as jnp
import numpy as np
from jax import lax
from jax.experimental import pallas as pl
from jax.experimental.pallas import tpu as pltpu
from jax.sharding import PartitionSpec as P

D = 2048
HEADS = 32
KV = 4
HD = 64
FF = 5632
V = 32000
SEQS = 2

eps = 1e-05
z_weight = 0.0001
momentum_rate = 0.5
average_rate = 0.5
clip_level = 0.01

GROUP = HEADS // KV
QG = GROUP * HD
FFG = FF // KV
VG = V // KV
ATTN_IN = QG + 2 * HD
NPARAM = D * (2 * HEADS * HD + 2 * KV * HD + 3 * FF + 2 * V + 3)
BASE = 1.5 * math.sqrt(NPARAM) / clip_level
EMB_AT = VG // 128 * 128
EMB_W = 2 * VG - EMB_AT
EMB_STEPS = 7
EMB_BLOCK = EMB_W // EMB_STEPS

f32 = jnp.float32
bf16 = jnp.bfloat16
NEG = -1e30


def dot_nn(a, b):
    return lax.dot_general(a, b, (((1,), (0,)), ((), ())), preferred_element_type=f32)


def dot_nt(a, b):
    return lax.dot_general(a, b, (((1,), (1,)), ((), ())), preferred_element_type=f32)


def dot_tn(a, b):
    return lax.dot_general(a, b, (((0,), (0,)), ((), ())), preferred_element_type=f32)


def cost(flops, nbytes, trans=0):
    return pl.CostEstimate(flops=int(flops), bytes_accessed=int(nbytes), transcendentals=int(trans))


def params(**kw):
    return pltpu.CompilerParams(vmem_limit_bytes=56 * 1024 * 1024, **kw)


def one_hot(ids, base, width):
    column = lax.broadcasted_iota(jnp.int32, (ids.shape[0], width), 1) + base
    return jnp.where(ids == column, jnp.float32(1.0), jnp.float32(0.0)).astype(bf16)


def lookup_kernel(rows, ids_ref, w_ref, out_ref, acc_ref):
    step = pl.program_id(0)
    w = w_ref[...].astype(bf16)
    total = ids_ref.shape[0]

    @pl.when(step == 0)
    def _():
        acc_ref[...] = jnp.zeros_like(acc_ref)

    for r in range(0, total, rows):
        part = pl.ds(r, rows)
        acc_ref[part, :] += dot_nt(one_hot(ids_ref[part, :], step * EMB_BLOCK, EMB_BLOCK), w)

    @pl.when(step == EMB_STEPS - 1)
    def _():
        out_ref[...] = acc_ref[...].astype(bf16)


def lookup(ids, w_vocab):
    total, rows = ids.shape[0], w_vocab.shape[0]
    return pl.pallas_call(
        functools.partial(lookup_kernel, min(512, total)),
        grid=(EMB_STEPS,),
        in_specs=[
            pl.BlockSpec((total, 1), lambda i: (0, 0)),
            pl.BlockSpec((pl.Element(rows), pl.Element(EMB_BLOCK)), lambda i: (0, (EMB_AT // 128 + EMB_BLOCK // 128 * i) * 128)),
        ],
        out_specs=pl.BlockSpec((total, rows), lambda i: (0, 0)),
        out_shape=jax.ShapeDtypeStruct((total, rows), bf16),
        scratch_shapes=[pltpu.VMEM((total, rows), f32)],
        compiler_params=params(),
        cost_estimate=cost(2 * total * rows * EMB_W, rows * EMB_W * 4),
        name="embed_lookup",
    )(ids, w_vocab)


def embed_grad_kernel(rows, ids_ref, dxt_ref, out_ref, sq_ref):
    step = pl.program_id(0)
    total = ids_ref.shape[0]
    acc = jnp.zeros(out_ref.shape, f32)
    for r in range(0, total, rows):
        hot = one_hot(ids_ref[pl.ds(r, rows), :], step * EMB_BLOCK, EMB_BLOCK)
        acc = acc + dot_nn(dxt_ref[:, pl.ds(r, rows)], hot)
    out_ref[...] = acc.astype(bf16)
    square = acc * acc
    lanes = sum(square[:, k : k + 128] for k in range(0, EMB_BLOCK, 128))
    part = sum(lanes[k : k + 8] for k in range(0, lanes.shape[0], 8))

    @pl.when(step == 0)
    def _():
        sq_ref[...] = jnp.zeros_like(sq_ref)

    sq_ref[...] += part


def embed_grad(ids, dxt):
    rows, total = dxt.shape
    return pl.pallas_call(
        functools.partial(embed_grad_kernel, min(512, total)),
        grid=(EMB_STEPS,),
        in_specs=[
            pl.BlockSpec((total, 1), lambda i: (0, 0)),
            pl.BlockSpec((rows, total), lambda i: (0, 0)),
        ],
        out_specs=[
            pl.BlockSpec((rows, EMB_BLOCK), lambda i: (0, i)),
            pl.BlockSpec((8, 128), lambda i: (0, 0)),
        ],
        out_shape=[
            jax.ShapeDtypeStruct((rows, EMB_W), bf16),
            jax.ShapeDtypeStruct((8, 128), f32),
        ],
        compiler_params=params(),
        cost_estimate=cost(2 * total * rows * EMB_W, rows * EMB_W * 2),
        name="embed_grad",
    )(ids, dxt)


def partner(x):
    width = x.shape[1]
    lane = lax.broadcasted_iota(jnp.int32, x.shape, 1)
    return jnp.where(lane % HD < HD // 2, pltpu.roll(x, width - HD // 2, 1), pltpu.roll(x, HD // 2, 1))


def qkv_kernel(a_ref, w_ref, cos_ref, sin_ref, q_ref, kv_ref):
    raw = dot_nn(a_ref[...], w_ref[...])
    cosine, sine = cos_ref[...], sin_ref[...]
    for j in range(0, QG, 128):
        x = raw[:, j : j + 128]
        rot = (x * cosine + partner(x) * sine).astype(bf16)
        q_ref[:, j : j + 128] = rot * jnp.asarray(HD**-0.5, bf16)
    x = raw[:, QG:]
    lane = lax.broadcasted_iota(jnp.int32, x.shape, 1)
    kv_ref[...] = jnp.where(lane < HD, x * cosine + partner(x) * sine, x).astype(bf16)


def qkv(a1, w_in, cosine, sine):
    tok = a1.shape[0]
    return pl.pallas_call(
        qkv_kernel,
        out_shape=[
            jax.ShapeDtypeStruct((tok, QG), bf16),
            jax.ShapeDtypeStruct((tok, 2 * HD), bf16),
        ],
        compiler_params=params(),
        cost_estimate=cost(2 * tok * D * ATTN_IN, 2 * D * ATTN_IN + 2 * tok * D),
        name="qkv",
    )(a1, w_in, cosine, sine)


def split_kv(kv_ref, parts_ref):
    kv = kv_ref[...].reshape(-1, 2 * HD).astype(f32)
    lane = lax.broadcasted_iota(jnp.int32, kv.shape, 1)
    swapped = pltpu.roll(kv, HD, 1)
    zero = jnp.zeros_like(kv)
    low = lane < HD
    parts_ref[0] = jnp.where(low, kv, zero).astype(bf16)
    parts_ref[1] = jnp.where(low, zero, swapped).astype(bf16)
    parts_ref[2] = jnp.where(low, swapped, zero).astype(bf16)
    parts_ref[3] = jnp.where(low, zero, kv).astype(bf16)


def attn_kernel(q_ref, kv_ref, qpos_ref, kpos_ref, o_ref, parts_ref):
    @pl.when(pl.program_id(1) == 0)
    def _():
        split_kv(kv_ref, parts_ref)

    q = q_ref[...]
    allowed = kpos_ref[...] <= qpos_ref[...]
    out = None
    for g in range(2):
        s = jnp.where(allowed, dot_nt(q, parts_ref[g]), NEG)
        p = jnp.exp(s - jnp.max(s, axis=1, keepdims=True))
        p = p * (1.0 / jnp.sum(p, axis=1, keepdims=True))
        part = dot_nn(p.astype(bf16), parts_ref[2 + g])
        out = part if out is None else out + part
    o_ref[...] = out.astype(bf16)


def attn(q, kv_every, qpos, kpos):
    n_ctx, _, seq_tok, _ = kv_every.shape
    keys = n_ctx * seq_tok
    pairs = QG // 128
    return pl.pallas_call(
        attn_kernel,
        grid=(SEQS, pairs),
        in_specs=[
            pl.BlockSpec((seq_tok, 128), lambda s, p: (s, p)),
            pl.BlockSpec((n_ctx, 1, seq_tok, 2 * HD), lambda s, p: (0, s, 0, 0)),
            pl.BlockSpec((seq_tok, 1), lambda s, p: (0, 0)),
            pl.BlockSpec((1, keys), lambda s, p: (0, 0)),
        ],
        out_specs=pl.BlockSpec((seq_tok, 128), lambda s, p: (s, p)),
        out_shape=jax.ShapeDtypeStruct((SEQS * seq_tok, QG), bf16),
        scratch_shapes=[pltpu.VMEM((4, keys, 2 * HD), bf16)],
        compiler_params=params(),
        cost_estimate=cost(
            8 * SEQS * seq_tok * keys * QG, 4 * SEQS * seq_tok * QG, SEQS * GROUP * seq_tok * keys
        ),
        name="attn_fwd",
    )(q, kv_every, qpos.reshape(seq_tok, 1), kpos.reshape(1, keys))


def attn_back_kernel(
    pairs, q_ref, do_ref, kv_ref, qpos_ref, kpos_ref, cos_ref, sin_ref, dq_ref, dkv_ref, parts_ref, acc_ref
):
    pair = pl.program_id(1)

    @pl.when(pair == 0)
    def _():
        split_kv(kv_ref, parts_ref)
        acc_ref[...] = jnp.zeros_like(acc_ref)

    q = q_ref[...]
    do = do_ref[...]
    allowed = kpos_ref[...] <= qpos_ref[...]
    dq = None
    for g in range(2):
        s = jnp.where(allowed, dot_nt(parts_ref[g], q), NEG)
        p = jnp.exp(s - jnp.max(s, axis=0, keepdims=True))
        p = p * (1.0 / jnp.sum(p, axis=0, keepdims=True))
        dp = dot_nt(parts_ref[2 + g], do)
        delta = jnp.sum(p * dp, axis=0, keepdims=True)
        ds = (p * (dp - delta)).astype(bf16)
        part = dot_tn(ds, parts_ref[g])
        dq = part if dq is None else dq + part
        acc_ref[g] += dot_nn(ds, q)
        acc_ref[2 + g] += dot_nn(p.astype(bf16), do)
    dq = dq * (HD**-0.5)
    dq_ref[...] = (dq * cos_ref[...] - partner(dq) * sin_ref[...]).astype(bf16)

    @pl.when(pair == pairs - 1)
    def _():
        lane = lax.broadcasted_iota(jnp.int32, acc_ref.shape[1:], 1)
        grad_k = acc_ref[0] + pltpu.roll(acc_ref[1], HD, 1)
        grad_v = pltpu.roll(acc_ref[2], HD, 1) + acc_ref[3]
        dkv_ref[...] = jnp.where(lane < HD, grad_k, grad_v).astype(bf16).reshape(dkv_ref.shape)


def attn_back(q, do, kv_every, qpos, kpos, cosine, sine):
    n_ctx, _, seq_tok, _ = kv_every.shape
    keys = n_ctx * seq_tok
    pairs = QG // 128
    return pl.pallas_call(
        functools.partial(attn_back_kernel, pairs),
        grid=(SEQS, pairs),
        in_specs=[
            pl.BlockSpec((seq_tok, 128), lambda s, p: (s, p)),
            pl.BlockSpec((seq_tok, 128), lambda s, p: (s, p)),
            pl.BlockSpec((n_ctx, 1, seq_tok, 2 * HD), lambda s, p: (0, s, 0, 0)),
            pl.BlockSpec((1, seq_tok), lambda s, p: (0, 0)),
            pl.BlockSpec((keys, 1), lambda s, p: (0, 0)),
            pl.BlockSpec((seq_tok, 128), lambda s, p: (s, 0)),
            pl.BlockSpec((seq_tok, 128), lambda s, p: (s, 0)),
        ],
        out_specs=[
            pl.BlockSpec((seq_tok, 128), lambda s, p: (s, p)),
            pl.BlockSpec((n_ctx, 1, seq_tok, 2 * HD), lambda s, p: (0, s, 0, 0)),
        ],
        out_shape=[
            jax.ShapeDtypeStruct((SEQS * seq_tok, QG), bf16),
            jax.ShapeDtypeStruct(kv_every.shape, bf16),
        ],
        scratch_shapes=[
            pltpu.VMEM((4, keys, 2 * HD), bf16),
            pltpu.VMEM((4, keys, 2 * HD), f32),
        ],
        compiler_params=params(),
        cost_estimate=cost(
            20 * SEQS * seq_tok * keys * QG, 8 * SEQS * seq_tok * QG, SEQS * GROUP * seq_tok * keys
        ),
        name="attn_bwd",
    )(q, do, kv_every, qpos.reshape(1, seq_tok), kpos.reshape(keys, 1), cosine, sine)


def kv_back_kernel(parts_ref, cos_ref, sin_ref, out_ref):
    x = parts_ref[0].astype(f32)
    for k in range(1, parts_ref.shape[0]):
        x = x + parts_ref[k].astype(f32)
    lane = lax.broadcasted_iota(jnp.int32, x.shape, 1)
    out_ref[...] = jnp.where(lane < HD, x * cos_ref[...] - partner(x) * sin_ref[...], x).astype(bf16)


def kv_back(parts, cosine, sine):
    return pl.pallas_call(
        kv_back_kernel,
        out_shape=jax.ShapeDtypeStruct(parts.shape[1:], bf16),
        compiler_params=params(),
        name="kv_bwd",
    )(parts, cosine, sine)


def update_piece(factor, rate, grad, w_ref, m_ref, a_ref, outs, columns):
    new_ref, moment_ref, average_ref, copy_ref = outs
    grad = factor * grad
    moment = momentum_rate * m_ref[:, columns] + grad
    new = w_ref[:, columns] - rate * (grad + momentum_rate * moment)
    new_ref[:, columns] = new
    moment_ref[:, columns] = moment
    average_ref[:, columns] = average_rate * a_ref[:, columns] + (1.0 - average_rate) * new
    copy_ref[:, columns] = new.astype(bf16)


def layer_update_kernel(spreads, factor_ref, *refs):
    grads, (w_ref, m_ref, a_ref), outs = refs[:-7], refs[-7:-4], refs[-4:]
    factor = factor_ref[0, 0]
    for source, inner, outer, width, spread in spreads:
        grad = grads[source][:, inner : inner + width].astype(f32)
        update_piece(factor, BASE * spread, grad, w_ref, m_ref, a_ref, outs, slice(outer, outer + width))


def vocab_update_kernel(part, factor_ref, head_ref, embed_ref, w_ref, m_ref, a_ref, *outs):
    factor = factor_ref[0, 0]
    head_rate = BASE * 2.0 * D**-0.5
    for k in range(head_ref.shape[0]):
        low, high = k * part, min((k + 1) * part, EMB_AT)
        if low >= high:
            continue
        grad = head_ref[k, :, : high - low].astype(f32)
        update_piece(factor, head_rate, grad, w_ref, m_ref, a_ref, outs, slice(low, high))
    edge = EMB_AT - EMB_AT // part * part
    grad_head = head_ref[EMB_AT // part, :, edge : edge + 128].astype(f32)
    grad_embed = embed_ref[:, :128].astype(f32)
    own = lax.broadcasted_iota(jnp.int32, grad_head.shape, 1) < VG - EMB_AT
    update_piece(
        factor,
        jnp.where(own, head_rate, BASE),
        jnp.where(own, grad_head, grad_embed),
        w_ref,
        m_ref,
        a_ref,
        outs,
        slice(EMB_AT, EMB_AT + 128),
    )
    for low in range(128, EMB_W, 1024):
        high = min(low + 1024, EMB_W)
        grad = embed_ref[:, low:high].astype(f32)
        update_piece(factor, BASE, grad, w_ref, m_ref, a_ref, outs, slice(EMB_AT + low, EMB_AT + high))


def call_update(kernel, factor, grads, grad_specs, w, m, a, rows, name):
    total, width = w.shape
    block = pl.BlockSpec((rows, width), lambda i: (i, 0))
    return pl.pallas_call(
        kernel,
        grid=(total // rows,),
        in_specs=[pl.BlockSpec(memory_space=pltpu.SMEM)] + grad_specs + [block] * 3,
        out_specs=[block] * 4,
        out_shape=[jax.ShapeDtypeStruct(w.shape, f32)] * 3 + [jax.ShapeDtypeStruct(w.shape, bf16)],
        compiler_params=params(),
        cost_estimate=cost(10 * total * width, 28 * total * width),
        name=name,
    )(factor.reshape(1, 1), *grads, w, m, a)


def norm_parts(x):
    scale = lax.rsqrt(jnp.mean(x * x, axis=-1, keepdims=True) + eps)
    return x * scale, scale


def norm_back(dy, unit, scale, gain):
    scaled = dy * gain
    dx = scale * (scaled - unit * jnp.mean(scaled * unit, axis=-1, keepdims=True))
    return dx, jnp.sum(dy * unit, axis=0)


def local(
    token_ids,
    labels,
    answer_mask,
    pair_map,
    w_layer,
    w_vocab,
    gains,
    mom_layer,
    mom_vocab,
    mom_gains,
    avg_layer,
    avg_vocab,
    avg_gains,
):
    n_ctx = lax.axis_size("ctx")
    n_head = lax.axis_size("head")
    place = lax.axis_index("ctx")
    shard = lax.axis_index("head")
    tok = token_ids.shape[0]
    rows = w_layer.shape[0]
    seq_tok = tok // SEQS
    span = seq_tok // 2
    chunk = seq_tok // n_head
    own = SEQS * chunk
    length = n_ctx * seq_tok
    part = -(-VG // (n_ctx * 128)) * 128

    def turn(x, axis):
        return lax.dynamic_slice_in_dim(
            jnp.concatenate([x, x], axis), shard * chunk, seq_tok, axis
        )

    def turn_back(x, axis):
        return lax.dynamic_slice_in_dim(
            jnp.concatenate([x, x], axis), seq_tok - shard * chunk, seq_tok, axis
        )

    def head_scatter(x):
        sums = x[:, 0].astype(f32)
        for s in range(1, n_head):
            sent = lax.ppermute(x[:, s], "head", [(i, (i + s) % n_head) for i in range(n_head)])
            sums = sums + sent.astype(f32)
        return sums

    def head_gather(x):
        pieces = [x]
        for s in range(1, n_head):
            pieces.append(lax.ppermute(x, "head", [(i, (i - s) % n_head) for i in range(n_head)]))
        return jnp.stack(pieces, axis=1)

    def sum_own(partial):
        split = partial.astype(bf16).reshape(SEQS, n_head, chunk, D)
        return head_scatter(split).reshape(own, D)

    def spread_all(x):
        return head_gather(x.astype(bf16).reshape(SEQS, chunk, D)).reshape(tok, D)

    every = lax.all_gather(jnp.stack([token_ids, labels, answer_mask]), "ctx", axis=1)
    every = every.reshape(3, n_ctx, SEQS, seq_tok)
    turned = turn(every, 3)
    ids_all, labels_all, mask_all = (turned[k].reshape(n_ctx * tok) for k in range(3))
    count = jnp.sum(every[2].astype(f32))

    layer_b = w_layer.astype(bf16)
    ends = np.cumsum([0, ATTN_IN, QG, 2 * FFG, FFG])
    w_in, w_out, w_gu, w_down = (
        lax.all_gather(layer_b[:, ends[k] : ends[k + 1]], "ctx", axis=0, tiled=True) for k in range(4)
    )
    gain_rows = lax.all_gather(gains.astype(bf16).T, "ctx", axis=1, tiled=True).astype(f32)
    head_b = jnp.pad(w_vocab[:, :VG].astype(bf16), ((0, 0), (0, n_ctx * part - VG)))
    w_head = lax.all_to_all(
        head_b.reshape(rows, n_ctx, part).transpose(1, 0, 2), "ctx", 0, 0, tiled=True
    ).reshape(D, part)

    offset_id = shard * VG
    local_ids = ids_all - offset_id
    inside = (local_ids >= 0) & (local_ids < VG)
    slots = jnp.where(inside, local_ids + (VG - EMB_AT), -1).reshape(-1, 1)
    picked = lookup(slots, w_vocab).reshape(n_ctx * SEQS, n_head, chunk, rows)
    picked = head_scatter(picked).astype(bf16).reshape(n_ctx * own, rows)
    x0 = lax.all_to_all(picked, "ctx", 0, 1, tiled=True).astype(f32)

    unit0, scale0 = norm_parts(x0)
    a1 = spread_all(unit0 * gain_rows[0])
    row = (jnp.arange(seq_tok, dtype=jnp.int32) + shard * chunk) % seq_tok

    def positions(index):
        index = index[:, None]
        at = jnp.where(row // span == 0, index, 2 * n_ctx - 1 - index)
        return at * span + row % span

    qpos = positions(pair_map[place][None])[0]
    kpos = positions(pair_map).reshape(length)
    half = HD // 2
    inverse = 10000.0 ** (-2.0 * np.arange(half) / HD)
    ramp = np.clip((2048.0 * inverse / (2.0 * math.pi) - 1.0) / 31.0, 0.0, 1.0)
    freq = np.tile(((1.0 - ramp) * inverse / 4.0 + ramp * inverse).astype(np.float32), 128 // half)
    sign = np.where(np.arange(128) % HD < half, -1.0, 1.0).astype(np.float32)
    mscale = 0.1 * math.log(4.0) + 1.0
    angle = jnp.tile(qpos, SEQS).astype(f32)[:, None] * freq[None, :]
    cosine = jnp.cos(angle) * mscale
    sine = jnp.sin(angle) * (mscale * sign)[None, :]
    q, kv_own = qkv(a1, w_in, cosine, sine)
    kv_every = lax.all_gather(kv_own, "ctx").reshape(n_ctx, SEQS, seq_tok, 2 * HD)
    attn_b = attn(q, kv_every, qpos, kpos)
    x1 = x0 + sum_own(dot_nt(attn_b, w_out))

    unit1, scale1 = norm_parts(x1)
    a2 = spread_all(unit1 * gain_rows[1])
    gate_up = dot_nn(a2, w_gu)

    def glu(values):
        return jax.nn.silu(values[:, :FFG]) * values[:, FFG:]

    hidden_f, glu_back = jax.vjp(glu, gate_up)
    hidden_b = hidden_f.astype(bf16)
    x2 = x1 + sum_own(dot_nt(hidden_b, w_down))

    unit2, scale2 = norm_parts(x2)
    final_b = spread_all(unit2 * gain_rows[2])
    final_all = lax.all_gather(final_b, "ctx", axis=0, tiled=True)
    column = place * part + jnp.arange(part, dtype=jnp.int32)
    logits = jnp.where((column < VG)[None, :], dot_nn(final_all, w_head), NEG)
    row_top = jnp.max(logits, axis=-1)
    row_total = jnp.sum(jnp.exp(logits - row_top[:, None]), axis=-1)
    slot = jnp.where(column < VG, column + offset_id, -1)
    hit = slot[None, :] == labels_all[:, None]
    label_logit = jnp.sum(jnp.where(hit, logits, 0.0), axis=-1)

    def merge(stats):
        top = jnp.max(stats[:, 0], axis=0)
        total = jnp.sum(stats[:, 1] * jnp.exp(stats[:, 0] - top), axis=0)
        return jnp.stack([top, total, jnp.sum(stats[:, 2], axis=0)])

    stats = jnp.stack([row_top, row_total, label_logit])
    stats = merge(lax.all_gather(stats, "ctx"))
    stats = turn_back(stats.reshape(3, n_ctx * SEQS, seq_tok), 2)
    stats = merge(lax.all_gather(stats, "head"))
    lse = stats[0] + jnp.log(stats[1])
    valid = every[2].astype(f32).reshape(n_ctx * SEQS, seq_tok)
    loss = jnp.sum(valid * (lse - stats[2] + z_weight * lse * lse)) / count
    lse = turn(lse, 1).reshape(n_ctx * tok)
    weight = mask_all.astype(f32) / count
    soft = jnp.exp(logits - lse[:, None])
    dlog_b = (
        weight[:, None] * ((1.0 + 2.0 * z_weight * lse)[:, None] * soft - hit.astype(f32))
    ).astype(bf16)
    d_final = lax.psum_scatter(
        dot_nt(dlog_b, w_head).astype(bf16), "ctx", scatter_dimension=0, tiled=True
    )
    d_head = dot_tn(final_all, dlog_b)
    head_sq = jnp.sum(d_head * d_head)
    g_head = lax.all_to_all(d_head.astype(bf16).reshape(n_ctx, rows, part), "ctx", 0, 0, tiled=True)

    dx2, d_gain2 = norm_back(sum_own(d_final), unit2, scale2, gain_rows[2])
    dyf_b = spread_all(dx2)
    d_hidden = dot_nn(dyf_b, w_down)
    d_gate_up_b = glu_back(d_hidden)[0].astype(bf16)
    dx1_norm, d_gain1 = norm_back(sum_own(dot_nt(d_gate_up_b, w_gu)), unit1, scale1, gain_rows[1])
    dx1 = dx2 + dx1_norm
    dya_b = spread_all(dx1)
    d_attn_b = dot_nn(dya_b, w_out).astype(bf16)
    d_q, d_kv = attn_back(q, d_attn_b, kv_every, qpos, kpos, cosine, sine)
    d_kv = lax.all_to_all(d_kv.reshape(n_ctx, tok, 2 * HD), "ctx", 0, 0, tiled=True)
    d_raw_b = jnp.concatenate([d_q, kv_back(d_kv, cosine, sine)], axis=1)
    dx0_norm, d_gain0 = norm_back(sum_own(dot_nt(d_raw_b, w_in)), unit0, scale0, gain_rows[0])
    dx0 = dx1 + dx0_norm

    g_ff = lax.psum_scatter(
        jnp.concatenate([dot_tn(a2, d_gate_up_b), dot_tn(dyf_b, hidden_b)], axis=1).astype(bf16),
        "ctx",
        scatter_dimension=0,
        tiled=True,
    )
    g_at = lax.psum_scatter(
        jnp.concatenate([dot_tn(a1, d_raw_b), dot_tn(dya_b, attn_b)], axis=1).astype(bf16),
        "ctx",
        scatter_dimension=0,
        tiled=True,
    )
    extra = jnp.pad(jnp.stack([d_gain0, d_gain1, d_gain2]), ((0, 13), (0, 0)))
    moved = lax.all_to_all(jnp.concatenate([dx0, extra]).astype(bf16), "ctx", 1, 0, tiled=True)
    moved = moved.reshape(n_ctx, own + 16, rows)
    gain_part = jnp.sum(moved[:, own : own + 8].astype(f32), axis=0)
    gain_all = lax.all_gather(gain_part, "head")
    grad_gain = jnp.sum(gain_all, axis=0)[:3].T
    dx0_all = head_gather(moved[:, :own].reshape(n_ctx * SEQS, chunk, rows)).reshape(n_ctx * tok, rows)
    g_embed, embed_sq = embed_grad(slots, dx0_all.T)

    squares = (
        jnp.sum(jnp.square(g_ff.astype(f32)))
        + jnp.sum(jnp.square(g_at.astype(f32)))
        + head_sq
        + jnp.sum(embed_sq)
        + jnp.sum(grad_gain * grad_gain) / n_head
    )
    squares = jnp.sum(lax.all_gather(jnp.broadcast_to(squares, (8, 128)), "head"), axis=0)
    total_sq = jnp.sum(lax.all_gather(squares, "ctx"), axis=0)[0, 0]
    grad_norm = jnp.sqrt(total_sq)
    factor = jnp.minimum(1.0, clip_level / grad_norm)

    wide = 16
    spreads = (
        (1, 0, 0, ATTN_IN, D**-0.5),
        (1, ATTN_IN, ATTN_IN, QG, (length / (4.0 * HEADS * HD)) ** 0.5),
        (0, 0, ATTN_IN + QG, 2 * FFG, D**-0.5),
        (0, 2 * FFG, ATTN_IN + QG + 2 * FFG, FFG, FF**-0.5),
    )
    layer = call_update(
        functools.partial(layer_update_kernel, spreads),
        factor,
        (g_ff, g_at),
        [
            pl.BlockSpec((wide, g_ff.shape[1]), lambda i: (i, 0)),
            pl.BlockSpec((wide, g_at.shape[1]), lambda i: (i, 0)),
        ],
        w_layer,
        mom_layer,
        avg_layer,
        wide,
        "layer_update",
    )
    vocab = call_update(
        functools.partial(vocab_update_kernel, part),
        factor,
        (g_head, g_embed),
        [
            pl.BlockSpec((n_ctx, wide, part), lambda i: (0, i, 0)),
            pl.BlockSpec((wide, EMB_W), lambda i: (i, 0)),
        ],
        w_vocab,
        mom_vocab,
        avg_vocab,
        wide,
        "vocab_update",
    )
    grad = factor * grad_gain
    gains_moment = momentum_rate * mom_gains + grad
    gains_new = gains - BASE * 0.1 * (grad + momentum_rate * gains_moment)
    gains_average = average_rate * avg_gains + (1.0 - average_rate) * gains_new
    return (
        *layer,
        *vocab,
        gains_new,
        gains_moment,
        gains_average,
        gains_new.astype(bf16),
        loss,
        grad_norm,
    )


def solution(mesh):
    token, split, gain = P("ctx"), P("ctx", "head"), P("ctx", None)
    in_specs = (token, token, token, P()) + (split, split, gain) * 3
    out_specs = (split,) * 8 + (gain,) * 4 + (P(), P())
    return jax.shard_map(local, mesh=mesh, in_specs=in_specs, out_specs=out_specs, check_vma=False)
```

time: 3120 us -> 960 us (0.31)
  local copies, waits for them, and re-layouts: 931 us -> 48.8 us
  blocking collectives: 943 us -> 105 us
  waiting for transfers between devices: 652 us -> 413 us
  other arithmetic: 211 us -> 55.1 us
  loops' own time: 151 us -> 0 us
  Pallas kernels: 0 us -> 120 us
  starting transfers between devices: 1.01 us -> 92.1 us
  matrix products: 175 us -> 92.3 us
    reduce_scatter x1 -> x0, blocking collectives: 850 us -> none  [local(): lax.psum_scatter(jnp.concatenate(parts, axis=1).astype(jnp.bfloat16), 'ct...]
    all_gather x2 -> x5, waiting for transfers between devices: 423 us -> 0.05 us  [the longest x4 0.05 us: local(): lax.all_gather(layer_b[:, ends[k]:ends[k + 1]], 'ctx', axis=0, tiled=True)]
    concatenate x3 -> x1, local copies, waits for them, and re-layouts: 353 us -> 0.01 us  [local(): jnp.concatenate([dx0, extra]).astype(bf16)]
    psum x6 -> x0, waiting for transfers between devices: 220 us -> none  [the longest x1 66.1 us: local(): lax.psum(contract_first(attn_b, w_out).astype(jnp.bfloat16), 'head')]
    ppermute x0 -> x36, waiting for transfers between devices: none -> 187 us  [the longest x18 110 us: head_gather(): lax.ppermute(x, 'head', [(i, (i - s) % n_head) for i in range(n_head)])]
    another operation x196 -> x0, loops' own time: 151 us -> none  [the longest x1 32.3 us: local(): lax.scan(out_step, jnp.zeros((nblk, group, span, HD), f32), (kv_blocks, k...]
    unnamed x136 -> x127, local copies, waits for them, and re-layouts: 161 us -> 15.1 us
    reduce_scatter x1 -> x3, waiting for transfers between devices: 9 us -> 142 us  [the longest x1 72.9 us: local(): lax.psum_scatter(jnp.concatenate([dot_tn(a2, d_gate_up_b), dot_tn(dyf_b,...]
  transfers between devices with their start and end apart: 9 -> 49, of which waited for: 9 -> 26; matrix products, arithmetic and copies ran while one was open for 4% -> 13% of each run, Pallas kernels for 0% -> 6%
where the time goes in v1:
time: 960 us; the launch traced here: 949 us
  waiting for transfers between devices  413 us (43%)
  Pallas kernels  120 us (12%)
  blocking collectives  105 us (11%)
  matrix products  92.3 us (10%)
  starting transfers between devices  92.1 us (10%)
  other arithmetic  55.1 us (6%)
  local copies, waits for them, and re-layouts  48.8 us (5%)
  between operations  23.7 us (2%)
    ppermute x18, waiting for transfers between devices, head_gather(): lax.ppermute(x, 'head', [(i, (i - s) % n_head) for i in range(n_head)])  110 us
    ppermute x18, waiting for transfers between devices, head_scatter(): lax.ppermute(x[:, s], 'head', [(i, (i + s) % n_head) for i in range(n_hea...  77.6 us
    reduce_scatter x1, waiting for transfers between devices, local(): lax.psum_scatter(jnp.concatenate([dot_tn(a2, d_gate_up_b), dot_tn(dyf_b,...  72.9 us
    all_to_all x1, waiting for transfers between devices, local(): lax.all_to_all(head_b.reshape(rows, n_ctx, part).transpose(1, 0, 2), 'ctx...  70.1 us
    reduce_scatter x1, waiting for transfers between devices, local(): lax.psum_scatter(dot_nt(dlog_b, w_head).astype(bf16), 'ctx', scatter_dime...  68.9 us
    pallas_call x2, Pallas kernels, call_update(): pl.pallas_call(kernel, grid=(total // rows,), in_specs=[pl.BlockSpec(memo...  57.6 us
    ppermute x18, starting transfers between devices, head_gather(): lax.ppermute(x, 'head', [(i, (i - s) % n_head) for i in range(n_head)])  43.5 us
    dot_general x5, matrix products, dot_tn(): lax.dot_general(a, b, (((0,), (0,)), ((), ())), preferred_element_type=f32)  33.2 us
  transfers between devices with their start and end apart: 49, of which 26 were waited for; matrix products, arithmetic and copies ran while one was open for 13% of the time, Pallas kernels for 6%

profile of v1, /device:TPU:0, one launch (start us, length us, event | category | flops | bytes accessed | tf_op | source)
XLA Modules:
  0.0 949.4 jit_solution(6425800198935071046)
XLA Ops:
  14.0 10.6 %all-gather = s32[3,2048]{1,0:T(4,128)S(1)} all-gather(s32[3,256]{1,0:T(4,128)S(1)} %pad_add_fusion), channel_id=3, replica_groups=mesh['ctx'=8,'head'=4] {'ctx'}, dimensions={1}, use_global_device_ids=true | all-gather | bytes 27648 | tf_op jit(solution)/shard_map/all_gather | solution.py:452
  26.1 14.4 %embed_lookup.1 = bf16[2048,256]{1,0:T(8,128)(2,1)} custom-call(s32[2048,1]{1,0:T(8,128)} %copy.220.ids_ref, f32[256,16000]{1,0:T(8,128)} %w_ref.3), custom_call_target="tpu_custom_call" | custom-call | flops 8455716864 | bytes 8257536 | tf_op jit(solution)/shard_map/embed_lookup/pallas_call | solution.py:88
  48.5 8.9 all_gather.59
  70.1 6.1 all-to-all-done
  77.0 6.6 collective-permute-start.3
  84.5 5.9 collective-permute-done.3
  90.4 16.0 %collective-permute-done.4 = bf16[2,32,2048]{2,1,0:T(8,128)(2,1)S(1)} collective-permute-done((bf16[2,32,2048]{2,1,0:T(8,128)(2,1)S(1)}, bf16[2,32,2048]{2,1,0:T(8,128)(2,1)S(1)}, u32[]{:S(2)}, u32[]{:S(2)}) %collective-permute-start.4) | collective-permute-done | bytes 262176 | tf_op jit(solution)/shard_map/ppermute | solution.py:442
  107.5 4.3 qkv.1
  111.9 13.1 %all-gather.1 = bf16[2048,128]{1,0:T(8,128)(2,1)} all-gather(bf16[256,128]{1,0:T(8,128)(2,1)} %get-tuple-element.29), channel_id=4, replica_groups=mesh['ctx'=8,'head'=4] {'ctx'}, dimensions={0}, use_global_device_ids=true | all-gather | bytes 589824 | tf_op jit(solution)/shard_map/all_gather | solution.py:498
  125.0 9.0 attn_fwd.1
  140.6 7.1 collective-permute-done.6
  147.7 10.3 %collective-permute-done.7 = bf16[2,32,2048]{2,1,0:T(8,128)(2,1)S(1)} collective-permute-done((bf16[2,32,2048]{2,1,0:T(8,128)(2,1)S(1)}, bf16[2,32,2048]{2,1,0:T(8,128)(2,1)S(1)}, u32[]{:S(2)}, u32[]{:S(2)}) %collective-permute-start.7) | collective-permute-done | bytes 262176 | tf_op jit(solution)/shard_map/ppermute | solution.py:435
  159.1 6.0 collective-permute-start.9
  166.5 5.4 collective-permute-done.9
  171.9 17.0 %collective-permute-done.10 = bf16[2,32,2048]{2,1,0:T(8,128)(2,1)S(1)} collective-permute-done((bf16[2,32,2048]{2,1,0:T(8,128)(2,1)S(1)}, bf16[2,32,2048]{2,1,0:T(8,128)(2,1)S(1)}, u32[]{:S(2)}, u32[]{:S(2)}) %collective-permute-start.10) | collective-permute-done | bytes 262176 | tf_op jit(solution)/shard_map/ppermute | solution.py:442
  189.1 6.7 fusion.96
  197.8 4.7 convolution_convert_fusion.8
  206.5 7.2 collective-permute-done.12
  213.7 9.1 collective-permute-done.13
  223.9 6.0 collective-permute-start.15
  230.8 5.8 collective-permute-done.15
  236.7 16.3 %collective-permute-done.16 = bf16[2,32,2048]{2,1,0:T(8,128)(2,1)S(1)} collective-permute-done((bf16[2,32,2048]{2,1,0:T(8,128)(2,1)S(1)}, bf16[2,32,2048]{2,1,0:T(8,128)(2,1)S(1)}, u32[]{:S(2)}, u32[]{:S(2)}) %collective-permute-start.16) | collective-permute-done | bytes 262176 | tf_op jit(solution)/shard_map/ppermute | solution.py:442
  254.1 6.0 slice.226
  260.1 6.4 copy.300
  266.5 5.2 convert_select_fusion
  271.8 4.6 all-to-all-start.1
  277.8 70.1 %all-to-all-done.1 = bf16[8,256,1024]{1,2,0:T(8,128)(2,1)} async-done(((bf16[8,256,1024]{1,2,0:T(8,128)(2,1)}), bf16[8,256,1024]{1,2,0:T(8,128)(2,1)}, u32[]{:S(2)}, u32[]{:S(2)}) %all-to-all-start.1) | async-done | bytes 4194336 | tf_op jit(solution)/shard_map/all_to_all | solution.py:465
  347.9 6.4 copy.240
  354.3 13.2 %select_reduce_fusion = (f32[2048]{0:T(1024)S(1)}, f32[2048,1024]{0,1:T(8,128)S(1)}) fusion(pred[1024]{0:T(1024)(128)(4,1)S(1)} %fusion.71, bf16[2048,2048]{1,0:T(8,128)(2,1)} %all-gather.21.cloned.1.call-done, bf16[2048,1024]{1,0:T(8,128)(2,1)} %bitcast.305), kind=kOutput, calls=%fused_computation.12 | convolution fusion | flops 8594126848 | bytes 20980736 | tf_op jit(solution)/shard_map/dot_general | solution.py:44
  370.7 8.6 all-gather.6
  379.6 13.7 %all-gather.3 = f32[12,16,128]{2,1,0:T(8,128)S(1)} all-gather(f32[3,16,128]{2,1,0:T(8,128)S(1)} %fusion.57), channel_id=6, replica_groups=mesh['ctx'=8,'head'=4] {'head'}, dimensions={0}, use_global_device_ids=true | all-gather | bytes 122880 | tf_op jit(solution)/shard_map/all_gather | solution.py:532
  394.0 14.3 %convolution_convert_fusion.2 = bf16[2048,2048]{1,0:T(8,128)(2,1)} fusion(bf16[2048,1024]{1,0:T(8,128)(2,1)S(1)} %bitcast.306, f32[2048,1024]{0,1:T(8,128)S(1)} %get-tuple-element.105, f32[2048]{0:T(1024)S(1)} %get-tuple-element.64, f32[2048]{0:T(1024)S(1)} %get-tuple-element.63, s32[2048]{0:T(1024)} %bitcast.381, f32[2048]{0:T(1024)S(1)} %bitcast.385, ...), kind=kOutput, calls=%fused_computation.11 | convolution fusion | flops 8610906112 | bytes 21009408 | tf_op jit(solution)/shard_map/dot_general | solution.py:48
  408.3 68.9 %reduce-scatter.4.cloned.1.call-done = bf16[256,2048]{1,0:T(8,128)(2,1)} async-done(((bf16[2048,2048]{1,0:T(8,128)(2,1)}), bf16[256,2048]{1,0:T(8,128)(2,1)}) %reduce-scatter.4.cloned.1.call-update) | async-done | bytes 1048592 | tf_op jit(solution)/shard_map/reduce_scatter | solution.py:542
  483.8 5.8 collective-permute-done.18
  489.6 9.9 %collective-permute-done.19 = bf16[2,32,2048]{2,1,0:T(8,128)(2,1)S(1)} collective-permute-done((bf16[2,32,2048]{2,1,0:T(8,128)(2,1)S(1)}, bf16[2,32,2048]{2,1,0:T(8,128)(2,1)S(1)}, u32[]{:S(2)}, u32[]{:S(2)}) %collective-permute-start.19) | collective-permute-done | bytes 262176 | tf_op jit(solution)/shard_map/ppermute | solution.py:435
  501.5 7.0 collective-permute-start.21
  509.2 6.1 collective-permute-done.21
  515.3 16.9 %collective-permute-done.22 = bf16[2,32,2048]{2,1,0:T(8,128)(2,1)S(1)} collective-permute-done((bf16[2,32,2048]{2,1,0:T(8,128)(2,1)S(1)}, bf16[2,32,2048]{2,1,0:T(8,128)(2,1)S(1)}, u32[]{:S(2)}, u32[]{:S(2)}) %collective-permute-start.22) | collective-permute-done | bytes 262176 | tf_op jit(solution)/shard_map/ppermute | solution.py:442
  532.4 5.0 fusion.31
  537.5 8.5 convolution_convert_fusion.5
  550.2 7.1 collective-permute-done.24
  557.3 9.5 collective-permute-done.25
  568.6 5.7 collective-permute-start.27
  577.6 3.9 collective-permute-done.27
  581.4 16.4 %collective-permute-done.28 = bf16[2,32,2048]{2,1,0:T(8,128)(2,1)S(1)} collective-permute-done((bf16[2,32,2048]{2,1,0:T(8,128)(2,1)}, bf16[2,32,2048]{2,1,0:T(8,128)(2,1)S(1)}, u32[]{:S(2)}, u32[]{:S(2)}) %collective-permute-start.28) | collective-permute-done | bytes 262176 | tf_op jit(solution)/shard_map/ppermute | solution.py:442
  601.4 18.7 %attn_bwd.1 = (bf16[256,512]{1,0:T(8,128)(2,1)}, bf16[8,2,128,128]{3,2,1,0:T(8,128)(2,1)}) custom-call(bf16[256,512]{1,0:T(8,128)(2,1)} %get-tuple-element.28.q_ref, bf16[256,512]{1,0:T(8,128)(2,1)} %convolution_convert_fusion.9.do_ref, bf16[8,2,128,128]{3,2,1,0:T(8,128)(2,1)} %bitcast.339, s32[1,128]{1,0:T(1,128)} %fusion.72.qpos_ref, ...), custom_call_target="tpu_custom_call" | custom-call | flops 2684354560 | bytes 1048576 | tf_op jit(solution)/shard_map/attn_bwd/pallas_call | solution.py:271
  620.1 4.3 all-to-all-start.2
  626.5 7.7 all-to-all-done.2.parts_ref
  642.1 4.5 convolution_convert_fusion.1
  646.6 5.6 convolution_convert_fusion
  652.3 9.8 %pad_maximum_fusion = bf16[2048,4224]{1,0:T(8,128)(2,1)} fusion(bf16[2048,1408]{1,0:T(8,128)(2,1)} %convolution_convert_fusion.1, bf16[2048,2816]{1,0:T(8,128)(2,1)S(1)} %convolution_convert_fusion), kind=kLoop, calls=%fused_computation | loop fusion | flops 34603008 | bytes 34603008 | tf_op jit(solution)/shard_map/concatenate | solution.py:564
  668.4 3.4 collective-permute-start.32
  679.2 7.9 collective-permute-done.31
  692.0 4.1 all-to-all-start.3
  696.2 19.0 %fusion.92 = (bf16[2048,1024]{1,0:T(8,128)(2,1)}, f32[]{:T(128)}) fusion(bf16[2048,2048]{1,0:T(8,128)(2,1)} %all-gather.21.cloned.1.call-done, f32[2048,1024]{0,1:T(8,128)} %copy-done.6, f32[2048]{0:T(1024)} %copy-done.45, f32[2048]{0:T(1024)} %copy-done.44, s32[2048]{0:T(1024)} %bitcast.382, f32[2048]{0:T(1024)} %bitcast.386, s32[1024]{0:T(1024)S(1)} %copy-done.36, ...), kind=kOutput, calls=%fused_computation.247 | convolution fusion | flops 8613003264 | bytes 21009412 | tf_op jit(solution)/shard_map/dot_general | solution.py:52
  715.2 4.8 all-to-all-start.4
  721.3 6.1 collective-permute-start.33
  729.1 29.1 %all-gather.4 = f32[32,256]{1,0:T(8,128)S(1)} all-gather(f32[8,256]{1,0:T(8,128)S(1)} %convert_reduce_fusion), channel_id=7, replica_groups=mesh['ctx'=8,'head'=4] {'head'}, dimensions={0}, use_global_device_ids=true | all-gather | bytes 40960 | tf_op jit(solution)/shard_map/all_gather | solution.py:579
  761.2 13.8 %embed_grad.1 = (bf16[256,8064]{1,0:T(8,128)(2,1)}, f32[8,128]{1,0:T(8,128)}) custom-call(s32[2048,1]{1,0:T(8,128)} %copy.220.ids_ref, bf16[256,2048]{1,0:T(8,128)(2,1)} %bitcast.329), custom_call_target="tpu_custom_call" | custom-call | flops 8455716864 | bytes 4128768 | tf_op jit(solution)/shard_map/embed_grad/pallas_call | solution.py:125
  778.2 72.9 %reduce-scatter.6.cloned.1.call-done.refs_0_ = bf16[256,4224]{1,0:T(8,128)(2,1)} async-done(((bf16[2048,4224]{1,0:T(8,128)(2,1)}), bf16[256,4224]{1,0:T(8,128)(2,1)}) %reduce-scatter.6.cloned.1.call-update) | async-done | bytes 2162704 | tf_op jit(solution)/shard_map/reduce_scatter | solution.py:563
  859.2 11.7 %all-reduce.3 = f32[4]{0:T(128)S(1)} all-reduce(f32[4]{0:T(128)S(1)} %dynamic-update-slice), channel_id=2, replica_groups=mesh['ctx'=8,'head'=4] {'head'}, use_global_device_ids=true, to_apply=%add.3 | all-reduce | flops 4 | bytes 32
  870.9 9.0 all-gather.5
  881.3 18.4 %layer_update.1 = (f32[256,5376]{1,0:T(8,128)}, f32[256,5376]{1,0:T(8,128)}, f32[256,5376]{1,0:T(8,128)}, bf16[256,5376]{1,0:T(8,128)(2,1)}) custom-call(f32[1,1]{1,0:T(1,128)} %bitcast.104.factor_ref, bf16[256,4224]{1,0:T(8,128)(2,1)} %reduce-scatter.6.cloned.1.call-done.refs_0_, bf16[256,1152]{1,0:T(8,128)(2,1)} %reduce-scatter.8.cloned.1.call-done.refs_1_, ...), custom_call_target="tpu_custom_call" | custom-call | flops 13762560 | bytes 38535168 | tf_op jit(solution)/shard_map/layer_update/pallas_call | solution.py:371
  900.9 39.1 %vocab_update.1 = (f32[256,16000]{1,0:T(8,128)}, f32[256,16000]{1,0:T(8,128)}, f32[256,16000]{1,0:T(8,128)}, bf16[256,16000]{1,0:T(8,128)(2,1)}) custom-call(f32[1,1]{1,0:T(1,128)} %bitcast.104.factor_ref, bf16[8,256,1024]{2,1,0:T(8,128)(2,1)} %all-to-all-done.4.head_ref, bf16[256,8064]{1,0:T(8,128)(2,1)} %get-tuple-element.37.embed_ref, ...), custom_call_target="tpu_custom_call" | custom-call | flops 40960000 | bytes 114688000 | tf_op jit(solution)/shard_map/vocab_update/pallas_call | solution.py:371
  (317 shorter events, 119.9 us)
Async XLA Ops:
  7.2 100.4 %all-gather.13.cloned.1.call-start = ((), (), s32[]{:S(2)}) async-start(), calls=%async_computation.8 | async-start | bytes 2949120 | tf_op jit(solution)/shard_map/all_gather | solution.py:461
  10.9 123.1 %all-gather.15.cloned.1.call-start = ((), (), s32[]{:S(2)}) async-start(), calls=%async_computation.9 | async-start | bytes 2359296 | tf_op jit(solution)/shard_map/all_gather | solution.py:461
  11.7 177.4 %all-gather.17.cloned.1.call-start = ((), (), s32[]{:S(2)}) async-start(), calls=%async_computation.10 | async-start | bytes 12976128 | tf_op jit(solution)/shard_map/all_gather | solution.py:461
  12.9 184.9 %all-gather.19.cloned.1.call-start = ((), (), s32[]{:S(2)}) async-start(), calls=%async_computation.11 | async-start | bytes 6488064 | tf_op jit(solution)/shard_map/all_gather | solution.py:461
  24.8 342.8 %copy-start.32 = (s32[1,8,2,128]{3,2,1,0:T(2,128)}, s32[1,8,2,128]{3,2,1,0:T(2,128)S(1)}, u32[]{:S(2)}) copy-start(s32[1,8,2,128]{3,2,1,0:T(2,128)S(1)} %get-tuple-element.97) | copy-start | bytes 24580
  26.1 42.7 %copy-start.55 = (f32[128]{0:T(128)S(1)}, f32[128]{0:T(128)}, u32[]{:S(2)}) copy-start(f32[128]{0:T(128)} %constant.139) | copy-start | bytes 1540
  26.1 42.7 %copy-start.56 = (f32[128]{0:T(128)S(1)}, f32[128]{0:T(128)}, u32[]{:S(2)}) copy-start(f32[128]{0:T(128)} %constant.140) | copy-start | bytes 1540
  41.7 18.5 %collective-permute-start = (bf16[16,32,256]{2,1,0:T(8,128)(2,1)S(1)}, bf16[16,32,256]{2,1,0:T(8,128)(2,1)S(1)}, u32[]{:S(2)}, u32[]{:S(2)}) collective-permute-start(bf16[16,32,256]{2,1,0:T(8,128)(2,1)S(1)} %get-tuple-element.90), channel_id=1, source_target_pairs={{0,1},{1,2},{2,3},{3,0},{4,5},{5,6},{6,7},{7,4},{8,9},{9,10},{10,1... | collective-permute-start | bytes 786440 | tf_op jit(solution)/shard_map/ppermute | solution.py:435
  43.3 20.2 %collective-permute-start.1 = (bf16[16,32,256]{2,1,0:T(8,128)(2,1)S(1)}, bf16[16,32,256]{2,1,0:T(8,128)(2,1)S(1)}, u32[]{:S(2)}, u32[]{:S(2)}) collective-permute-start(bf16[16,32,256]{2,1,0:T(8,128)(2,1)S(1)} %get-tuple-element.92), channel_id=1, source_target_pairs={{0,2},{1,3},{2,0},{3,1},{4,6},{5,7},{6,4},{7,5},{8,10},{9,11},{10,... | collective-permute-start | bytes 786440 | tf_op jit(solution)/shard_map/ppermute | solution.py:435
  45.9 17.6 %collective-permute-start.2 = (bf16[16,32,256]{2,1,0:T(8,128)(2,1)S(1)}, bf16[16,32,256]{2,1,0:T(8,128)(2,1)S(1)}, u32[]{:S(2)}, u32[]{:S(2)}) collective-permute-start(bf16[16,32,256]{2,1,0:T(8,128)(2,1)S(1)} %get-tuple-element.91), channel_id=1, source_target_pairs={{0,3},{1,0},{2,1},{3,2},{4,7},{5,4},{6,5},{7,6},{8,11},{9,8},{10,9... | collective-permute-start | bytes 786440 | tf_op jit(solution)/shard_map/ppermute | solution.py:435
  65.3 10.8 %all-to-all-start = ((bf16[8,64,256]{2,1,0:T(8,128)(2,1)}), bf16[8,64,256]{2,1,0:T(8,128)(2,1)S(1)}, u32[]{:S(2)}, u32[]{:S(2)}) async-start(bf16[8,64,256]{2,1,0:T(8,128)(2,1)} %bitcast.9), calls=%async_computation | async-start | bytes 524288 | tf_op jit(solution)/shard_map/all_to_all | solution.py:475
  68.8 285.5 %all-gather.21.cloned.1.call-start = ((), (), s32[]{:S(2)}) async-start(), calls=%async_computation.12 | async-start | bytes 9437184 | tf_op jit(solution)/shard_map/all_gather | solution.py:515
  76.6 81.4 %copy-start.2 = (f32[2,32,2048]{2,1,0:T(8,128)}, f32[2,32,2048]{2,1,0:T(8,128)S(1)}, u32[]{:S(2)}) copy-start(f32[2,32,2048]{2,1,0:T(8,128)S(1)} %reshape.1088) | copy-start | bytes 1572868
  77.0 13.4 %collective-permute-start.3 = (bf16[2,32,2048]{2,1,0:T(8,128)(2,1)S(1)}, bf16[2,32,2048]{2,1,0:T(8,128)(2,1)S(1)}, u32[]{:S(2)}, u32[]{:S(2)}) collective-permute-start(bf16[2,32,2048]{2,1,0:T(8,128)(2,1)S(1)} %multiply_convert_fusion.3), channel_id=1, source_target_pairs={{0,3},{1,0},{2,1},{3,2},{4,7},{5,4},{6,5},{7,6},{8,11},{9,8},{10,9... | collective-permute-start | bytes 786440 | tf_op jit(solution)/shard_map/ppermute | solution.py:442
  83.6 22.7 %collective-permute-start.4 = (bf16[2,32,2048]{2,1,0:T(8,128)(2,1)S(1)}, bf16[2,32,2048]{2,1,0:T(8,128)(2,1)S(1)}, u32[]{:S(2)}, u32[]{:S(2)}) collective-permute-start(bf16[2,32,2048]{2,1,0:T(8,128)(2,1)S(1)} %multiply_convert_fusion.3), channel_id=1, source_target_pairs={{0,2},{1,3},{2,0},{3,1},{4,6},{5,7},{6,4},{7,5},{8,10},{9,11},{10,... | collective-permute-start | bytes 786440 | tf_op jit(solution)/shard_map/ppermute | solution.py:442
  84.0 22.3 %collective-permute-start.5 = (bf16[2,32,2048]{2,1,0:T(8,128)(2,1)S(1)}, bf16[2,32,2048]{2,1,0:T(8,128)(2,1)S(1)}, u32[]{:S(2)}, u32[]{:S(2)}) collective-permute-start(bf16[2,32,2048]{2,1,0:T(8,128)(2,1)S(1)} %multiply_convert_fusion.3), channel_id=1, source_target_pairs={{0,1},{1,2},{2,3},{3,0},{4,5},{5,6},{6,7},{7,4},{8,9},{9,10},{10,1... | collective-permute-start | bytes 786440 | tf_op jit(solution)/shard_map/ppermute | solution.py:442
  136.5 11.2 %collective-permute-start.6 = (bf16[2,32,2048]{2,1,0:T(8,128)(2,1)S(1)}, bf16[2,32,2048]{2,1,0:T(8,128)(2,1)S(1)}, u32[]{:S(2)}, u32[]{:S(2)}) collective-permute-start(bf16[2,32,2048]{2,1,0:T(8,128)(2,1)S(1)} %get-tuple-element.87), channel_id=1, source_target_pairs={{0,1},{1,2},{2,3},{3,0},{4,5},{5,6},{6,7},{7,4},{8,9},{9,10},{10,1... | collective-permute-start | bytes 786440 | tf_op jit(solution)/shard_map/ppermute | solution.py:435
  136.6 21.4 %collective-permute-start.7 = (bf16[2,32,2048]{2,1,0:T(8,128)(2,1)S(1)}, bf16[2,32,2048]{2,1,0:T(8,128)(2,1)S(1)}, u32[]{:S(2)}, u32[]{:S(2)}) collective-permute-start(bf16[2,32,2048]{2,1,0:T(8,128)(2,1)S(1)} %get-tuple-element.88), channel_id=1, source_target_pairs={{0,2},{1,3},{2,0},{3,1},{4,6},{5,7},{6,4},{7,5},{8,10},{9,11},{10,... | collective-permute-start | bytes 786440 | tf_op jit(solution)/shard_map/ppermute | solution.py:435
  137.8 20.2 %collective-permute-start.8 = (bf16[2,32,2048]{2,1,0:T(8,128)(2,1)S(1)}, bf16[2,32,2048]{2,1,0:T(8,128)(2,1)S(1)}, u32[]{:S(2)}, u32[]{:S(2)}) collective-permute-start(bf16[2,32,2048]{2,1,0:T(8,128)(2,1)S(1)} %get-tuple-element.89), channel_id=1, source_target_pairs={{0,3},{1,0},{2,1},{3,2},{4,7},{5,4},{6,5},{7,6},{8,11},{9,8},{10,9... | collective-permute-start | bytes 786440 | tf_op jit(solution)/shard_map/ppermute | solution.py:435
  159.0 36.8 %copy-start.33 = (f32[2,32]{1,0:T(2,128)}, f32[2,32]{1,0:T(2,128)S(1)}, u32[]{:S(2)}) copy-start(f32[2,32]{1,0:T(2,128)S(1)} %add_rsqrt_fusion.1) | copy-start | bytes 772
  159.1 12.8 %collective-permute-start.9 = (bf16[2,32,2048]{2,1,0:T(8,128)(2,1)S(1)}, bf16[2,32,2048]{2,1,0:T(8,128)(2,1)S(1)}, u32[]{:S(2)}, u32[]{:S(2)}) collective-permute-start(bf16[2,32,2048]{2,1,0:T(8,128)(2,1)S(1)} %multiply_convert_fusion.2), channel_id=1, source_target_pairs={{0,3},{1,0},{2,1},{3,2},{4,7},{5,4},{6,5},{7,6},{8,11},{9,8},{10,9... | collective-permute-start | bytes 786440 | tf_op jit(solution)/shard_map/ppermute | solution.py:442
  165.1 23.7 %collective-permute-start.10 = (bf16[2,32,2048]{2,1,0:T(8,128)(2,1)S(1)}, bf16[2,32,2048]{2,1,0:T(8,128)(2,1)S(1)}, u32[]{:S(2)}, u32[]{:S(2)}) collective-permute-start(bf16[2,32,2048]{2,1,0:T(8,128)(2,1)S(1)} %multiply_convert_fusion.2), channel_id=1, source_target_pairs={{0,2},{1,3},{2,0},{3,1},{4,6},{5,7},{6,4},{7,5},{8,10},{9,11},{10,... | collective-permute-start | bytes 786440 | tf_op jit(solution)/shard_map/ppermute | solution.py:442
  166.2 22.7 %collective-permute-start.11 = (bf16[2,32,2048]{2,1,0:T(8,128)(2,1)S(1)}, bf16[2,32,2048]{2,1,0:T(8,128)(2,1)S(1)}, u32[]{:S(2)}, u32[]{:S(2)}) collective-permute-start(bf16[2,32,2048]{2,1,0:T(8,128)(2,1)S(1)} %multiply_convert_fusion.2), channel_id=1, source_target_pairs={{0,1},{1,2},{2,3},{3,0},{4,5},{5,6},{6,7},{7,4},{8,9},{9,10},{10,1... | collective-permute-start | bytes 786440 | tf_op jit(solution)/shard_map/ppermute | solution.py:442
  202.6 11.1 %collective-permute-start.12 = (bf16[2,32,2048]{2,1,0:T(8,128)(2,1)S(1)}, bf16[2,32,2048]{2,1,0:T(8,128)(2,1)S(1)}, u32[]{:S(2)}, u32[]{:S(2)}) collective-permute-start(bf16[2,32,2048]{2,1,0:T(8,128)(2,1)S(1)} %get-tuple-element.84), channel_id=1, source_target_pairs={{0,1},{1,2},{2,3},{3,0},{4,5},{5,6},{6,7},{7,4},{8,9},{9,10},{10,1... | collective-permute-start | bytes 786440 | tf_op jit(solution)/shard_map/ppermute | solution.py:435
  202.7 20.1 %collective-permute-start.13 = (bf16[2,32,2048]{2,1,0:T(8,128)(2,1)S(1)}, bf16[2,32,2048]{2,1,0:T(8,128)(2,1)S(1)}, u32[]{:S(2)}, u32[]{:S(2)}) collective-permute-start(bf16[2,32,2048]{2,1,0:T(8,128)(2,1)S(1)} %get-tuple-element.85), channel_id=1, source_target_pairs={{0,2},{1,3},{2,0},{3,1},{4,6},{5,7},{6,4},{7,5},{8,10},{9,11},{10,... | collective-permute-start | bytes 786440 | tf_op jit(solution)/shard_map/ppermute | solution.py:435
  203.6 19.2 %collective-permute-start.14 = (bf16[2,32,2048]{2,1,0:T(8,128)(2,1)S(1)}, bf16[2,32,2048]{2,1,0:T(8,128)(2,1)S(1)}, u32[]{:S(2)}, u32[]{:S(2)}) collective-permute-start(bf16[2,32,2048]{2,1,0:T(8,128)(2,1)S(1)} %get-tuple-element.86), channel_id=1, source_target_pairs={{0,3},{1,0},{2,1},{3,2},{4,7},{5,4},{6,5},{7,6},{8,11},{9,8},{10,9... | collective-permute-start | bytes 786440 | tf_op jit(solution)/shard_map/ppermute | solution.py:435
  223.8 36.3 %copy-start.26 = (f32[2,32]{1,0:T(2,128)}, f32[2,32]{1,0:T(2,128)S(1)}, u32[]{:S(2)}) copy-start(f32[2,32]{1,0:T(2,128)S(1)} %add_rsqrt_fusion) | copy-start | bytes 772
  223.9 12.7 %collective-permute-start.15 = (bf16[2,32,2048]{2,1,0:T(8,128)(2,1)S(1)}, bf16[2,32,2048]{2,1,0:T(8,128)(2,1)S(1)}, u32[]{:S(2)}, u32[]{:S(2)}) collective-permute-start(bf16[2,32,2048]{2,1,0:T(8,128)(2,1)S(1)} %multiply_convert_fusion.1), channel_id=1, source_target_pairs={{0,3},{1,0},{2,1},{3,2},{4,7},{5,4},{6,5},{7,6},{8,11},{9,8},{10,9... | collective-permute-start | bytes 786440 | tf_op jit(solution)/shard_map/ppermute | solution.py:442
  229.9 23.0 %collective-permute-start.16 = (bf16[2,32,2048]{2,1,0:T(8,128)(2,1)S(1)}, bf16[2,32,2048]{2,1,0:T(8,128)(2,1)S(1)}, u32[]{:S(2)}, u32[]{:S(2)}) collective-permute-start(bf16[2,32,2048]{2,1,0:T(8,128)(2,1)S(1)} %multiply_convert_fusion.1), channel_id=1, source_target_pairs={{0,2},{1,3},{2,0},{3,1},{4,6},{5,7},{6,4},{7,5},{8,10},{9,11},{10,... | collective-permute-start | bytes 786440 | tf_op jit(solution)/shard_map/ppermute | solution.py:442
  230.7 22.2 %collective-permute-start.17 = (bf16[2,32,2048]{2,1,0:T(8,128)(2,1)S(1)}, bf16[2,32,2048]{2,1,0:T(8,128)(2,1)S(1)}, u32[]{:S(2)}, u32[]{:S(2)}) collective-permute-start(bf16[2,32,2048]{2,1,0:T(8,128)(2,1)S(1)} %multiply_convert_fusion.1), channel_id=1, source_target_pairs={{0,1},{1,2},{2,3},{3,0},{4,5},{5,6},{6,7},{7,4},{8,9},{9,10},{10,1... | collective-permute-start | bytes 786440 | tf_op jit(solution)/shard_map/ppermute | solution.py:442
  271.8 76.1 %all-to-all-start.1 = ((bf16[8,256,1024]{1,2,0:T(8,128)(2,1)}), bf16[8,256,1024]{1,2,0:T(8,128)(2,1)}, u32[]{:S(2)}, u32[]{:S(2)}) async-start(bf16[8,256,1024]{1,2,0:T(8,128)(2,1)} %bitcast.291), calls=%async_computation.1 | async-start | bytes 8388608 | tf_op jit(solution)/shard_map/all_to_all | solution.py:465
  276.3 200.9 %reduce-scatter.4.cloned.1.call-start = ((), (), s32[]{:S(2)}) async-start(), calls=%async_computation.13 | async-start | bytes 9437184 | tf_op jit(solution)/shard_map/reduce_scatter | solution.py:542
  276.4 117.0 %copy-start.50 = (pred[1024]{0:T(1024)(128)(4,1)}, pred[1024]{0:T(1024)(128)(4,1)S(1)}, u32[]{:S(2)}) copy-start(pred[1024]{0:T(1024)(128)(4,1)S(1)} %fusion.71) | copy-start | bytes 3076
  276.4 117.0 %copy-start.35 = (s32[1024]{0:T(1024)}, s32[1024]{0:T(1024)S(1)}, u32[]{:S(2)}) copy-start(s32[1024]{0:T(1024)S(1)} %add_select_fusion.3) | copy-start | bytes 12292
  277.8 115.6 %copy-start.46 = (f32[1,8,2,128]{3,2,1,0:T(2,128)}, f32[1,8,2,128]{3,2,1,0:T(2,128)S(1)}, u32[]{:S(2)}) copy-start(f32[1,8,2,128]{3,2,1,0:T(2,128)S(1)} %fusion.66) | copy-start | bytes 24580
  408.3 91.3 %copy-start.27 = (f32[2,32]{1,0:T(2,128)S(1)}, f32[2,32]{1,0:T(2,128)}, u32[]{:S(2)}) copy-start(f32[2,32]{1,0:T(2,128)} %copy-done.26) | copy-start | bytes 772
  478.4 54.0 %copy-start.15 = (f32[256,2816]{1,0:T(8,128)S(1)}, f32[256,2816]{1,0:T(8,128)}, u32[]{:S(2)}) copy-start(f32[256,2816]{1,0:T(8,128)} %copy-done.14) | copy-start | bytes 8650756
  478.4 11.2 %collective-permute-start.18 = (bf16[2,32,2048]{2,1,0:T(8,128)(2,1)S(1)}, bf16[2,32,2048]{2,1,0:T(8,128)(2,1)S(1)}, u32[]{:S(2)}, u32[]{:S(2)}) collective-permute-start(bf16[2,32,2048]{2,1,0:T(8,128)(2,1)S(1)} %get-tuple-element.81), channel_id=1, source_target_pairs={{0,1},{1,2},{2,3},{3,0},{4,5},{5,6},{6,7},{7,4},{8,9},{9,10},{10,1... | collective-permute-start | bytes 786440 | tf_op jit(solution)/shard_map/ppermute | solution.py:435
  480.0 19.6 %collective-permute-start.19 = (bf16[2,32,2048]{2,1,0:T(8,128)(2,1)S(1)}, bf16[2,32,2048]{2,1,0:T(8,128)(2,1)S(1)}, u32[]{:S(2)}, u32[]{:S(2)}) collective-permute-start(bf16[2,32,2048]{2,1,0:T(8,128)(2,1)S(1)} %get-tuple-element.82), channel_id=1, source_target_pairs={{0,2},{1,3},{2,0},{3,1},{4,6},{5,7},{6,4},{7,5},{8,10},{9,11},{10,... | collective-permute-start | bytes 786440 | tf_op jit(solution)/shard_map/ppermute | solution.py:435
  482.4 17.2 %collective-permute-start.20 = (bf16[2,32,2048]{2,1,0:T(8,128)(2,1)S(1)}, bf16[2,32,2048]{2,1,0:T(8,128)(2,1)S(1)}, u32[]{:S(2)}, u32[]{:S(2)}) collective-permute-start(bf16[2,32,2048]{2,1,0:T(8,128)(2,1)S(1)} %get-tuple-element.83), channel_id=1, source_target_pairs={{0,3},{1,0},{2,1},{3,2},{4,7},{5,4},{6,5},{7,6},{8,11},{9,8},{10,9... | collective-permute-start | bytes 786440 | tf_op jit(solution)/shard_map/ppermute | solution.py:435
  501.4 66.3 %copy-start.4 = (f32[2,32,2048]{2,1,0:T(8,128)}, f32[2,32,2048]{2,1,0:T(8,128)S(1)}, u32[]{:S(2)}) copy-start(f32[2,32,2048]{2,1,0:T(8,128)S(1)} %get-tuple-element.62) | copy-start | bytes 1572868
  501.4 66.3 %copy-start.42 = (f32[2,32]{1,0:T(2,128)}, f32[2,32]{1,0:T(2,128)S(1)}, u32[]{:S(2)}) copy-start(f32[2,32]{1,0:T(2,128)S(1)} %broadcast_multiply_fusion.2) | copy-start | bytes 772
  501.5 13.8 %collective-permute-start.21 = (bf16[2,32,2048]{2,1,0:T(8,128)(2,1)S(1)}, bf16[2,32,2048]{2,1,0:T(8,128)(2,1)S(1)}, u32[]{:S(2)}, u32[]{:S(2)}) collective-permute-start(bf16[2,32,2048]{2,1,0:T(8,128)(2,1)S(1)} %fusion.37), channel_id=1, source_target_pairs={{0,3},{1,0},{2,1},{3,2},{4,7},{5,4},{6,5},{7,6},{8,11},{9,8},{10,9... | collective-permute-start | bytes 786440 | tf_op jit(solution)/shard_map/ppermute | solution.py:442
  508.6 23.6 %collective-permute-start.22 = (bf16[2,32,2048]{2,1,0:T(8,128)(2,1)S(1)}, bf16[2,32,2048]{2,1,0:T(8,128)(2,1)S(1)}, u32[]{:S(2)}, u32[]{:S(2)}) collective-permute-start(bf16[2,32,2048]{2,1,0:T(8,128)(2,1)S(1)} %fusion.37), channel_id=1, source_target_pairs={{0,2},{1,3},{2,0},{3,1},{4,6},{5,7},{6,4},{7,5},{8,10},{9,11},{10,... | collective-permute-start | bytes 786440 | tf_op jit(solution)/shard_map/ppermute | solution.py:442
  509.1 23.1 %collective-permute-start.23 = (bf16[2,32,2048]{2,1,0:T(8,128)(2,1)S(1)}, bf16[2,32,2048]{2,1,0:T(8,128)(2,1)S(1)}, u32[]{:S(2)}, u32[]{:S(2)}) collective-permute-start(bf16[2,32,2048]{2,1,0:T(8,128)(2,1)S(1)} %fusion.37), channel_id=1, source_target_pairs={{0,1},{1,2},{2,3},{3,0},{4,5},{5,6},{6,7},{7,4},{8,9},{9,10},{10,1... | collective-permute-start | bytes 786440 | tf_op jit(solution)/shard_map/ppermute | solution.py:442
  546.1 11.1 %collective-permute-start.24 = (bf16[2,32,2048]{2,1,0:T(8,128)(2,1)S(1)}, bf16[2,32,2048]{2,1,0:T(8,128)(2,1)S(1)}, u32[]{:S(2)}, u32[]{:S(2)}) collective-permute-start(bf16[2,32,2048]{2,1,0:T(8,128)(2,1)S(1)} %get-tuple-element.78), channel_id=1, source_target_pairs={{0,1},{1,2},{2,3},{3,0},{4,5},{5,6},{6,7},{7,4},{8,9},{9,10},{10,1... | collective-permute-start | bytes 786440 | tf_op jit(solution)/shard_map/ppermute | solution.py:435
  546.2 20.5 %collective-permute-start.25 = (bf16[2,32,2048]{2,1,0:T(8,128)(2,1)S(1)}, bf16[2,32,2048]{2,1,0:T(8,128)(2,1)S(1)}, u32[]{:S(2)}, u32[]{:S(2)}) collective-permute-start(bf16[2,32,2048]{2,1,0:T(8,128)(2,1)S(1)} %get-tuple-element.79), channel_id=1, source_target_pairs={{0,2},{1,3},{2,0},{3,1},{4,6},{5,7},{6,4},{7,5},{8,10},{9,11},{10,... | collective-permute-start | bytes 786440 | tf_op jit(solution)/shard_map/ppermute | solution.py:435
  547.0 52.9 %copy-start.20 = (bf16[2048,512]{1,0:T(8,128)(2,1)S(1)}, bf16[2048,512]{1,0:T(8,128)(2,1)}, u32[]{:S(2)}) copy-start(bf16[2048,512]{1,0:T(8,128)(2,1)} %all-gather.15.cloned.1.call-done) | copy-start | bytes 6291460
  547.0 19.7 %collective-permute-start.26 = (bf16[2,32,2048]{2,1,0:T(8,128)(2,1)S(1)}, bf16[2,32,2048]{2,1,0:T(8,128)(2,1)S(1)}, u32[]{:S(2)}, u32[]{:S(2)}) collective-permute-start(bf16[2,32,2048]{2,1,0:T(8,128)(2,1)S(1)} %get-tuple-element.80), channel_id=1, source_target_pairs={{0,3},{1,0},{2,1},{3,2},{4,7},{5,4},{6,5},{7,6},{8,11},{9,8},{10,9... | collective-permute-start | bytes 786440 | tf_op jit(solution)/shard_map/ppermute | solution.py:435
  568.6 12.8 %collective-permute-start.27 = (bf16[2,32,2048]{2,1,0:T(8,128)(2,1)}, bf16[2,32,2048]{2,1,0:T(8,128)(2,1)S(1)}, u32[]{:S(2)}, u32[]{:S(2)}) collective-permute-start(bf16[2,32,2048]{2,1,0:T(8,128)(2,1)} %add_convert_fusion.1), channel_id=1, source_target_pairs={{0,3},{1,0},{2,1},{3,2},{4,7},{5,4},{6,5},{7,6},{8,11},{9,8},{10,9... | collective-permute-start | bytes 786440 | tf_op jit(solution)/shard_map/ppermute | solution.py:442
  574.4 23.4 %collective-permute-start.28 = (bf16[2,32,2048]{2,1,0:T(8,128)(2,1)}, bf16[2,32,2048]{2,1,0:T(8,128)(2,1)S(1)}, u32[]{:S(2)}, u32[]{:S(2)}) collective-permute-start(bf16[2,32,2048]{2,1,0:T(8,128)(2,1)} %add_convert_fusion.1), channel_id=1, source_target_pairs={{0,2},{1,3},{2,0},{3,1},{4,6},{5,7},{6,4},{7,5},{8,10},{9,11},{10,... | collective-permute-start | bytes 786440 | tf_op jit(solution)/shard_map/ppermute | solution.py:442
  575.3 22.4 %collective-permute-start.29 = (bf16[2,32,2048]{2,1,0:T(8,128)(2,1)}, bf16[2,32,2048]{2,1,0:T(8,128)(2,1)S(1)}, u32[]{:S(2)}, u32[]{:S(2)}) collective-permute-start(bf16[2,32,2048]{2,1,0:T(8,128)(2,1)} %add_convert_fusion.1), channel_id=1, source_target_pairs={{0,1},{1,2},{2,3},{3,0},{4,5},{5,6},{6,7},{7,4},{8,9},{9,10},{10,1... | collective-permute-start | bytes 786440 | tf_op jit(solution)/shard_map/ppermute | solution.py:442
  620.1 14.0 %all-to-all-start.2 = ((bf16[8,256,128]{2,1,0:T(8,128)(2,1)}), bf16[8,256,128]{2,1,0:T(8,128)(2,1)}, u32[]{:S(2)}, u32[]{:S(2)}) async-start(bf16[8,256,128]{2,1,0:T(8,128)(2,1)} %bitcast.340), calls=%async_computation.4 | async-start | bytes 1048576 | tf_op jit(solution)/shard_map/all_to_all | solution.py:558
  624.4 151.8 %reduce-scatter.8.cloned.1.call-start = ((), (), s32[]{:S(2)}) async-start(), calls=%async_computation.15 | async-start | bytes 5308416 | tf_op jit(solution)/shard_map/reduce_scatter | solution.py:569
  640.7 210.4 %reduce-scatter.6.cloned.1.call-start = ((), (), s32[]{:S(2)}) async-start(), calls=%async_computation.14 | async-start | bytes 19464192 | tf_op jit(solution)/shard_map/reduce_scatter | solution.py:563
  667.8 11.4 %collective-permute-start.30 = (bf16[2,32,2048]{2,1,0:T(8,128)(2,1)}, bf16[2,32,2048]{2,1,0:T(8,128)(2,1)}, u32[]{:S(2)}, u32[]{:S(2)}) collective-permute-start(bf16[2,32,2048]{2,1,0:T(8,128)(2,1)} %get-tuple-element.75), channel_id=1, source_target_pairs={{0,1},{1,2},{2,3},{3,0},{4,5},{5,6},{6,7},{7,4},{8,9},{9,10},{10,1... | collective-permute-start | bytes 786440 | tf_op jit(solution)/shard_map/ppermute | solution.py:435
  667.8 19.3 %collective-permute-start.31 = (bf16[2,32,2048]{2,1,0:T(8,128)(2,1)}, bf16[2,32,2048]{2,1,0:T(8,128)(2,1)}, u32[]{:S(2)}, u32[]{:S(2)}) collective-permute-start(bf16[2,32,2048]{2,1,0:T(8,128)(2,1)} %get-tuple-element.76), channel_id=1, source_target_pairs={{0,2},{1,3},{2,0},{3,1},{4,6},{5,7},{6,4},{7,5},{8,10},{9,11},{10,... | collective-permute-start | bytes 786440 | tf_op jit(solution)/shard_map/ppermute | solution.py:435
  668.4 18.7 %collective-permute-start.32 = (bf16[2,32,2048]{2,1,0:T(8,128)(2,1)}, bf16[2,32,2048]{2,1,0:T(8,128)(2,1)}, u32[]{:S(2)}, u32[]{:S(2)}) collective-permute-start(bf16[2,32,2048]{2,1,0:T(8,128)(2,1)} %get-tuple-element.77), channel_id=1, source_target_pairs={{0,3},{1,0},{2,1},{3,2},{4,7},{5,4},{6,5},{7,6},{8,11},{9,8},{10,9... | collective-permute-start | bytes 786440 | tf_op jit(solution)/shard_map/ppermute | solution.py:435
  692.0 23.2 %all-to-all-start.3 = ((bf16[80,8,256]{2,0,1:T(8,128)(2,1)}), bf16[80,8,256]{2,0,1:T(8,128)(2,1)S(1)}, u32[]{:S(2)}, u32[]{:S(2)}) async-start(bf16[80,8,256]{2,0,1:T(8,128)(2,1)} %pad_maximum_fusion.9), calls=%async_computation.6 | async-start | bytes 655360 | tf_op jit(solution)/shard_map/all_to_all | solution.py:576
  715.2 185.7 %all-to-all-start.4 = ((bf16[8,256,1024]{2,1,0:T(8,128)(2,1)}), bf16[8,256,1024]{2,1,0:T(8,128)(2,1)}, u32[]{:S(2)}, u32[]{:S(2)}) async-start(bf16[8,256,1024]{2,1,0:T(8,128)(2,1)} %bitcast.304), calls=%async_computation.7 | async-start | bytes 8388608 | tf_op jit(solution)/shard_map/all_to_all | solution.py:547
  721.3 38.2 %collective-permute-start.33 = (bf16[16,32,256]{2,1,0:T(8,128)(2,1)S(1)}, bf16[16,32,256]{2,1,0:T(8,128)(2,1)S(1)}, u32[]{:S(2)}, u32[]{:S(2)}) collective-permute-start(bf16[16,32,256]{2,1,0:T(8,128)(2,1)S(1)} %bitcast.331), channel_id=1, source_target_pairs={{0,3},{1,0},{2,1},{3,2},{4,7},{5,4},{6,5},{7,6},{8,11},{9,8},{10,9... | collective-permute-start | bytes 786440 | tf_op jit(solution)/shard_map/ppermute | solution.py:442
  727.4 32.1 %collective-permute-start.34 = (bf16[16,32,256]{2,1,0:T(8,128)(2,1)S(1)}, bf16[16,32,256]{2,1,0:T(8,128)(2,1)S(1)}, u32[]{:S(2)}, u32[]{:S(2)}) collective-permute-start(bf16[16,32,256]{2,1,0:T(8,128)(2,1)S(1)} %bitcast.332), channel_id=1, source_target_pairs={{0,2},{1,3},{2,0},{3,1},{4,6},{5,7},{6,4},{7,5},{8,10},{9,11},{10,... | collective-permute-start | bytes 786440 | tf_op jit(solution)/shard_map/ppermute | solution.py:442
  729.1 30.4 %collective-permute-start.35 = (bf16[16,32,256]{2,1,0:T(8,128)(2,1)S(1)}, bf16[16,32,256]{2,1,0:T(8,128)(2,1)S(1)}, u32[]{:S(2)}, u32[]{:S(2)}) collective-permute-start(bf16[16,32,256]{2,1,0:T(8,128)(2,1)S(1)} %bitcast.333), channel_id=1, source_target_pairs={{0,1},{1,2},{2,3},{3,0},{4,5},{5,6},{6,7},{7,4},{8,9},{9,10},{10,1... | collective-permute-start | bytes 786440 | tf_op jit(solution)/shard_map/ppermute | solution.py:442
  900.3 39.8 %copy-start.38 = (f32[256,3]{0,1:T(4,128)}, f32[256,3]{0,1:T(4,128)S(1)}, u32[]{:S(2)}) copy-start(f32[256,3]{0,1:T(4,128)S(1)} %get-tuple-element.58) | copy-start | bytes 9220
  (44 other events, 495.8 us)
Sparse Core Ops, SparseCore 0:
  11.0 32.6 all-gather.12
  46.2 28.3 all-gather.14
  77.0 69.0 all-gather.16
  148.5 42.8 all-gather.18
  254.2 86.2 all-gather.20
  408.4 68.7 reduce-scatter.3
  640.8 50.2 reduce-scatter.7
  694.8 156.3 reduce-scatter.5

commit v2 on v1

--- a/solution.py
+++ b/solution.py
@@ -165,6 +165,17 @@
     tok = a1.shape[0]
     return pl.pallas_call(
         qkv_kernel,
+        grid=(1,),
+        in_specs=[
+            pl.BlockSpec((tok, D), lambda i: (0, 0)),
+            pl.BlockSpec((D, ATTN_IN), lambda i: (0, 0)),
+            pl.BlockSpec((tok, 128), lambda i: (0, 0)),
+            pl.BlockSpec((tok, 128), lambda i: (0, 0)),
+        ],
+        out_specs=[
+            pl.BlockSpec((tok, QG), lambda i: (0, 0)),
+            pl.BlockSpec((tok, 2 * HD), lambda i: (0, 0)),
+        ],
         out_shape=[
             jax.ShapeDtypeStruct((tok, QG), bf16),
             jax.ShapeDtypeStruct((tok, 2 * HD), bf16),
@@ -315,6 +326,188 @@
         compiler_params=params(),
         name="kv_bwd",
     )(parts, cosine, sine)
+
+
+def head_cast_kernel(block, w_ref, *outs):
+    column = lax.broadcasted_iota(jnp.int32, w_ref.shape, 1) + pl.program_id(0) * block
+    w = jnp.where(column < VG, w_ref[...], 0.0).astype(bf16)
+    count = w.shape[0] // len(outs)
+    for k, out_ref in enumerate(outs):
+        out_ref[...] = w[k * count : (k + 1) * count]
+
+
+def head_cast(w_vocab, width, parts):
+    rows = w_vocab.shape[0]
+    block = 1024
+    return pl.pallas_call(
+        functools.partial(head_cast_kernel, block),
+        grid=(width // block,),
+        in_specs=[pl.BlockSpec((rows, block), lambda i: (0, i))],
+        out_specs=[pl.BlockSpec((rows // parts, block), lambda i: (0, i))] * parts,
+        out_shape=[jax.ShapeDtypeStruct((rows // parts, width), bf16)] * parts,
+        compiler_params=params(),
+        cost_estimate=cost(rows * width, rows * width * 6),
+        name="head_cast",
+    )(w_vocab)
+
+
+def joined(pieces, parts):
+    for k in range(0, len(pieces), parts):
+        run = [piece[...] for piece in pieces[k : k + parts]]
+        yield k // parts, run[0] if parts == 1 else jnp.concatenate(run, axis=0)
+
+
+def logits_kernel(steps, parts, at_ref, x_ref, slot_ref, *refs):
+    pieces, (out_ref, stats_ref, top_ref, total_ref, label_ref) = refs[:-5], refs[-5:]
+    step = pl.program_id(0)
+    block = out_ref.shape[1]
+
+    @pl.when(step == 0)
+    def _():
+        top_ref[...] = jnp.full_like(top_ref, NEG)
+        total_ref[...] = jnp.zeros_like(total_ref)
+        label_ref[...] = jnp.zeros_like(label_ref)
+
+    logits = None
+    for k, w in joined(pieces, parts):
+        at = pl.multiple_of(at_ref[k], 128)
+        term = dot_nn(x_ref[:, pl.ds(at, w.shape[0])], w)
+        logits = term if logits is None else logits + term
+    column = lax.broadcasted_iota(jnp.int32, logits.shape, 1) + step * block
+    logits = jnp.where(column < VG, logits, NEG)
+    out_ref[...] = logits
+    top = top_ref[...]
+    new_top = jnp.maximum(top, jnp.max(logits, axis=1, keepdims=True))
+    total_ref[...] = total_ref[...] * jnp.exp(top - new_top) + jnp.sum(
+        jnp.exp(logits - new_top), axis=1, keepdims=True
+    )
+    top_ref[...] = new_top
+    label_ref[...] += jnp.sum(jnp.where(column == slot_ref[...], logits, 0.0), axis=1, keepdims=True)
+
+    @pl.when(step == steps - 1)
+    def _():
+        lane = lax.broadcasted_iota(jnp.int32, (x_ref.shape[0], 128), 1)
+        packed = jnp.where(lane == 0, top_ref[...], jnp.where(lane == 1, total_ref[...], label_ref[...]))
+        stats_ref[...] = packed.T[:8]
+
+
+def head_logits(x, slots, pieces, at):
+    tok = x.shape[0]
+    width = pieces[0].shape[1]
+    block = 1024
+    steps = width // block
+    return pl.pallas_call(
+        functools.partial(logits_kernel, steps, len(pieces) // at.shape[0]),
+        grid=(steps,),
+        in_specs=[
+            pl.BlockSpec(memory_space=pltpu.SMEM),
+            pl.BlockSpec((tok, D), lambda i: (0, 0)),
+            pl.BlockSpec((tok, 1), lambda i: (0, 0)),
+        ]
+        + [pl.BlockSpec((piece.shape[0], block), lambda i: (0, i)) for piece in pieces],
+        out_specs=[
+            pl.BlockSpec((tok, block), lambda i: (0, i)),
+            pl.BlockSpec((8, tok), lambda i: (0, 0)),
+        ],
+        out_shape=[
+            jax.ShapeDtypeStruct((tok, width), f32),
+            jax.ShapeDtypeStruct((8, tok), f32),
+        ],
+        scratch_shapes=[pltpu.VMEM((tok, 1), f32)] * 3,
+        compiler_params=params(),
+        cost_estimate=cost(2 * tok * D * width, 2 * D * width + 4 * tok * width, tok * width),
+        name="head_logits",
+    )(at, x, slots, *pieces)
+
+
+def dlogits_kernel(steps, parts, at_ref, logits_ref, values_ref, slot_ref, *refs):
+    pieces, (dlog_ref, dx_ref, acc_ref) = refs[:-3], refs[-3:]
+    step = pl.program_id(0)
+    tok, block = logits_ref.shape
+    logits = logits_ref[...]
+    lse = values_ref[:, 0:1]
+    weight = values_ref[:, 1:2]
+    column = lax.broadcasted_iota(jnp.int32, logits.shape, 1) + step * block
+    hit = jnp.where(column == slot_ref[...], 1.0, 0.0)
+    soft = jnp.exp(logits - lse)
+    dlog = (weight * ((1.0 + 2.0 * z_weight * lse) * soft - hit)).astype(bf16)
+    part = dlog_ref.shape[2]
+    for k in range(dlog_ref.shape[0]):
+        dlog_ref[k] = dlog[:, k * part : (k + 1) * part]
+
+    @pl.when(step == 0)
+    def _():
+        acc_ref[...] = jnp.zeros_like(acc_ref)
+
+    for k, w in joined(pieces, parts):
+        at = pl.multiple_of(at_ref[k], 128)
+        acc_ref[:, pl.ds(at, w.shape[0])] += dot_nt(dlog, w)
+
+    @pl.when(step == steps - 1)
+    def _():
+        dx_ref[...] = acc_ref[...].astype(bf16)
+
+
+def head_dlogits(logits, values, slots, pieces, at, part):
+    tok, width = logits.shape
+    block = 1024
+    steps = width // block
+    return pl.pallas_call(
+        functools.partial(dlogits_kernel, steps, len(pieces) // at.shape[0]),
+        grid=(steps,),
+        in_specs=[
+            pl.BlockSpec(memory_space=pltpu.SMEM),
+            pl.BlockSpec((tok, block), lambda i: (0, i)),
+            pl.BlockSpec((tok, values.shape[1]), lambda i: (0, 0)),
+            pl.BlockSpec((tok, 1), lambda i: (0, 0)),
+        ]
+        + [pl.BlockSpec((piece.shape[0], block), lambda i: (0, i)) for piece in pieces],
+        out_specs=[
+            pl.BlockSpec((block // part, tok, part), lambda i: (i, 0, 0)),
+            pl.BlockSpec((tok, D), lambda i: (0, 0)),
+        ],
+        out_shape=[
+            jax.ShapeDtypeStruct((width // part, tok, part), bf16),
+            jax.ShapeDtypeStruct((tok, D), bf16),
+        ],
+        scratch_shapes=[pltpu.VMEM((tok, D), f32)],
+        compiler_params=params(),
+        cost_estimate=cost(2 * tok * D * width, 2 * D * width + 6 * tok * width, tok * width),
+        name="head_dlogits",
+    )(at, logits, values, slots, *pieces)
+
+
+def outer_kernel(a_ref, da_ref, b_ref, db_ref, out_ref, *, a_steps):
+    step = pl.program_id(0)
+
+    @pl.when(step < a_steps)
+    def _():
+        out_ref[...] = dot_tn(a_ref[...], da_ref[...]).astype(bf16)
+
+    @pl.when(step >= a_steps)
+    def _():
+        out_ref[...] = dot_tn(b_ref[...], db_ref[...]).astype(bf16)
+
+
+def outer_pair(a, da, b, db, block, rows, name):
+    tok = a.shape[0]
+    a_steps, b_steps = da.shape[1] // block, db.shape[1] // block
+    width = da.shape[1] + db.shape[1]
+    return pl.pallas_call(
+        functools.partial(outer_kernel, a_steps=a_steps),
+        grid=(a_steps + b_steps, D // rows),
+        in_specs=[
+            pl.BlockSpec((tok, rows), lambda i, j: (0, j)),
+            pl.BlockSpec((tok, block), lambda i, j: (0, jnp.minimum(i, a_steps - 1))),
+            pl.BlockSpec((tok, rows), lambda i, j: (0, j)),
+            pl.BlockSpec((tok, block), lambda i, j: (0, jnp.maximum(i - a_steps, 0))),
+        ],
+        out_specs=pl.BlockSpec((rows, block), lambda i, j: (j, i)),
+        out_shape=jax.ShapeDtypeStruct((D, width), bf16),
+        compiler_params=params(),
+        cost_estimate=cost(2 * tok * D * width, 2 * D * width + 4 * tok * D),
+        name=name,
+    )(a, da, b, db)
 
 
 def update_piece(factor, rate, grad, w_ref, m_ref, a_ref, outs, columns):
@@ -449,28 +642,33 @@
     def spread_all(x):
         return head_gather(x.astype(bf16).reshape(SEQS, chunk, D)).reshape(tok, D)
 
-    every = lax.all_gather(jnp.stack([token_ids, labels, answer_mask]), "ctx", axis=1)
-    every = every.reshape(3, n_ctx, SEQS, seq_tok)
-    turned = turn(every, 3)
-    ids_all, labels_all, mask_all = (turned[k].reshape(n_ctx * tok) for k in range(3))
-    count = jnp.sum(every[2].astype(f32))
-
     layer_b = w_layer.astype(bf16)
-    ends = np.cumsum([0, ATTN_IN, QG, 2 * FFG, FFG])
-    w_in, w_out, w_gu, w_down = (
-        lax.all_gather(layer_b[:, ends[k] : ends[k + 1]], "ctx", axis=0, tiled=True) for k in range(4)
-    )
-    gain_rows = lax.all_gather(gains.astype(bf16).T, "ctx", axis=1, tiled=True).astype(f32)
-    head_b = jnp.pad(w_vocab[:, :VG].astype(bf16), ((0, 0), (0, n_ctx * part - VG)))
-    w_head = lax.all_to_all(
-        head_b.reshape(rows, n_ctx, part).transpose(1, 0, 2), "ctx", 0, 0, tiled=True
-    ).reshape(D, part)
+    edge = ATTN_IN + QG
+    w_attn = lax.all_gather(layer_b[:, :edge], "ctx", axis=0, tiled=True)
+    w_ff = lax.all_gather(layer_b[:, edge:], "ctx", axis=0, tiled=True)
+    w_out, w_gu, w_down = w_attn[:, ATTN_IN:], w_ff[:, : 2 * FFG], w_ff[:, 2 * FFG :]
+    corners = n_ctx == 8
+    head_own = head_cast(w_vocab, n_ctx * part, 2 if corners else 1)
+
+    def swap(x, bit):
+        return lax.ppermute(x, "ctx", [(i, i ^ bit) for i in range(n_ctx)])
+
+    gain_own = lax.reduce_precision(gains, exponent_bits=8, mantissa_bits=7).T.reshape(3 * rows)
+    every = jnp.concatenate([token_ids.astype(f32), answer_mask.astype(f32), gain_own])
+    every = lax.all_gather(every, "ctx")
+    ids_all = every[:, :tok].astype(jnp.int32).reshape(n_ctx, SEQS, seq_tok)
+    ids_all = turn(ids_all, 2).reshape(n_ctx * tok)
+    count = jnp.sum(every[:, tok : 2 * tok])
+    gain_rows = jnp.moveaxis(every[:, 2 * tok :].reshape(n_ctx, 3, rows), 1, 0).reshape(3, D)
+    labels_own = turn(labels.reshape(SEQS, seq_tok), 1).reshape(tok)
+    mask_own = turn(answer_mask.reshape(SEQS, seq_tok), 1).reshape(tok)
 
     offset_id = shard * VG
     local_ids = ids_all - offset_id
     inside = (local_ids >= 0) & (local_ids < VG)
     slots = jnp.where(inside, local_ids + (VG - EMB_AT), -1).reshape(-1, 1)
     picked = lookup(slots, w_vocab).reshape(n_ctx * SEQS, n_head, chunk, rows)
+    picked, *head_own = lax.optimization_barrier((picked, *head_own))
     picked = head_scatter(picked).astype(bf16).reshape(n_ctx * own, rows)
     x0 = lax.all_to_all(picked, "ctx", 0, 1, tiled=True).astype(f32)
 
@@ -494,13 +692,22 @@
     angle = jnp.tile(qpos, SEQS).astype(f32)[:, None] * freq[None, :]
     cosine = jnp.cos(angle) * mscale
     sine = jnp.sin(angle) * (mscale * sign)[None, :]
-    q, kv_own = qkv(a1, w_in, cosine, sine)
+    q, kv_own = qkv(a1, w_attn, cosine, sine)
     kv_every = lax.all_gather(kv_own, "ctx").reshape(n_ctx, SEQS, seq_tok, 2 * HD)
+    kv_every, *head_own = lax.optimization_barrier((kv_every, *head_own))
+    if corners:
+        low, high = head_own
+        y_low, x_high, x_low, y_high = swap(low, 4), swap(high, 2), swap(low, 2), swap(high, 4)
+        near = [low, high, swap(low, 1), swap(high, 1)]
     attn_b = attn(q, kv_every, qpos, kpos)
     x1 = x0 + sum_own(dot_nt(attn_b, w_out))
 
     unit1, scale1 = norm_parts(x1)
     a2 = spread_all(unit1 * gain_rows[1])
+    if corners:
+        a2, y_low, x_high = lax.optimization_barrier((a2, y_low, x_high))
+        far_low, far_high = swap(y_low, 2), swap(x_high, 4)
+        over_y_low, over_x_high = swap(y_low, 1), swap(x_high, 1)
     gate_up = dot_nn(a2, w_gu)
 
     def glu(values):
@@ -508,92 +715,97 @@
 
     hidden_f, glu_back = jax.vjp(glu, gate_up)
     hidden_b = hidden_f.astype(bf16)
-    x2 = x1 + sum_own(dot_nt(hidden_b, w_down))
+    second = sum_own(dot_nt(hidden_b, w_down))
+    if corners:
+        second, x_low, y_high = lax.optimization_barrier((second, x_low, y_high))
+    x2 = x1 + second
 
     unit2, scale2 = norm_parts(x2)
     final_b = spread_all(unit2 * gain_rows[2])
-    final_all = lax.all_gather(final_b, "ctx", axis=0, tiled=True)
-    column = place * part + jnp.arange(part, dtype=jnp.int32)
-    logits = jnp.where((column < VG)[None, :], dot_nn(final_all, w_head), NEG)
-    row_top = jnp.max(logits, axis=-1)
-    row_total = jnp.sum(jnp.exp(logits - row_top[:, None]), axis=-1)
-    slot = jnp.where(column < VG, column + offset_id, -1)
-    hit = slot[None, :] == labels_all[:, None]
-    label_logit = jnp.sum(jnp.where(hit, logits, 0.0), axis=-1)
-
-    def merge(stats):
-        top = jnp.max(stats[:, 0], axis=0)
-        total = jnp.sum(stats[:, 1] * jnp.exp(stats[:, 0] - top), axis=0)
-        return jnp.stack([top, total, jnp.sum(stats[:, 2], axis=0)])
-
-    stats = jnp.stack([row_top, row_total, label_logit])
-    stats = merge(lax.all_gather(stats, "ctx"))
-    stats = turn_back(stats.reshape(3, n_ctx * SEQS, seq_tok), 2)
-    stats = merge(lax.all_gather(stats, "head"))
-    lse = stats[0] + jnp.log(stats[1])
-    valid = every[2].astype(f32).reshape(n_ctx * SEQS, seq_tok)
-    loss = jnp.sum(valid * (lse - stats[2] + z_weight * lse * lse)) / count
-    lse = turn(lse, 1).reshape(n_ctx * tok)
-    weight = mask_all.astype(f32) / count
-    soft = jnp.exp(logits - lse[:, None])
-    dlog_b = (
-        weight[:, None] * ((1.0 + 2.0 * z_weight * lse)[:, None] * soft - hit.astype(f32))
-    ).astype(bf16)
-    d_final = lax.psum_scatter(
-        dot_nt(dlog_b, w_head).astype(bf16), "ctx", scatter_dimension=0, tiled=True
-    )
-    d_head = dot_tn(final_all, dlog_b)
-    head_sq = jnp.sum(d_head * d_head)
-    g_head = lax.all_to_all(d_head.astype(bf16).reshape(n_ctx, rows, part), "ctx", 0, 0, tiled=True)
+    label_ids = labels_own - offset_id
+    label_slots = jnp.where((label_ids >= 0) & (label_ids < VG), label_ids, -1).reshape(tok, 1)
+    if corners:
+        over_x_low, over_y_high = swap(x_low, 1), swap(y_high, 1)
+        final_b, far_low, far_high = lax.optimization_barrier((final_b, far_low, far_high))
+        head_pieces = [*near, x_low, x_high, over_x_low, over_x_high, y_low, y_high, over_y_low, over_y_high]
+        head_pieces += [far_low, far_high, swap(far_low, 1), swap(far_high, 1)]
+        head_at = jnp.stack([(place ^ bits) * rows for bits in (0, 1, 2, 3, 4, 5, 6, 7)])
+    else:
+        head_pieces = [lax.all_gather(head_own[0], "ctx", axis=0, tiled=True)]
+        head_at = jnp.zeros((1,), jnp.int32)
+    logits, stats = head_logits(final_b, label_slots, head_pieces, head_at)
+    stats, final_late = lax.optimization_barrier((stats, final_b))
+    pieces = [stats]
+    for s in range(1, n_head):
+        sent = lax.ppermute(stats, "head", [(i, (i - s) % n_head) for i in range(n_head)])
+        sent = sent.reshape(8, SEQS, n_head, chunk)
+        pieces.append(jnp.roll(sent, s, axis=2).reshape(8, tok))
+    doubled = jnp.stack(pieces + pieces)
+    stats = lax.dynamic_slice_in_dim(doubled, n_head - shard, n_head, 0)
+    top = jnp.max(stats[:, 0], axis=0)
+    total = jnp.sum(stats[:, 1] * jnp.exp(stats[:, 0] - top), axis=0)
+    lse = top + jnp.log(total)
+    weight = mask_own.astype(f32) / count
+    terms = weight * (lse - jnp.sum(stats[:, 2], axis=0) + z_weight * lse * lse)
+    loss_part = jnp.sum(turn_back(terms.reshape(SEQS, seq_tok), 1))
+    values = jnp.stack([lse, weight] + [weight] * 6).T
+    dlog_b, d_final = head_dlogits(logits, values, label_slots, head_pieces, head_at, part)
+    final_all = lax.all_gather(final_late, "ctx", axis=0, tiled=True)
+    dlog_all = lax.all_to_all(dlog_b, "ctx", 0, 0, tiled=True).reshape(n_ctx * tok, part)
 
     dx2, d_gain2 = norm_back(sum_own(d_final), unit2, scale2, gain_rows[2])
-    dyf_b = spread_all(dx2)
+    dyf_b, dlog_all, final_all = lax.optimization_barrier((spread_all(dx2), dlog_all, final_all))
     d_hidden = dot_nn(dyf_b, w_down)
     d_gate_up_b = glu_back(d_hidden)[0].astype(bf16)
-    dx1_norm, d_gain1 = norm_back(sum_own(dot_nt(d_gate_up_b, w_gu)), unit1, scale1, gain_rows[1])
+    d_second = sum_own(dot_nt(d_gate_up_b, w_gu))
+    d_head = dot_tn(final_all, dlog_all)
+    head_sq = jnp.sum(d_head * d_head)
+    d_second, d_head = lax.optimization_barrier((d_second, d_head.astype(bf16)))
+    g_head = lax.all_to_all(d_head.reshape(n_ctx, rows, part), "ctx", 0, 0, tiled=True)
+    dx1_norm, d_gain1 = norm_back(d_second, unit1, scale1, gain_rows[1])
     dx1 = dx2 + dx1_norm
-    dya_b = spread_all(dx1)
+    d_ff = outer_pair(a2, d_gate_up_b, dyf_b, hidden_b, FFG, 512, "ff_weight_grad")
+    dya_b, d_ff, g_head = lax.optimization_barrier((spread_all(dx1), d_ff, g_head))
+    g_ff = lax.psum_scatter(d_ff, "ctx", scatter_dimension=0, tiled=True)
     d_attn_b = dot_nn(dya_b, w_out).astype(bf16)
     d_q, d_kv = attn_back(q, d_attn_b, kv_every, qpos, kpos, cosine, sine)
     d_kv = lax.all_to_all(d_kv.reshape(n_ctx, tok, 2 * HD), "ctx", 0, 0, tiled=True)
     d_raw_b = jnp.concatenate([d_q, kv_back(d_kv, cosine, sine)], axis=1)
-    dx0_norm, d_gain0 = norm_back(sum_own(dot_nt(d_raw_b, w_in)), unit0, scale0, gain_rows[0])
+    dx0_norm, d_gain0 = norm_back(sum_own(dot_nt(d_raw_b, w_attn[:, :ATTN_IN])), unit0, scale0, gain_rows[0])
     dx0 = dx1 + dx0_norm
 
-    g_ff = lax.psum_scatter(
-        jnp.concatenate([dot_tn(a2, d_gate_up_b), dot_tn(dyf_b, hidden_b)], axis=1).astype(bf16),
-        "ctx",
-        scatter_dimension=0,
-        tiled=True,
-    )
-    g_at = lax.psum_scatter(
-        jnp.concatenate([dot_tn(a1, d_raw_b), dot_tn(dya_b, attn_b)], axis=1).astype(bf16),
-        "ctx",
-        scatter_dimension=0,
-        tiled=True,
-    )
+    d_at = outer_pair(a1, d_raw_b, dya_b, attn_b, 128, 2048, "attn_weight_grad")
+    g_at = lax.all_to_all(d_at.reshape(n_ctx, rows, d_at.shape[1]), "ctx", 0, 0, tiled=True)
+    g_at = jnp.sum(g_at.astype(f32), axis=0)
     extra = jnp.pad(jnp.stack([d_gain0, d_gain1, d_gain2]), ((0, 13), (0, 0)))
     moved = lax.all_to_all(jnp.concatenate([dx0, extra]).astype(bf16), "ctx", 1, 0, tiled=True)
     moved = moved.reshape(n_ctx, own + 16, rows)
-    gain_part = jnp.sum(moved[:, own : own + 8].astype(f32), axis=0)
-    gain_all = lax.all_gather(gain_part, "head")
-    grad_gain = jnp.sum(gain_all, axis=0)[:3].T
-    dx0_all = head_gather(moved[:, :own].reshape(n_ctx * SEQS, chunk, rows)).reshape(n_ctx * tok, rows)
-    g_embed, embed_sq = embed_grad(slots, dx0_all.T)
+    gain_part = jnp.sum(moved[:, own:].astype(f32), axis=0).astype(bf16)
+    moved = jnp.concatenate([moved[:, :own].reshape(n_ctx * own, rows), gain_part])
+    pieces = [moved]
+    for s in range(1, n_head):
+        pieces.append(lax.ppermute(moved, "head", [(i, (i - s) % n_head) for i in range(n_head)]))
+    gain_all = jnp.stack([piece[n_ctx * own :] for piece in pieces + pieces])
+    gain_all = lax.dynamic_slice_in_dim(gain_all, n_head - shard, n_head, 0)
+    grad_gain = jnp.sum(gain_all.astype(f32), axis=0)[:3].T
+    dx0_all = jnp.stack([piece[: n_ctx * own].reshape(n_ctx * SEQS, chunk, rows) for piece in pieces], axis=1)
+    g_embed, embed_sq = embed_grad(slots, dx0_all.reshape(n_ctx * tok, rows).T)
 
     squares = (
         jnp.sum(jnp.square(g_ff.astype(f32)))
-        + jnp.sum(jnp.square(g_at.astype(f32)))
+        + jnp.sum(jnp.square(g_at))
         + head_sq
         + jnp.sum(embed_sq)
         + jnp.sum(grad_gain * grad_gain) / n_head
     )
-    squares = jnp.sum(lax.all_gather(jnp.broadcast_to(squares, (8, 128)), "head"), axis=0)
-    total_sq = jnp.sum(lax.all_gather(squares, "ctx"), axis=0)[0, 0]
-    grad_norm = jnp.sqrt(total_sq)
+    squares = jnp.sum(lax.all_gather(jnp.full((8, 128), squares), "head"), axis=0)
+    lane = lax.broadcasted_iota(jnp.int32, (8, 128), 1)
+    totals = jnp.sum(lax.all_gather(jnp.where(lane == 0, squares, loss_part), "ctx"), axis=0)
+    loss = totals[0, 1]
+    grad_norm = jnp.sqrt(totals[0, 0])
     factor = jnp.minimum(1.0, clip_level / grad_norm)
 
-    wide = 16
+    wide = 32
     spreads = (
         (1, 0, 0, ATTN_IN, D**-0.5),
         (1, ATTN_IN, ATTN_IN, QG, (length / (4.0 * HEADS * HD)) ** 0.5),
@@ -619,13 +831,13 @@
         factor,
         (g_head, g_embed),
         [
-            pl.BlockSpec((n_ctx, wide, part), lambda i: (0, i, 0)),
-            pl.BlockSpec((wide, EMB_W), lambda i: (i, 0)),
+            pl.BlockSpec((n_ctx, wide // 2, part), lambda i: (0, i, 0)),
+            pl.BlockSpec((wide // 2, EMB_W), lambda i: (i, 0)),
         ],
         w_vocab,
         mom_vocab,
         avg_vocab,
-        wide,
+        wide // 2,
         "vocab_update",
     )
     grad = factor * grad_gain

time: 960 us -> 791 us (0.82)
  waiting for transfers between devices: 413 us -> 298 us
  Pallas kernels: 120 us -> 191 us
  matrix products: 92.3 us -> 46.6 us
  blocking collectives: 105 us -> 62.4 us
  local copies, waits for them, and re-layouts: 48.8 us -> 19.4 us
  other arithmetic: 55.1 us -> 32.7 us
  starting transfers between devices: 92.1 us -> 111 us
    reduce_scatter x3 -> x1, waiting for transfers between devices: 142 us -> 0.01 us  [local(): g_ff = lax.psum_scatter(d_ff, 'ctx', scatter_dimension=0, tiled=True)]
    pallas_call x1 -> x6, Pallas kernels: 4.33 us -> 78.8 us  [the longest x2 24.1 us: outer_pair(): pl.pallas_call(functools.partial(outer_kernel, a_steps=a_steps), grid=(a_...]
    ppermute x0 -> x20, waiting for transfers between devices: none -> 72.9 us  [the longest x14 50.4 us: swap(): return lax.ppermute(x, 'ctx', [(i, i ^ bit) for i in range(n_ctx)])]
    all_gather x6 -> x2, blocking collectives: 79.9 us -> 18.8 us  [the longest x1 10.6 us: local(): every = lax.all_gather(every, 'ctx')]
    all_to_all x3, waiting for transfers between devices: 77.7 us -> 52.1 us  [the longest x1 28.7 us: local(): lax.all_to_all(d_at.reshape(n_ctx, rows, d_at.shape[1]), 'ctx', 0, 0, til...]
    ppermute x0 -> x20, starting transfers between devices: none -> 21.8 us  [the longest x3 9.01 us: local(): lax.ppermute(moved, 'head', [(i, (i - s) % n_head) for i in range(n_head)])]
    ppermute x18 -> x15, waiting for transfers between devices: 110 us -> 88.6 us  [head_gather(): lax.ppermute(x, 'head', [(i, (i - s) % n_head) for i in range(n_head)])]
    dot_general x5 -> x1, matrix products: 33.2 us -> 13.7 us  [dot_tn(): lax.dot_general(a, b, (((0,), (0,)), ((), ())), preferred_element_type=f32)]
  transfers between devices with their start and end apart: 49 -> 62, of which waited for: 26 -> 36; matrix products, arithmetic and copies ran while one was open for 13% -> 9% of each run, Pallas kernels for 6% -> 15%
where the time goes in v2:
time: 791 us; the launch traced here: 782 us
  waiting for transfers between devices  298 us (38%)
  Pallas kernels  191 us (24%)
  starting transfers between devices  111 us (14%)
  blocking collectives  62.4 us (8%)
  matrix products  46.6 us (6%)
  other arithmetic  32.7 us (4%)
  between operations  21 us (3%)
  local copies, waits for them, and re-layouts  19.4 us (2%)
    ppermute x15, waiting for transfers between devices, head_gather(): lax.ppermute(x, 'head', [(i, (i - s) % n_head) for i in range(n_head)])  88.6 us
    ppermute x18, waiting for transfers between devices, head_scatter(): lax.ppermute(x[:, s], 'head', [(i, (i + s) % n_head) for i in range(n_hea...  74 us
    pallas_call x2, Pallas kernels, call_update(): pl.pallas_call(kernel, grid=(total // rows,), in_specs=[pl.BlockSpec(memo...  54.1 us
    ppermute x14, waiting for transfers between devices, swap(): return lax.ppermute(x, 'ctx', [(i, i ^ bit) for i in range(n_ctx)])  50.4 us
    ppermute x18, starting transfers between devices, head_scatter(): lax.ppermute(x[:, s], 'head', [(i, (i + s) % n_head) for i in range(n_hea...  35.3 us
    ppermute x15, starting transfers between devices, head_gather(): lax.ppermute(x, 'head', [(i, (i - s) % n_head) for i in range(n_head)])  32.5 us
    all_to_all x1, waiting for transfers between devices, local(): lax.all_to_all(d_at.reshape(n_ctx, rows, d_at.shape[1]), 'ctx', 0, 0, til...  28.7 us
    pallas_call x2, Pallas kernels, outer_pair(): pl.pallas_call(functools.partial(outer_kernel, a_steps=a_steps), grid=(a_...  24.1 us
  transfers between devices with their start and end apart: 62, of which 36 were waited for; matrix products, arithmetic and copies ran while one was open for 9% of the time, Pallas kernels for 15%

profile of v2, /device:TPU:0, one launch (start us, length us, event | category | flops | bytes accessed | tf_op | source)
XLA Modules:
  0.0 782.0 jit_solution(2900244095813250591)
XLA Ops:
  12.7 10.6 %all-gather.2 = f32[8,1,1280]{2,1,0:T(1,128)S(1)} all-gather(f32[1,1,1280]{2,1,0:T(1,128)S(1)} %reshape.858), channel_id=3, replica_groups=mesh['ctx'=8,'head'=4] {'ctx'}, dimensions={0}, use_global_device_ids=true | all-gather | bytes 46080 | tf_op jit(solution)/shard_map/all_gather | solution.py:658
  25.4 7.7 head_cast.1
  33.1 14.3 %embed_lookup.1 = bf16[2048,256]{1,0:T(8,128)(2,1)} custom-call(s32[2048,1]{1,0:T(8,128)} %copy.206.ids_ref, f32[256,16000]{1,0:T(8,128)} %w_ref.5), custom_call_target="tpu_custom_call" | custom-call | flops 8455716864 | bytes 8257536 | tf_op jit(solution)/shard_map/embed_lookup/pallas_call | solution.py:88
  59.7 10.7 %collective-permute-done.1 = bf16[16,32,256]{2,1,0:T(8,128)(2,1)S(1)} collective-permute-done((bf16[16,32,256]{2,1,0:T(8,128)(2,1)S(1)}, bf16[16,32,256]{2,1,0:T(8,128)(2,1)S(1)}, u32[]{:S(2)}, u32[]{:S(2)}) %collective-permute-start.1) | collective-permute-done | bytes 262176 | tf_op jit(solution)/shard_map/ppermute | solution.py:628
  72.2 3.4 all-to-all-start
  76.9 8.8 %all-to-all-done = bf16[8,64,256]{2,1,0:T(8,128)(2,1)S(1)} async-done(((bf16[8,64,256]{2,1,0:T(8,128)(2,1)}), bf16[8,64,256]{2,1,0:T(8,128)(2,1)S(1)}, u32[]{:S(2)}, u32[]{:S(2)}) %all-to-all-start) | async-done | bytes 262176 | tf_op jit(solution)/shard_map/all_to_all | solution.py:673
  87.3 7.2 collective-permute-start.3
  95.3 5.8 collective-permute-done.3
  101.2 14.0 %collective-permute-done.4 = bf16[2,32,2048]{2,1,0:T(8,128)(2,1)S(1)} collective-permute-done((bf16[2,32,2048]{2,1,0:T(8,128)(2,1)S(1)}, bf16[2,32,2048]{2,1,0:T(8,128)(2,1)S(1)}, u32[]{:S(2)}, u32[]{:S(2)}) %collective-permute-start.4) | collective-permute-done | bytes 262176 | tf_op jit(solution)/shard_map/ppermute | solution.py:635
  116.3 3.9 qkv.1
  120.2 13.8 %all-gather.1 = bf16[2048,128]{1,0:T(8,128)(2,1)} all-gather(bf16[256,128]{1,0:T(8,128)(2,1)} %get-tuple-element.63), channel_id=4, replica_groups=mesh['ctx'=8,'head'=4] {'ctx'}, dimensions={0}, use_global_device_ids=true | all-gather | bytes 589824 | tf_op jit(solution)/shard_map/all_gather | solution.py:696
  136.0 9.0 %attn_fwd.1.db_ref = bf16[256,512]{1,0:T(8,128)(2,1)} custom-call(bf16[256,512]{1,0:T(8,128)(2,1)} %get-tuple-element.62.q_ref, bf16[8,2,128,128]{3,2,1,0:T(8,128)(2,1)} %bitcast.369, s32[128,1]{1,0:T(8,128)} %fusion.56.qpos_ref, s32[1,1024]{1,0:T(1,128)} %bitcast.413), custom_call_target="tpu_custom_call" | custom-call | flops 1073741824 | bytes 524288 | tf_op jit(solution)/shard_map/attn_fwd/pallas_call | solution.py:222
  152.2 6.5 collective-permute-done.6
  158.7 10.1 %collective-permute-done.7 = bf16[2,32,2048]{2,1,0:T(8,128)(2,1)S(1)} collective-permute-done((bf16[2,32,2048]{2,1,0:T(8,128)(2,1)S(1)}, bf16[2,32,2048]{2,1,0:T(8,128)(2,1)S(1)}, u32[]{:S(2)}, u32[]{:S(2)}) %collective-permute-start.7) | collective-permute-done | bytes 262176 | tf_op jit(solution)/shard_map/ppermute | solution.py:628
  169.9 6.4 collective-permute-start.9
  177.2 5.8 collective-permute-done.9
  183.8 15.2 %collective-permute-done.10 = bf16[2,32,2048]{2,1,0:T(8,128)(2,1)S(1)} collective-permute-done((bf16[2,32,2048]{2,1,0:T(8,128)(2,1)S(1)}, bf16[2,32,2048]{2,1,0:T(8,128)(2,1)S(1)}, u32[]{:S(2)}, u32[]{:S(2)}) %collective-permute-start.10) | collective-permute-done | bytes 262176 | tf_op jit(solution)/shard_map/ppermute | solution.py:635
  201.1 6.6 fusion.2
  208.1 5.3 fusion.16
  217.5 7.2 collective-permute-done.14
  224.7 8.5 %collective-permute-done.15 = bf16[2,32,2048]{2,1,0:T(8,128)(2,1)S(1)} collective-permute-done((bf16[2,32,2048]{2,1,0:T(8,128)(2,1)S(1)}, bf16[2,32,2048]{2,1,0:T(8,128)(2,1)S(1)}, u32[]{:S(2)}, u32[]{:S(2)}) %collective-permute-start.15) | collective-permute-done | bytes 262176 | tf_op jit(solution)/shard_map/ppermute | solution.py:628
  233.3 6.1 collective-permute-done.17.refs_4_
  239.4 5.9 collective-permute-done.18.refs_9_
  250.6 3.6 collective-permute-done.19
  254.2 13.1 %collective-permute-done.20 = bf16[2,32,2048]{2,1,0:T(8,128)(2,1)S(1)} collective-permute-done((bf16[2,32,2048]{2,1,0:T(8,128)(2,1)S(1)}, bf16[2,32,2048]{2,1,0:T(8,128)(2,1)S(1)}, u32[]{:S(2)}, u32[]{:S(2)}) %collective-permute-start.20) | collective-permute-done | bytes 262176 | tf_op jit(solution)/shard_map/ppermute | solution.py:635
  269.0 24.5 %collective-permute-done.22.refs_12_ = bf16[128,8192]{1,0:T(8,128)(2,1)} collective-permute-done((bf16[128,8192]{1,0:T(8,128)(2,1)}, bf16[128,8192]{1,0:T(8,128)(2,1)}, u32[]{:S(2)}, u32[]{:S(2)}) %collective-permute-start.22) | collective-permute-done | bytes 2097184 | tf_op jit(solution)/shard_map/ppermute | solution.py:654
  310.0 20.0 %head_logits.1 = (f32[256,8192]{1,0:T(8,128)}, f32[8,256]{1,0:T(8,128)}) custom-call(s32[8]{0:T(128)} %stack.159.at_ref, bf16[256,2048]{1,0:T(8,128)(2,1)} %bitcast.314, s32[256,1]{1,0:T(8,128)} %and_select_fusion.slot_ref, bf16[128,8192]{1,0:T(8,128)(2,1)} %get-tuple-element.67.refs_0_, bf16[128,8192]{1,0:T(8,128)(2,1)} %get-tuple-element.68.refs_1_, ...), custom_call_target="tpu_custom_call" | custom-call | flops 8589934592 | bytes 41943040 | tf_op jit(solution)/shard_map/head_logits/pallas_call | solution.py:399
  339.8 23.2 %head_dlogits.1 = (bf16[8,256,1024]{2,1,0:T(8,128)(2,1)}, bf16[256,2048]{1,0:T(8,128)(2,1)}) custom-call(s32[8]{0:T(128)} %stack.159.at_ref, f32[256,8192]{1,0:T(8,128)} %get-tuple-element.78.logits_ref, f32[256,8]{1,0:T(8,128)} %bitcast.368, s32[256,1]{1,0:T(8,128)} %and_select_fusion.slot_ref, bf16[128,8192]{1,0:T(8,128)(2,1)} %get-tuple-element.67.refs_0_, ...), custom_call_target="tpu_custom_call" | custom-call | flops 8589934592 | bytes 46137344 | tf_op jit(solution)/shard_map/head_dlogits/pallas_call | solution.py:455
  363.0 4.7 all-to-all-start.1
  368.2 4.5 collective-permute-start.36
  372.7 6.7 collective-permute-done.35
  379.4 10.9 %collective-permute-done.36 = bf16[2,32,2048]{2,1,0:T(8,128)(2,1)S(1)} collective-permute-done((bf16[2,32,2048]{2,1,0:T(8,128)(2,1)S(1)}, bf16[2,32,2048]{2,1,0:T(8,128)(2,1)S(1)}, u32[]{:S(2)}, u32[]{:S(2)}) %collective-permute-start.36) | collective-permute-done | bytes 262176 | tf_op jit(solution)/shard_map/ppermute | solution.py:628
  390.8 4.1 collective-permute-start.38
  395.0 3.5 collective-permute-start.39
  398.7 5.0 collective-permute-done.38
  403.6 18.0 %collective-permute-done.39 = bf16[2,32,2048]{2,1,0:T(8,128)(2,1)S(1)} collective-permute-done((bf16[2,32,2048]{2,1,0:T(8,128)(2,1)S(1)}, bf16[2,32,2048]{2,1,0:T(8,128)(2,1)S(1)}, u32[]{:S(2)}, u32[]{:S(2)}) %collective-permute-start.39) | collective-permute-done | bytes 262176 | tf_op jit(solution)/shard_map/ppermute | solution.py:635
  421.8 5.9 all-to-all-done.1
  427.8 5.5 fusion.47
  433.5 8.1 %fusion.10 = bf16[256,2048]{1,0:T(8,128)(2,1)S(1)} fusion(bf16[256,2816]{1,0:T(8,128)(2,1)S(1)} %add_convert_fusion.da_ref, bf16[2048,4224]{1,0:T(8,128)(2,1)} %all-gather.9.cloned.1.call-done), kind=kOutput, calls=%fused_computation.14 | convolution fusion | flops 2953314304 | bytes 14024704 | tf_op jit(solution)/shard_map/dot_general | solution.py:48
  447.0 13.7 %multiply_reduce_fusion = (f32[]{:T(128)}, bf16[2048,1024]{1,0:T(8,128)(2,1)}) fusion(bf16[2048,2048]{1,0:T(8,128)(2,1)S(1)} %bitcast.420, bf16[2048,1024]{1,0:T(8,128)(2,1)} %bitcast.79), kind=kOutput, calls=%fused_computation.5 | convolution fusion | flops 8596226048 | bytes 16777220 | tf_op jit(solution)/shard_map/dot_general | solution.py:52
  460.8 4.7 all-to-all-start.2
  466.2 6.7 collective-permute-start.44
  473.8 15.2 %ff_weight_grad.1 = bf16[2048,4224]{1,0:T(8,128)(2,1)} custom-call(bf16[256,2048]{1,0:T(8,128)(2,1)} %bitcast.329, bf16[256,2816]{1,0:T(8,128)(2,1)} %copy-done.3, bf16[256,2048]{1,0:T(8,128)(2,1)} %bitcast.331, bf16[256,1408]{1,0:T(8,128)(2,1)} %copy-done.10), custom_call_target="tpu_custom_call" | custom-call | flops 4429185024 | bytes 19398656 | tf_op jit(solution)/shard_map/ff_weight_grad/pallas_call | solution.py:496
  489.0 8.0 %collective-permute-done.45 = bf16[2,32,2048]{2,1,0:T(8,128)(2,1)S(1)} collective-permute-done((bf16[2,32,2048]{2,1,0:T(8,128)(2,1)S(1)}, bf16[2,32,2048]{2,1,0:T(8,128)(2,1)S(1)}, u32[]{:S(2)}, u32[]{:S(2)}) %collective-permute-start.45) | collective-permute-done | bytes 262176 | tf_op jit(solution)/shard_map/ppermute | solution.py:635
  497.1 17.5 %all-to-all-done.2.head_ref = bf16[8,256,1024]{2,1,0:T(8,128)(2,1)} async-done(((bf16[8,256,1024]{2,1,0:T(8,128)(2,1)}), bf16[8,256,1024]{2,1,0:T(8,128)(2,1)}, u32[]{:S(2)}, u32[]{:S(2)}) %all-to-all-start.2) | async-done | bytes 4194336 | tf_op jit(solution)/shard_map/all_to_all | solution.py:764
  517.5 3.1 fusion.25.do_ref
  520.6 18.8 %attn_bwd.1 = (bf16[256,512]{1,0:T(8,128)(2,1)}, bf16[8,2,128,128]{3,2,1,0:T(8,128)(2,1)}) custom-call(bf16[256,512]{1,0:T(8,128)(2,1)} %get-tuple-element.62.q_ref, bf16[256,512]{1,0:T(8,128)(2,1)} %fusion.25.do_ref, bf16[8,2,128,128]{3,2,1,0:T(8,128)(2,1)} %bitcast.370, s32[1,128]{1,0:T(1,128)} %fusion.82.qpos_ref, s32[1024,1]{1,0:T(8,128)} %copy.242.kpos_ref, ...), custom_call_target="tpu_custom_call" | custom-call | flops 2684354560 | bytes 1048576 | tf_op jit(solution)/shard_map/attn_bwd/pallas_call | solution.py:282
  539.4 13.8 %all_to_all.46.parts_ref = bf16[8,256,128]{2,1,0:T(8,128)(2,1)} all-to-all(bf16[8,256,128]{2,1,0:T(8,128)(2,1)} %bitcast.371), channel_id=1, replica_groups=mesh['ctx'=8,'head'=4] {'ctx'}, dimensions={0} | all-to-all | bytes 1048576 | tf_op jit(solution)/shard_map/all_to_all | solution.py:772
  557.4 8.5 %collective-permute-start.47 = (bf16[2,32,2048]{2,1,0:T(8,128)(2,1)S(1)}, bf16[2,32,2048]{2,1,0:T(8,128)(2,1)S(1)}, u32[]{:S(2)}, u32[]{:S(2)}) collective-permute-start(bf16[2,32,2048]{2,1,0:T(8,128)(2,1)S(1)} %get-tuple-element.131), channel_id=1, source_target_pairs={{0,1},{1,2},{2,3},{3,0},{4,5},{5,6},{6,7},{7,4},{8,9},{9,10},{10,1... | collective-permute-start | bytes 786440 | tf_op jit(solution)/shard_map/ppermute | solution.py:628
  568.4 4.2 collective-permute-done.47
  572.6 8.6 %collective-permute-done.48 = bf16[2,32,2048]{2,1,0:T(8,128)(2,1)S(1)} collective-permute-done((bf16[2,32,2048]{2,1,0:T(8,128)(2,1)S(1)}, bf16[2,32,2048]{2,1,0:T(8,128)(2,1)S(1)}, u32[]{:S(2)}, u32[]{:S(2)}) %collective-permute-start.48) | collective-permute-done | bytes 262176 | tf_op jit(solution)/shard_map/ppermute | solution.py:628
  582.8 3.4 all-to-all-start.5
  587.0 8.9 %attn_weight_grad.1 = bf16[2048,1152]{1,0:T(8,128)(2,1)} custom-call(bf16[256,2048]{1,0:T(8,128)(2,1)} %bitcast.317, bf16[256,640]{1,0:T(8,128)(2,1)} %pad_maximum_fusion.6.da_ref, bf16[256,2048]{1,0:T(8,128)(2,1)} %bitcast.325, bf16[256,512]{1,0:T(8,128)(2,1)} %attn_fwd.1.db_ref), custom_call_target="tpu_custom_call" | custom-call | flops 1207959552 | bytes 6815744 | tf_op jit(solution)/shard_map/attn_weight_grad/pallas_call | solution.py:496
  597.7 4.7 all-to-all-start.4
  602.5 8.4 %collective-permute-start.50 = (bf16[528,256]{1,0:T(8,128)(2,1)S(1)}, bf16[528,256]{1,0:T(8,128)(2,1)S(1)}, u32[]{:S(2)}, u32[]{:S(2)}) collective-permute-start(bf16[528,256]{1,0:T(8,128)(2,1)S(1)} %pad_maximum_fusion.8), channel_id=1, source_target_pairs={{0,3},{1,0},{2,1},{3,2},{4,7},{5,4},{6,5},{7,6},{8,11},{9,8},{10,9... | collective-permute-start | bytes 811016 | tf_op jit(solution)/shard_map/ppermute | solution.py:787
  612.1 5.7 collective-permute-done.50
  617.9 16.4 %collective-permute-done.51 = bf16[528,256]{1,0:T(8,128)(2,1)S(1)} collective-permute-done((bf16[528,256]{1,0:T(8,128)(2,1)S(1)}, bf16[528,256]{1,0:T(8,128)(2,1)S(1)}, u32[]{:S(2)}, u32[]{:S(2)}) %collective-permute-start.51) | collective-permute-done | bytes 270368 | tf_op jit(solution)/shard_map/ppermute | solution.py:787
  637.3 13.7 %embed_grad.1 = (bf16[256,8064]{1,0:T(8,128)(2,1)}, f32[8,128]{1,0:T(8,128)}) custom-call(s32[2048,1]{1,0:T(8,128)} %copy.206.ids_ref, bf16[256,2048]{1,0:T(8,128)(2,1)} %bitcast.351), custom_call_target="tpu_custom_call" | custom-call | flops 8455716864 | bytes 4128768 | tf_op jit(solution)/shard_map/embed_grad/pallas_call | solution.py:125
  652.3 28.7 %all-to-all-done.4 = bf16[8,256,1152]{2,1,0:T(8,128)(2,1)} async-done(((bf16[8,256,1152]{2,1,0:T(8,128)(2,1)}), bf16[8,256,1152]{2,1,0:T(8,128)(2,1)}, u32[]{:S(2)}, u32[]{:S(2)}) %all-to-all-start.4) | async-done | bytes 4718624 | tf_op jit(solution)/shard_map/all_to_all | solution.py:778
  685.0 3.3 multiply_reduce_fusion.1
  692.4 16.0 %all-reduce.3 = f32[4]{0:T(128)S(1)} all-reduce(f32[4]{0:T(128)S(1)} %dynamic-update-slice), channel_id=2, replica_groups=mesh['ctx'=8,'head'=4] {'head'}, use_global_device_ids=true, to_apply=%add.3 | all-reduce | flops 4 | bytes 32
  709.1 8.1 %all_gather.36 = f32[8,8,128]{2,1,0:T(8,128)S(1)} all-gather(f32[1,8,128]{2,1,0:T(8,128)S(1)} %bitcast_select_fusion), channel_id=1, replica_groups=mesh['ctx'=8,'head'=4] {'ctx'}, dimensions={0}, use_global_device_ids=true | all-gather | bytes 36864 | tf_op jit(solution)/shard_map/all_gather | solution.py:803
  719.8 39.1 %vocab_update.1 = (f32[256,16000]{1,0:T(8,128)}, f32[256,16000]{1,0:T(8,128)}, f32[256,16000]{1,0:T(8,128)}, bf16[256,16000]{1,0:T(8,128)(2,1)}) custom-call(f32[1,1]{1,0:T(1,128)} %bitcast.123.factor_ref, bf16[8,256,1024]{2,1,0:T(8,128)(2,1)} %all-to-all-done.2.head_ref, bf16[256,8064]{1,0:T(8,128)(2,1)} %get-tuple-element.99.embed_ref, ...), custom_call_target="tpu_custom_call" | custom-call | flops 40960000 | bytes 114688000 | tf_op jit(solution)/shard_map/vocab_update/pallas_call | solution.py:564
  758.9 15.0 %layer_update.1 = (f32[256,5376]{1,0:T(8,128)}, f32[256,5376]{1,0:T(8,128)}, f32[256,5376]{1,0:T(8,128)}, bf16[256,5376]{1,0:T(8,128)(2,1)}) custom-call(f32[1,1]{1,0:T(1,128)} %bitcast.123.factor_ref, bf16[256,4224]{1,0:T(8,128)(2,1)} %reduce-scatter.2.cloned.1.call-done.refs_0_, f32[256,1152]{1,0:T(8,128)} %copy-done, f32[256,5376]{1,0:T(8,128)} %refs_2_.1, ...), custom_call_target="tpu_custom_call" | custom-call | flops 13762560 | bytes 38535168 | tf_op jit(solution)/shard_map/layer_update/pallas_call | solution.py:564
  (306 shorter events, 112.6 us)
Async XLA Ops:
  7.2 109.2 %all-gather.7.cloned.1.call-start = ((), (), s32[]{:S(2)}) async-start(), calls=%async_computation.7 | async-start | bytes 5308416 | tf_op jit(solution)/shard_map/all_gather | solution.py:647
  11.0 190.1 %all-gather.9.cloned.1.call-start = ((), (), s32[]{:S(2)}) async-start(), calls=%async_computation.8 | async-start | bytes 19464192 | tf_op jit(solution)/shard_map/all_gather | solution.py:648
  48.5 11.2 %collective-permute-start = (bf16[16,32,256]{2,1,0:T(8,128)(2,1)S(1)}, bf16[16,32,256]{2,1,0:T(8,128)(2,1)S(1)}, u32[]{:S(2)}, u32[]{:S(2)}) collective-permute-start(bf16[16,32,256]{2,1,0:T(8,128)(2,1)S(1)} %get-tuple-element.146), channel_id=1, source_target_pairs={{0,1},{1,2},{2,3},{3,0},{4,5},{5,6},{6,7},{7,4},{8,9},{9,10},{10,1... | collective-permute-start | bytes 786440 | tf_op jit(solution)/shard_map/ppermute | solution.py:628
  50.1 20.2 %collective-permute-start.1 = (bf16[16,32,256]{2,1,0:T(8,128)(2,1)S(1)}, bf16[16,32,256]{2,1,0:T(8,128)(2,1)S(1)}, u32[]{:S(2)}, u32[]{:S(2)}) collective-permute-start(bf16[16,32,256]{2,1,0:T(8,128)(2,1)S(1)} %get-tuple-element.147), channel_id=1, source_target_pairs={{0,2},{1,3},{2,0},{3,1},{4,6},{5,7},{6,4},{7,5},{8,10},{9,11},{10,... | collective-permute-start | bytes 786440 | tf_op jit(solution)/shard_map/ppermute | solution.py:628
  53.7 16.6 %collective-permute-start.2 = (bf16[16,32,256]{2,1,0:T(8,128)(2,1)S(1)}, bf16[16,32,256]{2,1,0:T(8,128)(2,1)S(1)}, u32[]{:S(2)}, u32[]{:S(2)}) collective-permute-start(bf16[16,32,256]{2,1,0:T(8,128)(2,1)S(1)} %slice_bitcast_fusion.23), channel_id=1, source_target_pairs={{0,3},{1,0},{2,1},{3,2},{4,7},{5,4},{6,5},{7,6},{8,11},{9,8},{10,9... | collective-permute-start | bytes 786440 | tf_op jit(solution)/shard_map/ppermute | solution.py:628
  72.2 13.5 %all-to-all-start = ((bf16[8,64,256]{2,1,0:T(8,128)(2,1)}), bf16[8,64,256]{2,1,0:T(8,128)(2,1)S(1)}, u32[]{:S(2)}, u32[]{:S(2)}) async-start(bf16[8,64,256]{2,1,0:T(8,128)(2,1)} %bitcast.8), calls=%async_computation | async-start | bytes 524288 | tf_op jit(solution)/shard_map/all_to_all | solution.py:673
  75.6 352.2 %all-gather.11.cloned.1.call-start = ((), (), s32[]{:S(2)}) async-start(), calls=%async_computation.9 | async-start | bytes 9437184 | tf_op jit(solution)/shard_map/all_gather | solution.py:753
  87.3 13.9 %collective-permute-start.3 = (bf16[2,32,2048]{2,1,0:T(8,128)(2,1)S(1)}, bf16[2,32,2048]{2,1,0:T(8,128)(2,1)S(1)}, u32[]{:S(2)}, u32[]{:S(2)}) collective-permute-start(bf16[2,32,2048]{2,1,0:T(8,128)(2,1)S(1)} %multiply_convert_fusion.3), channel_id=1, source_target_pairs={{0,3},{1,0},{2,1},{3,2},{4,7},{5,4},{6,5},{7,6},{8,11},{9,8},{10,9... | collective-permute-start | bytes 786440 | tf_op jit(solution)/shard_map/ppermute | solution.py:635
  94.5 20.7 %collective-permute-start.4 = (bf16[2,32,2048]{2,1,0:T(8,128)(2,1)S(1)}, bf16[2,32,2048]{2,1,0:T(8,128)(2,1)S(1)}, u32[]{:S(2)}, u32[]{:S(2)}) collective-permute-start(bf16[2,32,2048]{2,1,0:T(8,128)(2,1)S(1)} %multiply_convert_fusion.3), channel_id=1, source_target_pairs={{0,2},{1,3},{2,0},{3,1},{4,6},{5,7},{6,4},{7,5},{8,10},{9,11},{10,... | collective-permute-start | bytes 786440 | tf_op jit(solution)/shard_map/ppermute | solution.py:635
  94.9 20.2 %collective-permute-start.5 = (bf16[2,32,2048]{2,1,0:T(8,128)(2,1)S(1)}, bf16[2,32,2048]{2,1,0:T(8,128)(2,1)S(1)}, u32[]{:S(2)}, u32[]{:S(2)}) collective-permute-start(bf16[2,32,2048]{2,1,0:T(8,128)(2,1)S(1)} %multiply_convert_fusion.3), channel_id=1, source_target_pairs={{0,1},{1,2},{2,3},{3,0},{4,5},{5,6},{6,7},{7,4},{8,9},{9,10},{10,1... | collective-permute-start | bytes 786440 | tf_op jit(solution)/shard_map/ppermute | solution.py:635
  134.0 67.1 %collective-permute-start.12 = (bf16[128,8192]{1,0:T(8,128)(2,1)S(1)}, bf16[128,8192]{1,0:T(8,128)(2,1)}, u32[]{:S(2)}, u32[]{:S(2)}) collective-permute-start(bf16[128,8192]{1,0:T(8,128)(2,1)S(1)} %copy-done.1), channel_id=1, source_target_pairs={{0,16},{4,20},{8,24},{12,28},{16,0},{20,4},{24,8},{28,12},{1,17},{... | collective-permute-start | bytes 6291464 | tf_op jit(solution)/shard_map/ppermute | solution.py:654
  134.9 66.2 %collective-permute-start.13 = (bf16[128,8192]{1,0:T(8,128)(2,1)}, bf16[128,8192]{1,0:T(8,128)(2,1)}, u32[]{:S(2)}, u32[]{:S(2)}) collective-permute-start(bf16[128,8192]{1,0:T(8,128)(2,1)} %get-tuple-element.68.refs_1_), channel_id=1, source_target_pairs={{0,8},{4,12},{8,0},{12,4},{16,24},{20,28},{24,16},{28,20},{1,9},{5... | collective-permute-start | bytes 6291464 | tf_op jit(solution)/shard_map/ppermute | solution.py:654
  147.5 11.1 %collective-permute-start.6 = (bf16[2,32,2048]{2,1,0:T(8,128)(2,1)S(1)}, bf16[2,32,2048]{2,1,0:T(8,128)(2,1)S(1)}, u32[]{:S(2)}, u32[]{:S(2)}) collective-permute-start(bf16[2,32,2048]{2,1,0:T(8,128)(2,1)S(1)} %get-tuple-element.143), channel_id=1, source_target_pairs={{0,1},{1,2},{2,3},{3,0},{4,5},{5,6},{6,7},{7,4},{8,9},{9,10},{10,1... | collective-permute-start | bytes 786440 | tf_op jit(solution)/shard_map/ppermute | solution.py:628
  147.6 21.2 %collective-permute-start.7 = (bf16[2,32,2048]{2,1,0:T(8,128)(2,1)S(1)}, bf16[2,32,2048]{2,1,0:T(8,128)(2,1)S(1)}, u32[]{:S(2)}, u32[]{:S(2)}) collective-permute-start(bf16[2,32,2048]{2,1,0:T(8,128)(2,1)S(1)} %get-tuple-element.144), channel_id=1, source_target_pairs={{0,2},{1,3},{2,0},{3,1},{4,6},{5,7},{6,4},{7,5},{8,10},{9,11},{10,... | collective-permute-start | bytes 786440 | tf_op jit(solution)/shard_map/ppermute | solution.py:628
  149.3 19.5 %collective-permute-start.8 = (bf16[2,32,2048]{2,1,0:T(8,128)(2,1)S(1)}, bf16[2,32,2048]{2,1,0:T(8,128)(2,1)S(1)}, u32[]{:S(2)}, u32[]{:S(2)}) collective-permute-start(bf16[2,32,2048]{2,1,0:T(8,128)(2,1)S(1)} %get-tuple-element.145), channel_id=1, source_target_pairs={{0,3},{1,0},{2,1},{3,2},{4,7},{5,4},{6,5},{7,6},{8,11},{9,8},{10,9... | collective-permute-start | bytes 786440 | tf_op jit(solution)/shard_map/ppermute | solution.py:628
  169.9 13.1 %collective-permute-start.9 = (bf16[2,32,2048]{2,1,0:T(8,128)(2,1)S(1)}, bf16[2,32,2048]{2,1,0:T(8,128)(2,1)S(1)}, u32[]{:S(2)}, u32[]{:S(2)}) collective-permute-start(bf16[2,32,2048]{2,1,0:T(8,128)(2,1)S(1)} %multiply_convert_fusion.2), channel_id=1, source_target_pairs={{0,3},{1,0},{2,1},{3,2},{4,7},{5,4},{6,5},{7,6},{8,11},{9,8},{10,9... | collective-permute-start | bytes 786440 | tf_op jit(solution)/shard_map/ppermute | solution.py:635
  176.3 22.7 %collective-permute-start.10 = (bf16[2,32,2048]{2,1,0:T(8,128)(2,1)S(1)}, bf16[2,32,2048]{2,1,0:T(8,128)(2,1)S(1)}, u32[]{:S(2)}, u32[]{:S(2)}) collective-permute-start(bf16[2,32,2048]{2,1,0:T(8,128)(2,1)S(1)} %multiply_convert_fusion.2), channel_id=1, source_target_pairs={{0,2},{1,3},{2,0},{3,1},{4,6},{5,7},{6,4},{7,5},{8,10},{9,11},{10,... | collective-permute-start | bytes 786440 | tf_op jit(solution)/shard_map/ppermute | solution.py:635
  176.7 23.2 %collective-permute-start.11 = (bf16[2,32,2048]{2,1,0:T(8,128)(2,1)S(1)}, bf16[2,32,2048]{2,1,0:T(8,128)(2,1)S(1)}, u32[]{:S(2)}, u32[]{:S(2)}) collective-permute-start(bf16[2,32,2048]{2,1,0:T(8,128)(2,1)S(1)} %multiply_convert_fusion.2), channel_id=1, source_target_pairs={{0,1},{1,2},{2,3},{3,0},{4,5},{5,6},{6,7},{7,4},{8,9},{9,10},{10,1... | collective-permute-start | bytes 786440 | tf_op jit(solution)/shard_map/ppermute | solution.py:635
  183.1 56.3 %collective-permute-start.17 = (bf16[128,8192]{1,0:T(8,128)(2,1)S(1)}, bf16[128,8192]{1,0:T(8,128)(2,1)}, u32[]{:S(2)}, u32[]{:S(2)}) collective-permute-start(bf16[128,8192]{1,0:T(8,128)(2,1)S(1)} %copy-done.1), channel_id=1, source_target_pairs={{0,8},{4,12},{8,0},{12,4},{16,24},{20,28},{24,16},{28,20},{1,9},{5... | collective-permute-start | bytes 6291464 | tf_op jit(solution)/shard_map/ppermute | solution.py:654
  199.0 46.3 %collective-permute-start.18 = (bf16[128,8192]{1,0:T(8,128)(2,1)}, bf16[128,8192]{1,0:T(8,128)(2,1)}, u32[]{:S(2)}, u32[]{:S(2)}) collective-permute-start(bf16[128,8192]{1,0:T(8,128)(2,1)} %get-tuple-element.68.refs_1_), channel_id=1, source_target_pairs={{0,16},{4,20},{8,24},{12,28},{16,0},{20,4},{24,8},{28,12},{1,17},{... | collective-permute-start | bytes 6291464 | tf_op jit(solution)/shard_map/ppermute | solution.py:654
  213.6 11.1 %collective-permute-start.14 = (bf16[2,32,2048]{2,1,0:T(8,128)(2,1)S(1)}, bf16[2,32,2048]{2,1,0:T(8,128)(2,1)S(1)}, u32[]{:S(2)}, u32[]{:S(2)}) collective-permute-start(bf16[2,32,2048]{2,1,0:T(8,128)(2,1)S(1)} %get-tuple-element.140), channel_id=1, source_target_pairs={{0,1},{1,2},{2,3},{3,0},{4,5},{5,6},{6,7},{7,4},{8,9},{9,10},{10,1... | collective-permute-start | bytes 786440 | tf_op jit(solution)/shard_map/ppermute | solution.py:628
  213.6 19.5 %collective-permute-start.15 = (bf16[2,32,2048]{2,1,0:T(8,128)(2,1)S(1)}, bf16[2,32,2048]{2,1,0:T(8,128)(2,1)S(1)}, u32[]{:S(2)}, u32[]{:S(2)}) collective-permute-start(bf16[2,32,2048]{2,1,0:T(8,128)(2,1)S(1)} %get-tuple-element.142), channel_id=1, source_target_pairs={{0,2},{1,3},{2,0},{3,1},{4,6},{5,7},{6,4},{7,5},{8,10},{9,11},{10,... | collective-permute-start | bytes 786440 | tf_op jit(solution)/shard_map/ppermute | solution.py:628
  214.4 18.8 %collective-permute-start.16 = (bf16[2,32,2048]{2,1,0:T(8,128)(2,1)S(1)}, bf16[2,32,2048]{2,1,0:T(8,128)(2,1)S(1)}, u32[]{:S(2)}, u32[]{:S(2)}) collective-permute-start(bf16[2,32,2048]{2,1,0:T(8,128)(2,1)S(1)} %get-tuple-element.141), channel_id=1, source_target_pairs={{0,3},{1,0},{2,1},{3,2},{4,7},{5,4},{6,5},{7,6},{8,11},{9,8},{10,9... | collective-permute-start | bytes 786440 | tf_op jit(solution)/shard_map/ppermute | solution.py:628
  217.5 51.5 %copy-start.5 = (f32[8,8,8,256]{3,2,0,1:T(8,128)}, f32[8,8,8,256]{3,2,0,1:T(8,128)S(1)}, u32[]{:S(2)}) copy-start(f32[8,8,8,256]{3,2,0,1:T(8,128)S(1)} %copy.272) | copy-start | bytes 1572868
  246.5 7.7 collective-permute-start.19
  246.6 20.7 %collective-permute-start.20 = (bf16[2,32,2048]{2,1,0:T(8,128)(2,1)S(1)}, bf16[2,32,2048]{2,1,0:T(8,128)(2,1)S(1)}, u32[]{:S(2)}, u32[]{:S(2)}) collective-permute-start(bf16[2,32,2048]{2,1,0:T(8,128)(2,1)S(1)} %bitcast.361), channel_id=1, source_target_pairs={{0,2},{1,3},{2,0},{3,1},{4,6},{5,7},{6,4},{7,5},{8,10},{9,11},{10,... | collective-permute-start | bytes 786440 | tf_op jit(solution)/shard_map/ppermute | solution.py:635
  246.7 20.7 %collective-permute-start.21 = (bf16[2,32,2048]{2,1,0:T(8,128)(2,1)S(1)}, bf16[2,32,2048]{2,1,0:T(8,128)(2,1)S(1)}, u32[]{:S(2)}, u32[]{:S(2)}) collective-permute-start(bf16[2,32,2048]{2,1,0:T(8,128)(2,1)S(1)} %bitcast.362), channel_id=1, source_target_pairs={{0,1},{1,2},{2,3},{3,0},{4,5},{5,6},{6,7},{7,4},{8,9},{9,10},{10,1... | collective-permute-start | bytes 786440 | tf_op jit(solution)/shard_map/ppermute | solution.py:635
  248.6 44.9 %collective-permute-start.22 = (bf16[128,8192]{1,0:T(8,128)(2,1)}, bf16[128,8192]{1,0:T(8,128)(2,1)}, u32[]{:S(2)}, u32[]{:S(2)}) collective-permute-start(bf16[128,8192]{1,0:T(8,128)(2,1)} %collective-permute-done.12.refs_8_), channel_id=1, source_target_pairs={{0,8},{4,12},{8,0},{12,4},{16,24},{20,28},{24,16},{28,20},{1,9},{5... | collective-permute-start | bytes 6291464 | tf_op jit(solution)/shard_map/ppermute | solution.py:654
  249.5 44.6 %collective-permute-start.23 = (bf16[128,8192]{1,0:T(8,128)(2,1)}, bf16[128,8192]{1,0:T(8,128)(2,1)}, u32[]{:S(2)}, u32[]{:S(2)}) collective-permute-start(bf16[128,8192]{1,0:T(8,128)(2,1)} %collective-permute-done.13.refs_5_), channel_id=1, source_target_pairs={{0,16},{4,20},{8,24},{12,28},{16,0},{20,4},{24,8},{28,12},{1,17},{... | collective-permute-start | bytes 6291464 | tf_op jit(solution)/shard_map/ppermute | solution.py:654
  254.2 39.9 %collective-permute-start.24 = (bf16[128,8192]{1,0:T(8,128)(2,1)S(1)}, bf16[128,8192]{1,0:T(8,128)(2,1)}, u32[]{:S(2)}, u32[]{:S(2)}) collective-permute-start(bf16[128,8192]{1,0:T(8,128)(2,1)S(1)} %copy-done.1), channel_id=1, source_target_pairs={{0,4},{4,0},{8,12},{12,8},{16,20},{20,16},{24,28},{28,24},{1,5},{5... | collective-permute-start | bytes 6291464 | tf_op jit(solution)/shard_map/ppermute | solution.py:654
  267.3 27.3 %collective-permute-start.25 = (bf16[128,8192]{1,0:T(8,128)(2,1)}, bf16[128,8192]{1,0:T(8,128)(2,1)}, u32[]{:S(2)}, u32[]{:S(2)}) collective-permute-start(bf16[128,8192]{1,0:T(8,128)(2,1)} %get-tuple-element.68.refs_1_), channel_id=1, source_target_pairs={{0,4},{4,0},{8,12},{12,8},{16,20},{20,16},{24,28},{28,24},{1,5},{5... | collective-permute-start | bytes 6291464 | tf_op jit(solution)/shard_map/ppermute | solution.py:654
  267.3 27.4 %collective-permute-start.27 = (bf16[128,8192]{1,0:T(8,128)(2,1)}, bf16[128,8192]{1,0:T(8,128)(2,1)}, u32[]{:S(2)}, u32[]{:S(2)}) collective-permute-start(bf16[128,8192]{1,0:T(8,128)(2,1)} %collective-permute-done.13.refs_5_), channel_id=1, source_target_pairs={{0,4},{4,0},{8,12},{12,8},{16,20},{20,16},{24,28},{28,24},{1,5},{5... | collective-permute-start | bytes 6291464 | tf_op jit(solution)/shard_map/ppermute | solution.py:654
  293.5 4.5 collective-permute-start.28
  294.1 6.9 collective-permute-start.26
  294.1 9.8 %collective-permute-start.29 = (bf16[128,8192]{1,0:T(8,128)(2,1)}, bf16[128,8192]{1,0:T(8,128)(2,1)S(1)}, u32[]{:S(2)}, u32[]{:S(2)}) collective-permute-start(bf16[128,8192]{1,0:T(8,128)(2,1)} %collective-permute-done.18.refs_9_), channel_id=1, source_target_pairs={{0,4},{4,0},{8,12},{12,8},{16,20},{20,16},{24,28},{28,24},{1,5},{5... | collective-permute-start | bytes 6291464 | tf_op jit(solution)/shard_map/ppermute | solution.py:654
  294.6 12.4 %collective-permute-start.30 = (bf16[128,8192]{1,0:T(8,128)(2,1)}, bf16[128,8192]{1,0:T(8,128)(2,1)}, u32[]{:S(2)}, u32[]{:S(2)}) collective-permute-start(bf16[128,8192]{1,0:T(8,128)(2,1)} %collective-permute-done.22.refs_12_), channel_id=1, source_target_pairs={{0,4},{4,0},{8,12},{12,8},{16,20},{20,16},{24,28},{28,24},{1,5},{5... | collective-permute-start | bytes 6291464 | tf_op jit(solution)/shard_map/ppermute | solution.py:654
  294.7 15.3 %collective-permute-start.31 = (bf16[128,8192]{1,0:T(8,128)(2,1)}, bf16[128,8192]{1,0:T(8,128)(2,1)}, u32[]{:S(2)}, u32[]{:S(2)}) collective-permute-start(bf16[128,8192]{1,0:T(8,128)(2,1)} %collective-permute-done.23.refs_13_), channel_id=1, source_target_pairs={{0,4},{4,0},{8,12},{12,8},{16,20},{20,16},{24,28},{28,24},{1,5},{5... | collective-permute-start | bytes 6291464 | tf_op jit(solution)/shard_map/ppermute | solution.py:654
  330.0 6.4 collective-permute-start.34
  331.6 4.9 collective-permute-start.33
  333.0 4.2 collective-permute-start.32
  363.0 64.8 %all-to-all-start.1 = ((bf16[8,256,1024]{2,1,0:T(8,128)(2,1)}), bf16[8,256,1024]{2,1,0:T(8,128)(2,1)}, u32[]{:S(2)}, u32[]{:S(2)}) async-start(bf16[8,256,1024]{2,1,0:T(8,128)(2,1)} %get-tuple-element.82), calls=%async_computation.1 | async-start | bytes 8388608 | tf_op jit(solution)/shard_map/all_to_all | solution.py:754
  367.8 11.6 %collective-permute-start.35 = (bf16[2,32,2048]{2,1,0:T(8,128)(2,1)S(1)}, bf16[2,32,2048]{2,1,0:T(8,128)(2,1)S(1)}, u32[]{:S(2)}, u32[]{:S(2)}) collective-permute-start(bf16[2,32,2048]{2,1,0:T(8,128)(2,1)S(1)} %get-tuple-element.137), channel_id=1, source_target_pairs={{0,1},{1,2},{2,3},{3,0},{4,5},{5,6},{6,7},{7,4},{8,9},{9,10},{10,1... | collective-permute-start | bytes 786440 | tf_op jit(solution)/shard_map/ppermute | solution.py:628
  368.2 22.1 %collective-permute-start.36 = (bf16[2,32,2048]{2,1,0:T(8,128)(2,1)S(1)}, bf16[2,32,2048]{2,1,0:T(8,128)(2,1)S(1)}, u32[]{:S(2)}, u32[]{:S(2)}) collective-permute-start(bf16[2,32,2048]{2,1,0:T(8,128)(2,1)S(1)} %get-tuple-element.139), channel_id=1, source_target_pairs={{0,2},{1,3},{2,0},{3,1},{4,6},{5,7},{6,4},{7,5},{8,10},{9,11},{10,... | collective-permute-start | bytes 786440 | tf_op jit(solution)/shard_map/ppermute | solution.py:628
  372.7 17.6 %collective-permute-start.37 = (bf16[2,32,2048]{2,1,0:T(8,128)(2,1)S(1)}, bf16[2,32,2048]{2,1,0:T(8,128)(2,1)S(1)}, u32[]{:S(2)}, u32[]{:S(2)}) collective-permute-start(bf16[2,32,2048]{2,1,0:T(8,128)(2,1)S(1)} %get-tuple-element.138), channel_id=1, source_target_pairs={{0,3},{1,0},{2,1},{3,2},{4,7},{5,4},{6,5},{7,6},{8,11},{9,8},{10,9... | collective-permute-start | bytes 786440 | tf_op jit(solution)/shard_map/ppermute | solution.py:628
  390.8 12.8 %collective-permute-start.38 = (bf16[2,32,2048]{2,1,0:T(8,128)(2,1)S(1)}, bf16[2,32,2048]{2,1,0:T(8,128)(2,1)S(1)}, u32[]{:S(2)}, u32[]{:S(2)}) collective-permute-start(bf16[2,32,2048]{2,1,0:T(8,128)(2,1)S(1)} %bitcast.364), channel_id=1, source_target_pairs={{0,3},{1,0},{2,1},{3,2},{4,7},{5,4},{6,5},{7,6},{8,11},{9,8},{10,9... | collective-permute-start | bytes 786440 | tf_op jit(solution)/shard_map/ppermute | solution.py:635
  395.0 26.7 %collective-permute-start.39 = (bf16[2,32,2048]{2,1,0:T(8,128)(2,1)S(1)}, bf16[2,32,2048]{2,1,0:T(8,128)(2,1)S(1)}, u32[]{:S(2)}, u32[]{:S(2)}) collective-permute-start(bf16[2,32,2048]{2,1,0:T(8,128)(2,1)S(1)} %bitcast.365), channel_id=1, source_target_pairs={{0,2},{1,3},{2,0},{3,1},{4,6},{5,7},{6,4},{7,5},{8,10},{9,11},{10,... | collective-permute-start | bytes 786440 | tf_op jit(solution)/shard_map/ppermute | solution.py:635
  398.5 23.2 %collective-permute-start.40 = (bf16[2,32,2048]{2,1,0:T(8,128)(2,1)S(1)}, bf16[2,32,2048]{2,1,0:T(8,128)(2,1)S(1)}, u32[]{:S(2)}, u32[]{:S(2)}) collective-permute-start(bf16[2,32,2048]{2,1,0:T(8,128)(2,1)S(1)} %bitcast.366), channel_id=1, source_target_pairs={{0,1},{1,2},{2,3},{3,0},{4,5},{5,6},{6,7},{7,4},{8,9},{9,10},{10,1... | collective-permute-start | bytes 786440 | tf_op jit(solution)/shard_map/ppermute | solution.py:635
  441.6 19.0 %collective-permute-start.41 = (bf16[2,32,2048]{2,1,0:T(8,128)(2,1)S(1)}, bf16[2,32,2048]{2,1,0:T(8,128)(2,1)S(1)}, u32[]{:S(2)}, u32[]{:S(2)}) collective-permute-start(bf16[2,32,2048]{2,1,0:T(8,128)(2,1)S(1)} %get-tuple-element.134), channel_id=1, source_target_pairs={{0,1},{1,2},{2,3},{3,0},{4,5},{5,6},{6,7},{7,4},{8,9},{9,10},{10,1... | collective-permute-start | bytes 786440 | tf_op jit(solution)/shard_map/ppermute | solution.py:628
  443.1 17.5 %collective-permute-start.42 = (bf16[2,32,2048]{2,1,0:T(8,128)(2,1)S(1)}, bf16[2,32,2048]{2,1,0:T(8,128)(2,1)S(1)}, u32[]{:S(2)}, u32[]{:S(2)}) collective-permute-start(bf16[2,32,2048]{2,1,0:T(8,128)(2,1)S(1)} %get-tuple-element.136), channel_id=1, source_target_pairs={{0,2},{1,3},{2,0},{3,1},{4,6},{5,7},{6,4},{7,5},{8,10},{9,11},{10,... | collective-permute-start | bytes 786440 | tf_op jit(solution)/shard_map/ppermute | solution.py:628
  445.6 15.1 %collective-permute-start.43 = (bf16[2,32,2048]{2,1,0:T(8,128)(2,1)S(1)}, bf16[2,32,2048]{2,1,0:T(8,128)(2,1)S(1)}, u32[]{:S(2)}, u32[]{:S(2)}) collective-permute-start(bf16[2,32,2048]{2,1,0:T(8,128)(2,1)S(1)} %get-tuple-element.135), channel_id=1, source_target_pairs={{0,3},{1,0},{2,1},{3,2},{4,7},{5,4},{6,5},{7,6},{8,11},{9,8},{10,9... | collective-permute-start | bytes 786440 | tf_op jit(solution)/shard_map/ppermute | solution.py:628
  460.8 53.8 %all-to-all-start.2 = ((bf16[8,256,1024]{2,1,0:T(8,128)(2,1)}), bf16[8,256,1024]{2,1,0:T(8,128)(2,1)}, u32[]{:S(2)}, u32[]{:S(2)}) async-start(bf16[8,256,1024]{2,1,0:T(8,128)(2,1)} %bitcast.326), calls=%async_computation.2 | async-start | bytes 8388608 | tf_op jit(solution)/shard_map/all_to_all | solution.py:764
  465.5 219.5 %reduce-scatter.2.cloned.1.call-start = ((), (), s32[]{:S(2)}) async-start(), calls=%async_computation.10 | async-start | bytes 19464192 | tf_op jit(solution)/shard_map/reduce_scatter | solution.py:769
  466.2 22.8 %collective-permute-start.44 = (bf16[2,32,2048]{2,1,0:T(8,128)(2,1)S(1)}, bf16[2,32,2048]{2,1,0:T(8,128)(2,1)S(1)}, u32[]{:S(2)}, u32[]{:S(2)}) collective-permute-start(bf16[2,32,2048]{2,1,0:T(8,128)(2,1)S(1)} %bitcast.353), channel_id=1, source_target_pairs={{0,3},{1,0},{2,1},{3,2},{4,7},{5,4},{6,5},{7,6},{8,11},{9,8},{10,9... | collective-permute-start | bytes 786440 | tf_op jit(solution)/shard_map/ppermute | solution.py:635
  472.9 24.0 %collective-permute-start.45 = (bf16[2,32,2048]{2,1,0:T(8,128)(2,1)S(1)}, bf16[2,32,2048]{2,1,0:T(8,128)(2,1)S(1)}, u32[]{:S(2)}, u32[]{:S(2)}) collective-permute-start(bf16[2,32,2048]{2,1,0:T(8,128)(2,1)S(1)} %bitcast.354), channel_id=1, source_target_pairs={{0,2},{1,3},{2,0},{3,1},{4,6},{5,7},{6,4},{7,5},{8,10},{9,11},{10,... | collective-permute-start | bytes 786440 | tf_op jit(solution)/shard_map/ppermute | solution.py:635
  473.4 23.5 %collective-permute-start.46 = (bf16[2,32,2048]{2,1,0:T(8,128)(2,1)S(1)}, bf16[2,32,2048]{2,1,0:T(8,128)(2,1)S(1)}, u32[]{:S(2)}, u32[]{:S(2)}) collective-permute-start(bf16[2,32,2048]{2,1,0:T(8,128)(2,1)S(1)} %bitcast.355), channel_id=1, source_target_pairs={{0,1},{1,2},{2,3},{3,0},{4,5},{5,6},{6,7},{7,4},{8,9},{9,10},{10,1... | collective-permute-start | bytes 786440 | tf_op jit(solution)/shard_map/ppermute | solution.py:635
  557.4 15.2 %collective-permute-start.47 = (bf16[2,32,2048]{2,1,0:T(8,128)(2,1)S(1)}, bf16[2,32,2048]{2,1,0:T(8,128)(2,1)S(1)}, u32[]{:S(2)}, u32[]{:S(2)}) collective-permute-start(bf16[2,32,2048]{2,1,0:T(8,128)(2,1)S(1)} %get-tuple-element.131), channel_id=1, source_target_pairs={{0,1},{1,2},{2,3},{3,0},{4,5},{5,6},{6,7},{7,4},{8,9},{9,10},{10,1... | collective-permute-start | bytes 786440 | tf_op jit(solution)/shard_map/ppermute | solution.py:628
  565.9 15.3 %collective-permute-start.48 = (bf16[2,32,2048]{2,1,0:T(8,128)(2,1)S(1)}, bf16[2,32,2048]{2,1,0:T(8,128)(2,1)S(1)}, u32[]{:S(2)}, u32[]{:S(2)}) collective-permute-start(bf16[2,32,2048]{2,1,0:T(8,128)(2,1)S(1)} %get-tuple-element.132), channel_id=1, source_target_pairs={{0,2},{1,3},{2,0},{3,1},{4,6},{5,7},{6,4},{7,5},{8,10},{9,11},{10,... | collective-permute-start | bytes 786440 | tf_op jit(solution)/shard_map/ppermute | solution.py:628
  565.9 15.3 %collective-permute-start.49 = (bf16[2,32,2048]{2,1,0:T(8,128)(2,1)S(1)}, bf16[2,32,2048]{2,1,0:T(8,128)(2,1)S(1)}, u32[]{:S(2)}, u32[]{:S(2)}) collective-permute-start(bf16[2,32,2048]{2,1,0:T(8,128)(2,1)S(1)} %get-tuple-element.133), channel_id=1, source_target_pairs={{0,3},{1,0},{2,1},{3,2},{4,7},{5,4},{6,5},{7,6},{8,11},{9,8},{10,9... | collective-permute-start | bytes 786440 | tf_op jit(solution)/shard_map/ppermute | solution.py:628
  582.8 14.9 %all-to-all-start.5 = ((bf16[80,8,256]{2,0,1:T(8,128)(2,1)}), bf16[80,8,256]{2,0,1:T(8,128)(2,1)S(1)}, u32[]{:S(2)}, u32[]{:S(2)}) async-start(bf16[80,8,256]{2,0,1:T(8,128)(2,1)} %copy.247), calls=%async_computation.6 | async-start | bytes 655360 | tf_op jit(solution)/shard_map/all_to_all | solution.py:781
  597.7 83.3 %all-to-all-start.4 = ((bf16[8,256,1152]{2,1,0:T(8,128)(2,1)}), bf16[8,256,1152]{2,1,0:T(8,128)(2,1)}, u32[]{:S(2)}, u32[]{:S(2)}) async-start(bf16[8,256,1152]{2,1,0:T(8,128)(2,1)} %bitcast.313), calls=%async_computation.5 | async-start | bytes 9437184 | tf_op jit(solution)/shard_map/all_to_all | solution.py:778
  602.5 15.3 %collective-permute-start.50 = (bf16[528,256]{1,0:T(8,128)(2,1)S(1)}, bf16[528,256]{1,0:T(8,128)(2,1)S(1)}, u32[]{:S(2)}, u32[]{:S(2)}) collective-permute-start(bf16[528,256]{1,0:T(8,128)(2,1)S(1)} %pad_maximum_fusion.8), channel_id=1, source_target_pairs={{0,3},{1,0},{2,1},{3,2},{4,7},{5,4},{6,5},{7,6},{8,11},{9,8},{10,9... | collective-permute-start | bytes 811016 | tf_op jit(solution)/shard_map/ppermute | solution.py:787
  610.9 23.4 %collective-permute-start.51 = (bf16[528,256]{1,0:T(8,128)(2,1)S(1)}, bf16[528,256]{1,0:T(8,128)(2,1)S(1)}, u32[]{:S(2)}, u32[]{:S(2)}) collective-permute-start(bf16[528,256]{1,0:T(8,128)(2,1)S(1)} %pad_maximum_fusion.8), channel_id=1, source_target_pairs={{0,2},{1,3},{2,0},{3,1},{4,6},{5,7},{6,4},{7,5},{8,10},{9,11},{10,... | collective-permute-start | bytes 811016 | tf_op jit(solution)/shard_map/ppermute | solution.py:787
  610.9 23.4 %collective-permute-start.52 = (bf16[528,256]{1,0:T(8,128)(2,1)S(1)}, bf16[528,256]{1,0:T(8,128)(2,1)S(1)}, u32[]{:S(2)}, u32[]{:S(2)}) collective-permute-start(bf16[528,256]{1,0:T(8,128)(2,1)S(1)} %pad_maximum_fusion.8), channel_id=1, source_target_pairs={{0,1},{1,2},{2,3},{3,0},{4,5},{5,6},{6,7},{7,4},{8,9},{9,10},{10,1... | collective-permute-start | bytes 811016 | tf_op jit(solution)/shard_map/ppermute | solution.py:787
  684.1 74.9 %copy-start = (f32[256,1152]{1,0:T(8,128)}, f32[256,1152]{1,0:T(8,128)S(1)}, u32[]{:S(2)}) copy-start(f32[256,1152]{1,0:T(8,128)S(1)} %convert_reduce_fusion.refs_1_) | copy-start | bytes 3538948
  (30 other events, 516.2 us)
Sparse Core Ops, SparseCore 0:
  11.1 41.4 all-gather.6
  55.1 109.2 all-gather.8
  330.1 64.5 all-gather.10
  514.7 158.9 reduce-scatter.1

commit v3 on v2

--- a/solution.py
+++ b/solution.py
@@ -698,7 +698,7 @@
     if corners:
         low, high = head_own
         y_low, x_high, x_low, y_high = swap(low, 4), swap(high, 2), swap(low, 2), swap(high, 4)
-        near = [low, high, swap(low, 1), swap(high, 1)]
+        over_low, over_high = swap(low, 1), swap(high, 1)
     attn_b = attn(q, kv_every, qpos, kpos)
     x1 = x0 + sum_own(dot_nt(attn_b, w_out))
 
@@ -717,7 +717,10 @@
     hidden_b = hidden_f.astype(bf16)
     second = sum_own(dot_nt(hidden_b, w_down))
     if corners:
-        second, x_low, y_high = lax.optimization_barrier((second, x_low, y_high))
+        second, *placed = lax.optimization_barrier(
+            (second, x_low, y_high)
+        )
+        x_low, y_high = placed
     x2 = x1 + second
 
     unit2, scale2 = norm_parts(x2)
@@ -727,7 +730,7 @@
     if corners:
         over_x_low, over_y_high = swap(x_low, 1), swap(y_high, 1)
         final_b, far_low, far_high = lax.optimization_barrier((final_b, far_low, far_high))
-        head_pieces = [*near, x_low, x_high, over_x_low, over_x_high, y_low, y_high, over_y_low, over_y_high]
+        head_pieces = [low, high, over_low, over_high, x_low, x_high, over_x_low, over_x_high, y_low, y_high, over_y_low, over_y_high]
         head_pieces += [far_low, far_high, swap(far_low, 1), swap(far_high, 1)]
         head_at = jnp.stack([(place ^ bits) * rows for bits in (0, 1, 2, 3, 4, 5, 6, 7)])
     else:
@@ -754,31 +757,57 @@
     dlog_all = lax.all_to_all(dlog_b, "ctx", 0, 0, tiled=True).reshape(n_ctx * tok, part)
 
     dx2, d_gain2 = norm_back(sum_own(d_final), unit2, scale2, gain_rows[2])
-    dyf_b, dlog_all, final_all = lax.optimization_barrier((spread_all(dx2), dlog_all, final_all))
+    dyf_b = spread_all(dx2)
     d_hidden = dot_nn(dyf_b, w_down)
     d_gate_up_b = glu_back(d_hidden)[0].astype(bf16)
     d_second = sum_own(dot_nt(d_gate_up_b, w_gu))
+    d_ff = outer_pair(a2, d_gate_up_b, dyf_b, hidden_b, FFG, 512, "ff_weight_grad")
+    d_second, d_ff, dlog_all, final_all = lax.optimization_barrier((d_second, d_ff, dlog_all, final_all))
+    g_ff = lax.psum_scatter(d_ff, "ctx", scatter_dimension=0, tiled=True)
+    dx1_norm, d_gain1 = norm_back(d_second, unit1, scale1, gain_rows[1])
+    dx1 = dx2 + dx1_norm
     d_head = dot_tn(final_all, dlog_all)
     head_sq = jnp.sum(d_head * d_head)
-    d_second, d_head = lax.optimization_barrier((d_second, d_head.astype(bf16)))
-    g_head = lax.all_to_all(d_head.reshape(n_ctx, rows, part), "ctx", 0, 0, tiled=True)
-    dx1_norm, d_gain1 = norm_back(d_second, unit1, scale1, gain_rows[1])
-    dx1 = dx2 + dx1_norm
-    d_ff = outer_pair(a2, d_gate_up_b, dyf_b, hidden_b, FFG, 512, "ff_weight_grad")
-    dya_b, d_ff, g_head = lax.optimization_barrier((spread_all(dx1), d_ff, g_head))
-    g_ff = lax.psum_scatter(d_ff, "ctx", scatter_dimension=0, tiled=True)
+    dya_b, d_head = lax.optimization_barrier((spread_all(dx1), d_head.astype(bf16)))
     d_attn_b = dot_nn(dya_b, w_out).astype(bf16)
     d_q, d_kv = attn_back(q, d_attn_b, kv_every, qpos, kpos, cosine, sine)
     d_kv = lax.all_to_all(d_kv.reshape(n_ctx, tok, 2 * HD), "ctx", 0, 0, tiled=True)
     d_raw_b = jnp.concatenate([d_q, kv_back(d_kv, cosine, sine)], axis=1)
-    dx0_norm, d_gain0 = norm_back(sum_own(dot_nt(d_raw_b, w_attn[:, :ATTN_IN])), unit0, scale0, gain_rows[0])
+    d_first = sum_own(dot_nt(d_raw_b, w_attn[:, :ATTN_IN]))
+    d_at = outer_pair(a1, d_raw_b, dya_b, attn_b, 128, 2048, "attn_weight_grad")
+    if corners:
+        core, along_x, along_y = place & 1, (place >> 1) & 1, place >> 2
+
+        def total(kept, sent):
+            return kept.astype(f32) + sent.astype(f32)
+
+        def split(x, mine, axis, bit):
+            kept = lax.dynamic_index_in_dim(x, mine, axis, keepdims=False)
+            return kept, swap(lax.dynamic_index_in_dim(x, 1 - mine, axis, keepdims=False), bit)
+
+        kept, sent = split(d_at.reshape(2, 2, 2, rows, ATTN_IN + QG), core, 2, 1)
+        d_first, sent = lax.optimization_barrier((d_first, sent))
+        d_pair = total(kept, sent).astype(bf16)
+        d_in, d_out = d_pair[..., :ATTN_IN], d_pair[..., ATTN_IN:]
+    dx0_norm, d_gain0 = norm_back(d_first, unit0, scale0, gain_rows[0])
     dx0 = dx1 + dx0_norm
 
-    d_at = outer_pair(a1, d_raw_b, dya_b, attn_b, 128, 2048, "attn_weight_grad")
-    g_at = lax.all_to_all(d_at.reshape(n_ctx, rows, d_at.shape[1]), "ctx", 0, 0, tiled=True)
-    g_at = jnp.sum(g_at.astype(f32), axis=0)
     extra = jnp.pad(jnp.stack([d_gain0, d_gain1, d_gain2]), ((0, 13), (0, 0)))
     moved = lax.all_to_all(jnp.concatenate([dx0, extra]).astype(bf16), "ctx", 1, 0, tiled=True)
+    if corners:
+        moved, d_in, d_out = lax.optimization_barrier((moved, d_in, d_out))
+        in_kept, in_sent = split(d_in, along_x, 1, 2)
+        out_kept, out_sent = split(d_out, along_y, 0, 4)
+        d_in, d_out = total(in_kept, in_sent).astype(bf16), total(out_kept, out_sent).astype(bf16)
+        in_kept, in_sent = split(d_in, along_y, 0, 4)
+        out_kept, out_sent = split(d_out, along_x, 0, 2)
+        d_head, in_sent, out_sent = lax.optimization_barrier((d_head, in_sent, out_sent))
+        g_in, g_out = total(in_kept, in_sent), total(out_kept, out_sent)
+    else:
+        moved, d_head, d_at, g_ff = lax.optimization_barrier((moved, d_head, d_at, g_ff))
+        g_at = lax.psum_scatter(d_at, "ctx", scatter_dimension=0, tiled=True).astype(f32)
+        g_in, g_out = g_at[:, :ATTN_IN], g_at[:, ATTN_IN:]
+    g_head = lax.all_to_all(d_head.reshape(n_ctx, rows, part), "ctx", 0, 0, tiled=True)
     moved = moved.reshape(n_ctx, own + 16, rows)
     gain_part = jnp.sum(moved[:, own:].astype(f32), axis=0).astype(bf16)
     moved = jnp.concatenate([moved[:, :own].reshape(n_ctx * own, rows), gain_part])
@@ -793,12 +822,18 @@
 
     squares = (
         jnp.sum(jnp.square(g_ff.astype(f32)))
-        + jnp.sum(jnp.square(g_at))
+        + jnp.sum(jnp.square(g_in))
+        + jnp.sum(jnp.square(g_out))
         + head_sq
         + jnp.sum(embed_sq)
         + jnp.sum(grad_gain * grad_gain) / n_head
     )
-    squares = jnp.sum(lax.all_gather(jnp.full((8, 128), squares), "head"), axis=0)
+    squares = jnp.full((8, 128), squares)
+    if n_head & (n_head - 1):
+        squares = jnp.sum(lax.all_gather(squares, "head"), axis=0)
+    else:
+        for step in range(n_head.bit_length() - 1):
+            squares = squares + lax.ppermute(squares, "head", [(i, i ^ (1 << step)) for i in range(n_head)])
     lane = lax.broadcasted_iota(jnp.int32, (8, 128), 1)
     totals = jnp.sum(lax.all_gather(jnp.where(lane == 0, squares, loss_part), "ctx"), axis=0)
     loss = totals[0, 1]
@@ -808,17 +843,18 @@
     wide = 32
     spreads = (
         (1, 0, 0, ATTN_IN, D**-0.5),
-        (1, ATTN_IN, ATTN_IN, QG, (length / (4.0 * HEADS * HD)) ** 0.5),
+        (2, 0, ATTN_IN, QG, (length / (4.0 * HEADS * HD)) ** 0.5),
         (0, 0, ATTN_IN + QG, 2 * FFG, D**-0.5),
         (0, 2 * FFG, ATTN_IN + QG + 2 * FFG, FFG, FF**-0.5),
     )
     layer = call_update(
         functools.partial(layer_update_kernel, spreads),
         factor,
-        (g_ff, g_at),
+        (g_ff, g_in, g_out),
         [
             pl.BlockSpec((wide, g_ff.shape[1]), lambda i: (i, 0)),
-            pl.BlockSpec((wide, g_at.shape[1]), lambda i: (i, 0)),
+            pl.BlockSpec((wide, ATTN_IN), lambda i: (i, 0)),
+            pl.BlockSpec((wide, QG), lambda i: (i, 0)),
         ],
         w_layer,
         mom_layer,
@@ -826,6 +862,7 @@
         wide,
         "layer_update",
     )
+    g_head, *layer = lax.optimization_barrier((g_head, *layer))
     vocab = call_update(
         functools.partial(vocab_update_kernel, part),
         factor,

time: 791 us -> 743 us (0.939)
  waiting for transfers between devices: 298 us -> 263 us
  blocking collectives: 62.4 us -> 38.3 us
    all_to_all x1, waiting for transfers between devices: 17.5 us -> 0.01 us  [local(): lax.all_to_all(d_head.reshape(n_ctx, rows, part), 'ctx', 0, 0, tiled=True)]
    unnamed x1 -> x0, blocking collectives: 16 us -> none
    ppermute x3, waiting for transfers between devices: 22.1 us -> 8.2 us  [local(): lax.ppermute(moved, 'head', [(i, (i - s) % n_head) for i in range(n_head)])]
    all_to_all x1 -> x0, blocking collectives: 13.8 us -> none  [local(): lax.all_to_all(d_kv.reshape(n_ctx, tok, 2 * HD), 'ctx', 0, 0, tiled=True)]
    all_to_all x1, waiting for transfers between devices: 28.7 us -> 15.7 us  [local(): lax.all_to_all(d_kv.reshape(n_ctx, tok, 2 * HD), 'ctx', 0, 0, tiled=True)]
    ppermute x14 -> x19, waiting for transfers between devices: 50.4 us -> 60.3 us  [swap(): return lax.ppermute(x, 'ctx', [(i, i ^ bit) for i in range(n_ctx)])]
    ppermute x18, starting transfers between devices: 35.3 us -> 26.7 us  [head_scatter(): lax.ppermute(x[:, s], 'head', [(i, (i + s) % n_head) for i in range(n_hea...]
    ppermute x15, waiting for transfers between devices: 88.6 us -> 80.6 us  [head_gather(): lax.ppermute(x, 'head', [(i, (i - s) % n_head) for i in range(n_head)])]
  transfers between devices with their start and end apart: 62 -> 69, of which waited for: 36 -> 39; matrix products, arithmetic and copies ran while one was open for 9% -> 14% of each run, Pallas kernels for 15% -> 18%
where the time goes in v3:
time: 743 us; the launch traced here: 733 us
  waiting for transfers between devices  263 us (35%)
  Pallas kernels  191 us (26%)
  starting transfers between devices  106 us (14%)
  matrix products  49.3 us (7%)
  blocking collectives  38.3 us (5%)
  other arithmetic  38.1 us (5%)
  local copies, waits for them, and re-layouts  25.9 us (3%)
  between operations  21.5 us (3%)
    ppermute x15, waiting for transfers between devices, head_gather(): lax.ppermute(x, 'head', [(i, (i - s) % n_head) for i in range(n_head)])  80.6 us
    ppermute x18, waiting for transfers between devices, head_scatter(): lax.ppermute(x[:, s], 'head', [(i, (i + s) % n_head) for i in range(n_hea...  77 us
    ppermute x19, waiting for transfers between devices, swap(): return lax.ppermute(x, 'ctx', [(i, i ^ bit) for i in range(n_ctx)])  60.3 us
    pallas_call x2, Pallas kernels, call_update(): pl.pallas_call(kernel, grid=(total // rows,), in_specs=[pl.BlockSpec(memo...  54.1 us
    ppermute x15, starting transfers between devices, head_gather(): lax.ppermute(x, 'head', [(i, (i - s) % n_head) for i in range(n_head)])  31.7 us
    ppermute x18, starting transfers between devices, head_scatter(): lax.ppermute(x[:, s], 'head', [(i, (i + s) % n_head) for i in range(n_hea...  26.7 us
    pallas_call x2, Pallas kernels, outer_pair(): pl.pallas_call(functools.partial(outer_kernel, a_steps=a_steps), grid=(a_...  23.9 us
    pallas_call x1, Pallas kernels, head_dlogits(): pl.pallas_call(functools.partial(dlogits_kernel, steps, len(pieces) // at...  23.1 us
  transfers between devices with their start and end apart: 69, of which 39 were waited for; matrix products, arithmetic and copies ran while one was open for 14% of the time, Pallas kernels for 18%

profile of v3, /device:TPU:0, one launch (start us, length us, event | category | flops | bytes accessed | tf_op | source)
XLA Modules:
  0.0 732.8 jit_solution(16350038027163897065)
XLA Ops:
  12.7 10.6 %all-gather.3 = f32[8,1,1280]{2,1,0:T(1,128)S(1)} all-gather(f32[1,1,1280]{2,1,0:T(1,128)S(1)} %reshape.821), channel_id=2, replica_groups=mesh['ctx'=8,'head'=4] {'ctx'}, dimensions={0}, use_global_device_ids=true | all-gather | bytes 46080 | tf_op jit(solution)/shard_map/all_gather | solution.py:658
  25.4 7.7 %head_cast.1 = (bf16[128,8192]{1,0:T(8,128)(2,1)}, bf16[128,8192]{1,0:T(8,128)(2,1)}) custom-call(f32[256,16000]{1,0:T(8,128)} %w_ref.5), custom_call_target="tpu_custom_call" | custom-call | flops 2097152 | bytes 12582912 | tf_op jit(solution)/shard_map/head_cast/pallas_call | solution.py:342
  33.1 14.3 %embed_lookup.1 = bf16[2048,256]{1,0:T(8,128)(2,1)} custom-call(s32[2048,1]{1,0:T(8,128)} %copy.252.ids_ref, f32[256,16000]{1,0:T(8,128)} %w_ref.5), custom_call_target="tpu_custom_call" | custom-call | flops 8455716864 | bytes 8257536 | tf_op jit(solution)/shard_map/embed_lookup/pallas_call | solution.py:88
  59.7 10.7 %collective-permute-done.1 = bf16[16,32,256]{2,1,0:T(8,128)(2,1)S(1)} collective-permute-done((bf16[16,32,256]{2,1,0:T(8,128)(2,1)S(1)}, bf16[16,32,256]{2,1,0:T(8,128)(2,1)S(1)}, u32[]{:S(2)}, u32[]{:S(2)}) %collective-permute-start.1) | collective-permute-done | bytes 262176 | tf_op jit(solution)/shard_map/ppermute | solution.py:628
  72.2 3.4 all-to-all-start
  76.9 8.8 %all-to-all-done = bf16[8,64,256]{2,1,0:T(8,128)(2,1)S(1)} async-done(((bf16[8,64,256]{2,1,0:T(8,128)(2,1)}), bf16[8,64,256]{2,1,0:T(8,128)(2,1)S(1)}, u32[]{:S(2)}, u32[]{:S(2)}) %all-to-all-start) | async-done | bytes 262176 | tf_op jit(solution)/shard_map/all_to_all | solution.py:673
  87.3 7.2 collective-permute-start.3
  95.3 5.8 collective-permute-done.3
  101.1 14.0 %collective-permute-done.4 = bf16[2,32,2048]{2,1,0:T(8,128)(2,1)S(1)} collective-permute-done((bf16[2,32,2048]{2,1,0:T(8,128)(2,1)S(1)}, bf16[2,32,2048]{2,1,0:T(8,128)(2,1)S(1)}, u32[]{:S(2)}, u32[]{:S(2)}) %collective-permute-start.4) | collective-permute-done | bytes 262176 | tf_op jit(solution)/shard_map/ppermute | solution.py:635
  116.3 3.9 qkv.1
  120.2 13.8 %all-gather.1 = bf16[2048,128]{1,0:T(8,128)(2,1)} all-gather(bf16[256,128]{1,0:T(8,128)(2,1)} %get-tuple-element.74), channel_id=3, replica_groups=mesh['ctx'=8,'head'=4] {'ctx'}, dimensions={0}, use_global_device_ids=true | all-gather | bytes 589824 | tf_op jit(solution)/shard_map/all_gather | solution.py:696
  136.0 9.0 %attn_fwd.1.db_ref = bf16[256,512]{1,0:T(8,128)(2,1)} custom-call(bf16[256,512]{1,0:T(8,128)(2,1)} %get-tuple-element.73.q_ref, bf16[8,2,128,128]{3,2,1,0:T(8,128)(2,1)} %bitcast.391, s32[128,1]{1,0:T(8,128)} %fusion.55.qpos_ref, s32[1,1024]{1,0:T(1,128)} %bitcast.435), custom_call_target="tpu_custom_call" | custom-call | flops 1073741824 | bytes 524288 | tf_op jit(solution)/shard_map/attn_fwd/pallas_call | solution.py:222
  152.2 6.5 collective-permute-done.6
  158.7 10.1 %collective-permute-done.7 = bf16[2,32,2048]{2,1,0:T(8,128)(2,1)S(1)} collective-permute-done((bf16[2,32,2048]{2,1,0:T(8,128)(2,1)S(1)}, bf16[2,32,2048]{2,1,0:T(8,128)(2,1)S(1)}, u32[]{:S(2)}, u32[]{:S(2)}) %collective-permute-start.7) | collective-permute-done | bytes 262176 | tf_op jit(solution)/shard_map/ppermute | solution.py:628
  169.9 6.4 collective-permute-start.9
  177.3 5.7 collective-permute-done.9
  183.8 15.2 %collective-permute-done.10 = bf16[2,32,2048]{2,1,0:T(8,128)(2,1)S(1)} collective-permute-done((bf16[2,32,2048]{2,1,0:T(8,128)(2,1)S(1)}, bf16[2,32,2048]{2,1,0:T(8,128)(2,1)S(1)}, u32[]{:S(2)}, u32[]{:S(2)}) %collective-permute-start.10) | collective-permute-done | bytes 262176 | tf_op jit(solution)/shard_map/ppermute | solution.py:635
  201.1 6.6 fusion.2
  208.2 5.3 fusion.17
  214.4 3.1 collective-permute-start.16
  217.5 7.2 collective-permute-done.14
  224.7 8.5 %collective-permute-done.15 = bf16[2,32,2048]{2,1,0:T(8,128)(2,1)S(1)} collective-permute-done((bf16[2,32,2048]{2,1,0:T(8,128)(2,1)S(1)}, bf16[2,32,2048]{2,1,0:T(8,128)(2,1)S(1)}, u32[]{:S(2)}, u32[]{:S(2)}) %collective-permute-start.15) | collective-permute-done | bytes 262176 | tf_op jit(solution)/shard_map/ppermute | solution.py:628
  233.3 6.1 collective-permute-done.17.refs_4_
  239.4 5.9 collective-permute-done.18.refs_9_
  250.6 3.6 collective-permute-done.19
  254.2 13.1 %collective-permute-done.20 = bf16[2,32,2048]{2,1,0:T(8,128)(2,1)S(1)} collective-permute-done((bf16[2,32,2048]{2,1,0:T(8,128)(2,1)S(1)}, bf16[2,32,2048]{2,1,0:T(8,128)(2,1)S(1)}, u32[]{:S(2)}, u32[]{:S(2)}) %collective-permute-start.20) | collective-permute-done | bytes 262176 | tf_op jit(solution)/shard_map/ppermute | solution.py:635
  269.0 24.5 %collective-permute-done.22.refs_12_ = bf16[128,8192]{1,0:T(8,128)(2,1)} collective-permute-done((bf16[128,8192]{1,0:T(8,128)(2,1)}, bf16[128,8192]{1,0:T(8,128)(2,1)}, u32[]{:S(2)}, u32[]{:S(2)}) %collective-permute-start.22) | collective-permute-done | bytes 2097184 | tf_op jit(solution)/shard_map/ppermute | solution.py:654
  303.8 3.1 collective-permute-done.30.refs_14_
  310.0 20.0 %head_logits.1 = (f32[256,8192]{1,0:T(8,128)}, f32[8,256]{1,0:T(8,128)}) custom-call(s32[8]{0:T(128)} %stack.159.at_ref, bf16[256,2048]{1,0:T(8,128)(2,1)} %bitcast.333, s32[256,1]{1,0:T(8,128)} %and_select_fusion.slot_ref, bf16[128,8192]{1,0:T(8,128)(2,1)} %get-tuple-element.78.refs_0_, bf16[128,8192]{1,0:T(8,128)(2,1)} %get-tuple-element.79.refs_1_, ...), custom_call_target="tpu_custom_call" | custom-call | flops 8589934592 | bytes 41943040 | tf_op jit(solution)/shard_map/head_logits/pallas_call | solution.py:399
  339.8 23.1 %head_dlogits.1 = (bf16[8,256,1024]{2,1,0:T(8,128)(2,1)}, bf16[256,2048]{1,0:T(8,128)(2,1)}) custom-call(s32[8]{0:T(128)} %stack.159.at_ref, f32[256,8192]{1,0:T(8,128)} %get-tuple-element.89.logits_ref, f32[256,8]{1,0:T(8,128)} %bitcast.390, s32[256,1]{1,0:T(8,128)} %and_select_fusion.slot_ref, bf16[128,8192]{1,0:T(8,128)(2,1)} %get-tuple-element.78.refs_0_, ...), custom_call_target="tpu_custom_call" | custom-call | flops 8589934592 | bytes 46137344 | tf_op jit(solution)/shard_map/head_dlogits/pallas_call | solution.py:455
  364.4 4.5 collective-permute-start.36
  369.0 6.6 collective-permute-done.35
  375.6 7.7 %collective-permute-done.36 = bf16[2,32,2048]{2,1,0:T(8,128)(2,1)S(1)} collective-permute-done((bf16[2,32,2048]{2,1,0:T(8,128)(2,1)S(1)}, bf16[2,32,2048]{2,1,0:T(8,128)(2,1)S(1)}, u32[]{:S(2)}, u32[]{:S(2)}) %collective-permute-start.36) | collective-permute-done | bytes 262176 | tf_op jit(solution)/shard_map/ppermute | solution.py:628
  384.9 5.8 collective-permute-start.38
  392.5 4.6 all-to-all-start.1
  397.6 17.9 %collective-permute-done.39 = bf16[2,32,2048]{2,1,0:T(8,128)(2,1)S(1)} collective-permute-done((bf16[2,32,2048]{2,1,0:T(8,128)(2,1)S(1)}, bf16[2,32,2048]{2,1,0:T(8,128)(2,1)S(1)}, u32[]{:S(2)}, u32[]{:S(2)}) %collective-permute-start.39) | collective-permute-done | bytes 262176 | tf_op jit(solution)/shard_map/ppermute | solution.py:635
  415.7 5.9 fusion.46
  421.7 8.0 %fusion.11 = bf16[256,2048]{1,0:T(8,128)(2,1)S(1)} fusion(bf16[256,2816]{1,0:T(8,128)(2,1)S(1)} %add_convert_fusion.da_ref, bf16[2048,4224]{1,0:T(8,128)(2,1)} %all-gather.10.cloned.1.call-done), kind=kOutput, calls=%fused_computation.15 | convolution fusion | flops 2953314304 | bytes 14024704 | tf_op jit(solution)/shard_map/dot_general | solution.py:48
  430.9 3.7 collective-permute-start.43
  434.6 15.1 %ff_weight_grad.1 = bf16[2048,4224]{1,0:T(8,128)(2,1)} custom-call(bf16[256,2048]{1,0:T(8,128)(2,1)} %bitcast.351, bf16[256,2816]{1,0:T(8,128)(2,1)} %copy-done.2, bf16[256,2048]{1,0:T(8,128)(2,1)} %bitcast.353, bf16[256,1408]{1,0:T(8,128)(2,1)} %copy-done.7), custom_call_target="tpu_custom_call" | custom-call | flops 4429185024 | bytes 19398656 | tf_op jit(solution)/shard_map/ff_weight_grad/pallas_call | solution.py:496
  456.0 4.7 collective-permute-start.44
  462.9 16.8 %multiply_reduce_fusion = (f32[]{:T(128)}, bf16[2048,1024]{1,0:T(8,128)(2,1)}) fusion(bf16[2048,2048]{1,0:T(8,128)(2,1)} %all-gather.12.cloned.1.call-done, bf16[2048,1024]{1,0:T(8,128)(2,1)} %bitcast.85), kind=kOutput, calls=%fused_computation.4 | convolution fusion | flops 8596226048 | bytes 16777220 | tf_op jit(solution)/shard_map/dot_general | solution.py:52
  479.7 5.3 collective-permute-done.45
  485.1 3.4 fusion.27.do_ref
  488.5 18.8 %attn_bwd.1 = (bf16[256,512]{1,0:T(8,128)(2,1)}, bf16[8,2,128,128]{3,2,1,0:T(8,128)(2,1)}) custom-call(bf16[256,512]{1,0:T(8,128)(2,1)} %get-tuple-element.73.q_ref, bf16[256,512]{1,0:T(8,128)(2,1)} %fusion.27.do_ref, bf16[8,2,128,128]{3,2,1,0:T(8,128)(2,1)} %bitcast.392, s32[1,128]{1,0:T(1,128)} %fusion.82.qpos_ref, s32[1024,1]{1,0:T(8,128)} %copy.288.kpos_ref, ...), custom_call_target="tpu_custom_call" | custom-call | flops 2684354560 | bytes 1048576 | tf_op jit(solution)/shard_map/attn_bwd/pallas_call | solution.py:282
  507.3 3.5 all-to-all-start.2
  510.9 15.7 %all-to-all-done.2.parts_ref = bf16[8,256,128]{2,1,0:T(8,128)(2,1)S(1)} async-done(((bf16[8,256,128]{2,1,0:T(8,128)(2,1)}), bf16[8,256,128]{2,1,0:T(8,128)(2,1)S(1)}, u32[]{:S(2)}, u32[]{:S(2)}) %all-to-all-start.2) | async-done | bytes 524320 | tf_op jit(solution)/shard_map/all_to_all | solution.py:774
  531.2 8.8 %attn_weight_grad.1 = bf16[2048,1152]{1,0:T(8,128)(2,1)} custom-call(bf16[256,2048]{1,0:T(8,128)(2,1)} %bitcast.336, bf16[256,640]{1,0:T(8,128)(2,1)} %pad_maximum_fusion.6.da_ref, bf16[256,2048]{1,0:T(8,128)(2,1)} %bitcast.347, bf16[256,512]{1,0:T(8,128)(2,1)} %attn_fwd.1.db_ref), custom_call_target="tpu_custom_call" | custom-call | flops 1207959552 | bytes 6815744 | tf_op jit(solution)/shard_map/attn_weight_grad/pallas_call | solution.py:496
  540.0 3.3 dynamic-slice_bitcast_fusion
  549.0 7.5 %collective-permute-done.47 = bf16[2,32,2048]{2,1,0:T(8,128)(2,1)S(1)} collective-permute-done((bf16[2,32,2048]{2,1,0:T(8,128)(2,1)}, bf16[2,32,2048]{2,1,0:T(8,128)(2,1)S(1)}, u32[]{:S(2)}, u32[]{:S(2)}) %collective-permute-start.47) | collective-permute-done | bytes 262176 | tf_op jit(solution)/shard_map/ppermute | solution.py:628
  556.5 10.0 %collective-permute-done.48 = bf16[2,32,2048]{2,1,0:T(8,128)(2,1)S(1)} collective-permute-done((bf16[2,32,2048]{2,1,0:T(8,128)(2,1)S(1)}, bf16[2,32,2048]{2,1,0:T(8,128)(2,1)S(1)}, u32[]{:S(2)}, u32[]{:S(2)}) %collective-permute-start.48) | collective-permute-done | bytes 262176 | tf_op jit(solution)/shard_map/ppermute | solution.py:628
  568.1 3.6 all-to-all-start.3
  575.0 7.2 all-to-all-done.3
  582.2 3.4 collective-permute-start.55
  588.0 4.5 collective-permute-done.55
  592.5 5.6 collective-permute-done.53
  605.5 3.7 collective-permute-done.56
  611.3 4.7 all-to-all-start.4
  619.0 13.9 %embed_grad.1 = (bf16[256,8064]{1,0:T(8,128)(2,1)}, f32[8,128]{1,0:T(8,128)}) custom-call(s32[2048,1]{1,0:T(8,128)} %copy.252.ids_ref, bf16[256,2048]{1,0:T(8,128)(2,1)} %bitcast.373), custom_call_target="tpu_custom_call" | custom-call | flops 8455716864 | bytes 4128768 | tf_op jit(solution)/shard_map/embed_grad/pallas_call | solution.py:125
  637.3 3.3 multiply_reduce_fusion.1
  643.9 3.7 collective-permute-start.58
  654.3 13.9 %all-gather.2 = f32[64,128]{1,0:T(8,128)S(1)} all-gather(f32[8,128]{1,0:T(8,128)S(1)} %add_select_fusion.3), channel_id=4, replica_groups=mesh['ctx'=8,'head'=4] {'ctx'}, dimensions={0}, use_global_device_ids=true | all-gather | bytes 36864 | tf_op jit(solution)/shard_map/all_gather | solution.py:838
  669.6 15.0 %layer_update.1 = (f32[256,5376]{1,0:T(8,128)}, f32[256,5376]{1,0:T(8,128)}, f32[256,5376]{1,0:T(8,128)}, bf16[256,5376]{1,0:T(8,128)(2,1)}) custom-call(f32[1,1]{1,0:T(1,128)} %bitcast.133.factor_ref, bf16[256,4224]{1,0:T(8,128)(2,1)} %reduce-scatter.2.cloned.1.call-done.refs_0_, f32[256,640]{1,0:T(8,128)} %get-tuple-element.141.refs_1_, ...), custom_call_target="tpu_custom_call" | custom-call | flops 13762560 | bytes 38535168 | tf_op jit(solution)/shard_map/layer_update/pallas_call | solution.py:564
  685.8 39.1 %vocab_update.1 = (f32[256,16000]{1,0:T(8,128)}, f32[256,16000]{1,0:T(8,128)}, f32[256,16000]{1,0:T(8,128)}, bf16[256,16000]{1,0:T(8,128)(2,1)}) custom-call(f32[1,1]{1,0:T(1,128)} %bitcast.133.factor_ref, bf16[8,256,1024]{2,1,0:T(8,128)(2,1)} %all-to-all-done.4.head_ref, bf16[256,8064]{1,0:T(8,128)(2,1)} %get-tuple-element.121.embed_ref, ...), custom_call_target="tpu_custom_call" | custom-call | flops 40960000 | bytes 114688000 | tf_op jit(solution)/shard_map/vocab_update/pallas_call | solution.py:564
  (340 shorter events, 128.8 us)
Async XLA Ops:
  7.2 109.2 %all-gather.8.cloned.1.call-start = ((), (), s32[]{:S(2)}) async-start(), calls=%async_computation.6 | async-start | bytes 5308416 | tf_op jit(solution)/shard_map/all_gather | solution.py:647
  11.0 190.1 %all-gather.10.cloned.1.call-start = ((), (), s32[]{:S(2)}) async-start(), calls=%async_computation.7 | async-start | bytes 19464192 | tf_op jit(solution)/shard_map/all_gather | solution.py:648
  48.5 11.2 %collective-permute-start = (bf16[16,32,256]{2,1,0:T(8,128)(2,1)S(1)}, bf16[16,32,256]{2,1,0:T(8,128)(2,1)S(1)}, u32[]{:S(2)}, u32[]{:S(2)}) collective-permute-start(bf16[16,32,256]{2,1,0:T(8,128)(2,1)S(1)} %get-tuple-element.171), channel_id=1, source_target_pairs={{0,1},{1,2},{2,3},{3,0},{4,5},{5,6},{6,7},{7,4},{8,9},{9,10},{10,1... | collective-permute-start | bytes 786440 | tf_op jit(solution)/shard_map/ppermute | solution.py:628
  50.1 20.2 %collective-permute-start.1 = (bf16[16,32,256]{2,1,0:T(8,128)(2,1)S(1)}, bf16[16,32,256]{2,1,0:T(8,128)(2,1)S(1)}, u32[]{:S(2)}, u32[]{:S(2)}) collective-permute-start(bf16[16,32,256]{2,1,0:T(8,128)(2,1)S(1)} %get-tuple-element.172), channel_id=1, source_target_pairs={{0,2},{1,3},{2,0},{3,1},{4,6},{5,7},{6,4},{7,5},{8,10},{9,11},{10,... | collective-permute-start | bytes 786440 | tf_op jit(solution)/shard_map/ppermute | solution.py:628
  53.7 16.7 %collective-permute-start.2 = (bf16[16,32,256]{2,1,0:T(8,128)(2,1)S(1)}, bf16[16,32,256]{2,1,0:T(8,128)(2,1)S(1)}, u32[]{:S(2)}, u32[]{:S(2)}) collective-permute-start(bf16[16,32,256]{2,1,0:T(8,128)(2,1)S(1)} %slice_bitcast_fusion.23), channel_id=1, source_target_pairs={{0,3},{1,0},{2,1},{3,2},{4,7},{5,4},{6,5},{7,6},{8,11},{9,8},{10,9... | collective-permute-start | bytes 786440 | tf_op jit(solution)/shard_map/ppermute | solution.py:628
  72.2 13.5 %all-to-all-start = ((bf16[8,64,256]{2,1,0:T(8,128)(2,1)}), bf16[8,64,256]{2,1,0:T(8,128)(2,1)S(1)}, u32[]{:S(2)}, u32[]{:S(2)}) async-start(bf16[8,64,256]{2,1,0:T(8,128)(2,1)} %bitcast.8), calls=%async_computation | async-start | bytes 524288 | tf_op jit(solution)/shard_map/all_to_all | solution.py:673
  75.6 376.9 %all-gather.12.cloned.1.call-start = ((), (), s32[]{:S(2)}) async-start(), calls=%async_computation.8 | async-start | bytes 9437184 | tf_op jit(solution)/shard_map/all_gather | solution.py:756
  87.3 13.9 %collective-permute-start.3 = (bf16[2,32,2048]{2,1,0:T(8,128)(2,1)S(1)}, bf16[2,32,2048]{2,1,0:T(8,128)(2,1)S(1)}, u32[]{:S(2)}, u32[]{:S(2)}) collective-permute-start(bf16[2,32,2048]{2,1,0:T(8,128)(2,1)S(1)} %multiply_convert_fusion.3), channel_id=1, source_target_pairs={{0,3},{1,0},{2,1},{3,2},{4,7},{5,4},{6,5},{7,6},{8,11},{9,8},{10,9... | collective-permute-start | bytes 786440 | tf_op jit(solution)/shard_map/ppermute | solution.py:635
  94.5 20.7 %collective-permute-start.4 = (bf16[2,32,2048]{2,1,0:T(8,128)(2,1)S(1)}, bf16[2,32,2048]{2,1,0:T(8,128)(2,1)S(1)}, u32[]{:S(2)}, u32[]{:S(2)}) collective-permute-start(bf16[2,32,2048]{2,1,0:T(8,128)(2,1)S(1)} %multiply_convert_fusion.3), channel_id=1, source_target_pairs={{0,2},{1,3},{2,0},{3,1},{4,6},{5,7},{6,4},{7,5},{8,10},{9,11},{10,... | collective-permute-start | bytes 786440 | tf_op jit(solution)/shard_map/ppermute | solution.py:635
  94.9 20.2 %collective-permute-start.5 = (bf16[2,32,2048]{2,1,0:T(8,128)(2,1)S(1)}, bf16[2,32,2048]{2,1,0:T(8,128)(2,1)S(1)}, u32[]{:S(2)}, u32[]{:S(2)}) collective-permute-start(bf16[2,32,2048]{2,1,0:T(8,128)(2,1)S(1)} %multiply_convert_fusion.3), channel_id=1, source_target_pairs={{0,1},{1,2},{2,3},{3,0},{4,5},{5,6},{6,7},{7,4},{8,9},{9,10},{10,1... | collective-permute-start | bytes 786440 | tf_op jit(solution)/shard_map/ppermute | solution.py:635
  134.0 67.1 %collective-permute-start.12 = (bf16[128,8192]{1,0:T(8,128)(2,1)S(1)}, bf16[128,8192]{1,0:T(8,128)(2,1)}, u32[]{:S(2)}, u32[]{:S(2)}) collective-permute-start(bf16[128,8192]{1,0:T(8,128)(2,1)S(1)} %copy-done), channel_id=1, source_target_pairs={{0,16},{4,20},{8,24},{12,28},{16,0},{20,4},{24,8},{28,12},{1,17},{... | collective-permute-start | bytes 6291464 | tf_op jit(solution)/shard_map/ppermute | solution.py:654
  134.9 66.2 %collective-permute-start.13 = (bf16[128,8192]{1,0:T(8,128)(2,1)}, bf16[128,8192]{1,0:T(8,128)(2,1)}, u32[]{:S(2)}, u32[]{:S(2)}) collective-permute-start(bf16[128,8192]{1,0:T(8,128)(2,1)} %get-tuple-element.79.refs_1_), channel_id=1, source_target_pairs={{0,8},{4,12},{8,0},{12,4},{16,24},{20,28},{24,16},{28,20},{1,9},{5... | collective-permute-start | bytes 6291464 | tf_op jit(solution)/shard_map/ppermute | solution.py:654
  147.5 11.1 %collective-permute-start.6 = (bf16[2,32,2048]{2,1,0:T(8,128)(2,1)S(1)}, bf16[2,32,2048]{2,1,0:T(8,128)(2,1)S(1)}, u32[]{:S(2)}, u32[]{:S(2)}) collective-permute-start(bf16[2,32,2048]{2,1,0:T(8,128)(2,1)S(1)} %get-tuple-element.168), channel_id=1, source_target_pairs={{0,1},{1,2},{2,3},{3,0},{4,5},{5,6},{6,7},{7,4},{8,9},{9,10},{10,1... | collective-permute-start | bytes 786440 | tf_op jit(solution)/shard_map/ppermute | solution.py:628
  147.6 21.2 %collective-permute-start.7 = (bf16[2,32,2048]{2,1,0:T(8,128)(2,1)S(1)}, bf16[2,32,2048]{2,1,0:T(8,128)(2,1)S(1)}, u32[]{:S(2)}, u32[]{:S(2)}) collective-permute-start(bf16[2,32,2048]{2,1,0:T(8,128)(2,1)S(1)} %get-tuple-element.169), channel_id=1, source_target_pairs={{0,2},{1,3},{2,0},{3,1},{4,6},{5,7},{6,4},{7,5},{8,10},{9,11},{10,... | collective-permute-start | bytes 786440 | tf_op jit(solution)/shard_map/ppermute | solution.py:628
  149.3 19.5 %collective-permute-start.8 = (bf16[2,32,2048]{2,1,0:T(8,128)(2,1)S(1)}, bf16[2,32,2048]{2,1,0:T(8,128)(2,1)S(1)}, u32[]{:S(2)}, u32[]{:S(2)}) collective-permute-start(bf16[2,32,2048]{2,1,0:T(8,128)(2,1)S(1)} %get-tuple-element.170), channel_id=1, source_target_pairs={{0,3},{1,0},{2,1},{3,2},{4,7},{5,4},{6,5},{7,6},{8,11},{9,8},{10,9... | collective-permute-start | bytes 786440 | tf_op jit(solution)/shard_map/ppermute | solution.py:628
  169.9 13.1 %collective-permute-start.9 = (bf16[2,32,2048]{2,1,0:T(8,128)(2,1)S(1)}, bf16[2,32,2048]{2,1,0:T(8,128)(2,1)S(1)}, u32[]{:S(2)}, u32[]{:S(2)}) collective-permute-start(bf16[2,32,2048]{2,1,0:T(8,128)(2,1)S(1)} %multiply_convert_fusion.2), channel_id=1, source_target_pairs={{0,3},{1,0},{2,1},{3,2},{4,7},{5,4},{6,5},{7,6},{8,11},{9,8},{10,9... | collective-permute-start | bytes 786440 | tf_op jit(solution)/shard_map/ppermute | solution.py:635
  176.3 22.7 %collective-permute-start.10 = (bf16[2,32,2048]{2,1,0:T(8,128)(2,1)S(1)}, bf16[2,32,2048]{2,1,0:T(8,128)(2,1)S(1)}, u32[]{:S(2)}, u32[]{:S(2)}) collective-permute-start(bf16[2,32,2048]{2,1,0:T(8,128)(2,1)S(1)} %multiply_convert_fusion.2), channel_id=1, source_target_pairs={{0,2},{1,3},{2,0},{3,1},{4,6},{5,7},{6,4},{7,5},{8,10},{9,11},{10,... | collective-permute-start | bytes 786440 | tf_op jit(solution)/shard_map/ppermute | solution.py:635
  176.7 23.2 %collective-permute-start.11 = (bf16[2,32,2048]{2,1,0:T(8,128)(2,1)S(1)}, bf16[2,32,2048]{2,1,0:T(8,128)(2,1)S(1)}, u32[]{:S(2)}, u32[]{:S(2)}) collective-permute-start(bf16[2,32,2048]{2,1,0:T(8,128)(2,1)S(1)} %multiply_convert_fusion.2), channel_id=1, source_target_pairs={{0,1},{1,2},{2,3},{3,0},{4,5},{5,6},{6,7},{7,4},{8,9},{9,10},{10,1... | collective-permute-start | bytes 786440 | tf_op jit(solution)/shard_map/ppermute | solution.py:635
  183.1 56.3 %collective-permute-start.17 = (bf16[128,8192]{1,0:T(8,128)(2,1)S(1)}, bf16[128,8192]{1,0:T(8,128)(2,1)}, u32[]{:S(2)}, u32[]{:S(2)}) collective-permute-start(bf16[128,8192]{1,0:T(8,128)(2,1)S(1)} %copy-done), channel_id=1, source_target_pairs={{0,8},{4,12},{8,0},{12,4},{16,24},{20,28},{24,16},{28,20},{1,9},{5... | collective-permute-start | bytes 6291464 | tf_op jit(solution)/shard_map/ppermute | solution.py:654
  199.0 46.3 %collective-permute-start.18 = (bf16[128,8192]{1,0:T(8,128)(2,1)}, bf16[128,8192]{1,0:T(8,128)(2,1)}, u32[]{:S(2)}, u32[]{:S(2)}) collective-permute-start(bf16[128,8192]{1,0:T(8,128)(2,1)} %get-tuple-element.79.refs_1_), channel_id=1, source_target_pairs={{0,16},{4,20},{8,24},{12,28},{16,0},{20,4},{24,8},{28,12},{1,17},{... | collective-permute-start | bytes 6291464 | tf_op jit(solution)/shard_map/ppermute | solution.py:654
  213.6 11.1 %collective-permute-start.14 = (bf16[2,32,2048]{2,1,0:T(8,128)(2,1)S(1)}, bf16[2,32,2048]{2,1,0:T(8,128)(2,1)S(1)}, u32[]{:S(2)}, u32[]{:S(2)}) collective-permute-start(bf16[2,32,2048]{2,1,0:T(8,128)(2,1)S(1)} %get-tuple-element.165), channel_id=1, source_target_pairs={{0,1},{1,2},{2,3},{3,0},{4,5},{5,6},{6,7},{7,4},{8,9},{9,10},{10,1... | collective-permute-start | bytes 786440 | tf_op jit(solution)/shard_map/ppermute | solution.py:628
  213.6 19.5 %collective-permute-start.15 = (bf16[2,32,2048]{2,1,0:T(8,128)(2,1)S(1)}, bf16[2,32,2048]{2,1,0:T(8,128)(2,1)S(1)}, u32[]{:S(2)}, u32[]{:S(2)}) collective-permute-start(bf16[2,32,2048]{2,1,0:T(8,128)(2,1)S(1)} %get-tuple-element.167), channel_id=1, source_target_pairs={{0,2},{1,3},{2,0},{3,1},{4,6},{5,7},{6,4},{7,5},{8,10},{9,11},{10,... | collective-permute-start | bytes 786440 | tf_op jit(solution)/shard_map/ppermute | solution.py:628
  214.4 18.8 %collective-permute-start.16 = (bf16[2,32,2048]{2,1,0:T(8,128)(2,1)S(1)}, bf16[2,32,2048]{2,1,0:T(8,128)(2,1)S(1)}, u32[]{:S(2)}, u32[]{:S(2)}) collective-permute-start(bf16[2,32,2048]{2,1,0:T(8,128)(2,1)S(1)} %get-tuple-element.166), channel_id=1, source_target_pairs={{0,3},{1,0},{2,1},{3,2},{4,7},{5,4},{6,5},{7,6},{8,11},{9,8},{10,9... | collective-permute-start | bytes 786440 | tf_op jit(solution)/shard_map/ppermute | solution.py:628
  246.5 7.7 %collective-permute-start.19 = (bf16[2,32,2048]{2,1,0:T(8,128)(2,1)S(1)}, bf16[2,32,2048]{2,1,0:T(8,128)(2,1)S(1)}, u32[]{:S(2)}, u32[]{:S(2)}) collective-permute-start(bf16[2,32,2048]{2,1,0:T(8,128)(2,1)S(1)} %bitcast.382), channel_id=1, source_target_pairs={{0,3},{1,0},{2,1},{3,2},{4,7},{5,4},{6,5},{7,6},{8,11},{9,8},{10,9... | collective-permute-start | bytes 786440 | tf_op jit(solution)/shard_map/ppermute | solution.py:635
  246.6 20.7 %collective-permute-start.20 = (bf16[2,32,2048]{2,1,0:T(8,128)(2,1)S(1)}, bf16[2,32,2048]{2,1,0:T(8,128)(2,1)S(1)}, u32[]{:S(2)}, u32[]{:S(2)}) collective-permute-start(bf16[2,32,2048]{2,1,0:T(8,128)(2,1)S(1)} %bitcast.383), channel_id=1, source_target_pairs={{0,2},{1,3},{2,0},{3,1},{4,6},{5,7},{6,4},{7,5},{8,10},{9,11},{10,... | collective-permute-start | bytes 786440 | tf_op jit(solution)/shard_map/ppermute | solution.py:635
  246.7 20.7 %collective-permute-start.21 = (bf16[2,32,2048]{2,1,0:T(8,128)(2,1)S(1)}, bf16[2,32,2048]{2,1,0:T(8,128)(2,1)S(1)}, u32[]{:S(2)}, u32[]{:S(2)}) collective-permute-start(bf16[2,32,2048]{2,1,0:T(8,128)(2,1)S(1)} %bitcast.384), channel_id=1, source_target_pairs={{0,1},{1,2},{2,3},{3,0},{4,5},{5,6},{6,7},{7,4},{8,9},{9,10},{10,1... | collective-permute-start | bytes 786440 | tf_op jit(solution)/shard_map/ppermute | solution.py:635
  248.6 44.9 %collective-permute-start.22 = (bf16[128,8192]{1,0:T(8,128)(2,1)}, bf16[128,8192]{1,0:T(8,128)(2,1)}, u32[]{:S(2)}, u32[]{:S(2)}) collective-permute-start(bf16[128,8192]{1,0:T(8,128)(2,1)} %collective-permute-done.12.refs_8_), channel_id=1, source_target_pairs={{0,8},{4,12},{8,0},{12,4},{16,24},{20,28},{24,16},{28,20},{1,9},{5... | collective-permute-start | bytes 6291464 | tf_op jit(solution)/shard_map/ppermute | solution.py:654
  249.5 44.6 %collective-permute-start.23 = (bf16[128,8192]{1,0:T(8,128)(2,1)}, bf16[128,8192]{1,0:T(8,128)(2,1)}, u32[]{:S(2)}, u32[]{:S(2)}) collective-permute-start(bf16[128,8192]{1,0:T(8,128)(2,1)} %collective-permute-done.13.refs_5_), channel_id=1, source_target_pairs={{0,16},{4,20},{8,24},{12,28},{16,0},{20,4},{24,8},{28,12},{1,17},{... | collective-permute-start | bytes 6291464 | tf_op jit(solution)/shard_map/ppermute | solution.py:654
  254.2 39.9 %collective-permute-start.24 = (bf16[128,8192]{1,0:T(8,128)(2,1)S(1)}, bf16[128,8192]{1,0:T(8,128)(2,1)}, u32[]{:S(2)}, u32[]{:S(2)}) collective-permute-start(bf16[128,8192]{1,0:T(8,128)(2,1)S(1)} %copy-done), channel_id=1, source_target_pairs={{0,4},{4,0},{8,12},{12,8},{16,20},{20,16},{24,28},{28,24},{1,5},{5... | collective-permute-start | bytes 6291464 | tf_op jit(solution)/shard_map/ppermute | solution.py:654
  267.3 27.3 %collective-permute-start.25 = (bf16[128,8192]{1,0:T(8,128)(2,1)}, bf16[128,8192]{1,0:T(8,128)(2,1)}, u32[]{:S(2)}, u32[]{:S(2)}) collective-permute-start(bf16[128,8192]{1,0:T(8,128)(2,1)} %get-tuple-element.79.refs_1_), channel_id=1, source_target_pairs={{0,4},{4,0},{8,12},{12,8},{16,20},{20,16},{24,28},{28,24},{1,5},{5... | collective-permute-start | bytes 6291464 | tf_op jit(solution)/shard_map/ppermute | solution.py:654
  267.3 27.3 %collective-permute-start.27 = (bf16[128,8192]{1,0:T(8,128)(2,1)}, bf16[128,8192]{1,0:T(8,128)(2,1)}, u32[]{:S(2)}, u32[]{:S(2)}) collective-permute-start(bf16[128,8192]{1,0:T(8,128)(2,1)} %collective-permute-done.13.refs_5_), channel_id=1, source_target_pairs={{0,4},{4,0},{8,12},{12,8},{16,20},{20,16},{24,28},{28,24},{1,5},{5... | collective-permute-start | bytes 6291464 | tf_op jit(solution)/shard_map/ppermute | solution.py:654
  294.1 6.9 collective-permute-start.26
  294.1 9.8 %collective-permute-start.29 = (bf16[128,8192]{1,0:T(8,128)(2,1)}, bf16[128,8192]{1,0:T(8,128)(2,1)S(1)}, u32[]{:S(2)}, u32[]{:S(2)}) collective-permute-start(bf16[128,8192]{1,0:T(8,128)(2,1)} %collective-permute-done.18.refs_9_), channel_id=1, source_target_pairs={{0,4},{4,0},{8,12},{12,8},{16,20},{20,16},{24,28},{28,24},{1,5},{5... | collective-permute-start | bytes 6291464 | tf_op jit(solution)/shard_map/ppermute | solution.py:654
  294.6 12.4 %collective-permute-start.30 = (bf16[128,8192]{1,0:T(8,128)(2,1)}, bf16[128,8192]{1,0:T(8,128)(2,1)}, u32[]{:S(2)}, u32[]{:S(2)}) collective-permute-start(bf16[128,8192]{1,0:T(8,128)(2,1)} %collective-permute-done.22.refs_12_), channel_id=1, source_target_pairs={{0,4},{4,0},{8,12},{12,8},{16,20},{20,16},{24,28},{28,24},{1,5},{5... | collective-permute-start | bytes 6291464 | tf_op jit(solution)/shard_map/ppermute | solution.py:654
  294.7 15.3 %collective-permute-start.31 = (bf16[128,8192]{1,0:T(8,128)(2,1)}, bf16[128,8192]{1,0:T(8,128)(2,1)}, u32[]{:S(2)}, u32[]{:S(2)}) collective-permute-start(bf16[128,8192]{1,0:T(8,128)(2,1)} %collective-permute-done.23.refs_13_), channel_id=1, source_target_pairs={{0,4},{4,0},{8,12},{12,8},{16,20},{20,16},{24,28},{28,24},{1,5},{5... | collective-permute-start | bytes 6291464 | tf_op jit(solution)/shard_map/ppermute | solution.py:654
  330.0 6.4 collective-permute-start.34
  364.1 11.6 %collective-permute-start.35 = (bf16[2,32,2048]{2,1,0:T(8,128)(2,1)S(1)}, bf16[2,32,2048]{2,1,0:T(8,128)(2,1)S(1)}, u32[]{:S(2)}, u32[]{:S(2)}) collective-permute-start(bf16[2,32,2048]{2,1,0:T(8,128)(2,1)S(1)} %get-tuple-element.162), channel_id=1, source_target_pairs={{0,1},{1,2},{2,3},{3,0},{4,5},{5,6},{6,7},{7,4},{8,9},{9,10},{10,1... | collective-permute-start | bytes 786440 | tf_op jit(solution)/shard_map/ppermute | solution.py:628
  364.4 18.9 %collective-permute-start.36 = (bf16[2,32,2048]{2,1,0:T(8,128)(2,1)S(1)}, bf16[2,32,2048]{2,1,0:T(8,128)(2,1)S(1)}, u32[]{:S(2)}, u32[]{:S(2)}) collective-permute-start(bf16[2,32,2048]{2,1,0:T(8,128)(2,1)S(1)} %get-tuple-element.164), channel_id=1, source_target_pairs={{0,2},{1,3},{2,0},{3,1},{4,6},{5,7},{6,4},{7,5},{8,10},{9,11},{10,... | collective-permute-start | bytes 786440 | tf_op jit(solution)/shard_map/ppermute | solution.py:628
  369.0 14.4 %collective-permute-start.37 = (bf16[2,32,2048]{2,1,0:T(8,128)(2,1)S(1)}, bf16[2,32,2048]{2,1,0:T(8,128)(2,1)S(1)}, u32[]{:S(2)}, u32[]{:S(2)}) collective-permute-start(bf16[2,32,2048]{2,1,0:T(8,128)(2,1)S(1)} %get-tuple-element.163), channel_id=1, source_target_pairs={{0,3},{1,0},{2,1},{3,2},{4,7},{5,4},{6,5},{7,6},{8,11},{9,8},{10,9... | collective-permute-start | bytes 786440 | tf_op jit(solution)/shard_map/ppermute | solution.py:628
  384.9 12.7 %collective-permute-start.38 = (bf16[2,32,2048]{2,1,0:T(8,128)(2,1)S(1)}, bf16[2,32,2048]{2,1,0:T(8,128)(2,1)S(1)}, u32[]{:S(2)}, u32[]{:S(2)}) collective-permute-start(bf16[2,32,2048]{2,1,0:T(8,128)(2,1)S(1)} %bitcast.386), channel_id=1, source_target_pairs={{0,3},{1,0},{2,1},{3,2},{4,7},{5,4},{6,5},{7,6},{8,11},{9,8},{10,9... | collective-permute-start | bytes 786440 | tf_op jit(solution)/shard_map/ppermute | solution.py:635
  390.7 24.8 %collective-permute-start.39 = (bf16[2,32,2048]{2,1,0:T(8,128)(2,1)S(1)}, bf16[2,32,2048]{2,1,0:T(8,128)(2,1)S(1)}, u32[]{:S(2)}, u32[]{:S(2)}) collective-permute-start(bf16[2,32,2048]{2,1,0:T(8,128)(2,1)S(1)} %bitcast.387), channel_id=1, source_target_pairs={{0,2},{1,3},{2,0},{3,1},{4,6},{5,7},{6,4},{7,5},{8,10},{9,11},{10,... | collective-permute-start | bytes 786440 | tf_op jit(solution)/shard_map/ppermute | solution.py:635
  392.5 23.1 %collective-permute-start.40 = (bf16[2,32,2048]{2,1,0:T(8,128)(2,1)S(1)}, bf16[2,32,2048]{2,1,0:T(8,128)(2,1)S(1)}, u32[]{:S(2)}, u32[]{:S(2)}) collective-permute-start(bf16[2,32,2048]{2,1,0:T(8,128)(2,1)S(1)} %bitcast.388), channel_id=1, source_target_pairs={{0,1},{1,2},{2,3},{3,0},{4,5},{5,6},{6,7},{7,4},{8,9},{9,10},{10,1... | collective-permute-start | bytes 786440 | tf_op jit(solution)/shard_map/ppermute | solution.py:635
  392.5 60.0 %all-to-all-start.1 = ((bf16[8,256,1024]{2,1,0:T(8,128)(2,1)}), bf16[8,256,1024]{2,1,0:T(8,128)(2,1)}, u32[]{:S(2)}, u32[]{:S(2)}) async-start(bf16[8,256,1024]{2,1,0:T(8,128)(2,1)} %get-tuple-element.93), calls=%async_computation.1 | async-start | bytes 8388608 | tf_op jit(solution)/shard_map/all_to_all | solution.py:757
  397.0 240.3 %reduce-scatter.2.cloned.1.call-start = ((), (), s32[]{:S(2)}) async-start(), calls=%async_computation.9 | async-start | bytes 19464192 | tf_op jit(solution)/shard_map/reduce_scatter | solution.py:766
  430.7 19.0 %collective-permute-start.41 = (bf16[2,32,2048]{2,1,0:T(8,128)(2,1)S(1)}, bf16[2,32,2048]{2,1,0:T(8,128)(2,1)S(1)}, u32[]{:S(2)}, u32[]{:S(2)}) collective-permute-start(bf16[2,32,2048]{2,1,0:T(8,128)(2,1)S(1)} %get-tuple-element.159), channel_id=1, source_target_pairs={{0,1},{1,2},{2,3},{3,0},{4,5},{5,6},{6,7},{7,4},{8,9},{9,10},{10,1... | collective-permute-start | bytes 786440 | tf_op jit(solution)/shard_map/ppermute | solution.py:628
  430.8 20.5 %collective-permute-start.42 = (bf16[2,32,2048]{2,1,0:T(8,128)(2,1)S(1)}, bf16[2,32,2048]{2,1,0:T(8,128)(2,1)S(1)}, u32[]{:S(2)}, u32[]{:S(2)}) collective-permute-start(bf16[2,32,2048]{2,1,0:T(8,128)(2,1)S(1)} %get-tuple-element.161), channel_id=1, source_target_pairs={{0,2},{1,3},{2,0},{3,1},{4,6},{5,7},{6,4},{7,5},{8,10},{9,11},{10,... | collective-permute-start | bytes 786440 | tf_op jit(solution)/shard_map/ppermute | solution.py:628
  430.9 20.5 %collective-permute-start.43 = (bf16[2,32,2048]{2,1,0:T(8,128)(2,1)S(1)}, bf16[2,32,2048]{2,1,0:T(8,128)(2,1)S(1)}, u32[]{:S(2)}, u32[]{:S(2)}) collective-permute-start(bf16[2,32,2048]{2,1,0:T(8,128)(2,1)S(1)} %get-tuple-element.160), channel_id=1, source_target_pairs={{0,3},{1,0},{2,1},{3,2},{4,7},{5,4},{6,5},{7,6},{8,11},{9,8},{10,9... | collective-permute-start | bytes 786440 | tf_op jit(solution)/shard_map/ppermute | solution.py:628
  456.0 23.7 %collective-permute-start.44 = (bf16[2,32,2048]{2,1,0:T(8,128)(2,1)S(1)}, bf16[2,32,2048]{2,1,0:T(8,128)(2,1)S(1)}, u32[]{:S(2)}, u32[]{:S(2)}) collective-permute-start(bf16[2,32,2048]{2,1,0:T(8,128)(2,1)S(1)} %bitcast.375), channel_id=1, source_target_pairs={{0,3},{1,0},{2,1},{3,2},{4,7},{5,4},{6,5},{7,6},{8,11},{9,8},{10,9... | collective-permute-start | bytes 786440 | tf_op jit(solution)/shard_map/ppermute | solution.py:635
  460.7 24.3 %collective-permute-start.45 = (bf16[2,32,2048]{2,1,0:T(8,128)(2,1)S(1)}, bf16[2,32,2048]{2,1,0:T(8,128)(2,1)S(1)}, u32[]{:S(2)}, u32[]{:S(2)}) collective-permute-start(bf16[2,32,2048]{2,1,0:T(8,128)(2,1)S(1)} %bitcast.376), channel_id=1, source_target_pairs={{0,2},{1,3},{2,0},{3,1},{4,6},{5,7},{6,4},{7,5},{8,10},{9,11},{10,... | collective-permute-start | bytes 786440 | tf_op jit(solution)/shard_map/ppermute | solution.py:635
  462.8 22.2 %collective-permute-start.46 = (bf16[2,32,2048]{2,1,0:T(8,128)(2,1)S(1)}, bf16[2,32,2048]{2,1,0:T(8,128)(2,1)S(1)}, u32[]{:S(2)}, u32[]{:S(2)}) collective-permute-start(bf16[2,32,2048]{2,1,0:T(8,128)(2,1)S(1)} %bitcast.377), channel_id=1, source_target_pairs={{0,1},{1,2},{2,3},{3,0},{4,5},{5,6},{6,7},{7,4},{8,9},{9,10},{10,1... | collective-permute-start | bytes 786440 | tf_op jit(solution)/shard_map/ppermute | solution.py:635
  507.3 19.2 %all-to-all-start.2 = ((bf16[8,256,128]{2,1,0:T(8,128)(2,1)}), bf16[8,256,128]{2,1,0:T(8,128)(2,1)S(1)}, u32[]{:S(2)}, u32[]{:S(2)}) async-start(bf16[8,256,128]{2,1,0:T(8,128)(2,1)} %bitcast.393), calls=%async_computation.2 | async-start | bytes 1048576 | tf_op jit(solution)/shard_map/all_to_all | solution.py:774
  543.3 23.3 %collective-permute-start.50 = (bf16[2,2,256,1152]{3,2,1,0:T(8,128)(2,1)}, bf16[2,2,256,1152]{3,2,1,0:T(8,128)(2,1)}, u32[]{:S(2)}, u32[]{:S(2)}) collective-permute-start(bf16[2,2,256,1152]{3,2,1,0:T(8,128)(2,1)} %dynamic-slice_bitcast_fusion), channel_id=1, source_target_pairs={{0,4},{4,0},{8,12},{12,8},{16,20},{20,16},{24,28},{28,24},{1,5},{5... | collective-permute-start | bytes 7077896 | tf_op jit(solution)/shard_map/ppermute | solution.py:654
  545.2 11.3 %collective-permute-start.47 = (bf16[2,32,2048]{2,1,0:T(8,128)(2,1)}, bf16[2,32,2048]{2,1,0:T(8,128)(2,1)S(1)}, u32[]{:S(2)}, u32[]{:S(2)}) collective-permute-start(bf16[2,32,2048]{2,1,0:T(8,128)(2,1)} %get-tuple-element.156), channel_id=1, source_target_pairs={{0,1},{1,2},{2,3},{3,0},{4,5},{5,6},{6,7},{7,4},{8,9},{9,10},{10,1... | collective-permute-start | bytes 786440 | tf_op jit(solution)/shard_map/ppermute | solution.py:628
  545.2 21.4 %collective-permute-start.48 = (bf16[2,32,2048]{2,1,0:T(8,128)(2,1)S(1)}, bf16[2,32,2048]{2,1,0:T(8,128)(2,1)S(1)}, u32[]{:S(2)}, u32[]{:S(2)}) collective-permute-start(bf16[2,32,2048]{2,1,0:T(8,128)(2,1)S(1)} %get-tuple-element.158), channel_id=1, source_target_pairs={{0,2},{1,3},{2,0},{3,1},{4,6},{5,7},{6,4},{7,5},{8,10},{9,11},{10,... | collective-permute-start | bytes 786440 | tf_op jit(solution)/shard_map/ppermute | solution.py:628
  546.0 20.5 %collective-permute-start.49 = (bf16[2,32,2048]{2,1,0:T(8,128)(2,1)S(1)}, bf16[2,32,2048]{2,1,0:T(8,128)(2,1)S(1)}, u32[]{:S(2)}, u32[]{:S(2)}) collective-permute-start(bf16[2,32,2048]{2,1,0:T(8,128)(2,1)S(1)} %get-tuple-element.157), channel_id=1, source_target_pairs={{0,3},{1,0},{2,1},{3,2},{4,7},{5,4},{6,5},{7,6},{8,11},{9,8},{10,9... | collective-permute-start | bytes 786440 | tf_op jit(solution)/shard_map/ppermute | solution.py:628
  568.1 14.0 %all-to-all-start.3 = ((bf16[80,8,256]{2,0,1:T(8,128)(2,1)}), bf16[80,8,256]{2,0,1:T(8,128)(2,1)S(1)}, u32[]{:S(2)}, u32[]{:S(2)}) async-start(bf16[80,8,256]{2,0,1:T(8,128)(2,1)} %copy.292), calls=%async_computation.3 | async-start | bytes 655360 | tf_op jit(solution)/shard_map/all_to_all | solution.py:796
  582.2 10.3 %collective-permute-start.55 = (bf16[528,256]{1,0:T(8,128)(2,1)S(1)}, bf16[528,256]{1,0:T(8,128)(2,1)S(1)}, u32[]{:S(2)}, u32[]{:S(2)}) collective-permute-start(bf16[528,256]{1,0:T(8,128)(2,1)S(1)} %pad_maximum_fusion.8), channel_id=1, source_target_pairs={{0,3},{1,0},{2,1},{3,2},{4,7},{5,4},{6,5},{7,6},{8,11},{9,8},{10,9... | collective-permute-start | bytes 811016 | tf_op jit(solution)/shard_map/ppermute | solution.py:816
  585.6 12.5 %collective-permute-start.53 = (bf16[2,256,512]{2,1,0:T(8,128)(2,1)S(1)}, bf16[2,256,512]{2,1,0:T(8,128)(2,1)S(1)}, u32[]{:S(2)}, u32[]{:S(2)}) collective-permute-start(bf16[2,256,512]{2,1,0:T(8,128)(2,1)S(1)} %dynamic-slice_bitcast_fusion.2), channel_id=1, source_target_pairs={{0,16},{4,20},{8,24},{12,28},{16,0},{20,4},{24,8},{28,12},{1,17},{... | collective-permute-start | bytes 1572872 | tf_op jit(solution)/shard_map/ppermute | solution.py:654
  586.3 16.7 %collective-permute-start.51 = (bf16[2,256,640]{2,1,0:T(8,128)(2,1)S(1)}, bf16[2,256,640]{2,1,0:T(8,128)(2,1)S(1)}, u32[]{:S(2)}, u32[]{:S(2)}) collective-permute-start(bf16[2,256,640]{2,1,0:T(8,128)(2,1)S(1)} %dynamic-slice_bitcast_fusion.1), channel_id=1, source_target_pairs={{0,8},{4,12},{8,0},{12,4},{16,24},{20,28},{24,16},{28,20},{1,9},{5... | collective-permute-start | bytes 1966088 | tf_op jit(solution)/shard_map/ppermute | solution.py:654
  586.9 22.3 %collective-permute-start.56 = (bf16[528,256]{1,0:T(8,128)(2,1)S(1)}, bf16[528,256]{1,0:T(8,128)(2,1)S(1)}, u32[]{:S(2)}, u32[]{:S(2)}) collective-permute-start(bf16[528,256]{1,0:T(8,128)(2,1)S(1)} %pad_maximum_fusion.8), channel_id=1, source_target_pairs={{0,2},{1,3},{2,0},{3,1},{4,6},{5,7},{6,4},{7,5},{8,10},{9,11},{10,... | collective-permute-start | bytes 811016 | tf_op jit(solution)/shard_map/ppermute | solution.py:816
  587.9 21.3 %collective-permute-start.57 = (bf16[528,256]{1,0:T(8,128)(2,1)S(1)}, bf16[528,256]{1,0:T(8,128)(2,1)S(1)}, u32[]{:S(2)}, u32[]{:S(2)}) collective-permute-start(bf16[528,256]{1,0:T(8,128)(2,1)S(1)} %pad_maximum_fusion.8), channel_id=1, source_target_pairs={{0,1},{1,2},{2,3},{3,0},{4,5},{5,6},{6,7},{7,4},{8,9},{9,10},{10,1... | collective-permute-start | bytes 811016 | tf_op jit(solution)/shard_map/ppermute | solution.py:816
  598.3 10.9 %collective-permute-start.54 = (bf16[256,512]{1,0:T(8,128)(2,1)S(1)}, bf16[256,512]{1,0:T(8,128)(2,1)S(1)}, u32[]{:S(2)}, u32[]{:S(2)}) collective-permute-start(bf16[256,512]{1,0:T(8,128)(2,1)S(1)} %dynamic-slice_bitcast_fusion.4), channel_id=1, source_target_pairs={{0,8},{4,12},{8,0},{12,4},{16,24},{20,28},{24,16},{28,20},{1,9},{5... | collective-permute-start | bytes 786440 | tf_op jit(solution)/shard_map/ppermute | solution.py:654
  603.2 7.4 %collective-permute-start.52 = (bf16[256,640]{1,0:T(8,128)(2,1)S(1)}, bf16[256,640]{1,0:T(8,128)(2,1)S(1)}, u32[]{:S(2)}, u32[]{:S(2)}) collective-permute-start(bf16[256,640]{1,0:T(8,128)(2,1)S(1)} %dynamic-slice_bitcast_fusion.3), channel_id=1, source_target_pairs={{0,16},{4,20},{8,24},{12,28},{16,0},{20,4},{24,8},{28,12},{1,17},{... | collective-permute-start | bytes 983048 | tf_op jit(solution)/shard_map/ppermute | solution.py:654
  611.3 73.9 %all-to-all-start.4 = ((bf16[8,256,1024]{2,1,0:T(8,128)(2,1)}), bf16[8,256,1024]{2,1,0:T(8,128)(2,1)}, u32[]{:S(2)}, u32[]{:S(2)}) async-start(bf16[8,256,1024]{2,1,0:T(8,128)(2,1)} %bitcast.348), calls=%async_computation.4 | async-start | bytes 8388608 | tf_op jit(solution)/shard_map/all_to_all | solution.py:810
  (46 other events, 507.2 us)
Sparse Core Ops, SparseCore 0:
  11.1 41.4 all-gather.7
  55.1 109.2 all-gather.9
  330.1 53.5 all-gather.11
  452.6 129.4 reduce-scatter.1

commit v4 on v3

--- a/solution.py
+++ b/solution.py
@@ -357,8 +357,40 @@
         yield k // parts, run[0] if parts == 1 else jnp.concatenate(run, axis=0)
 
 
-def logits_kernel(steps, parts, at_ref, x_ref, slot_ref, *refs):
-    pieces, (out_ref, stats_ref, top_ref, total_ref, label_ref) = refs[:-5], refs[-5:]
+def partial_kernel(parts, at_ref, x_ref, *refs):
+    pieces, out_ref = refs[:-1], refs[-1]
+    logits = None
+    for k, w in joined(pieces, parts):
+        at = pl.multiple_of(at_ref[k], 128)
+        term = dot_nn(x_ref[:, pl.ds(at, w.shape[0])], w)
+        logits = term if logits is None else logits + term
+    out_ref[...] = logits
+
+
+def head_partial(x, pieces, at):
+    tok = x.shape[0]
+    width = pieces[0].shape[1]
+    rows = sum(piece.shape[0] for piece in pieces)
+    block = 1024
+    return pl.pallas_call(
+        functools.partial(partial_kernel, len(pieces) // at.shape[0]),
+        grid=(width // block,),
+        in_specs=[
+            pl.BlockSpec(memory_space=pltpu.SMEM),
+            pl.BlockSpec((tok, D), lambda i: (0, 0)),
+        ]
+        + [pl.BlockSpec((piece.shape[0], block), lambda i: (0, i)) for piece in pieces],
+        out_specs=pl.BlockSpec((tok, block), lambda i: (0, i)),
+        out_shape=jax.ShapeDtypeStruct((tok, width), f32),
+        compiler_params=params(),
+        cost_estimate=cost(2 * tok * rows * width, 2 * rows * width + 4 * tok * width),
+        name="head_partial",
+    )(at, x, *pieces)
+
+
+def logits_kernel(steps, parts, based, at_ref, x_ref, slot_ref, *refs):
+    base = refs[:based]
+    pieces, (out_ref, stats_ref, top_ref, total_ref, label_ref) = refs[based:-5], refs[-5:]
     step = pl.program_id(0)
     block = out_ref.shape[1]
 
@@ -368,7 +400,7 @@
         total_ref[...] = jnp.zeros_like(total_ref)
         label_ref[...] = jnp.zeros_like(label_ref)
 
-    logits = None
+    logits = base[0][...] if based else None
     for k, w in joined(pieces, parts):
         at = pl.multiple_of(at_ref[k], 128)
         term = dot_nn(x_ref[:, pl.ds(at, w.shape[0])], w)
@@ -391,19 +423,21 @@
         stats_ref[...] = packed.T[:8]
 
 
-def head_logits(x, slots, pieces, at):
+def head_logits(x, slots, base, pieces, at):
     tok = x.shape[0]
+    rows = sum(piece.shape[0] for piece in pieces)
     width = pieces[0].shape[1]
     block = 1024
     steps = width // block
     return pl.pallas_call(
-        functools.partial(logits_kernel, steps, len(pieces) // at.shape[0]),
+        functools.partial(logits_kernel, steps, len(pieces) // at.shape[0], len(base)),
         grid=(steps,),
         in_specs=[
             pl.BlockSpec(memory_space=pltpu.SMEM),
             pl.BlockSpec((tok, D), lambda i: (0, 0)),
             pl.BlockSpec((tok, 1), lambda i: (0, 0)),
         ]
+        + [pl.BlockSpec((tok, block), lambda i: (0, i)) for _ in base]
         + [pl.BlockSpec((piece.shape[0], block), lambda i: (0, i)) for piece in pieces],
         out_specs=[
             pl.BlockSpec((tok, block), lambda i: (0, i)),
@@ -415,9 +449,9 @@
         ],
         scratch_shapes=[pltpu.VMEM((tok, 1), f32)] * 3,
         compiler_params=params(),
-        cost_estimate=cost(2 * tok * D * width, 2 * D * width + 4 * tok * width, tok * width),
+        cost_estimate=cost(2 * tok * rows * width, 2 * rows * width + 8 * tok * width, tok * width),
         name="head_logits",
-    )(at, x, slots, *pieces)
+    )(at, x, slots, *base, *pieces)
 
 
 def dlogits_kernel(steps, parts, at_ref, logits_ref, values_ref, slot_ref, *refs):
@@ -668,12 +702,14 @@
     inside = (local_ids >= 0) & (local_ids < VG)
     slots = jnp.where(inside, local_ids + (VG - EMB_AT), -1).reshape(-1, 1)
     picked = lookup(slots, w_vocab).reshape(n_ctx * SEQS, n_head, chunk, rows)
-    picked, *head_own = lax.optimization_barrier((picked, *head_own))
     picked = head_scatter(picked).astype(bf16).reshape(n_ctx * own, rows)
     x0 = lax.all_to_all(picked, "ctx", 0, 1, tiled=True).astype(f32)
 
     unit0, scale0 = norm_parts(x0)
     a1 = spread_all(unit0 * gain_rows[0])
+    if corners:
+        over = [swap(x, 1) for x in head_own]
+        a1, low, high, over_low, over_high = lax.optimization_barrier((a1, *head_own, *over))
     row = (jnp.arange(seq_tok, dtype=jnp.int32) + shard * chunk) % seq_tok
 
     def positions(index):
@@ -694,11 +730,9 @@
     sine = jnp.sin(angle) * (mscale * sign)[None, :]
     q, kv_own = qkv(a1, w_attn, cosine, sine)
     kv_every = lax.all_gather(kv_own, "ctx").reshape(n_ctx, SEQS, seq_tok, 2 * HD)
-    kv_every, *head_own = lax.optimization_barrier((kv_every, *head_own))
     if corners:
-        low, high = head_own
+        kv_every, low, high = lax.optimization_barrier((kv_every, low, high))
         y_low, x_high, x_low, y_high = swap(low, 4), swap(high, 2), swap(low, 2), swap(high, 4)
-        over_low, over_high = swap(low, 1), swap(high, 1)
     attn_b = attn(q, kv_every, qpos, kpos)
     x1 = x0 + sum_own(dot_nt(attn_b, w_out))
 
@@ -707,7 +741,6 @@
     if corners:
         a2, y_low, x_high = lax.optimization_barrier((a2, y_low, x_high))
         far_low, far_high = swap(y_low, 2), swap(x_high, 4)
-        over_y_low, over_x_high = swap(y_low, 1), swap(x_high, 1)
     gate_up = dot_nn(a2, w_gu)
 
     def glu(values):
@@ -717,10 +750,7 @@
     hidden_b = hidden_f.astype(bf16)
     second = sum_own(dot_nt(hidden_b, w_down))
     if corners:
-        second, *placed = lax.optimization_barrier(
-            (second, x_low, y_high)
-        )
-        x_low, y_high = placed
+        second, x_low, y_high = lax.optimization_barrier((second, x_low, y_high))
     x2 = x1 + second
 
     unit2, scale2 = norm_parts(x2)
@@ -728,15 +758,18 @@
     label_ids = labels_own - offset_id
     label_slots = jnp.where((label_ids >= 0) & (label_ids < VG), label_ids, -1).reshape(tok, 1)
     if corners:
-        over_x_low, over_y_high = swap(x_low, 1), swap(y_high, 1)
-        final_b, far_low, far_high = lax.optimization_barrier((final_b, far_low, far_high))
-        head_pieces = [low, high, over_low, over_high, x_low, x_high, over_x_low, over_x_high, y_low, y_high, over_y_low, over_y_high]
-        head_pieces += [far_low, far_high, swap(far_low, 1), swap(far_high, 1)]
-        head_at = jnp.stack([(place ^ bits) * rows for bits in (0, 1, 2, 3, 4, 5, 6, 7)])
+        near = [low, high, over_low, over_high, x_low, x_high, y_low, y_high]
+        head_at = jnp.stack([(place ^ bits) * rows for bits in (0, 1, 2, 4, 3, 5, 6, 7)])
+        base = head_partial(final_b, near, head_at[:4])
+        base, far_low, far_high = lax.optimization_barrier((base, far_low, far_high))
+        far = [swap(x, 1) for x in (x_low, x_high, y_low, y_high)]
+        far += [far_low, far_high, swap(far_low, 1), swap(far_high, 1)]
+        head_pieces = near + far
+        logits, stats = head_logits(final_b, label_slots, [base], far, head_at[4:])
     else:
         head_pieces = [lax.all_gather(head_own[0], "ctx", axis=0, tiled=True)]
         head_at = jnp.zeros((1,), jnp.int32)
-    logits, stats = head_logits(final_b, label_slots, head_pieces, head_at)
+        logits, stats = head_logits(final_b, label_slots, [], head_pieces, head_at)
     stats, final_late = lax.optimization_barrier((stats, final_b))
     pieces = [stats]
     for s in range(1, n_head):
@@ -771,10 +804,8 @@
     dya_b, d_head = lax.optimization_barrier((spread_all(dx1), d_head.astype(bf16)))
     d_attn_b = dot_nn(dya_b, w_out).astype(bf16)
     d_q, d_kv = attn_back(q, d_attn_b, kv_every, qpos, kpos, cosine, sine)
+    d_out = dot_tn(dya_b, attn_b).astype(bf16)
     d_kv = lax.all_to_all(d_kv.reshape(n_ctx, tok, 2 * HD), "ctx", 0, 0, tiled=True)
-    d_raw_b = jnp.concatenate([d_q, kv_back(d_kv, cosine, sine)], axis=1)
-    d_first = sum_own(dot_nt(d_raw_b, w_attn[:, :ATTN_IN]))
-    d_at = outer_pair(a1, d_raw_b, dya_b, attn_b, 128, 2048, "attn_weight_grad")
     if corners:
         core, along_x, along_y = place & 1, (place >> 1) & 1, place >> 2
 
@@ -785,28 +816,36 @@
             kept = lax.dynamic_index_in_dim(x, mine, axis, keepdims=False)
             return kept, swap(lax.dynamic_index_in_dim(x, 1 - mine, axis, keepdims=False), bit)
 
-        kept, sent = split(d_at.reshape(2, 2, 2, rows, ATTN_IN + QG), core, 2, 1)
-        d_first, sent = lax.optimization_barrier((d_first, sent))
-        d_pair = total(kept, sent).astype(bf16)
-        d_in, d_out = d_pair[..., :ATTN_IN], d_pair[..., ATTN_IN:]
+        out_kept, out_sent = split(d_out.reshape(2, 2, 2, rows, QG), core, 2, 1)
+    d_raw_b = jnp.concatenate([d_q, kv_back(d_kv, cosine, sine)], axis=1)
+    d_first = sum_own(dot_nt(d_raw_b, w_attn[:, :ATTN_IN]))
+    d_in = dot_tn(a1, d_raw_b).astype(bf16)
+    if corners:
+        d_first, d_in, out_sent = lax.optimization_barrier((d_first, d_in, out_sent))
+        d_out = total(out_kept, out_sent).astype(bf16)
+        in_kept, in_sent = split(d_in.reshape(2, 2, 2, rows, ATTN_IN), core, 2, 1)
     dx0_norm, d_gain0 = norm_back(d_first, unit0, scale0, gain_rows[0])
     dx0 = dx1 + dx0_norm
 
     extra = jnp.pad(jnp.stack([d_gain0, d_gain1, d_gain2]), ((0, 13), (0, 0)))
     moved = lax.all_to_all(jnp.concatenate([dx0, extra]).astype(bf16), "ctx", 1, 0, tiled=True)
     if corners:
-        moved, d_in, d_out = lax.optimization_barrier((moved, d_in, d_out))
+        moved, in_sent, d_out = lax.optimization_barrier((moved, in_sent, d_out))
+        d_in = total(in_kept, in_sent).astype(bf16)
         in_kept, in_sent = split(d_in, along_x, 1, 2)
         out_kept, out_sent = split(d_out, along_y, 0, 4)
         d_in, d_out = total(in_kept, in_sent).astype(bf16), total(out_kept, out_sent).astype(bf16)
         in_kept, in_sent = split(d_in, along_y, 0, 4)
         out_kept, out_sent = split(d_out, along_x, 0, 2)
-        d_head, in_sent, out_sent = lax.optimization_barrier((d_head, in_sent, out_sent))
+        ff_sq = jnp.sum(jnp.square(g_ff.astype(f32)))
+        d_head, in_sent, out_sent, ff_sq = lax.optimization_barrier((d_head, in_sent, out_sent, ff_sq))
         g_in, g_out = total(in_kept, in_sent), total(out_kept, out_sent)
     else:
-        moved, d_head, d_at, g_ff = lax.optimization_barrier((moved, d_head, d_at, g_ff))
-        g_at = lax.psum_scatter(d_at, "ctx", scatter_dimension=0, tiled=True).astype(f32)
-        g_in, g_out = g_at[:, :ATTN_IN], g_at[:, ATTN_IN:]
+        moved, d_head, d_in, d_out, g_ff = lax.optimization_barrier((moved, d_head, d_in, d_out, g_ff))
+        g_in, g_out = (
+            lax.psum_scatter(x, "ctx", scatter_dimension=0, tiled=True).astype(f32) for x in (d_in, d_out)
+        )
+        ff_sq = jnp.sum(jnp.square(g_ff.astype(f32)))
     g_head = lax.all_to_all(d_head.reshape(n_ctx, rows, part), "ctx", 0, 0, tiled=True)
     moved = moved.reshape(n_ctx, own + 16, rows)
     gain_part = jnp.sum(moved[:, own:].astype(f32), axis=0).astype(bf16)
@@ -821,7 +860,7 @@
     g_embed, embed_sq = embed_grad(slots, dx0_all.reshape(n_ctx * tok, rows).T)
 
     squares = (
-        jnp.sum(jnp.square(g_ff.astype(f32)))
+        ff_sq
         + jnp.sum(jnp.square(g_in))
         + jnp.sum(jnp.square(g_out))
         + head_sq

time: 743 us -> 723 us (0.973)
  waiting for transfers between devices: 263 us -> 220 us
    ppermute x19 -> x20, waiting for transfers between devices: 60.3 us -> 25.1 us  [swap(): return lax.ppermute(x, 'ctx', [(i, i ^ bit) for i in range(n_ctx)])]
    pallas_call x0 -> x1, Pallas kernels: none -> 13.6 us  [head_partial(): pl.pallas_call(functools.partial(partial_kernel, len(pieces) // at.shape[...]
    ppermute x15, waiting for transfers between devices: 80.6 us -> 71.5 us  [head_gather(): lax.ppermute(x, 'head', [(i, (i - s) % n_head) for i in range(n_head)])]
    pallas_call x2 -> x1, Pallas kernels: 23.9 us -> 15.2 us  [outer_pair(): pl.pallas_call(functools.partial(outer_kernel, a_steps=a_steps), grid=(a_...]
    ppermute x18, waiting for transfers between devices: 77 us -> 68.3 us  [head_scatter(): lax.ppermute(x[:, s], 'head', [(i, (i + s) % n_head) for i in range(n_hea...]
    ppermute x3, waiting for transfers between devices: 8.2 us -> 16.4 us  [local(): lax.ppermute(moved, 'head', [(i, (i - s) % n_head) for i in range(n_head)])]
    dot_general x1 -> x3, matrix products: 16.8 us -> 18.5 us  [dot_tn(): lax.dot_general(a, b, (((0,), (0,)), ((), ())), preferred_element_type=f32)]
  transfers between devices with their start and end apart: 69 -> 70, of which waited for: 39 -> 37; matrix products, arithmetic and copies ran while one was open for 14% -> 17% of each run, Pallas kernels for 18% -> 19%
where the time goes in v4:
time: 723 us; the launch traced here: 713 us
  waiting for transfers between devices  220 us (30%)
  Pallas kernels  193 us (27%)
  starting transfers between devices  112 us (15%)
  matrix products  52.7 us (7%)
  other arithmetic  42.8 us (6%)
  blocking collectives  42.2 us (6%)
  local copies, waits for them, and re-layouts  29.5 us (4%)
  between operations  21.5 us (3%)
    ppermute x15, waiting for transfers between devices, head_gather(): lax.ppermute(x, 'head', [(i, (i - s) % n_head) for i in range(n_head)])  71.5 us
    ppermute x18, waiting for transfers between devices, head_scatter(): lax.ppermute(x[:, s], 'head', [(i, (i + s) % n_head) for i in range(n_hea...  68.3 us
    pallas_call x2, Pallas kernels, call_update(): pl.pallas_call(kernel, grid=(total // rows,), in_specs=[pl.BlockSpec(memo...  54.1 us
    ppermute x15, starting transfers between devices, head_gather(): lax.ppermute(x, 'head', [(i, (i - s) % n_head) for i in range(n_head)])  36.3 us
    ppermute x18, starting transfers between devices, head_scatter(): lax.ppermute(x[:, s], 'head', [(i, (i + s) % n_head) for i in range(n_hea...  26.8 us
    ppermute x20, waiting for transfers between devices, swap(): return lax.ppermute(x, 'ctx', [(i, i ^ bit) for i in range(n_ctx)])  25.1 us
    pallas_call x1, Pallas kernels, head_dlogits(): pl.pallas_call(functools.partial(dlogits_kernel, steps, len(pieces) // at...  23.3 us
    pallas_call x1, Pallas kernels, attn_back(): pl.pallas_call(functools.partial(attn_back_kernel, pairs), grid=(SEQS, pa...  18.8 us
  transfers between devices with their start and end apart: 70, of which 37 were waited for; matrix products, arithmetic and copies ran while one was open for 17% of the time, Pallas kernels for 19%

profile of v4, /device:TPU:0, one launch (start us, length us, event | category | flops | bytes accessed | tf_op | source)
XLA Modules:
  0.0 713.5 jit_solution(5946834120830772399)
XLA Ops:
  7.2 2.8 convert_element_type.324
  13.2 10.6 %all-gather.3 = f32[8,1,1280]{2,1,0:T(1,128)S(1)} all-gather(f32[1,1,1280]{2,1,0:T(1,128)S(1)} %reshape.828), channel_id=2, replica_groups=mesh['ctx'=8,'head'=4] {'ctx'}, dimensions={0}, use_global_device_ids=true | all-gather | bytes 46080 | tf_op jit(solution)/shard_map/all_gather | solution.py:692
  26.0 14.3 %embed_lookup.1 = bf16[2048,256]{1,0:T(8,128)(2,1)} custom-call(s32[2048,1]{1,0:T(8,128)} %copy.260.ids_ref, f32[256,16000]{1,0:T(8,128)} %w_ref.5), custom_call_target="tpu_custom_call" | custom-call | flops 8455716864 | bytes 8257536 | tf_op jit(solution)/shard_map/embed_lookup/pallas_call | solution.py:88
  47.7 7.7 %head_cast.1 = (bf16[128,8192]{1,0:T(8,128)(2,1)}, bf16[128,8192]{1,0:T(8,128)(2,1)}) custom-call(f32[256,16000]{1,0:T(8,128)} %w_ref.5), custom_call_target="tpu_custom_call" | custom-call | flops 2097152 | bytes 12582912 | tf_op jit(solution)/shard_map/head_cast/pallas_call | solution.py:342
  59.9 4.2 collective-permute-done.1
  66.0 3.4 all-to-all-start
  70.7 8.8 %all-to-all-done = bf16[8,64,256]{2,1,0:T(8,128)(2,1)S(1)} async-done(((bf16[8,64,256]{2,1,0:T(8,128)(2,1)}), bf16[8,64,256]{2,1,0:T(8,128)(2,1)S(1)}, u32[]{:S(2)}, u32[]{:S(2)}) %all-to-all-start) | async-done | bytes 262176 | tf_op jit(solution)/shard_map/all_to_all | solution.py:706
  81.2 7.1 collective-permute-start.3
  91.0 4.0 collective-permute-done.3
  95.0 14.1 %collective-permute-done.4 = bf16[2,32,2048]{2,1,0:T(8,128)(2,1)} collective-permute-done((bf16[2,32,2048]{2,1,0:T(8,128)(2,1)S(1)}, bf16[2,32,2048]{2,1,0:T(8,128)(2,1)}, u32[]{:S(2)}, u32[]{:S(2)}) %collective-permute-start.4) | collective-permute-done | bytes 262176 | tf_op jit(solution)/shard_map/ppermute | solution.py:669
  112.8 4.2 qkv.1
  116.9 13.6 %all-gather.1 = bf16[2048,128]{1,0:T(8,128)(2,1)} all-gather(bf16[256,128]{1,0:T(8,128)(2,1)} %get-tuple-element.78), channel_id=3, replica_groups=mesh['ctx'=8,'head'=4] {'ctx'}, dimensions={0}, use_global_device_ids=true | all-gather | bytes 589824 | tf_op jit(solution)/shard_map/all_gather | solution.py:732
  132.5 9.0 %attn_fwd.1 = bf16[256,512]{1,0:T(8,128)(2,1)} custom-call(bf16[256,512]{1,0:T(8,128)(2,1)} %get-tuple-element.77.q_ref, bf16[8,2,128,128]{3,2,1,0:T(8,128)(2,1)} %bitcast.406, s32[128,1]{1,0:T(8,128)} %fusion.56.qpos_ref, s32[1,1024]{1,0:T(1,128)} %bitcast.445), custom_call_target="tpu_custom_call" | custom-call | flops 1073741824 | bytes 524288 | tf_op jit(solution)/shard_map/attn_fwd/pallas_call | solution.py:222
  147.9 10.5 %collective-permute-done.10 = bf16[2,32,2048]{2,1,0:T(8,128)(2,1)S(1)} collective-permute-done((bf16[2,32,2048]{2,1,0:T(8,128)(2,1)S(1)}, bf16[2,32,2048]{2,1,0:T(8,128)(2,1)S(1)}, u32[]{:S(2)}, u32[]{:S(2)}) %collective-permute-start.10) | collective-permute-done | bytes 262176 | tf_op jit(solution)/shard_map/ppermute | solution.py:662
  160.2 8.8 %collective-permute-done.9 = bf16[2,32,2048]{2,1,0:T(8,128)(2,1)S(1)} collective-permute-done((bf16[2,32,2048]{2,1,0:T(8,128)(2,1)S(1)}, bf16[2,32,2048]{2,1,0:T(8,128)(2,1)S(1)}, u32[]{:S(2)}, u32[]{:S(2)}) %collective-permute-start.9) | collective-permute-done | bytes 262176 | tf_op jit(solution)/shard_map/ppermute | solution.py:662
  173.6 5.8 collective-permute-done.11
  180.1 14.1 %collective-permute-done.12 = bf16[2,32,2048]{2,1,0:T(8,128)(2,1)S(1)} collective-permute-done((bf16[2,32,2048]{2,1,0:T(8,128)(2,1)S(1)}, bf16[2,32,2048]{2,1,0:T(8,128)(2,1)S(1)}, u32[]{:S(2)}, u32[]{:S(2)}) %collective-permute-start.12) | collective-permute-done | bytes 262176 | tf_op jit(solution)/shard_map/ppermute | solution.py:669
  195.4 6.6 fusion.2
  202.5 5.3 fusion.17
  210.8 2.7 collective-permute-start.18
  213.6 5.5 collective-permute-done.16
  220.2 8.0 %collective-permute-done.17 = bf16[2,32,2048]{2,1,0:T(8,128)(2,1)S(1)} collective-permute-done((bf16[2,32,2048]{2,1,0:T(8,128)(2,1)S(1)}, bf16[2,32,2048]{2,1,0:T(8,128)(2,1)S(1)}, u32[]{:S(2)}, u32[]{:S(2)}) %collective-permute-start.17) | collective-permute-done | bytes 262176 | tf_op jit(solution)/shard_map/ppermute | solution.py:662
  229.6 10.0 %collective-permute-done.19.refs_4_ = bf16[128,8192]{1,0:T(8,128)(2,1)} collective-permute-done((bf16[128,8192]{1,0:T(8,128)(2,1)S(1)}, bf16[128,8192]{1,0:T(8,128)(2,1)}, u32[]{:S(2)}, u32[]{:S(2)}) %collective-permute-start.19) | collective-permute-done | bytes 2097184 | tf_op jit(solution)/shard_map/ppermute | solution.py:688
  239.6 3.4 collective-permute-done.20.refs_7_
  243.6 7.1 collective-permute-done.21
  250.6 11.3 %collective-permute-start.23 = (bf16[2,32,2048]{2,1,0:T(8,128)(2,1)S(1)}, bf16[2,32,2048]{2,1,0:T(8,128)(2,1)}, u32[]{:S(2)}, u32[]{:S(2)}) collective-permute-start(bf16[2,32,2048]{2,1,0:T(8,128)(2,1)S(1)} %bitcast.399), channel_id=1, source_target_pairs={{0,1},{1,2},{2,3},{3,0},{4,5},{5,6},{6,7},{7,4},{8,9},{9,10},{10,1... | collective-permute-start | bytes 786440 | tf_op jit(solution)/shard_map/ppermute | solution.py:669
  262.6 3.3 collective-permute-done.22
  268.7 13.6 %head_partial.1.refs_0_ = f32[256,8192]{1,0:T(8,128)} custom-call(s32[4]{0:T(128)} %pad_add_fusion.1.at_ref, bf16[256,2048]{1,0:T(8,128)(2,1)} %bitcast.352, bf16[128,8192]{1,0:T(8,128)(2,1)} %get-tuple-element.82.refs_0_, bf16[128,8192]{1,0:T(8,128)(2,1)} %get-tuple-element.83.refs_1_, bf16[128,8192]{1,0:T(8,128)(2,1)} %copy-done.2, ...), custom_call_target="tpu_custom_call" | custom-call | flops 4294967296 | bytes 25165824 | tf_op jit(solution)/shard_map/head_partial/pallas_call | solution.py:375
  288.8 3.0 collective-permute-done.30.refs_7_.refs_14_
  291.8 3.0 collective-permute-done.31.refs_8_.refs_15_
  294.8 17.0 %head_logits.1 = (f32[256,8192]{1,0:T(8,128)}, f32[8,256]{1,0:T(8,128)}) custom-call(s32[4]{0:T(128)} %pad_add_fusion.at_ref, bf16[256,2048]{1,0:T(8,128)(2,1)} %bitcast.353, s32[256,1]{1,0:T(8,128)} %and_select_fusion.slot_ref, f32[256,8192]{1,0:T(8,128)} %head_partial.1.refs_0_, bf16[128,8192]{1,0:T(8,128)(2,1)} %collective-permute-done.26.refs_1_.refs_8_, ...), custom_call_target="tpu_custom_call" | custom-call | flops 4294967296 | bytes 33554432 | tf_op jit(solution)/shard_map/head_logits/pallas_call | solution.py:432
  322.9 23.3 %head_dlogits.1 = (bf16[8,256,1024]{2,1,0:T(8,128)(2,1)}, bf16[256,2048]{1,0:T(8,128)(2,1)}) custom-call(s32[8]{0:T(128)} %stack.163.at_ref, f32[256,8192]{1,0:T(8,128)} %get-tuple-element.95.logits_ref, f32[256,8]{1,0:T(8,128)} %bitcast.405, s32[256,1]{1,0:T(8,128)} %and_select_fusion.slot_ref, bf16[128,8192]{1,0:T(8,128)(2,1)} %get-tuple-element.82.refs_0_, ...), custom_call_target="tpu_custom_call" | custom-call | flops 8589934592 | bytes 46137344 | tf_op jit(solution)/shard_map/head_dlogits/pallas_call | solution.py:489
  347.5 3.7 collective-permute-start.36
  351.3 7.2 %collective-permute-done.35 = bf16[2,32,2048]{2,1,0:T(8,128)(2,1)S(1)} collective-permute-done((bf16[2,32,2048]{2,1,0:T(8,128)(2,1)S(1)}, bf16[2,32,2048]{2,1,0:T(8,128)(2,1)S(1)}, u32[]{:S(2)}, u32[]{:S(2)}) %collective-permute-start.35) | collective-permute-done | bytes 262176 | tf_op jit(solution)/shard_map/ppermute | solution.py:662
  358.5 7.6 %collective-permute-done.36 = bf16[2,32,2048]{2,1,0:T(8,128)(2,1)S(1)} collective-permute-done((bf16[2,32,2048]{2,1,0:T(8,128)(2,1)S(1)}, bf16[2,32,2048]{2,1,0:T(8,128)(2,1)S(1)}, u32[]{:S(2)}, u32[]{:S(2)}) %collective-permute-start.36) | collective-permute-done | bytes 262176 | tf_op jit(solution)/shard_map/ppermute | solution.py:662
  367.6 6.3 collective-permute-start.38
  375.2 4.6 all-to-all-start.1
  380.6 17.6 %collective-permute-done.39 = bf16[2,32,2048]{2,1,0:T(8,128)(2,1)S(1)} collective-permute-done((bf16[2,32,2048]{2,1,0:T(8,128)(2,1)S(1)}, bf16[2,32,2048]{2,1,0:T(8,128)(2,1)S(1)}, u32[]{:S(2)}, u32[]{:S(2)}) %collective-permute-start.39) | collective-permute-done | bytes 262176 | tf_op jit(solution)/shard_map/ppermute | solution.py:669
  398.4 5.9 fusion.47
  404.4 8.0 %fusion.11 = bf16[256,2048]{1,0:T(8,128)(2,1)S(1)} fusion(bf16[256,2816]{1,0:T(8,128)(2,1)S(1)} %add_convert_fusion.da_ref, bf16[2048,4224]{1,0:T(8,128)(2,1)} %all-gather.10.cloned.1.call-done), kind=kOutput, calls=%fused_computation.17 | convolution fusion | flops 2953314304 | bytes 14024704 | tf_op jit(solution)/shard_map/dot_general | solution.py:48
  413.3 3.8 collective-permute-start.43
  417.1 15.2 %ff_weight_grad.1 = bf16[2048,4224]{1,0:T(8,128)(2,1)} custom-call(bf16[256,2048]{1,0:T(8,128)(2,1)} %bitcast.369, bf16[256,2816]{1,0:T(8,128)(2,1)} %copy-done.6, bf16[256,2048]{1,0:T(8,128)(2,1)} %bitcast.371, bf16[256,1408]{1,0:T(8,128)(2,1)} %copy-done.11), custom_call_target="tpu_custom_call" | custom-call | flops 4429185024 | bytes 19398656 | tf_op jit(solution)/shard_map/ff_weight_grad/pallas_call | solution.py:530
  440.2 5.3 collective-permute-start.44
  446.5 16.8 %multiply_reduce_fusion = (f32[]{:T(128)}, bf16[2048,1024]{1,0:T(8,128)(2,1)}) fusion(bf16[2048,2048]{1,0:T(8,128)(2,1)} %all-gather.12.cloned.1.call-done, bf16[2048,1024]{1,0:T(8,128)(2,1)} %bitcast.85), kind=kOutput, calls=%fused_computation.4 | convolution fusion | flops 8596226048 | bytes 16777220 | tf_op jit(solution)/shard_map/dot_general | solution.py:52
  463.2 5.2 collective-permute-done.45
  468.6 3.0 fusion.28.do_ref
  471.6 18.8 %attn_bwd.1 = (bf16[256,512]{1,0:T(8,128)(2,1)}, bf16[8,2,128,128]{3,2,1,0:T(8,128)(2,1)}) custom-call(bf16[256,512]{1,0:T(8,128)(2,1)} %get-tuple-element.77.q_ref, bf16[256,512]{1,0:T(8,128)(2,1)} %fusion.28.do_ref, bf16[8,2,128,128]{3,2,1,0:T(8,128)(2,1)} %bitcast.407, s32[1,128]{1,0:T(1,128)} %fusion.83.qpos_ref, s32[1024,1]{1,0:T(8,128)} %copy.296.kpos_ref, ...), custom_call_target="tpu_custom_call" | custom-call | flops 2684354560 | bytes 1048576 | tf_op jit(solution)/shard_map/attn_bwd/pallas_call | solution.py:282
  490.4 4.1 all-to-all-start.2
  495.8 14.4 %all-to-all-done.2.parts_ref = bf16[8,256,128]{2,1,0:T(8,128)(2,1)} async-done(((bf16[8,256,128]{2,1,0:T(8,128)(2,1)}), bf16[8,256,128]{2,1,0:T(8,128)(2,1)}, u32[]{:S(2)}, u32[]{:S(2)}) %all-to-all-start.2) | async-done | bytes 524320 | tf_op jit(solution)/shard_map/all_to_all | solution.py:808
  512.3 3.0 fusion.14
  516.7 2.8 collective-permute-start.49
  520.6 6.0 collective-permute-done.47
  526.6 7.0 collective-permute-done.48
  536.7 4.3 all-to-all-start.3
  543.5 9.1 %all-to-all-done.3 = bf16[80,8,256]{2,0,1:T(8,128)(2,1)} async-done(((bf16[80,8,256]{2,0,1:T(8,128)(2,1)}), bf16[80,8,256]{2,0,1:T(8,128)(2,1)}, u32[]{:S(2)}, u32[]{:S(2)}) %all-to-all-start.3) | async-done | bytes 327712 | tf_op jit(solution)/shard_map/all_to_all | solution.py:831
  554.4 6.0 collective-permute-start.56
  567.3 14.4 %collective-permute-done.57 = bf16[528,256]{1,0:T(8,128)(2,1)S(1)} collective-permute-done((bf16[528,256]{1,0:T(8,128)(2,1)S(1)}, bf16[528,256]{1,0:T(8,128)(2,1)S(1)}, u32[]{:S(2)}, u32[]{:S(2)}) %collective-permute-start.57) | collective-permute-done | bytes 270368 | tf_op jit(solution)/shard_map/ppermute | solution.py:855
  587.7 3.3 multiply_reduce_fusion.1
  592.0 4.6 all-to-all-start.4
  600.7 13.8 %embed_grad.1 = (bf16[256,8064]{1,0:T(8,128)(2,1)}, f32[8,128]{1,0:T(8,128)}) custom-call(s32[2048,1]{1,0:T(8,128)} %copy.260.ids_ref, bf16[256,2048]{1,0:T(8,128)(2,1)} %bitcast.384), custom_call_target="tpu_custom_call" | custom-call | flops 8455716864 | bytes 4128768 | tf_op jit(solution)/shard_map/embed_grad/pallas_call | solution.py:125
  622.5 3.2 collective-permute-done.59
  630.9 18.0 %all-gather.2 = f32[64,128]{1,0:T(8,128)S(1)} all-gather(f32[8,128]{1,0:T(8,128)S(1)} %add_select_fusion.3), channel_id=4, replica_groups=mesh['ctx'=8,'head'=4] {'ctx'}, dimensions={0}, use_global_device_ids=true | all-gather | bytes 36864 | tf_op jit(solution)/shard_map/all_gather | solution.py:877
  650.2 15.0 %layer_update.1 = (f32[256,5376]{1,0:T(8,128)}, f32[256,5376]{1,0:T(8,128)}, f32[256,5376]{1,0:T(8,128)}, bf16[256,5376]{1,0:T(8,128)(2,1)}) custom-call(f32[1,1]{1,0:T(1,128)} %bitcast.136.factor_ref, bf16[256,4224]{1,0:T(8,128)(2,1)} %reduce-scatter.2.cloned.1.call-done.refs_0_, f32[256,640]{1,0:T(8,128)} %get-tuple-element.149.refs_1_, ...), custom_call_target="tpu_custom_call" | custom-call | flops 13762560 | bytes 38535168 | tf_op jit(solution)/shard_map/layer_update/pallas_call | solution.py:598
  666.4 39.1 %vocab_update.1 = (f32[256,16000]{1,0:T(8,128)}, f32[256,16000]{1,0:T(8,128)}, f32[256,16000]{1,0:T(8,128)}, bf16[256,16000]{1,0:T(8,128)(2,1)}) custom-call(f32[1,1]{1,0:T(1,128)} %bitcast.136.factor_ref, bf16[8,256,1024]{2,1,0:T(8,128)(2,1)} %all-to-all-done.4.head_ref, bf16[256,8064]{1,0:T(8,128)(2,1)} %get-tuple-element.129.embed_ref, ...), custom_call_target="tpu_custom_call" | custom-call | flops 40960000 | bytes 114688000 | tf_op jit(solution)/shard_map/vocab_update/pallas_call | solution.py:598
  (335 shorter events, 128.6 us)
Async XLA Ops:
  7.2 104.3 %all-gather.8.cloned.1.call-start = ((), (), s32[]{:S(2)}) async-start(), calls=%async_computation.6 | async-start | bytes 5308416 | tf_op jit(solution)/shard_map/all_gather | solution.py:681
  10.9 184.4 %all-gather.10.cloned.1.call-start = ((), (), s32[]{:S(2)}) async-start(), calls=%async_computation.7 | async-start | bytes 19464192 | tf_op jit(solution)/shard_map/all_gather | solution.py:682
  42.1 17.8 %collective-permute-start = (bf16[16,32,256]{2,1,0:T(8,128)(2,1)}, bf16[16,32,256]{2,1,0:T(8,128)(2,1)S(1)}, u32[]{:S(2)}, u32[]{:S(2)}) collective-permute-start(bf16[16,32,256]{2,1,0:T(8,128)(2,1)} %get-tuple-element.181), channel_id=1, source_target_pairs={{0,1},{1,2},{2,3},{3,0},{4,5},{5,6},{6,7},{7,4},{8,9},{9,10},{10,1... | collective-permute-start | bytes 786440 | tf_op jit(solution)/shard_map/ppermute | solution.py:662
  43.7 20.4 %collective-permute-start.1 = (bf16[16,32,256]{2,1,0:T(8,128)(2,1)S(1)}, bf16[16,32,256]{2,1,0:T(8,128)(2,1)S(1)}, u32[]{:S(2)}, u32[]{:S(2)}) collective-permute-start(bf16[16,32,256]{2,1,0:T(8,128)(2,1)S(1)} %get-tuple-element.183), channel_id=1, source_target_pairs={{0,2},{1,3},{2,0},{3,1},{4,6},{5,7},{6,4},{7,5},{8,10},{9,11},{10,... | collective-permute-start | bytes 786440 | tf_op jit(solution)/shard_map/ppermute | solution.py:662
  46.3 17.8 %collective-permute-start.2 = (bf16[16,32,256]{2,1,0:T(8,128)(2,1)S(1)}, bf16[16,32,256]{2,1,0:T(8,128)(2,1)S(1)}, u32[]{:S(2)}, u32[]{:S(2)}) collective-permute-start(bf16[16,32,256]{2,1,0:T(8,128)(2,1)S(1)} %get-tuple-element.182), channel_id=1, source_target_pairs={{0,3},{1,0},{2,1},{3,2},{4,7},{5,4},{6,5},{7,6},{8,11},{9,8},{10,9... | collective-permute-start | bytes 786440 | tf_op jit(solution)/shard_map/ppermute | solution.py:662
  55.4 56.0 %collective-permute-start.6 = (bf16[128,8192]{1,0:T(8,128)(2,1)}, bf16[128,8192]{1,0:T(8,128)(2,1)S(1)}, u32[]{:S(2)}, u32[]{:S(2)}) collective-permute-start(bf16[128,8192]{1,0:T(8,128)(2,1)} %get-tuple-element.82.refs_0_), channel_id=1, source_target_pairs={{0,4},{4,0},{8,12},{12,8},{16,20},{20,16},{24,28},{28,24},{1,5},{5... | collective-permute-start | bytes 6291464 | tf_op jit(solution)/shard_map/ppermute | solution.py:688
  55.4 56.0 %collective-permute-start.7 = (bf16[128,8192]{1,0:T(8,128)(2,1)}, bf16[128,8192]{1,0:T(8,128)(2,1)}, u32[]{:S(2)}, u32[]{:S(2)}) collective-permute-start(bf16[128,8192]{1,0:T(8,128)(2,1)} %get-tuple-element.83.refs_1_), channel_id=1, source_target_pairs={{0,4},{4,0},{8,12},{12,8},{16,20},{20,16},{24,28},{28,24},{1,5},{5... | collective-permute-start | bytes 6291464 | tf_op jit(solution)/shard_map/ppermute | solution.py:688
  66.0 13.5 %all-to-all-start = ((bf16[8,64,256]{2,1,0:T(8,128)(2,1)}), bf16[8,64,256]{2,1,0:T(8,128)(2,1)S(1)}, u32[]{:S(2)}, u32[]{:S(2)}) async-start(bf16[8,64,256]{2,1,0:T(8,128)(2,1)} %bitcast.8), calls=%async_computation | async-start | bytes 524288 | tf_op jit(solution)/shard_map/all_to_all | solution.py:706
  69.4 366.5 %all-gather.12.cloned.1.call-start = ((), (), s32[]{:S(2)}) async-start(), calls=%async_computation.8 | async-start | bytes 9437184 | tf_op jit(solution)/shard_map/all_gather | solution.py:789
  81.2 13.8 %collective-permute-start.3 = (bf16[2,32,2048]{2,1,0:T(8,128)(2,1)S(1)}, bf16[2,32,2048]{2,1,0:T(8,128)(2,1)}, u32[]{:S(2)}, u32[]{:S(2)}) collective-permute-start(bf16[2,32,2048]{2,1,0:T(8,128)(2,1)S(1)} %multiply_convert_fusion.3), channel_id=1, source_target_pairs={{0,3},{1,0},{2,1},{3,2},{4,7},{5,4},{6,5},{7,6},{8,11},{9,8},{10,9... | collective-permute-start | bytes 786440 | tf_op jit(solution)/shard_map/ppermute | solution.py:669
  88.3 20.8 %collective-permute-start.4 = (bf16[2,32,2048]{2,1,0:T(8,128)(2,1)S(1)}, bf16[2,32,2048]{2,1,0:T(8,128)(2,1)}, u32[]{:S(2)}, u32[]{:S(2)}) collective-permute-start(bf16[2,32,2048]{2,1,0:T(8,128)(2,1)S(1)} %multiply_convert_fusion.3), channel_id=1, source_target_pairs={{0,2},{1,3},{2,0},{3,1},{4,6},{5,7},{6,4},{7,5},{8,10},{9,11},{10,... | collective-permute-start | bytes 786440 | tf_op jit(solution)/shard_map/ppermute | solution.py:669
  88.7 20.4 %collective-permute-start.5 = (bf16[2,32,2048]{2,1,0:T(8,128)(2,1)S(1)}, bf16[2,32,2048]{2,1,0:T(8,128)(2,1)}, u32[]{:S(2)}, u32[]{:S(2)}) collective-permute-start(bf16[2,32,2048]{2,1,0:T(8,128)(2,1)S(1)} %multiply_convert_fusion.3), channel_id=1, source_target_pairs={{0,1},{1,2},{2,3},{3,0},{4,5},{5,6},{6,7},{7,4},{8,9},{9,10},{10,1... | collective-permute-start | bytes 786440 | tf_op jit(solution)/shard_map/ppermute | solution.py:669
  130.5 64.9 %collective-permute-start.14 = (bf16[128,8192]{1,0:T(8,128)(2,1)S(1)}, bf16[128,8192]{1,0:T(8,128)(2,1)}, u32[]{:S(2)}, u32[]{:S(2)}) collective-permute-start(bf16[128,8192]{1,0:T(8,128)(2,1)S(1)} %copy-done.1), channel_id=1, source_target_pairs={{0,16},{4,20},{8,24},{12,28},{16,0},{20,4},{24,8},{28,12},{1,17},{... | collective-permute-start | bytes 6291464 | tf_op jit(solution)/shard_map/ppermute | solution.py:688
  131.5 63.8 %collective-permute-start.15 = (bf16[128,8192]{1,0:T(8,128)(2,1)}, bf16[128,8192]{1,0:T(8,128)(2,1)}, u32[]{:S(2)}, u32[]{:S(2)}) collective-permute-start(bf16[128,8192]{1,0:T(8,128)(2,1)} %get-tuple-element.83.refs_1_), channel_id=1, source_target_pairs={{0,8},{4,12},{8,0},{12,4},{16,24},{20,28},{24,16},{28,20},{1,9},{5... | collective-permute-start | bytes 6291464 | tf_op jit(solution)/shard_map/ppermute | solution.py:688
  144.0 14.4 %collective-permute-start.10 = (bf16[2,32,2048]{2,1,0:T(8,128)(2,1)S(1)}, bf16[2,32,2048]{2,1,0:T(8,128)(2,1)S(1)}, u32[]{:S(2)}, u32[]{:S(2)}) collective-permute-start(bf16[2,32,2048]{2,1,0:T(8,128)(2,1)S(1)} %get-tuple-element.180), channel_id=1, source_target_pairs={{0,3},{1,0},{2,1},{3,2},{4,7},{5,4},{6,5},{7,6},{8,11},{9,8},{10,9... | collective-permute-start | bytes 786440 | tf_op jit(solution)/shard_map/ppermute | solution.py:662
  144.1 16.1 %collective-permute-start.8 = (bf16[2,32,2048]{2,1,0:T(8,128)(2,1)S(1)}, bf16[2,32,2048]{2,1,0:T(8,128)(2,1)S(1)}, u32[]{:S(2)}, u32[]{:S(2)}) collective-permute-start(bf16[2,32,2048]{2,1,0:T(8,128)(2,1)S(1)} %get-tuple-element.178), channel_id=1, source_target_pairs={{0,1},{1,2},{2,3},{3,0},{4,5},{5,6},{6,7},{7,4},{8,9},{9,10},{10,1... | collective-permute-start | bytes 786440 | tf_op jit(solution)/shard_map/ppermute | solution.py:662
  146.1 23.0 %collective-permute-start.9 = (bf16[2,32,2048]{2,1,0:T(8,128)(2,1)S(1)}, bf16[2,32,2048]{2,1,0:T(8,128)(2,1)S(1)}, u32[]{:S(2)}, u32[]{:S(2)}) collective-permute-start(bf16[2,32,2048]{2,1,0:T(8,128)(2,1)S(1)} %get-tuple-element.179), channel_id=1, source_target_pairs={{0,2},{1,3},{2,0},{3,1},{4,6},{5,7},{6,4},{7,5},{8,10},{9,11},{10,... | collective-permute-start | bytes 786440 | tf_op jit(solution)/shard_map/ppermute | solution.py:662
  170.2 9.1 %collective-permute-start.11 = (bf16[2,32,2048]{2,1,0:T(8,128)(2,1)S(1)}, bf16[2,32,2048]{2,1,0:T(8,128)(2,1)S(1)}, u32[]{:S(2)}, u32[]{:S(2)}) collective-permute-start(bf16[2,32,2048]{2,1,0:T(8,128)(2,1)S(1)} %multiply_convert_fusion.2), channel_id=1, source_target_pairs={{0,3},{1,0},{2,1},{3,2},{4,7},{5,4},{6,5},{7,6},{8,11},{9,8},{10,9... | collective-permute-start | bytes 786440 | tf_op jit(solution)/shard_map/ppermute | solution.py:669
  172.5 21.7 %collective-permute-start.12 = (bf16[2,32,2048]{2,1,0:T(8,128)(2,1)S(1)}, bf16[2,32,2048]{2,1,0:T(8,128)(2,1)S(1)}, u32[]{:S(2)}, u32[]{:S(2)}) collective-permute-start(bf16[2,32,2048]{2,1,0:T(8,128)(2,1)S(1)} %multiply_convert_fusion.2), channel_id=1, source_target_pairs={{0,2},{1,3},{2,0},{3,1},{4,6},{5,7},{6,4},{7,5},{8,10},{9,11},{10,... | collective-permute-start | bytes 786440 | tf_op jit(solution)/shard_map/ppermute | solution.py:669
  172.5 22.6 %collective-permute-start.13 = (bf16[2,32,2048]{2,1,0:T(8,128)(2,1)S(1)}, bf16[2,32,2048]{2,1,0:T(8,128)(2,1)S(1)}, u32[]{:S(2)}, u32[]{:S(2)}) collective-permute-start(bf16[2,32,2048]{2,1,0:T(8,128)(2,1)S(1)} %multiply_convert_fusion.2), channel_id=1, source_target_pairs={{0,1},{1,2},{2,3},{3,0},{4,5},{5,6},{6,7},{7,4},{8,9},{9,10},{10,1... | collective-permute-start | bytes 786440 | tf_op jit(solution)/shard_map/ppermute | solution.py:669
  179.3 60.3 %collective-permute-start.19 = (bf16[128,8192]{1,0:T(8,128)(2,1)S(1)}, bf16[128,8192]{1,0:T(8,128)(2,1)}, u32[]{:S(2)}, u32[]{:S(2)}) collective-permute-start(bf16[128,8192]{1,0:T(8,128)(2,1)S(1)} %copy-done.1), channel_id=1, source_target_pairs={{0,8},{4,12},{8,0},{12,4},{16,24},{20,28},{24,16},{28,20},{1,9},{5... | collective-permute-start | bytes 6291464 | tf_op jit(solution)/shard_map/ppermute | solution.py:688
  194.2 48.8 %collective-permute-start.20 = (bf16[128,8192]{1,0:T(8,128)(2,1)}, bf16[128,8192]{1,0:T(8,128)(2,1)}, u32[]{:S(2)}, u32[]{:S(2)}) collective-permute-start(bf16[128,8192]{1,0:T(8,128)(2,1)} %get-tuple-element.83.refs_1_), channel_id=1, source_target_pairs={{0,16},{4,20},{8,24},{12,28},{16,0},{20,4},{24,8},{28,12},{1,17},{... | collective-permute-start | bytes 6291464 | tf_op jit(solution)/shard_map/ppermute | solution.py:688
  207.9 11.1 %collective-permute-start.16 = (bf16[2,32,2048]{2,1,0:T(8,128)(2,1)S(1)}, bf16[2,32,2048]{2,1,0:T(8,128)(2,1)S(1)}, u32[]{:S(2)}, u32[]{:S(2)}) collective-permute-start(bf16[2,32,2048]{2,1,0:T(8,128)(2,1)S(1)} %get-tuple-element.175), channel_id=1, source_target_pairs={{0,1},{1,2},{2,3},{3,0},{4,5},{5,6},{6,7},{7,4},{8,9},{9,10},{10,1... | collective-permute-start | bytes 786440 | tf_op jit(solution)/shard_map/ppermute | solution.py:662
  208.7 19.5 %collective-permute-start.17 = (bf16[2,32,2048]{2,1,0:T(8,128)(2,1)S(1)}, bf16[2,32,2048]{2,1,0:T(8,128)(2,1)S(1)}, u32[]{:S(2)}, u32[]{:S(2)}) collective-permute-start(bf16[2,32,2048]{2,1,0:T(8,128)(2,1)S(1)} %get-tuple-element.177), channel_id=1, source_target_pairs={{0,2},{1,3},{2,0},{3,1},{4,6},{5,7},{6,4},{7,5},{8,10},{9,11},{10,... | collective-permute-start | bytes 786440 | tf_op jit(solution)/shard_map/ppermute | solution.py:662
  210.8 17.4 %collective-permute-start.18 = (bf16[2,32,2048]{2,1,0:T(8,128)(2,1)S(1)}, bf16[2,32,2048]{2,1,0:T(8,128)(2,1)S(1)}, u32[]{:S(2)}, u32[]{:S(2)}) collective-permute-start(bf16[2,32,2048]{2,1,0:T(8,128)(2,1)S(1)} %get-tuple-element.176), channel_id=1, source_target_pairs={{0,3},{1,0},{2,1},{3,2},{4,7},{5,4},{6,5},{7,6},{8,11},{9,8},{10,9... | collective-permute-start | bytes 786440 | tf_op jit(solution)/shard_map/ppermute | solution.py:662
  219.0 67.2 %collective-permute-start.25 = (bf16[128,8192]{1,0:T(8,128)(2,1)}, bf16[128,8192]{1,0:T(8,128)(2,1)}, u32[]{:S(2)}, u32[]{:S(2)}) collective-permute-start(bf16[128,8192]{1,0:T(8,128)(2,1)} %collective-permute-done.15.refs_5_), channel_id=1, source_target_pairs={{0,16},{4,20},{8,24},{12,28},{16,0},{20,4},{24,8},{28,12},{1,17},{... | collective-permute-start | bytes 6291464 | tf_op jit(solution)/shard_map/ppermute | solution.py:688
  228.2 58.0 %collective-permute-start.27 = (bf16[128,8192]{1,0:T(8,128)(2,1)}, bf16[128,8192]{1,0:T(8,128)(2,1)}, u32[]{:S(2)}, u32[]{:S(2)}) collective-permute-start(bf16[128,8192]{1,0:T(8,128)(2,1)} %collective-permute-done.15.refs_5_), channel_id=1, source_target_pairs={{0,4},{4,0},{8,12},{12,8},{16,20},{20,16},{24,28},{28,24},{1,5},{5... | collective-permute-start | bytes 6291464 | tf_op jit(solution)/shard_map/ppermute | solution.py:688
  228.2 56.1 %collective-permute-start.24 = (bf16[128,8192]{1,0:T(8,128)(2,1)}, bf16[128,8192]{1,0:T(8,128)(2,1)}, u32[]{:S(2)}, u32[]{:S(2)}) collective-permute-start(bf16[128,8192]{1,0:T(8,128)(2,1)} %collective-permute-done.14.refs_6_), channel_id=1, source_target_pairs={{0,8},{4,12},{8,0},{12,4},{16,24},{20,28},{24,16},{28,20},{1,9},{5... | collective-permute-start | bytes 6291464 | tf_op jit(solution)/shard_map/ppermute | solution.py:688
  243.4 7.2 %collective-permute-start.21 = (bf16[2,32,2048]{2,1,0:T(8,128)(2,1)S(1)}, bf16[2,32,2048]{2,1,0:T(8,128)(2,1)S(1)}, u32[]{:S(2)}, u32[]{:S(2)}) collective-permute-start(bf16[2,32,2048]{2,1,0:T(8,128)(2,1)S(1)} %bitcast.397), channel_id=1, source_target_pairs={{0,3},{1,0},{2,1},{3,2},{4,7},{5,4},{6,5},{7,6},{8,11},{9,8},{10,9... | collective-permute-start | bytes 786440 | tf_op jit(solution)/shard_map/ppermute | solution.py:669
  243.5 22.4 %collective-permute-start.22 = (bf16[2,32,2048]{2,1,0:T(8,128)(2,1)S(1)}, bf16[2,32,2048]{2,1,0:T(8,128)(2,1)}, u32[]{:S(2)}, u32[]{:S(2)}) collective-permute-start(bf16[2,32,2048]{2,1,0:T(8,128)(2,1)S(1)} %bitcast.398), channel_id=1, source_target_pairs={{0,2},{1,3},{2,0},{3,1},{4,6},{5,7},{6,4},{7,5},{8,10},{9,11},{10,... | collective-permute-start | bytes 786440 | tf_op jit(solution)/shard_map/ppermute | solution.py:669
  250.6 15.2 %collective-permute-start.23 = (bf16[2,32,2048]{2,1,0:T(8,128)(2,1)S(1)}, bf16[2,32,2048]{2,1,0:T(8,128)(2,1)}, u32[]{:S(2)}, u32[]{:S(2)}) collective-permute-start(bf16[2,32,2048]{2,1,0:T(8,128)(2,1)S(1)} %bitcast.399), channel_id=1, source_target_pairs={{0,1},{1,2},{2,3},{3,0},{4,5},{5,6},{6,7},{7,4},{8,9},{9,10},{10,1... | collective-permute-start | bytes 786440 | tf_op jit(solution)/shard_map/ppermute | solution.py:669
  265.9 22.4 %collective-permute-start.28 = (bf16[128,8192]{1,0:T(8,128)(2,1)}, bf16[128,8192]{1,0:T(8,128)(2,1)S(1)}, u32[]{:S(2)}, u32[]{:S(2)}) collective-permute-start(bf16[128,8192]{1,0:T(8,128)(2,1)} %collective-permute-done.14.refs_6_), channel_id=1, source_target_pairs={{0,4},{4,0},{8,12},{12,8},{16,20},{20,16},{24,28},{28,24},{1,5},{5... | collective-permute-start | bytes 6291464 | tf_op jit(solution)/shard_map/ppermute | solution.py:688
  265.9 22.4 %collective-permute-start.26 = (bf16[128,8192]{1,0:T(8,128)(2,1)}, bf16[128,8192]{1,0:T(8,128)(2,1)}, u32[]{:S(2)}, u32[]{:S(2)}) collective-permute-start(bf16[128,8192]{1,0:T(8,128)(2,1)} %collective-permute-done.19.refs_4_), channel_id=1, source_target_pairs={{0,4},{4,0},{8,12},{12,8},{16,20},{20,16},{24,28},{28,24},{1,5},{5... | collective-permute-start | bytes 6291464 | tf_op jit(solution)/shard_map/ppermute | solution.py:688
  286.2 8.6 %collective-permute-start.31 = (bf16[128,8192]{1,0:T(8,128)(2,1)}, bf16[128,8192]{1,0:T(8,128)(2,1)}, u32[]{:S(2)}, u32[]{:S(2)}) collective-permute-start(bf16[128,8192]{1,0:T(8,128)(2,1)} %collective-permute-done.25.refs_6_.refs_13_), channel_id=1, source_target_pairs={{0,4},{4,0},{8,12},{12,8},{16,20},{20,16},{24,28},{28,24},{1,5},{5... | collective-permute-start | bytes 6291464 | tf_op jit(solution)/shard_map/ppermute | solution.py:688
  312.6 6.1 collective-permute-start.34
  347.4 11.1 %collective-permute-start.35 = (bf16[2,32,2048]{2,1,0:T(8,128)(2,1)S(1)}, bf16[2,32,2048]{2,1,0:T(8,128)(2,1)S(1)}, u32[]{:S(2)}, u32[]{:S(2)}) collective-permute-start(bf16[2,32,2048]{2,1,0:T(8,128)(2,1)S(1)} %get-tuple-element.172), channel_id=1, source_target_pairs={{0,1},{1,2},{2,3},{3,0},{4,5},{5,6},{6,7},{7,4},{8,9},{9,10},{10,1... | collective-permute-start | bytes 786440 | tf_op jit(solution)/shard_map/ppermute | solution.py:662
  347.5 18.6 %collective-permute-start.36 = (bf16[2,32,2048]{2,1,0:T(8,128)(2,1)S(1)}, bf16[2,32,2048]{2,1,0:T(8,128)(2,1)S(1)}, u32[]{:S(2)}, u32[]{:S(2)}) collective-permute-start(bf16[2,32,2048]{2,1,0:T(8,128)(2,1)S(1)} %get-tuple-element.174), channel_id=1, source_target_pairs={{0,2},{1,3},{2,0},{3,1},{4,6},{5,7},{6,4},{7,5},{8,10},{9,11},{10,... | collective-permute-start | bytes 786440 | tf_op jit(solution)/shard_map/ppermute | solution.py:662
  351.2 14.8 %collective-permute-start.37 = (bf16[2,32,2048]{2,1,0:T(8,128)(2,1)S(1)}, bf16[2,32,2048]{2,1,0:T(8,128)(2,1)S(1)}, u32[]{:S(2)}, u32[]{:S(2)}) collective-permute-start(bf16[2,32,2048]{2,1,0:T(8,128)(2,1)S(1)} %get-tuple-element.173), channel_id=1, source_target_pairs={{0,3},{1,0},{2,1},{3,2},{4,7},{5,4},{6,5},{7,6},{8,11},{9,8},{10,9... | collective-permute-start | bytes 786440 | tf_op jit(solution)/shard_map/ppermute | solution.py:662
  367.6 13.0 %collective-permute-start.38 = (bf16[2,32,2048]{2,1,0:T(8,128)(2,1)S(1)}, bf16[2,32,2048]{2,1,0:T(8,128)(2,1)S(1)}, u32[]{:S(2)}, u32[]{:S(2)}) collective-permute-start(bf16[2,32,2048]{2,1,0:T(8,128)(2,1)S(1)} %bitcast.401), channel_id=1, source_target_pairs={{0,3},{1,0},{2,1},{3,2},{4,7},{5,4},{6,5},{7,6},{8,11},{9,8},{10,9... | collective-permute-start | bytes 786440 | tf_op jit(solution)/shard_map/ppermute | solution.py:669
  373.9 24.3 %collective-permute-start.39 = (bf16[2,32,2048]{2,1,0:T(8,128)(2,1)S(1)}, bf16[2,32,2048]{2,1,0:T(8,128)(2,1)S(1)}, u32[]{:S(2)}, u32[]{:S(2)}) collective-permute-start(bf16[2,32,2048]{2,1,0:T(8,128)(2,1)S(1)} %bitcast.402), channel_id=1, source_target_pairs={{0,2},{1,3},{2,0},{3,1},{4,6},{5,7},{6,4},{7,5},{8,10},{9,11},{10,... | collective-permute-start | bytes 786440 | tf_op jit(solution)/shard_map/ppermute | solution.py:669
  375.2 23.1 %collective-permute-start.40 = (bf16[2,32,2048]{2,1,0:T(8,128)(2,1)S(1)}, bf16[2,32,2048]{2,1,0:T(8,128)(2,1)S(1)}, u32[]{:S(2)}, u32[]{:S(2)}) collective-permute-start(bf16[2,32,2048]{2,1,0:T(8,128)(2,1)S(1)} %bitcast.403), channel_id=1, source_target_pairs={{0,1},{1,2},{2,3},{3,0},{4,5},{5,6},{6,7},{7,4},{8,9},{9,10},{10,1... | collective-permute-start | bytes 786440 | tf_op jit(solution)/shard_map/ppermute | solution.py:669
  375.2 60.7 %all-to-all-start.1 = ((bf16[8,256,1024]{2,1,0:T(8,128)(2,1)}), bf16[8,256,1024]{2,1,0:T(8,128)(2,1)}, u32[]{:S(2)}, u32[]{:S(2)}) async-start(bf16[8,256,1024]{2,1,0:T(8,128)(2,1)} %get-tuple-element.99), calls=%async_computation.1 | async-start | bytes 8388608 | tf_op jit(solution)/shard_map/all_to_all | solution.py:790
  379.8 207.9 %reduce-scatter.2.cloned.1.call-start = ((), (), s32[]{:S(2)}) async-start(), calls=%async_computation.9 | async-start | bytes 19464192 | tf_op jit(solution)/shard_map/reduce_scatter | solution.py:799
  413.3 19.0 %collective-permute-start.41 = (bf16[2,32,2048]{2,1,0:T(8,128)(2,1)}, bf16[2,32,2048]{2,1,0:T(8,128)(2,1)S(1)}, u32[]{:S(2)}, u32[]{:S(2)}) collective-permute-start(bf16[2,32,2048]{2,1,0:T(8,128)(2,1)} %get-tuple-element.169), channel_id=1, source_target_pairs={{0,1},{1,2},{2,3},{3,0},{4,5},{5,6},{6,7},{7,4},{8,9},{9,10},{10,1... | collective-permute-start | bytes 786440 | tf_op jit(solution)/shard_map/ppermute | solution.py:662
  413.3 20.8 %collective-permute-start.42 = (bf16[2,32,2048]{2,1,0:T(8,128)(2,1)}, bf16[2,32,2048]{2,1,0:T(8,128)(2,1)S(1)}, u32[]{:S(2)}, u32[]{:S(2)}) collective-permute-start(bf16[2,32,2048]{2,1,0:T(8,128)(2,1)} %get-tuple-element.171), channel_id=1, source_target_pairs={{0,2},{1,3},{2,0},{3,1},{4,6},{5,7},{6,4},{7,5},{8,10},{9,11},{10,... | collective-permute-start | bytes 786440 | tf_op jit(solution)/shard_map/ppermute | solution.py:662
  413.3 21.5 %collective-permute-start.43 = (bf16[2,32,2048]{2,1,0:T(8,128)(2,1)S(1)}, bf16[2,32,2048]{2,1,0:T(8,128)(2,1)}, u32[]{:S(2)}, u32[]{:S(2)}) collective-permute-start(bf16[2,32,2048]{2,1,0:T(8,128)(2,1)S(1)} %get-tuple-element.170), channel_id=1, source_target_pairs={{0,3},{1,0},{2,1},{3,2},{4,7},{5,4},{6,5},{7,6},{8,11},{9,8},{10,9... | collective-permute-start | bytes 786440 | tf_op jit(solution)/shard_map/ppermute | solution.py:662
  440.2 23.0 %collective-permute-start.44 = (bf16[2,32,2048]{2,1,0:T(8,128)(2,1)S(1)}, bf16[2,32,2048]{2,1,0:T(8,128)(2,1)S(1)}, u32[]{:S(2)}, u32[]{:S(2)}) collective-permute-start(bf16[2,32,2048]{2,1,0:T(8,128)(2,1)S(1)} %bitcast.390), channel_id=1, source_target_pairs={{0,3},{1,0},{2,1},{3,2},{4,7},{5,4},{6,5},{7,6},{8,11},{9,8},{10,9... | collective-permute-start | bytes 786440 | tf_op jit(solution)/shard_map/ppermute | solution.py:669
  445.6 22.9 %collective-permute-start.45 = (bf16[2,32,2048]{2,1,0:T(8,128)(2,1)S(1)}, bf16[2,32,2048]{2,1,0:T(8,128)(2,1)S(1)}, u32[]{:S(2)}, u32[]{:S(2)}) collective-permute-start(bf16[2,32,2048]{2,1,0:T(8,128)(2,1)S(1)} %bitcast.391), channel_id=1, source_target_pairs={{0,2},{1,3},{2,0},{3,1},{4,6},{5,7},{6,4},{7,5},{8,10},{9,11},{10,... | collective-permute-start | bytes 786440 | tf_op jit(solution)/shard_map/ppermute | solution.py:669
  446.3 22.2 %collective-permute-start.46 = (bf16[2,32,2048]{2,1,0:T(8,128)(2,1)S(1)}, bf16[2,32,2048]{2,1,0:T(8,128)(2,1)S(1)}, u32[]{:S(2)}, u32[]{:S(2)}) collective-permute-start(bf16[2,32,2048]{2,1,0:T(8,128)(2,1)S(1)} %bitcast.392), channel_id=1, source_target_pairs={{0,1},{1,2},{2,3},{3,0},{4,5},{5,6},{6,7},{7,4},{8,9},{9,10},{10,1... | collective-permute-start | bytes 786440 | tf_op jit(solution)/shard_map/ppermute | solution.py:669
  490.4 19.9 %all-to-all-start.2 = ((bf16[8,256,128]{2,1,0:T(8,128)(2,1)}), bf16[8,256,128]{2,1,0:T(8,128)(2,1)}, u32[]{:S(2)}, u32[]{:S(2)}) async-start(bf16[8,256,128]{2,1,0:T(8,128)(2,1)} %bitcast.408), calls=%async_computation.2 | async-start | bytes 1048576 | tf_op jit(solution)/shard_map/all_to_all | solution.py:808
  495.4 38.3 %collective-permute-start.50 = (bf16[2,2,256,512]{3,2,1,0:T(8,128)(2,1)S(1)}, bf16[2,2,256,512]{3,2,1,0:T(8,128)(2,1)}, u32[]{:S(2)}, u32[]{:S(2)}) collective-permute-start(bf16[2,2,256,512]{3,2,1,0:T(8,128)(2,1)S(1)} %dynamic-slice_bitcast_fusion), channel_id=1, source_target_pairs={{0,4},{4,0},{8,12},{12,8},{16,20},{20,16},{24,28},{28,24},{1,5},{5... | collective-permute-start | bytes 3145736 | tf_op jit(solution)/shard_map/ppermute | solution.py:688
  515.5 11.1 %collective-permute-start.47 = (bf16[2,32,2048]{2,1,0:T(8,128)(2,1)S(1)}, bf16[2,32,2048]{2,1,0:T(8,128)(2,1)S(1)}, u32[]{:S(2)}, u32[]{:S(2)}) collective-permute-start(bf16[2,32,2048]{2,1,0:T(8,128)(2,1)S(1)} %get-tuple-element.166), channel_id=1, source_target_pairs={{0,1},{1,2},{2,3},{3,0},{4,5},{5,6},{6,7},{7,4},{8,9},{9,10},{10,1... | collective-permute-start | bytes 786440 | tf_op jit(solution)/shard_map/ppermute | solution.py:662
  515.5 18.0 %collective-permute-start.48 = (bf16[2,32,2048]{2,1,0:T(8,128)(2,1)S(1)}, bf16[2,32,2048]{2,1,0:T(8,128)(2,1)S(1)}, u32[]{:S(2)}, u32[]{:S(2)}) collective-permute-start(bf16[2,32,2048]{2,1,0:T(8,128)(2,1)S(1)} %get-tuple-element.168), channel_id=1, source_target_pairs={{0,2},{1,3},{2,0},{3,1},{4,6},{5,7},{6,4},{7,5},{8,10},{9,11},{10,... | collective-permute-start | bytes 786440 | tf_op jit(solution)/shard_map/ppermute | solution.py:662
  516.7 16.8 %collective-permute-start.49 = (bf16[2,32,2048]{2,1,0:T(8,128)(2,1)S(1)}, bf16[2,32,2048]{2,1,0:T(8,128)(2,1)S(1)}, u32[]{:S(2)}, u32[]{:S(2)}) collective-permute-start(bf16[2,32,2048]{2,1,0:T(8,128)(2,1)S(1)} %get-tuple-element.167), channel_id=1, source_target_pairs={{0,3},{1,0},{2,1},{3,2},{4,7},{5,4},{6,5},{7,6},{8,11},{9,8},{10,9... | collective-permute-start | bytes 786440 | tf_op jit(solution)/shard_map/ppermute | solution.py:662
  535.1 17.4 %collective-permute-start.51 = (bf16[2,2,256,640]{3,2,0,1:T(8,128)(2,1)}, bf16[2,2,256,640]{3,2,0,1:T(8,128)(2,1)}, u32[]{:S(2)}, u32[]{:S(2)}) collective-permute-start(bf16[2,2,256,640]{3,2,0,1:T(8,128)(2,1)} %bitcast.346), channel_id=1, source_target_pairs={{0,4},{4,0},{8,12},{12,8},{16,20},{20,16},{24,28},{28,24},{1,5},{5... | collective-permute-start | bytes 3932168 | tf_op jit(solution)/shard_map/ppermute | solution.py:688
  536.7 15.8 %all-to-all-start.3 = ((bf16[80,8,256]{2,0,1:T(8,128)(2,1)}), bf16[80,8,256]{2,0,1:T(8,128)(2,1)}, u32[]{:S(2)}, u32[]{:S(2)}) async-start(bf16[80,8,256]{2,0,1:T(8,128)(2,1)} %copy.301), calls=%async_computation.3 | async-start | bytes 655360 | tf_op jit(solution)/shard_map/all_to_all | solution.py:831
  554.4 12.8 %collective-permute-start.56 = (bf16[528,256]{1,0:T(8,128)(2,1)S(1)}, bf16[528,256]{1,0:T(8,128)(2,1)S(1)}, u32[]{:S(2)}, u32[]{:S(2)}) collective-permute-start(bf16[528,256]{1,0:T(8,128)(2,1)S(1)} %pad_maximum_fusion.8), channel_id=1, source_target_pairs={{0,3},{1,0},{2,1},{3,2},{4,7},{5,4},{6,5},{7,6},{8,11},{9,8},{10,9... | collective-permute-start | bytes 811016 | tf_op jit(solution)/shard_map/ppermute | solution.py:855
  560.4 21.3 %collective-permute-start.57 = (bf16[528,256]{1,0:T(8,128)(2,1)S(1)}, bf16[528,256]{1,0:T(8,128)(2,1)S(1)}, u32[]{:S(2)}, u32[]{:S(2)}) collective-permute-start(bf16[528,256]{1,0:T(8,128)(2,1)S(1)} %pad_maximum_fusion.8), channel_id=1, source_target_pairs={{0,2},{1,3},{2,0},{3,1},{4,6},{5,7},{6,4},{7,5},{8,10},{9,11},{10,... | collective-permute-start | bytes 811016 | tf_op jit(solution)/shard_map/ppermute | solution.py:855
  561.2 20.5 %collective-permute-start.58 = (bf16[528,256]{1,0:T(8,128)(2,1)S(1)}, bf16[528,256]{1,0:T(8,128)(2,1)S(1)}, u32[]{:S(2)}, u32[]{:S(2)}) collective-permute-start(bf16[528,256]{1,0:T(8,128)(2,1)S(1)} %pad_maximum_fusion.8), channel_id=1, source_target_pairs={{0,1},{1,2},{2,3},{3,0},{4,5},{5,6},{6,7},{7,4},{8,9},{9,10},{10,1... | collective-permute-start | bytes 811016 | tf_op jit(solution)/shard_map/ppermute | solution.py:855
  562.3 19.5 %collective-permute-start.54 = (bf16[2,256,512]{2,1,0:T(8,128)(2,1)S(1)}, bf16[2,256,512]{2,1,0:T(8,128)(2,1)S(1)}, u32[]{:S(2)}, u32[]{:S(2)}) collective-permute-start(bf16[2,256,512]{2,1,0:T(8,128)(2,1)S(1)} %dynamic-slice_bitcast_fusion.2), channel_id=1, source_target_pairs={{0,16},{4,20},{8,24},{12,28},{16,0},{20,4},{24,8},{28,12},{1,17},{... | collective-permute-start | bytes 1572872 | tf_op jit(solution)/shard_map/ppermute | solution.py:688
  564.7 19.6 %collective-permute-start.52 = (bf16[2,256,640]{2,1,0:T(8,128)(2,1)S(1)}, bf16[2,256,640]{2,1,0:T(8,128)(2,1)S(1)}, u32[]{:S(2)}, u32[]{:S(2)}) collective-permute-start(bf16[2,256,640]{2,1,0:T(8,128)(2,1)S(1)} %dynamic-slice_bitcast_fusion.1), channel_id=1, source_target_pairs={{0,8},{4,12},{8,0},{12,4},{16,24},{20,28},{24,16},{28,20},{1,9},{5... | collective-permute-start | bytes 1966088 | tf_op jit(solution)/shard_map/ppermute | solution.py:688
  582.7 8.3 %collective-permute-start.55 = (bf16[256,512]{1,0:T(8,128)(2,1)}, bf16[256,512]{1,0:T(8,128)(2,1)S(1)}, u32[]{:S(2)}, u32[]{:S(2)}) collective-permute-start(bf16[256,512]{1,0:T(8,128)(2,1)} %dynamic-slice_bitcast_fusion.4), channel_id=1, source_target_pairs={{0,8},{4,12},{8,0},{12,4},{16,24},{20,28},{24,16},{28,20},{1,9},{5... | collective-permute-start | bytes 786440 | tf_op jit(solution)/shard_map/ppermute | solution.py:688
  584.5 7.6 %collective-permute-start.53 = (bf16[256,640]{1,0:T(8,128)(2,1)S(1)}, bf16[256,640]{1,0:T(8,128)(2,1)S(1)}, u32[]{:S(2)}, u32[]{:S(2)}) collective-permute-start(bf16[256,640]{1,0:T(8,128)(2,1)S(1)} %dynamic-slice_bitcast_fusion.3), channel_id=1, source_target_pairs={{0,16},{4,20},{8,24},{12,28},{16,0},{20,4},{24,8},{28,12},{1,17},{... | collective-permute-start | bytes 983048 | tf_op jit(solution)/shard_map/ppermute | solution.py:688
  592.0 74.4 %all-to-all-start.4 = ((bf16[8,256,1024]{2,1,0:T(8,128)(2,1)}), bf16[8,256,1024]{2,1,0:T(8,128)(2,1)}, u32[]{:S(2)}, u32[]{:S(2)}) async-start(bf16[8,256,1024]{2,1,0:T(8,128)(2,1)} %bitcast.366), calls=%async_computation.5 | async-start | bytes 8388608 | tf_op jit(solution)/shard_map/all_to_all | solution.py:849
  (41 other events, 428.9 us)
Sparse Core Ops, SparseCore 0:
  11.1 41.4 all-gather.7
  55.1 112.8 all-gather.9
  312.0 54.2 all-gather.11
  436.1 132.3 reduce-scatter.1

commit v5 on v4

--- a/solution.py
+++ b/solution.py
@@ -32,7 +32,7 @@
 BASE = 1.5 * math.sqrt(NPARAM) / clip_level
 EMB_AT = VG // 128 * 128
 EMB_W = 2 * VG - EMB_AT
-EMB_STEPS = 7
+EMB_STEPS = 3
 EMB_BLOCK = EMB_W // EMB_STEPS
 
 f32 = jnp.float32
@@ -475,11 +475,12 @@
 
     for k, w in joined(pieces, parts):
         at = pl.multiple_of(at_ref[k], 128)
-        acc_ref[:, pl.ds(at, w.shape[0])] += dot_nt(dlog, w)
+        acc_ref[pl.ds(at, w.shape[0]), :] += dot_nt(w, dlog)
 
     @pl.when(step == steps - 1)
     def _():
-        dx_ref[...] = acc_ref[...].astype(bf16)
+        for k in range(0, acc_ref.shape[0], 256):
+            dx_ref[:, k : k + 256] = acc_ref[k : k + 256, :].T.astype(bf16)
 
 
 def head_dlogits(logits, values, slots, pieces, at, part):
@@ -504,7 +505,7 @@
             jax.ShapeDtypeStruct((width // part, tok, part), bf16),
             jax.ShapeDtypeStruct((tok, D), bf16),
         ],
-        scratch_shapes=[pltpu.VMEM((tok, D), f32)],
+        scratch_shapes=[pltpu.VMEM((D, tok), f32)],
         compiler_params=params(),
         cost_estimate=cost(2 * tok * D * width, 2 * D * width + 6 * tok * width, tok * width),
         name="head_dlogits",
@@ -837,15 +838,13 @@
         d_in, d_out = total(in_kept, in_sent).astype(bf16), total(out_kept, out_sent).astype(bf16)
         in_kept, in_sent = split(d_in, along_y, 0, 4)
         out_kept, out_sent = split(d_out, along_x, 0, 2)
-        ff_sq = jnp.sum(jnp.square(g_ff.astype(f32)))
-        d_head, in_sent, out_sent, ff_sq = lax.optimization_barrier((d_head, in_sent, out_sent, ff_sq))
+        d_head, in_sent, out_sent = lax.optimization_barrier((d_head, in_sent, out_sent))
         g_in, g_out = total(in_kept, in_sent), total(out_kept, out_sent)
     else:
         moved, d_head, d_in, d_out, g_ff = lax.optimization_barrier((moved, d_head, d_in, d_out, g_ff))
         g_in, g_out = (
             lax.psum_scatter(x, "ctx", scatter_dimension=0, tiled=True).astype(f32) for x in (d_in, d_out)
         )
-        ff_sq = jnp.sum(jnp.square(g_ff.astype(f32)))
     g_head = lax.all_to_all(d_head.reshape(n_ctx, rows, part), "ctx", 0, 0, tiled=True)
     moved = moved.reshape(n_ctx, own + 16, rows)
     gain_part = jnp.sum(moved[:, own:].astype(f32), axis=0).astype(bf16)
@@ -860,7 +859,7 @@
     g_embed, embed_sq = embed_grad(slots, dx0_all.reshape(n_ctx * tok, rows).T)
 
     squares = (
-        ff_sq
+        jnp.sum(jnp.square(g_ff.astype(f32)))
         + jnp.sum(jnp.square(g_in))
         + jnp.sum(jnp.square(g_out))
         + head_sq
@@ -871,8 +870,12 @@
     if n_head & (n_head - 1):
         squares = jnp.sum(lax.all_gather(squares, "head"), axis=0)
     else:
-        for step in range(n_head.bit_length() - 1):
-            squares = squares + lax.ppermute(squares, "head", [(i, i ^ (1 << step)) for i in range(n_head)])
+        level = [squares]
+        for s in range(1, n_head):
+            level.append(lax.ppermute(squares, "head", [(i, i ^ s) for i in range(n_head)]))
+        while len(level) > 1:
+            level = [a + b for a, b in zip(level[::2], level[1::2])]
+        squares = level[0]
     lane = lax.broadcasted_iota(jnp.int32, (8, 128), 1)
     totals = jnp.sum(lax.all_gather(jnp.where(lane == 0, squares, loss_part), "ctx"), axis=0)
     loss = totals[0, 1]

time: 723 us -> 720 us (level)
  starting transfers between devices: 112 us -> 130 us
  waiting for transfers between devices: 220 us -> 205 us
    ppermute x15, starting transfers between devices: 36.3 us -> 52.5 us  [head_gather(): lax.ppermute(x, 'head', [(i, (i - s) % n_head) for i in range(n_head)])]
    ppermute x15, waiting for transfers between devices: 71.5 us -> 59.1 us  [head_gather(): lax.ppermute(x, 'head', [(i, (i - s) % n_head) for i in range(n_head)])]
    ppermute x3, waiting for transfers between devices: 16.4 us -> 5.2 us  [local(): lax.ppermute(moved, 'head', [(i, (i - s) % n_head) for i in range(n_head)])]
    ppermute x20, waiting for transfers between devices: 25.1 us -> 34.3 us  [swap(): return lax.ppermute(x, 'ctx', [(i, i ^ bit) for i in range(n_ctx)])]
  transfers between devices with their start and end apart: 70 -> 71, of which waited for: 37 -> 38; matrix products, arithmetic and copies ran while one was open for 17% -> 16% of each run, Pallas kernels for 19% -> 19%
where the time goes in v5:
time: 720 us; the launch traced here: 709 us
  waiting for transfers between devices  205 us (28%)
  Pallas kernels  190 us (26%)
  starting transfers between devices  130 us (18%)
  matrix products  52.3 us (7%)
  other arithmetic  42.9 us (6%)
  blocking collectives  39.4 us (5%)
  local copies, waits for them, and re-layouts  27.7 us (4%)
  between operations  21.4 us (3%)
    ppermute x18, waiting for transfers between devices, head_scatter(): lax.ppermute(x[:, s], 'head', [(i, (i + s) % n_head) for i in range(n_hea...  69.3 us
    ppermute x15, waiting for transfers between devices, head_gather(): lax.ppermute(x, 'head', [(i, (i - s) % n_head) for i in range(n_head)])  59.1 us
    pallas_call x2, Pallas kernels, call_update(): pl.pallas_call(kernel, grid=(total // rows,), in_specs=[pl.BlockSpec(memo...  54.1 us
    ppermute x15, starting transfers between devices, head_gather(): lax.ppermute(x, 'head', [(i, (i - s) % n_head) for i in range(n_head)])  52.5 us
    ppermute x20, waiting for transfers between devices, swap(): return lax.ppermute(x, 'ctx', [(i, i ^ bit) for i in range(n_ctx)])  34.3 us
    ppermute x18, starting transfers between devices, head_scatter(): lax.ppermute(x[:, s], 'head', [(i, (i + s) % n_head) for i in range(n_hea...  26.5 us
    pallas_call x1, Pallas kernels, head_dlogits(): pl.pallas_call(functools.partial(dlogits_kernel, steps, len(pieces) // at...  22.9 us
    pallas_call x1, Pallas kernels, attn_back(): pl.pallas_call(functools.partial(attn_back_kernel, pairs), grid=(SEQS, pa...  18.8 us
  transfers between devices with their start and end apart: 71, of which 38 were waited for; matrix products, arithmetic and copies ran while one was open for 16% of the time, Pallas kernels for 19%

profile of v5, /device:TPU:0, one launch (start us, length us, event | category | flops | bytes accessed | tf_op | source)
XLA Modules:
  0.0 709.2 jit_solution(11134033809253528231)
XLA Ops:
  7.2 2.8 convert_element_type.324
  13.2 10.6 %all-gather.3 = f32[8,1,1280]{2,1,0:T(1,128)S(1)} all-gather(f32[1,1,1280]{2,1,0:T(1,128)S(1)} %reshape.828), channel_id=2, replica_groups=mesh['ctx'=8,'head'=4] {'ctx'}, dimensions={0}, use_global_device_ids=true | all-gather | bytes 46080 | tf_op jit(solution)/shard_map/all_gather | solution.py:693
  26.0 13.3 %embed_lookup.1 = bf16[2048,256]{1,0:T(8,128)(2,1)} custom-call(s32[2048,1]{1,0:T(8,128)} %copy.260.ids_ref, f32[256,16000]{1,0:T(8,128)} %w_ref.5), custom_call_target="tpu_custom_call" | custom-call | flops 8455716864 | bytes 8257536 | tf_op jit(solution)/shard_map/embed_lookup/pallas_call | solution.py:88
  46.6 7.8 %head_cast.1 = (bf16[128,8192]{1,0:T(8,128)(2,1)}, bf16[128,8192]{1,0:T(8,128)(2,1)}) custom-call(f32[256,16000]{1,0:T(8,128)} %w_ref.5), custom_call_target="tpu_custom_call" | custom-call | flops 2097152 | bytes 12582912 | tf_op jit(solution)/shard_map/head_cast/pallas_call | solution.py:342
  58.9 4.2 collective-permute-done.1
  65.0 3.4 all-to-all-start
  69.7 8.7 %all-to-all-done = bf16[8,64,256]{2,1,0:T(8,128)(2,1)S(1)} async-done(((bf16[8,64,256]{2,1,0:T(8,128)(2,1)}), bf16[8,64,256]{2,1,0:T(8,128)(2,1)S(1)}, u32[]{:S(2)}, u32[]{:S(2)}) %all-to-all-start) | async-done | bytes 262176 | tf_op jit(solution)/shard_map/all_to_all | solution.py:707
  80.1 7.2 %collective-permute-start.3 = (bf16[2,32,2048]{2,1,0:T(8,128)(2,1)S(1)}, bf16[2,32,2048]{2,1,0:T(8,128)(2,1)}, u32[]{:S(2)}, u32[]{:S(2)}) collective-permute-start(bf16[2,32,2048]{2,1,0:T(8,128)(2,1)S(1)} %multiply_convert_fusion.3), channel_id=1, source_target_pairs={{0,3},{1,0},{2,1},{3,2},{4,7},{5,4},{6,5},{7,6},{8,11},{9,8},{10,9... | collective-permute-start | bytes 786440 | tf_op jit(solution)/shard_map/ppermute | solution.py:670
  90.0 4.0 collective-permute-done.3
  94.0 14.0 %collective-permute-done.4 = bf16[2,32,2048]{2,1,0:T(8,128)(2,1)} collective-permute-done((bf16[2,32,2048]{2,1,0:T(8,128)(2,1)S(1)}, bf16[2,32,2048]{2,1,0:T(8,128)(2,1)}, u32[]{:S(2)}, u32[]{:S(2)}) %collective-permute-start.4) | collective-permute-done | bytes 262176 | tf_op jit(solution)/shard_map/ppermute | solution.py:670
  111.7 3.9 qkv.1
  115.6 14.0 %all-gather.1 = bf16[2048,128]{1,0:T(8,128)(2,1)} all-gather(bf16[256,128]{1,0:T(8,128)(2,1)} %get-tuple-element.77), channel_id=3, replica_groups=mesh['ctx'=8,'head'=4] {'ctx'}, dimensions={0}, use_global_device_ids=true | all-gather | bytes 589824 | tf_op jit(solution)/shard_map/all_gather | solution.py:733
  131.7 9.0 %attn_fwd.1 = bf16[256,512]{1,0:T(8,128)(2,1)} custom-call(bf16[256,512]{1,0:T(8,128)(2,1)} %get-tuple-element.76.q_ref, bf16[8,2,128,128]{3,2,1,0:T(8,128)(2,1)} %bitcast.406, s32[128,1]{1,0:T(8,128)} %fusion.56.qpos_ref, s32[1,1024]{1,0:T(1,128)} %bitcast.445), custom_call_target="tpu_custom_call" | custom-call | flops 1073741824 | bytes 524288 | tf_op jit(solution)/shard_map/attn_fwd/pallas_call | solution.py:222
  146.7 10.6 %collective-permute-done.10 = bf16[2,32,2048]{2,1,0:T(8,128)(2,1)S(1)} collective-permute-done((bf16[2,32,2048]{2,1,0:T(8,128)(2,1)S(1)}, bf16[2,32,2048]{2,1,0:T(8,128)(2,1)S(1)}, u32[]{:S(2)}, u32[]{:S(2)}) %collective-permute-start.10) | collective-permute-done | bytes 262176 | tf_op jit(solution)/shard_map/ppermute | solution.py:663
  159.0 8.8 %collective-permute-done.9 = bf16[2,32,2048]{2,1,0:T(8,128)(2,1)S(1)} collective-permute-done((bf16[2,32,2048]{2,1,0:T(8,128)(2,1)S(1)}, bf16[2,32,2048]{2,1,0:T(8,128)(2,1)S(1)}, u32[]{:S(2)}, u32[]{:S(2)}) %collective-permute-start.9) | collective-permute-done | bytes 262176 | tf_op jit(solution)/shard_map/ppermute | solution.py:663
  171.4 12.9 %collective-permute-start.13 = (bf16[2,32,2048]{2,1,0:T(8,128)(2,1)S(1)}, bf16[2,32,2048]{2,1,0:T(8,128)(2,1)S(1)}, u32[]{:S(2)}, u32[]{:S(2)}) collective-permute-start(bf16[2,32,2048]{2,1,0:T(8,128)(2,1)S(1)} %multiply_convert_fusion.2), channel_id=1, source_target_pairs={{0,1},{1,2},{2,3},{3,0},{4,5},{5,6},{6,7},{7,4},{8,9},{9,10},{10,1... | collective-permute-start | bytes 786440 | tf_op jit(solution)/shard_map/ppermute | solution.py:670
  188.1 5.3 collective-permute-done.13
  194.7 6.3 fusion.2
  201.4 5.3 fusion.17
  212.4 5.6 collective-permute-done.16
  219.5 8.8 %collective-permute-done.17 = bf16[2,32,2048]{2,1,0:T(8,128)(2,1)S(1)} collective-permute-done((bf16[2,32,2048]{2,1,0:T(8,128)(2,1)S(1)}, bf16[2,32,2048]{2,1,0:T(8,128)(2,1)S(1)}, u32[]{:S(2)}, u32[]{:S(2)}) %collective-permute-start.17) | collective-permute-done | bytes 262176 | tf_op jit(solution)/shard_map/ppermute | solution.py:663
  229.6 10.0 %collective-permute-done.19.refs_4_ = bf16[128,8192]{1,0:T(8,128)(2,1)} collective-permute-done((bf16[128,8192]{1,0:T(8,128)(2,1)S(1)}, bf16[128,8192]{1,0:T(8,128)(2,1)}, u32[]{:S(2)}, u32[]{:S(2)}) %collective-permute-start.19) | collective-permute-done | bytes 2097184 | tf_op jit(solution)/shard_map/ppermute | solution.py:689
  240.0 3.4 collective-permute-start.21
  243.4 6.7 collective-permute-done.21
  250.1 11.9 %collective-permute-start.23 = (bf16[2,32,2048]{2,1,0:T(8,128)(2,1)S(1)}, bf16[2,32,2048]{2,1,0:T(8,128)(2,1)}, u32[]{:S(2)}, u32[]{:S(2)}) collective-permute-start(bf16[2,32,2048]{2,1,0:T(8,128)(2,1)S(1)} %bitcast.399), channel_id=1, source_target_pairs={{0,1},{1,2},{2,3},{3,0},{4,5},{5,6},{6,7},{7,4},{8,9},{9,10},{10,1... | collective-permute-start | bytes 786440 | tf_op jit(solution)/shard_map/ppermute | solution.py:670
  262.5 3.3 collective-permute-done.22
  268.7 13.6 %head_partial.1.refs_0_ = f32[256,8192]{1,0:T(8,128)} custom-call(s32[4]{0:T(128)} %pad_add_fusion.1.at_ref, bf16[256,2048]{1,0:T(8,128)(2,1)} %bitcast.352, bf16[128,8192]{1,0:T(8,128)(2,1)} %get-tuple-element.81.refs_0_, bf16[128,8192]{1,0:T(8,128)(2,1)} %get-tuple-element.82.refs_1_, bf16[128,8192]{1,0:T(8,128)(2,1)} %copy-done.2, ...), custom_call_target="tpu_custom_call" | custom-call | flops 4294967296 | bytes 25165824 | tf_op jit(solution)/shard_map/head_partial/pallas_call | solution.py:375
  288.8 3.0 collective-permute-done.30.refs_7_.refs_14_
  291.8 3.0 collective-permute-done.31.refs_8_.refs_15_
  294.8 17.0 %head_logits.1 = (f32[256,8192]{1,0:T(8,128)}, f32[8,256]{1,0:T(8,128)}) custom-call(s32[4]{0:T(128)} %pad_add_fusion.at_ref, bf16[256,2048]{1,0:T(8,128)(2,1)} %bitcast.353, s32[256,1]{1,0:T(8,128)} %and_select_fusion.slot_ref, f32[256,8192]{1,0:T(8,128)} %head_partial.1.refs_0_, bf16[128,8192]{1,0:T(8,128)(2,1)} %collective-permute-done.26.refs_1_.refs_8_, ...), custom_call_target="tpu_custom_call" | custom-call | flops 4294967296 | bytes 33554432 | tf_op jit(solution)/shard_map/head_logits/pallas_call | solution.py:432
  322.9 22.9 %head_dlogits.1 = (bf16[8,256,1024]{2,1,0:T(8,128)(2,1)}, bf16[256,2048]{1,0:T(8,128)(2,1)}) custom-call(s32[8]{0:T(128)} %stack.163.at_ref, f32[256,8192]{1,0:T(8,128)} %get-tuple-element.94.logits_ref, f32[256,8]{1,0:T(8,128)} %bitcast.405, s32[256,1]{1,0:T(8,128)} %and_select_fusion.slot_ref, bf16[128,8192]{1,0:T(8,128)(2,1)} %get-tuple-element.81.refs_0_, ...), custom_call_target="tpu_custom_call" | custom-call | flops 8589934592 | bytes 46137344 | tf_op jit(solution)/shard_map/head_dlogits/pallas_call | solution.py:490
  347.0 3.2 collective-permute-start.36
  350.9 7.2 %collective-permute-done.35 = bf16[2,32,2048]{2,1,0:T(8,128)(2,1)S(1)} collective-permute-done((bf16[2,32,2048]{2,1,0:T(8,128)(2,1)S(1)}, bf16[2,32,2048]{2,1,0:T(8,128)(2,1)S(1)}, u32[]{:S(2)}, u32[]{:S(2)}) %collective-permute-start.35) | collective-permute-done | bytes 262176 | tf_op jit(solution)/shard_map/ppermute | solution.py:663
  358.1 7.7 %collective-permute-done.36 = bf16[2,32,2048]{2,1,0:T(8,128)(2,1)S(1)} collective-permute-done((bf16[2,32,2048]{2,1,0:T(8,128)(2,1)S(1)}, bf16[2,32,2048]{2,1,0:T(8,128)(2,1)S(1)}, u32[]{:S(2)}, u32[]{:S(2)}) %collective-permute-start.36) | collective-permute-done | bytes 262176 | tf_op jit(solution)/shard_map/ppermute | solution.py:663
  367.3 6.4 collective-permute-start.38
  374.9 4.6 all-to-all-start.1
  380.3 17.6 %collective-permute-done.39 = bf16[2,32,2048]{2,1,0:T(8,128)(2,1)S(1)} collective-permute-done((bf16[2,32,2048]{2,1,0:T(8,128)(2,1)S(1)}, bf16[2,32,2048]{2,1,0:T(8,128)(2,1)S(1)}, u32[]{:S(2)}, u32[]{:S(2)}) %collective-permute-start.39) | collective-permute-done | bytes 262176 | tf_op jit(solution)/shard_map/ppermute | solution.py:670
  398.1 5.9 fusion.47
  404.1 8.0 %fusion.11 = bf16[256,2048]{1,0:T(8,128)(2,1)S(1)} fusion(bf16[256,2816]{1,0:T(8,128)(2,1)S(1)} %add_convert_fusion.da_ref, bf16[2048,4224]{1,0:T(8,128)(2,1)} %all-gather.10.cloned.1.call-done), kind=kOutput, calls=%fused_computation.17 | convolution fusion | flops 2953314304 | bytes 14024704 | tf_op jit(solution)/shard_map/dot_general | solution.py:48
  413.0 3.8 collective-permute-start.43
  416.8 15.1 %ff_weight_grad.1 = bf16[2048,4224]{1,0:T(8,128)(2,1)} custom-call(bf16[256,2048]{1,0:T(8,128)(2,1)} %bitcast.369, bf16[256,2816]{1,0:T(8,128)(2,1)} %copy-done.6, bf16[256,2048]{1,0:T(8,128)(2,1)} %bitcast.371, bf16[256,1408]{1,0:T(8,128)(2,1)} %copy-done.11), custom_call_target="tpu_custom_call" | custom-call | flops 4429185024 | bytes 19398656 | tf_op jit(solution)/shard_map/ff_weight_grad/pallas_call | solution.py:531
  440.0 5.5 collective-permute-start.44
  446.4 16.8 %multiply_reduce_fusion = (f32[]{:T(128)}, bf16[2048,1024]{1,0:T(8,128)(2,1)}) fusion(bf16[2048,2048]{1,0:T(8,128)(2,1)} %all-gather.12.cloned.1.call-done, bf16[2048,1024]{1,0:T(8,128)(2,1)} %bitcast.85), kind=kOutput, calls=%fused_computation.4 | convolution fusion | flops 8596226048 | bytes 16777220 | tf_op jit(solution)/shard_map/dot_general | solution.py:52
  463.2 5.0 collective-permute-done.45
  468.3 3.0 fusion.28.do_ref
  471.3 18.8 %attn_bwd.1 = (bf16[256,512]{1,0:T(8,128)(2,1)}, bf16[8,2,128,128]{3,2,1,0:T(8,128)(2,1)}) custom-call(bf16[256,512]{1,0:T(8,128)(2,1)} %get-tuple-element.76.q_ref, bf16[256,512]{1,0:T(8,128)(2,1)} %fusion.28.do_ref, bf16[8,2,128,128]{3,2,1,0:T(8,128)(2,1)} %bitcast.407, s32[1,128]{1,0:T(1,128)} %fusion.83.qpos_ref, s32[1024,1]{1,0:T(8,128)} %copy.296.kpos_ref, ...), custom_call_target="tpu_custom_call" | custom-call | flops 2684354560 | bytes 1048576 | tf_op jit(solution)/shard_map/attn_bwd/pallas_call | solution.py:282
  490.1 4.2 all-to-all-start.2
  495.6 14.4 %all-to-all-done.2.parts_ref = bf16[8,256,128]{2,1,0:T(8,128)(2,1)} async-done(((bf16[8,256,128]{2,1,0:T(8,128)(2,1)}), bf16[8,256,128]{2,1,0:T(8,128)(2,1)}, u32[]{:S(2)}, u32[]{:S(2)}) %all-to-all-start.2) | async-done | bytes 524320 | tf_op jit(solution)/shard_map/all_to_all | solution.py:809
  512.1 3.0 fusion.14
  516.6 2.8 collective-permute-start.49
  520.5 5.8 collective-permute-done.47
  526.3 7.0 collective-permute-done.48
  536.5 4.2 all-to-all-start.3
  543.2 9.1 %all-to-all-done.3 = bf16[80,8,256]{2,0,1:T(8,128)(2,1)} async-done(((bf16[80,8,256]{2,0,1:T(8,128)(2,1)}), bf16[80,8,256]{2,0,1:T(8,128)(2,1)}, u32[]{:S(2)}, u32[]{:S(2)}) %all-to-all-start.3) | async-done | bytes 327712 | tf_op jit(solution)/shard_map/all_to_all | solution.py:832
  558.5 6.0 collective-permute-start.56
  565.1 10.6 %collective-permute-done.54 = bf16[2,256,512]{2,1,0:T(8,128)(2,1)S(1)} collective-permute-done((bf16[2,256,512]{2,1,0:T(8,128)(2,1)S(1)}, bf16[2,256,512]{2,1,0:T(8,128)(2,1)S(1)}, u32[]{:S(2)}, u32[]{:S(2)}) %collective-permute-start.54) | collective-permute-done | bytes 524320 | tf_op jit(solution)/shard_map/ppermute | solution.py:689
  581.8 5.2 collective-permute-done.57
  587.8 4.6 all-to-all-start.4
  596.7 12.6 %embed_grad.1 = (bf16[256,8064]{1,0:T(8,128)(2,1)}, f32[8,128]{1,0:T(8,128)}) custom-call(s32[2048,1]{1,0:T(8,128)} %copy.260.ids_ref, bf16[256,2048]{1,0:T(8,128)(2,1)} %bitcast.388), custom_call_target="tpu_custom_call" | custom-call | flops 8455716864 | bytes 4128768 | tf_op jit(solution)/shard_map/embed_grad/pallas_call | solution.py:125
  613.7 3.3 multiply_reduce_fusion.1
  626.0 3.3 collective-permute-done.61
  629.9 14.7 %all-gather.2 = f32[64,128]{1,0:T(8,128)S(1)} all-gather(f32[8,128]{1,0:T(8,128)S(1)} %add_select_fusion.3), channel_id=4, replica_groups=mesh['ctx'=8,'head'=4] {'ctx'}, dimensions={0}, use_global_device_ids=true | all-gather | bytes 36864 | tf_op jit(solution)/shard_map/all_gather | solution.py:880
  646.0 15.0 %layer_update.1 = (f32[256,5376]{1,0:T(8,128)}, f32[256,5376]{1,0:T(8,128)}, f32[256,5376]{1,0:T(8,128)}, bf16[256,5376]{1,0:T(8,128)(2,1)}) custom-call(f32[1,1]{1,0:T(1,128)} %bitcast.136.factor_ref, bf16[256,4224]{1,0:T(8,128)(2,1)} %reduce-scatter.2.cloned.1.call-done.refs_0_, f32[256,640]{1,0:T(8,128)} %get-tuple-element.147.refs_1_, ...), custom_call_target="tpu_custom_call" | custom-call | flops 13762560 | bytes 38535168 | tf_op jit(solution)/shard_map/layer_update/pallas_call | solution.py:599
  662.2 39.1 %vocab_update.1 = (f32[256,16000]{1,0:T(8,128)}, f32[256,16000]{1,0:T(8,128)}, f32[256,16000]{1,0:T(8,128)}, bf16[256,16000]{1,0:T(8,128)(2,1)}) custom-call(f32[1,1]{1,0:T(1,128)} %bitcast.136.factor_ref, bf16[8,256,1024]{2,1,0:T(8,128)(2,1)} %all-to-all-done.4.head_ref, bf16[256,8064]{1,0:T(8,128)(2,1)} %get-tuple-element.127.embed_ref, ...), custom_call_target="tpu_custom_call" | custom-call | flops 40960000 | bytes 114688000 | tf_op jit(solution)/shard_map/vocab_update/pallas_call | solution.py:599
  (336 shorter events, 132.9 us)
Async XLA Ops:
  7.2 103.3 %all-gather.8.cloned.1.call-start = ((), (), s32[]{:S(2)}) async-start(), calls=%async_computation.6 | async-start | bytes 5308416 | tf_op jit(solution)/shard_map/all_gather | solution.py:682
  10.9 183.7 %all-gather.10.cloned.1.call-start = ((), (), s32[]{:S(2)}) async-start(), calls=%async_computation.7 | async-start | bytes 19464192 | tf_op jit(solution)/shard_map/all_gather | solution.py:683
  41.1 17.8 %collective-permute-start = (bf16[16,32,256]{2,1,0:T(8,128)(2,1)}, bf16[16,32,256]{2,1,0:T(8,128)(2,1)S(1)}, u32[]{:S(2)}, u32[]{:S(2)}) collective-permute-start(bf16[16,32,256]{2,1,0:T(8,128)(2,1)} %get-tuple-element.179), channel_id=1, source_target_pairs={{0,1},{1,2},{2,3},{3,0},{4,5},{5,6},{6,7},{7,4},{8,9},{9,10},{10,1... | collective-permute-start | bytes 786440 | tf_op jit(solution)/shard_map/ppermute | solution.py:663
  42.7 20.4 %collective-permute-start.1 = (bf16[16,32,256]{2,1,0:T(8,128)(2,1)S(1)}, bf16[16,32,256]{2,1,0:T(8,128)(2,1)S(1)}, u32[]{:S(2)}, u32[]{:S(2)}) collective-permute-start(bf16[16,32,256]{2,1,0:T(8,128)(2,1)S(1)} %get-tuple-element.181), channel_id=1, source_target_pairs={{0,2},{1,3},{2,0},{3,1},{4,6},{5,7},{6,4},{7,5},{8,10},{9,11},{10,... | collective-permute-start | bytes 786440 | tf_op jit(solution)/shard_map/ppermute | solution.py:663
  45.3 17.8 %collective-permute-start.2 = (bf16[16,32,256]{2,1,0:T(8,128)(2,1)S(1)}, bf16[16,32,256]{2,1,0:T(8,128)(2,1)S(1)}, u32[]{:S(2)}, u32[]{:S(2)}) collective-permute-start(bf16[16,32,256]{2,1,0:T(8,128)(2,1)S(1)} %get-tuple-element.180), channel_id=1, source_target_pairs={{0,3},{1,0},{2,1},{3,2},{4,7},{5,4},{6,5},{7,6},{8,11},{9,8},{10,9... | collective-permute-start | bytes 786440 | tf_op jit(solution)/shard_map/ppermute | solution.py:663
  54.4 56.0 %collective-permute-start.6 = (bf16[128,8192]{1,0:T(8,128)(2,1)}, bf16[128,8192]{1,0:T(8,128)(2,1)S(1)}, u32[]{:S(2)}, u32[]{:S(2)}) collective-permute-start(bf16[128,8192]{1,0:T(8,128)(2,1)} %get-tuple-element.81.refs_0_), channel_id=1, source_target_pairs={{0,4},{4,0},{8,12},{12,8},{16,20},{20,16},{24,28},{28,24},{1,5},{5... | collective-permute-start | bytes 6291464 | tf_op jit(solution)/shard_map/ppermute | solution.py:689
  54.4 56.0 %collective-permute-start.7 = (bf16[128,8192]{1,0:T(8,128)(2,1)}, bf16[128,8192]{1,0:T(8,128)(2,1)}, u32[]{:S(2)}, u32[]{:S(2)}) collective-permute-start(bf16[128,8192]{1,0:T(8,128)(2,1)} %get-tuple-element.82.refs_1_), channel_id=1, source_target_pairs={{0,4},{4,0},{8,12},{12,8},{16,20},{20,16},{24,28},{28,24},{1,5},{5... | collective-permute-start | bytes 6291464 | tf_op jit(solution)/shard_map/ppermute | solution.py:689
  65.0 13.5 %all-to-all-start = ((bf16[8,64,256]{2,1,0:T(8,128)(2,1)}), bf16[8,64,256]{2,1,0:T(8,128)(2,1)S(1)}, u32[]{:S(2)}, u32[]{:S(2)}) async-start(bf16[8,64,256]{2,1,0:T(8,128)(2,1)} %bitcast.8), calls=%async_computation | async-start | bytes 524288 | tf_op jit(solution)/shard_map/all_to_all | solution.py:707
  68.4 367.2 %all-gather.12.cloned.1.call-start = ((), (), s32[]{:S(2)}) async-start(), calls=%async_computation.8 | async-start | bytes 9437184 | tf_op jit(solution)/shard_map/all_gather | solution.py:790
  80.1 13.9 %collective-permute-start.3 = (bf16[2,32,2048]{2,1,0:T(8,128)(2,1)S(1)}, bf16[2,32,2048]{2,1,0:T(8,128)(2,1)}, u32[]{:S(2)}, u32[]{:S(2)}) collective-permute-start(bf16[2,32,2048]{2,1,0:T(8,128)(2,1)S(1)} %multiply_convert_fusion.3), channel_id=1, source_target_pairs={{0,3},{1,0},{2,1},{3,2},{4,7},{5,4},{6,5},{7,6},{8,11},{9,8},{10,9... | collective-permute-start | bytes 786440 | tf_op jit(solution)/shard_map/ppermute | solution.py:670
  87.3 20.7 %collective-permute-start.4 = (bf16[2,32,2048]{2,1,0:T(8,128)(2,1)S(1)}, bf16[2,32,2048]{2,1,0:T(8,128)(2,1)}, u32[]{:S(2)}, u32[]{:S(2)}) collective-permute-start(bf16[2,32,2048]{2,1,0:T(8,128)(2,1)S(1)} %multiply_convert_fusion.3), channel_id=1, source_target_pairs={{0,2},{1,3},{2,0},{3,1},{4,6},{5,7},{6,4},{7,5},{8,10},{9,11},{10,... | collective-permute-start | bytes 786440 | tf_op jit(solution)/shard_map/ppermute | solution.py:670
  87.7 20.4 %collective-permute-start.5 = (bf16[2,32,2048]{2,1,0:T(8,128)(2,1)S(1)}, bf16[2,32,2048]{2,1,0:T(8,128)(2,1)}, u32[]{:S(2)}, u32[]{:S(2)}) collective-permute-start(bf16[2,32,2048]{2,1,0:T(8,128)(2,1)S(1)} %multiply_convert_fusion.3), channel_id=1, source_target_pairs={{0,1},{1,2},{2,3},{3,0},{4,5},{5,6},{6,7},{7,4},{8,9},{9,10},{10,1... | collective-permute-start | bytes 786440 | tf_op jit(solution)/shard_map/ppermute | solution.py:670
  129.7 64.9 %collective-permute-start.14 = (bf16[128,8192]{1,0:T(8,128)(2,1)S(1)}, bf16[128,8192]{1,0:T(8,128)(2,1)}, u32[]{:S(2)}, u32[]{:S(2)}) collective-permute-start(bf16[128,8192]{1,0:T(8,128)(2,1)S(1)} %copy-done.1), channel_id=1, source_target_pairs={{0,16},{4,20},{8,24},{12,28},{16,0},{20,4},{24,8},{28,12},{1,17},{... | collective-permute-start | bytes 6291464 | tf_op jit(solution)/shard_map/ppermute | solution.py:689
  130.3 64.4 %collective-permute-start.15 = (bf16[128,8192]{1,0:T(8,128)(2,1)}, bf16[128,8192]{1,0:T(8,128)(2,1)}, u32[]{:S(2)}, u32[]{:S(2)}) collective-permute-start(bf16[128,8192]{1,0:T(8,128)(2,1)} %get-tuple-element.82.refs_1_), channel_id=1, source_target_pairs={{0,8},{4,12},{8,0},{12,4},{16,24},{20,28},{24,16},{28,20},{1,9},{5... | collective-permute-start | bytes 6291464 | tf_op jit(solution)/shard_map/ppermute | solution.py:689
  143.2 14.1 %collective-permute-start.10 = (bf16[2,32,2048]{2,1,0:T(8,128)(2,1)S(1)}, bf16[2,32,2048]{2,1,0:T(8,128)(2,1)S(1)}, u32[]{:S(2)}, u32[]{:S(2)}) collective-permute-start(bf16[2,32,2048]{2,1,0:T(8,128)(2,1)S(1)} %get-tuple-element.178), channel_id=1, source_target_pairs={{0,3},{1,0},{2,1},{3,2},{4,7},{5,4},{6,5},{7,6},{8,11},{9,8},{10,9... | collective-permute-start | bytes 786440 | tf_op jit(solution)/shard_map/ppermute | solution.py:663
  143.3 15.8 %collective-permute-start.8 = (bf16[2,32,2048]{2,1,0:T(8,128)(2,1)S(1)}, bf16[2,32,2048]{2,1,0:T(8,128)(2,1)S(1)}, u32[]{:S(2)}, u32[]{:S(2)}) collective-permute-start(bf16[2,32,2048]{2,1,0:T(8,128)(2,1)S(1)} %get-tuple-element.176), channel_id=1, source_target_pairs={{0,1},{1,2},{2,3},{3,0},{4,5},{5,6},{6,7},{7,4},{8,9},{9,10},{10,1... | collective-permute-start | bytes 786440 | tf_op jit(solution)/shard_map/ppermute | solution.py:663
  145.3 22.6 %collective-permute-start.9 = (bf16[2,32,2048]{2,1,0:T(8,128)(2,1)S(1)}, bf16[2,32,2048]{2,1,0:T(8,128)(2,1)S(1)}, u32[]{:S(2)}, u32[]{:S(2)}) collective-permute-start(bf16[2,32,2048]{2,1,0:T(8,128)(2,1)S(1)} %get-tuple-element.177), channel_id=1, source_target_pairs={{0,2},{1,3},{2,0},{3,1},{4,6},{5,7},{6,4},{7,5},{8,10},{9,11},{10,... | collective-permute-start | bytes 786440 | tf_op jit(solution)/shard_map/ppermute | solution.py:663
  169.0 15.5 %collective-permute-start.11 = (bf16[2,32,2048]{2,1,0:T(8,128)(2,1)S(1)}, bf16[2,32,2048]{2,1,0:T(8,128)(2,1)S(1)}, u32[]{:S(2)}, u32[]{:S(2)}) collective-permute-start(bf16[2,32,2048]{2,1,0:T(8,128)(2,1)S(1)} %multiply_convert_fusion.2), channel_id=1, source_target_pairs={{0,3},{1,0},{2,1},{3,2},{4,7},{5,4},{6,5},{7,6},{8,11},{9,8},{10,9... | collective-permute-start | bytes 786440 | tf_op jit(solution)/shard_map/ppermute | solution.py:670
  171.4 16.1 %collective-permute-start.12 = (bf16[2,32,2048]{2,1,0:T(8,128)(2,1)S(1)}, bf16[2,32,2048]{2,1,0:T(8,128)(2,1)S(1)}, u32[]{:S(2)}, u32[]{:S(2)}) collective-permute-start(bf16[2,32,2048]{2,1,0:T(8,128)(2,1)S(1)} %multiply_convert_fusion.2), channel_id=1, source_target_pairs={{0,2},{1,3},{2,0},{3,1},{4,6},{5,7},{6,4},{7,5},{8,10},{9,11},{10,... | collective-permute-start | bytes 786440 | tf_op jit(solution)/shard_map/ppermute | solution.py:670
  171.4 22.0 %collective-permute-start.13 = (bf16[2,32,2048]{2,1,0:T(8,128)(2,1)S(1)}, bf16[2,32,2048]{2,1,0:T(8,128)(2,1)S(1)}, u32[]{:S(2)}, u32[]{:S(2)}) collective-permute-start(bf16[2,32,2048]{2,1,0:T(8,128)(2,1)S(1)} %multiply_convert_fusion.2), channel_id=1, source_target_pairs={{0,1},{1,2},{2,3},{3,0},{4,5},{5,6},{6,7},{7,4},{8,9},{9,10},{10,1... | collective-permute-start | bytes 786440 | tf_op jit(solution)/shard_map/ppermute | solution.py:670
  184.5 55.2 %collective-permute-start.19 = (bf16[128,8192]{1,0:T(8,128)(2,1)S(1)}, bf16[128,8192]{1,0:T(8,128)(2,1)}, u32[]{:S(2)}, u32[]{:S(2)}) collective-permute-start(bf16[128,8192]{1,0:T(8,128)(2,1)S(1)} %copy-done.1), channel_id=1, source_target_pairs={{0,8},{4,12},{8,0},{12,4},{16,24},{20,28},{24,16},{28,20},{1,9},{5... | collective-permute-start | bytes 6291464 | tf_op jit(solution)/shard_map/ppermute | solution.py:689
  187.5 52.1 %collective-permute-start.20 = (bf16[128,8192]{1,0:T(8,128)(2,1)}, bf16[128,8192]{1,0:T(8,128)(2,1)}, u32[]{:S(2)}, u32[]{:S(2)}) collective-permute-start(bf16[128,8192]{1,0:T(8,128)(2,1)} %get-tuple-element.82.refs_1_), channel_id=1, source_target_pairs={{0,16},{4,20},{8,24},{12,28},{16,0},{20,4},{24,8},{28,12},{1,17},{... | collective-permute-start | bytes 6291464 | tf_op jit(solution)/shard_map/ppermute | solution.py:689
  206.8 11.2 %collective-permute-start.16 = (bf16[2,32,2048]{2,1,0:T(8,128)(2,1)S(1)}, bf16[2,32,2048]{2,1,0:T(8,128)(2,1)S(1)}, u32[]{:S(2)}, u32[]{:S(2)}) collective-permute-start(bf16[2,32,2048]{2,1,0:T(8,128)(2,1)S(1)} %get-tuple-element.173), channel_id=1, source_target_pairs={{0,1},{1,2},{2,3},{3,0},{4,5},{5,6},{6,7},{7,4},{8,9},{9,10},{10,1... | collective-permute-start | bytes 786440 | tf_op jit(solution)/shard_map/ppermute | solution.py:663
  208.4 19.9 %collective-permute-start.17 = (bf16[2,32,2048]{2,1,0:T(8,128)(2,1)S(1)}, bf16[2,32,2048]{2,1,0:T(8,128)(2,1)S(1)}, u32[]{:S(2)}, u32[]{:S(2)}) collective-permute-start(bf16[2,32,2048]{2,1,0:T(8,128)(2,1)S(1)} %get-tuple-element.175), channel_id=1, source_target_pairs={{0,2},{1,3},{2,0},{3,1},{4,6},{5,7},{6,4},{7,5},{8,10},{9,11},{10,... | collective-permute-start | bytes 786440 | tf_op jit(solution)/shard_map/ppermute | solution.py:663
  210.8 17.4 %collective-permute-start.18 = (bf16[2,32,2048]{2,1,0:T(8,128)(2,1)S(1)}, bf16[2,32,2048]{2,1,0:T(8,128)(2,1)S(1)}, u32[]{:S(2)}, u32[]{:S(2)}) collective-permute-start(bf16[2,32,2048]{2,1,0:T(8,128)(2,1)S(1)} %get-tuple-element.174), channel_id=1, source_target_pairs={{0,3},{1,0},{2,1},{3,2},{4,7},{5,4},{6,5},{7,6},{8,11},{9,8},{10,9... | collective-permute-start | bytes 786440 | tf_op jit(solution)/shard_map/ppermute | solution.py:663
  218.0 66.3 %collective-permute-start.25 = (bf16[128,8192]{1,0:T(8,128)(2,1)}, bf16[128,8192]{1,0:T(8,128)(2,1)}, u32[]{:S(2)}, u32[]{:S(2)}) collective-permute-start(bf16[128,8192]{1,0:T(8,128)(2,1)} %collective-permute-done.15.refs_5_), channel_id=1, source_target_pairs={{0,16},{4,20},{8,24},{12,28},{16,0},{20,4},{24,8},{28,12},{1,17},{... | collective-permute-start | bytes 6291464 | tf_op jit(solution)/shard_map/ppermute | solution.py:689
  228.3 56.6 %collective-permute-start.27 = (bf16[128,8192]{1,0:T(8,128)(2,1)}, bf16[128,8192]{1,0:T(8,128)(2,1)}, u32[]{:S(2)}, u32[]{:S(2)}) collective-permute-start(bf16[128,8192]{1,0:T(8,128)(2,1)} %collective-permute-done.15.refs_5_), channel_id=1, source_target_pairs={{0,4},{4,0},{8,12},{12,8},{16,20},{20,16},{24,28},{28,24},{1,5},{5... | collective-permute-start | bytes 6291464 | tf_op jit(solution)/shard_map/ppermute | solution.py:689
  228.3 56.1 %collective-permute-start.24 = (bf16[128,8192]{1,0:T(8,128)(2,1)}, bf16[128,8192]{1,0:T(8,128)(2,1)}, u32[]{:S(2)}, u32[]{:S(2)}) collective-permute-start(bf16[128,8192]{1,0:T(8,128)(2,1)} %collective-permute-done.14.refs_6_), channel_id=1, source_target_pairs={{0,8},{4,12},{8,0},{12,4},{16,24},{20,28},{24,16},{28,20},{1,9},{5... | collective-permute-start | bytes 6291464 | tf_op jit(solution)/shard_map/ppermute | solution.py:689
  240.0 10.1 %collective-permute-start.21 = (bf16[2,32,2048]{2,1,0:T(8,128)(2,1)S(1)}, bf16[2,32,2048]{2,1,0:T(8,128)(2,1)S(1)}, u32[]{:S(2)}, u32[]{:S(2)}) collective-permute-start(bf16[2,32,2048]{2,1,0:T(8,128)(2,1)S(1)} %bitcast.397), channel_id=1, source_target_pairs={{0,3},{1,0},{2,1},{3,2},{4,7},{5,4},{6,5},{7,6},{8,11},{9,8},{10,9... | collective-permute-start | bytes 786440 | tf_op jit(solution)/shard_map/ppermute | solution.py:670
  243.4 22.5 %collective-permute-start.22 = (bf16[2,32,2048]{2,1,0:T(8,128)(2,1)S(1)}, bf16[2,32,2048]{2,1,0:T(8,128)(2,1)}, u32[]{:S(2)}, u32[]{:S(2)}) collective-permute-start(bf16[2,32,2048]{2,1,0:T(8,128)(2,1)S(1)} %bitcast.398), channel_id=1, source_target_pairs={{0,2},{1,3},{2,0},{3,1},{4,6},{5,7},{6,4},{7,5},{8,10},{9,11},{10,... | collective-permute-start | bytes 786440 | tf_op jit(solution)/shard_map/ppermute | solution.py:670
  250.1 15.8 %collective-permute-start.23 = (bf16[2,32,2048]{2,1,0:T(8,128)(2,1)S(1)}, bf16[2,32,2048]{2,1,0:T(8,128)(2,1)}, u32[]{:S(2)}, u32[]{:S(2)}) collective-permute-start(bf16[2,32,2048]{2,1,0:T(8,128)(2,1)S(1)} %bitcast.399), channel_id=1, source_target_pairs={{0,1},{1,2},{2,3},{3,0},{4,5},{5,6},{6,7},{7,4},{8,9},{9,10},{10,1... | collective-permute-start | bytes 786440 | tf_op jit(solution)/shard_map/ppermute | solution.py:670
  265.8 20.7 %collective-permute-start.28 = (bf16[128,8192]{1,0:T(8,128)(2,1)}, bf16[128,8192]{1,0:T(8,128)(2,1)S(1)}, u32[]{:S(2)}, u32[]{:S(2)}) collective-permute-start(bf16[128,8192]{1,0:T(8,128)(2,1)} %collective-permute-done.14.refs_6_), channel_id=1, source_target_pairs={{0,4},{4,0},{8,12},{12,8},{16,20},{20,16},{24,28},{28,24},{1,5},{5... | collective-permute-start | bytes 6291464 | tf_op jit(solution)/shard_map/ppermute | solution.py:689
  265.9 20.6 %collective-permute-start.26 = (bf16[128,8192]{1,0:T(8,128)(2,1)}, bf16[128,8192]{1,0:T(8,128)(2,1)}, u32[]{:S(2)}, u32[]{:S(2)}) collective-permute-start(bf16[128,8192]{1,0:T(8,128)(2,1)} %collective-permute-done.19.refs_4_), channel_id=1, source_target_pairs={{0,4},{4,0},{8,12},{12,8},{16,20},{20,16},{24,28},{28,24},{1,5},{5... | collective-permute-start | bytes 6291464 | tf_op jit(solution)/shard_map/ppermute | solution.py:689
  284.3 7.5 %collective-permute-start.30 = (bf16[128,8192]{1,0:T(8,128)(2,1)}, bf16[128,8192]{1,0:T(8,128)(2,1)}, u32[]{:S(2)}, u32[]{:S(2)}) collective-permute-start(bf16[128,8192]{1,0:T(8,128)(2,1)} %collective-permute-done.24.refs_5_.refs_12_), channel_id=1, source_target_pairs={{0,4},{4,0},{8,12},{12,8},{16,20},{20,16},{24,28},{28,24},{1,5},{5... | collective-permute-start | bytes 6291464 | tf_op jit(solution)/shard_map/ppermute | solution.py:689
  284.8 10.0 %collective-permute-start.31 = (bf16[128,8192]{1,0:T(8,128)(2,1)}, bf16[128,8192]{1,0:T(8,128)(2,1)}, u32[]{:S(2)}, u32[]{:S(2)}) collective-permute-start(bf16[128,8192]{1,0:T(8,128)(2,1)} %collective-permute-done.25.refs_6_.refs_13_), channel_id=1, source_target_pairs={{0,4},{4,0},{8,12},{12,8},{16,20},{20,16},{24,28},{28,24},{1,5},{5... | collective-permute-start | bytes 6291464 | tf_op jit(solution)/shard_map/ppermute | solution.py:689
  347.0 11.1 %collective-permute-start.35 = (bf16[2,32,2048]{2,1,0:T(8,128)(2,1)S(1)}, bf16[2,32,2048]{2,1,0:T(8,128)(2,1)S(1)}, u32[]{:S(2)}, u32[]{:S(2)}) collective-permute-start(bf16[2,32,2048]{2,1,0:T(8,128)(2,1)S(1)} %get-tuple-element.170), channel_id=1, source_target_pairs={{0,1},{1,2},{2,3},{3,0},{4,5},{5,6},{6,7},{7,4},{8,9},{9,10},{10,1... | collective-permute-start | bytes 786440 | tf_op jit(solution)/shard_map/ppermute | solution.py:663
  347.0 18.7 %collective-permute-start.36 = (bf16[2,32,2048]{2,1,0:T(8,128)(2,1)S(1)}, bf16[2,32,2048]{2,1,0:T(8,128)(2,1)S(1)}, u32[]{:S(2)}, u32[]{:S(2)}) collective-permute-start(bf16[2,32,2048]{2,1,0:T(8,128)(2,1)S(1)} %get-tuple-element.172), channel_id=1, source_target_pairs={{0,2},{1,3},{2,0},{3,1},{4,6},{5,7},{6,4},{7,5},{8,10},{9,11},{10,... | collective-permute-start | bytes 786440 | tf_op jit(solution)/shard_map/ppermute | solution.py:663
  350.3 15.5 %collective-permute-start.37 = (bf16[2,32,2048]{2,1,0:T(8,128)(2,1)S(1)}, bf16[2,32,2048]{2,1,0:T(8,128)(2,1)S(1)}, u32[]{:S(2)}, u32[]{:S(2)}) collective-permute-start(bf16[2,32,2048]{2,1,0:T(8,128)(2,1)S(1)} %get-tuple-element.171), channel_id=1, source_target_pairs={{0,3},{1,0},{2,1},{3,2},{4,7},{5,4},{6,5},{7,6},{8,11},{9,8},{10,9... | collective-permute-start | bytes 786440 | tf_op jit(solution)/shard_map/ppermute | solution.py:663
  367.3 13.1 %collective-permute-start.38 = (bf16[2,32,2048]{2,1,0:T(8,128)(2,1)S(1)}, bf16[2,32,2048]{2,1,0:T(8,128)(2,1)S(1)}, u32[]{:S(2)}, u32[]{:S(2)}) collective-permute-start(bf16[2,32,2048]{2,1,0:T(8,128)(2,1)S(1)} %bitcast.401), channel_id=1, source_target_pairs={{0,3},{1,0},{2,1},{3,2},{4,7},{5,4},{6,5},{7,6},{8,11},{9,8},{10,9... | collective-permute-start | bytes 786440 | tf_op jit(solution)/shard_map/ppermute | solution.py:670
  373.7 24.3 %collective-permute-start.39 = (bf16[2,32,2048]{2,1,0:T(8,128)(2,1)S(1)}, bf16[2,32,2048]{2,1,0:T(8,128)(2,1)S(1)}, u32[]{:S(2)}, u32[]{:S(2)}) collective-permute-start(bf16[2,32,2048]{2,1,0:T(8,128)(2,1)S(1)} %bitcast.402), channel_id=1, source_target_pairs={{0,2},{1,3},{2,0},{3,1},{4,6},{5,7},{6,4},{7,5},{8,10},{9,11},{10,... | collective-permute-start | bytes 786440 | tf_op jit(solution)/shard_map/ppermute | solution.py:670
  374.9 23.1 %collective-permute-start.40 = (bf16[2,32,2048]{2,1,0:T(8,128)(2,1)S(1)}, bf16[2,32,2048]{2,1,0:T(8,128)(2,1)S(1)}, u32[]{:S(2)}, u32[]{:S(2)}) collective-permute-start(bf16[2,32,2048]{2,1,0:T(8,128)(2,1)S(1)} %bitcast.403), channel_id=1, source_target_pairs={{0,1},{1,2},{2,3},{3,0},{4,5},{5,6},{6,7},{7,4},{8,9},{9,10},{10,1... | collective-permute-start | bytes 786440 | tf_op jit(solution)/shard_map/ppermute | solution.py:670
  374.9 60.7 %all-to-all-start.1 = ((bf16[8,256,1024]{2,1,0:T(8,128)(2,1)}), bf16[8,256,1024]{2,1,0:T(8,128)(2,1)}, u32[]{:S(2)}, u32[]{:S(2)}) async-start(bf16[8,256,1024]{2,1,0:T(8,128)(2,1)} %get-tuple-element.98), calls=%async_computation.1 | async-start | bytes 8388608 | tf_op jit(solution)/shard_map/all_to_all | solution.py:791
  379.5 234.2 %reduce-scatter.2.cloned.1.call-start = ((), (), s32[]{:S(2)}) async-start(), calls=%async_computation.9 | async-start | bytes 19464192 | tf_op jit(solution)/shard_map/reduce_scatter | solution.py:800
  413.0 18.9 %collective-permute-start.41 = (bf16[2,32,2048]{2,1,0:T(8,128)(2,1)}, bf16[2,32,2048]{2,1,0:T(8,128)(2,1)S(1)}, u32[]{:S(2)}, u32[]{:S(2)}) collective-permute-start(bf16[2,32,2048]{2,1,0:T(8,128)(2,1)} %get-tuple-element.167), channel_id=1, source_target_pairs={{0,1},{1,2},{2,3},{3,0},{4,5},{5,6},{6,7},{7,4},{8,9},{9,10},{10,1... | collective-permute-start | bytes 786440 | tf_op jit(solution)/shard_map/ppermute | solution.py:663
  413.0 20.8 %collective-permute-start.42 = (bf16[2,32,2048]{2,1,0:T(8,128)(2,1)}, bf16[2,32,2048]{2,1,0:T(8,128)(2,1)S(1)}, u32[]{:S(2)}, u32[]{:S(2)}) collective-permute-start(bf16[2,32,2048]{2,1,0:T(8,128)(2,1)} %get-tuple-element.169), channel_id=1, source_target_pairs={{0,2},{1,3},{2,0},{3,1},{4,6},{5,7},{6,4},{7,5},{8,10},{9,11},{10,... | collective-permute-start | bytes 786440 | tf_op jit(solution)/shard_map/ppermute | solution.py:663
  413.0 21.5 %collective-permute-start.43 = (bf16[2,32,2048]{2,1,0:T(8,128)(2,1)S(1)}, bf16[2,32,2048]{2,1,0:T(8,128)(2,1)}, u32[]{:S(2)}, u32[]{:S(2)}) collective-permute-start(bf16[2,32,2048]{2,1,0:T(8,128)(2,1)S(1)} %get-tuple-element.168), channel_id=1, source_target_pairs={{0,3},{1,0},{2,1},{3,2},{4,7},{5,4},{6,5},{7,6},{8,11},{9,8},{10,9... | collective-permute-start | bytes 786440 | tf_op jit(solution)/shard_map/ppermute | solution.py:663
  440.0 23.2 %collective-permute-start.44 = (bf16[2,32,2048]{2,1,0:T(8,128)(2,1)S(1)}, bf16[2,32,2048]{2,1,0:T(8,128)(2,1)S(1)}, u32[]{:S(2)}, u32[]{:S(2)}) collective-permute-start(bf16[2,32,2048]{2,1,0:T(8,128)(2,1)S(1)} %bitcast.390), channel_id=1, source_target_pairs={{0,3},{1,0},{2,1},{3,2},{4,7},{5,4},{6,5},{7,6},{8,11},{9,8},{10,9... | collective-permute-start | bytes 786440 | tf_op jit(solution)/shard_map/ppermute | solution.py:670
  445.4 22.7 %collective-permute-start.45 = (bf16[2,32,2048]{2,1,0:T(8,128)(2,1)S(1)}, bf16[2,32,2048]{2,1,0:T(8,128)(2,1)S(1)}, u32[]{:S(2)}, u32[]{:S(2)}) collective-permute-start(bf16[2,32,2048]{2,1,0:T(8,128)(2,1)S(1)} %bitcast.391), channel_id=1, source_target_pairs={{0,2},{1,3},{2,0},{3,1},{4,6},{5,7},{6,4},{7,5},{8,10},{9,11},{10,... | collective-permute-start | bytes 786440 | tf_op jit(solution)/shard_map/ppermute | solution.py:670
  446.0 22.2 %collective-permute-start.46 = (bf16[2,32,2048]{2,1,0:T(8,128)(2,1)S(1)}, bf16[2,32,2048]{2,1,0:T(8,128)(2,1)S(1)}, u32[]{:S(2)}, u32[]{:S(2)}) collective-permute-start(bf16[2,32,2048]{2,1,0:T(8,128)(2,1)S(1)} %bitcast.392), channel_id=1, source_target_pairs={{0,1},{1,2},{2,3},{3,0},{4,5},{5,6},{6,7},{7,4},{8,9},{9,10},{10,1... | collective-permute-start | bytes 786440 | tf_op jit(solution)/shard_map/ppermute | solution.py:670
  490.1 19.9 %all-to-all-start.2 = ((bf16[8,256,128]{2,1,0:T(8,128)(2,1)}), bf16[8,256,128]{2,1,0:T(8,128)(2,1)}, u32[]{:S(2)}, u32[]{:S(2)}) async-start(bf16[8,256,128]{2,1,0:T(8,128)(2,1)} %bitcast.408), calls=%async_computation.2 | async-start | bytes 1048576 | tf_op jit(solution)/shard_map/all_to_all | solution.py:809
  495.1 38.3 %collective-permute-start.50 = (bf16[2,2,256,512]{3,2,1,0:T(8,128)(2,1)S(1)}, bf16[2,2,256,512]{3,2,1,0:T(8,128)(2,1)}, u32[]{:S(2)}, u32[]{:S(2)}) collective-permute-start(bf16[2,2,256,512]{3,2,1,0:T(8,128)(2,1)S(1)} %dynamic-slice_bitcast_fusion), channel_id=1, source_target_pairs={{0,4},{4,0},{8,12},{12,8},{16,20},{20,16},{24,28},{28,24},{1,5},{5... | collective-permute-start | bytes 3145736 | tf_op jit(solution)/shard_map/ppermute | solution.py:689
  515.2 11.1 %collective-permute-start.47 = (bf16[2,32,2048]{2,1,0:T(8,128)(2,1)S(1)}, bf16[2,32,2048]{2,1,0:T(8,128)(2,1)S(1)}, u32[]{:S(2)}, u32[]{:S(2)}) collective-permute-start(bf16[2,32,2048]{2,1,0:T(8,128)(2,1)S(1)} %get-tuple-element.164), channel_id=1, source_target_pairs={{0,1},{1,2},{2,3},{3,0},{4,5},{5,6},{6,7},{7,4},{8,9},{9,10},{10,1... | collective-permute-start | bytes 786440 | tf_op jit(solution)/shard_map/ppermute | solution.py:663
  515.3 18.1 %collective-permute-start.48 = (bf16[2,32,2048]{2,1,0:T(8,128)(2,1)S(1)}, bf16[2,32,2048]{2,1,0:T(8,128)(2,1)S(1)}, u32[]{:S(2)}, u32[]{:S(2)}) collective-permute-start(bf16[2,32,2048]{2,1,0:T(8,128)(2,1)S(1)} %get-tuple-element.166), channel_id=1, source_target_pairs={{0,2},{1,3},{2,0},{3,1},{4,6},{5,7},{6,4},{7,5},{8,10},{9,11},{10,... | collective-permute-start | bytes 786440 | tf_op jit(solution)/shard_map/ppermute | solution.py:663
  516.6 16.7 %collective-permute-start.49 = (bf16[2,32,2048]{2,1,0:T(8,128)(2,1)S(1)}, bf16[2,32,2048]{2,1,0:T(8,128)(2,1)S(1)}, u32[]{:S(2)}, u32[]{:S(2)}) collective-permute-start(bf16[2,32,2048]{2,1,0:T(8,128)(2,1)S(1)} %get-tuple-element.165), channel_id=1, source_target_pairs={{0,3},{1,0},{2,1},{3,2},{4,7},{5,4},{6,5},{7,6},{8,11},{9,8},{10,9... | collective-permute-start | bytes 786440 | tf_op jit(solution)/shard_map/ppermute | solution.py:663
  534.9 17.4 %collective-permute-start.51 = (bf16[2,2,256,640]{3,2,0,1:T(8,128)(2,1)}, bf16[2,2,256,640]{3,2,0,1:T(8,128)(2,1)}, u32[]{:S(2)}, u32[]{:S(2)}) collective-permute-start(bf16[2,2,256,640]{3,2,0,1:T(8,128)(2,1)} %bitcast.346), channel_id=1, source_target_pairs={{0,4},{4,0},{8,12},{12,8},{16,20},{20,16},{24,28},{28,24},{1,5},{5... | collective-permute-start | bytes 3932168 | tf_op jit(solution)/shard_map/ppermute | solution.py:689
  536.5 15.8 %all-to-all-start.3 = ((bf16[80,8,256]{2,0,1:T(8,128)(2,1)}), bf16[80,8,256]{2,0,1:T(8,128)(2,1)}, u32[]{:S(2)}, u32[]{:S(2)}) async-start(bf16[80,8,256]{2,0,1:T(8,128)(2,1)} %copy.301), calls=%async_computation.3 | async-start | bytes 655360 | tf_op jit(solution)/shard_map/all_to_all | solution.py:832
  554.3 21.4 %collective-permute-start.54 = (bf16[2,256,512]{2,1,0:T(8,128)(2,1)S(1)}, bf16[2,256,512]{2,1,0:T(8,128)(2,1)S(1)}, u32[]{:S(2)}, u32[]{:S(2)}) collective-permute-start(bf16[2,256,512]{2,1,0:T(8,128)(2,1)S(1)} %dynamic-slice_bitcast_fusion.2), channel_id=1, source_target_pairs={{0,16},{4,20},{8,24},{12,28},{16,0},{20,4},{24,8},{28,12},{1,17},{... | collective-permute-start | bytes 1572872 | tf_op jit(solution)/shard_map/ppermute | solution.py:689
  556.7 22.5 %collective-permute-start.52 = (bf16[2,256,640]{2,1,0:T(8,128)(2,1)S(1)}, bf16[2,256,640]{2,1,0:T(8,128)(2,1)S(1)}, u32[]{:S(2)}, u32[]{:S(2)}) collective-permute-start(bf16[2,256,640]{2,1,0:T(8,128)(2,1)S(1)} %dynamic-slice_bitcast_fusion.1), channel_id=1, source_target_pairs={{0,8},{4,12},{8,0},{12,4},{16,24},{20,28},{24,16},{28,20},{1,9},{5... | collective-permute-start | bytes 1966088 | tf_op jit(solution)/shard_map/ppermute | solution.py:689
  558.5 23.2 %collective-permute-start.56 = (bf16[528,256]{1,0:T(8,128)(2,1)S(1)}, bf16[528,256]{1,0:T(8,128)(2,1)S(1)}, u32[]{:S(2)}, u32[]{:S(2)}) collective-permute-start(bf16[528,256]{1,0:T(8,128)(2,1)S(1)} %pad_maximum_fusion.8), channel_id=1, source_target_pairs={{0,3},{1,0},{2,1},{3,2},{4,7},{5,4},{6,5},{7,6},{8,11},{9,8},{10,9... | collective-permute-start | bytes 811016 | tf_op jit(solution)/shard_map/ppermute | solution.py:854
  564.5 22.5 %collective-permute-start.57 = (bf16[528,256]{1,0:T(8,128)(2,1)S(1)}, bf16[528,256]{1,0:T(8,128)(2,1)S(1)}, u32[]{:S(2)}, u32[]{:S(2)}) collective-permute-start(bf16[528,256]{1,0:T(8,128)(2,1)S(1)} %pad_maximum_fusion.8), channel_id=1, source_target_pairs={{0,2},{1,3},{2,0},{3,1},{4,6},{5,7},{6,4},{7,5},{8,10},{9,11},{10,... | collective-permute-start | bytes 811016 | tf_op jit(solution)/shard_map/ppermute | solution.py:854
  565.1 21.9 %collective-permute-start.58 = (bf16[528,256]{1,0:T(8,128)(2,1)S(1)}, bf16[528,256]{1,0:T(8,128)(2,1)S(1)}, u32[]{:S(2)}, u32[]{:S(2)}) collective-permute-start(bf16[528,256]{1,0:T(8,128)(2,1)S(1)} %pad_maximum_fusion.8), channel_id=1, source_target_pairs={{0,1},{1,2},{2,3},{3,0},{4,5},{5,6},{6,7},{7,4},{8,9},{9,10},{10,1... | collective-permute-start | bytes 811016 | tf_op jit(solution)/shard_map/ppermute | solution.py:854
  575.9 11.1 %collective-permute-start.55 = (bf16[256,512]{1,0:T(8,128)(2,1)S(1)}, bf16[256,512]{1,0:T(8,128)(2,1)S(1)}, u32[]{:S(2)}, u32[]{:S(2)}) collective-permute-start(bf16[256,512]{1,0:T(8,128)(2,1)S(1)} %dynamic-slice_bitcast_fusion.4), channel_id=1, source_target_pairs={{0,8},{4,12},{8,0},{12,4},{16,24},{20,28},{24,16},{28,20},{1,9},{5... | collective-permute-start | bytes 786440 | tf_op jit(solution)/shard_map/ppermute | solution.py:689
  579.5 8.0 %collective-permute-start.53 = (bf16[256,640]{1,0:T(8,128)(2,1)S(1)}, bf16[256,640]{1,0:T(8,128)(2,1)S(1)}, u32[]{:S(2)}, u32[]{:S(2)}) collective-permute-start(bf16[256,640]{1,0:T(8,128)(2,1)S(1)} %dynamic-slice_bitcast_fusion.3), channel_id=1, source_target_pairs={{0,16},{4,20},{8,24},{12,28},{16,0},{20,4},{24,8},{28,12},{1,17},{... | collective-permute-start | bytes 983048 | tf_op jit(solution)/shard_map/ppermute | solution.py:689
  587.8 73.8 %all-to-all-start.4 = ((bf16[8,256,1024]{2,1,0:T(8,128)(2,1)}), bf16[8,256,1024]{2,1,0:T(8,128)(2,1)}, u32[]{:S(2)}, u32[]{:S(2)}) async-start(bf16[8,256,1024]{2,1,0:T(8,128)(2,1)} %bitcast.366), calls=%async_computation.4 | async-start | bytes 8388608 | tf_op jit(solution)/shard_map/all_to_all | solution.py:848
  (42 other events, 429.7 us)
Sparse Core Ops, SparseCore 0:
  11.1 41.5 all-gather.7
  55.1 113.6 all-gather.9
  312.0 54.2 all-gather.11
  435.8 139.7 reduce-scatter.1

commit v6 on v5

--- a/solution.py
+++ b/solution.py
@@ -198,7 +198,7 @@
     parts_ref[3] = jnp.where(low, zero, kv).astype(bf16)
 
 
-def attn_kernel(q_ref, kv_ref, qpos_ref, kpos_ref, o_ref, parts_ref):
+def attn_kernel(q_ref, kv_ref, qpos_ref, kpos_ref, o_ref, lse_ref, parts_ref):
     @pl.when(pl.program_id(1) == 0)
     def _():
         split_kv(kv_ref, parts_ref)
@@ -206,13 +206,19 @@
     q = q_ref[...]
     allowed = kpos_ref[...] <= qpos_ref[...]
     out = None
+    norms = []
     for g in range(2):
         s = jnp.where(allowed, dot_nt(q, parts_ref[g]), NEG)
-        p = jnp.exp(s - jnp.max(s, axis=1, keepdims=True))
-        p = p * (1.0 / jnp.sum(p, axis=1, keepdims=True))
+        top = jnp.max(s, axis=1, keepdims=True)
+        p = jnp.exp(s - top)
+        total = jnp.sum(p, axis=1, keepdims=True)
+        p = p * (1.0 / total)
+        norms.append(top + jnp.log(total))
         part = dot_nn(p.astype(bf16), parts_ref[2 + g])
         out = part if out is None else out + part
     o_ref[...] = out.astype(bf16)
+    lane = lax.broadcasted_iota(jnp.int32, q.shape, 1)
+    lse_ref[0, 0] = jnp.where(lane == 0, norms[0], norms[1]).T[:8]
 
 
 def attn(q, kv_every, qpos, kpos):
@@ -228,8 +234,14 @@
             pl.BlockSpec((seq_tok, 1), lambda s, p: (0, 0)),
             pl.BlockSpec((1, keys), lambda s, p: (0, 0)),
         ],
-        out_specs=pl.BlockSpec((seq_tok, 128), lambda s, p: (s, p)),
-        out_shape=jax.ShapeDtypeStruct((SEQS * seq_tok, QG), bf16),
+        out_specs=[
+            pl.BlockSpec((seq_tok, 128), lambda s, p: (s, p)),
+            pl.BlockSpec((1, 1, 8, seq_tok), lambda s, p: (s, p, 0, 0)),
+        ],
+        out_shape=[
+            jax.ShapeDtypeStruct((SEQS * seq_tok, QG), bf16),
+            jax.ShapeDtypeStruct((SEQS, pairs, 8, seq_tok), f32),
+        ],
         scratch_shapes=[pltpu.VMEM((4, keys, 2 * HD), bf16)],
         compiler_params=params(),
         cost_estimate=cost(
@@ -240,7 +252,7 @@
 
 
 def attn_back_kernel(
-    pairs, q_ref, do_ref, kv_ref, qpos_ref, kpos_ref, cos_ref, sin_ref, dq_ref, dkv_ref, parts_ref, acc_ref
+    pairs, q_ref, do_ref, o_ref, lse_ref, kv_ref, qpos_ref, kpos_ref, cos_ref, sin_ref, dq_ref, dkv_ref, parts_ref, acc_ref
 ):
     pair = pl.program_id(1)
 
@@ -253,12 +265,12 @@
     do = do_ref[...]
     allowed = kpos_ref[...] <= qpos_ref[...]
     dq = None
+    shares = (do.astype(f32) * o_ref[...].astype(f32)).T
     for g in range(2):
         s = jnp.where(allowed, dot_nt(parts_ref[g], q), NEG)
-        p = jnp.exp(s - jnp.max(s, axis=0, keepdims=True))
-        p = p * (1.0 / jnp.sum(p, axis=0, keepdims=True))
+        p = jnp.exp(s - lse_ref[0, 0, g : g + 1])
         dp = dot_nt(parts_ref[2 + g], do)
-        delta = jnp.sum(p * dp, axis=0, keepdims=True)
+        delta = jnp.sum(shares[g * HD : (g + 1) * HD], axis=0, keepdims=True)
         ds = (p * (dp - delta)).astype(bf16)
         part = dot_tn(ds, parts_ref[g])
         dq = part if dq is None else dq + part
@@ -275,7 +287,7 @@
         dkv_ref[...] = jnp.where(lane < HD, grad_k, grad_v).astype(bf16).reshape(dkv_ref.shape)
 
 
-def attn_back(q, do, kv_every, qpos, kpos, cosine, sine):
+def attn_back(q, do, o, lse, kv_every, qpos, kpos, cosine, sine):
     n_ctx, _, seq_tok, _ = kv_every.shape
     keys = n_ctx * seq_tok
     pairs = QG // 128
@@ -285,6 +297,8 @@
         in_specs=[
             pl.BlockSpec((seq_tok, 128), lambda s, p: (s, p)),
             pl.BlockSpec((seq_tok, 128), lambda s, p: (s, p)),
+            pl.BlockSpec((seq_tok, 128), lambda s, p: (s, p)),
+            pl.BlockSpec((1, 1, 8, seq_tok), lambda s, p: (s, p, 0, 0)),
             pl.BlockSpec((n_ctx, 1, seq_tok, 2 * HD), lambda s, p: (0, s, 0, 0)),
             pl.BlockSpec((1, seq_tok), lambda s, p: (0, 0)),
             pl.BlockSpec((keys, 1), lambda s, p: (0, 0)),
@@ -308,7 +322,7 @@
             20 * SEQS * seq_tok * keys * QG, 8 * SEQS * seq_tok * QG, SEQS * GROUP * seq_tok * keys
         ),
         name="attn_bwd",
-    )(q, do, kv_every, qpos.reshape(1, seq_tok), kpos.reshape(keys, 1), cosine, sine)
+    )(q, do, o, lse, kv_every, qpos.reshape(1, seq_tok), kpos.reshape(keys, 1), cosine, sine)
 
 
 def kv_back_kernel(parts_ref, cos_ref, sin_ref, out_ref):
@@ -593,19 +607,31 @@
         update_piece(factor, BASE, grad, w_ref, m_ref, a_ref, outs, slice(EMB_AT + low, EMB_AT + high))
 
 
-def call_update(kernel, factor, grads, grad_specs, w, m, a, rows, name):
+def call_update(kernel, factor, grads, grad_specs, w, m, a, rows, name, span=None, earlier=()):
     total, width = w.shape
-    block = pl.BlockSpec((rows, width), lambda i: (i, 0))
-    return pl.pallas_call(
-        kernel,
-        grid=(total // rows,),
-        in_specs=[pl.BlockSpec(memory_space=pltpu.SMEM)] + grad_specs + [block] * 3,
+    first, steps = span or (0, total // rows)
+    block = pl.BlockSpec((rows, width), lambda i: (first + i, 0))
+    count = 4 + len(grads)
+    inner = kernel
+    if earlier:
+
+        def inner(*refs):
+            kernel(*refs[:count], *refs[count + len(earlier) :])
+
+    return pl.pallas_call(
+        inner,
+        grid=(steps,),
+        in_specs=[pl.BlockSpec(memory_space=pltpu.SMEM)]
+        + grad_specs
+        + [block] * 3
+        + [pl.BlockSpec(memory_space=pl.ANY)] * len(earlier),
         out_specs=[block] * 4,
         out_shape=[jax.ShapeDtypeStruct(w.shape, f32)] * 3 + [jax.ShapeDtypeStruct(w.shape, bf16)],
-        compiler_params=params(),
-        cost_estimate=cost(10 * total * width, 28 * total * width),
+        input_output_aliases={count + k: k for k in range(len(earlier))},
+        compiler_params=params(),
+        cost_estimate=cost(10 * steps * rows * width, 28 * steps * rows * width),
         name=name,
-    )(factor.reshape(1, 1), *grads, w, m, a)
+    )(factor.reshape(1, 1), *grads, w, m, a, *earlier)
 
 
 def norm_parts(x):
@@ -734,7 +760,7 @@
     if corners:
         kv_every, low, high = lax.optimization_barrier((kv_every, low, high))
         y_low, x_high, x_low, y_high = swap(low, 4), swap(high, 2), swap(low, 2), swap(high, 4)
-    attn_b = attn(q, kv_every, qpos, kpos)
+    attn_b, attn_lse = attn(q, kv_every, qpos, kpos)
     x1 = x0 + sum_own(dot_nt(attn_b, w_out))
 
     unit1, scale1 = norm_parts(x1)
@@ -802,9 +828,12 @@
     dx1 = dx2 + dx1_norm
     d_head = dot_tn(final_all, dlog_all)
     head_sq = jnp.sum(d_head * d_head)
-    dya_b, d_head = lax.optimization_barrier((spread_all(dx1), d_head.astype(bf16)))
+    d_head = d_head.astype(bf16).reshape(n_ctx, rows, part)
+    dya_b, d_head_a, d_head_b = lax.optimization_barrier(
+        (spread_all(dx1), d_head[:, : rows // 2], d_head[:, rows // 2 :])
+    )
     d_attn_b = dot_nn(dya_b, w_out).astype(bf16)
-    d_q, d_kv = attn_back(q, d_attn_b, kv_every, qpos, kpos, cosine, sine)
+    d_q, d_kv = attn_back(q, d_attn_b, attn_b, attn_lse, kv_every, qpos, kpos, cosine, sine)
     d_out = dot_tn(dya_b, attn_b).astype(bf16)
     d_kv = lax.all_to_all(d_kv.reshape(n_ctx, tok, 2 * HD), "ctx", 0, 0, tiled=True)
     if corners:
@@ -838,14 +867,14 @@
         d_in, d_out = total(in_kept, in_sent).astype(bf16), total(out_kept, out_sent).astype(bf16)
         in_kept, in_sent = split(d_in, along_y, 0, 4)
         out_kept, out_sent = split(d_out, along_x, 0, 2)
-        d_head, in_sent, out_sent = lax.optimization_barrier((d_head, in_sent, out_sent))
+        d_head_a, in_sent, out_sent = lax.optimization_barrier((d_head_a, in_sent, out_sent))
         g_in, g_out = total(in_kept, in_sent), total(out_kept, out_sent)
     else:
-        moved, d_head, d_in, d_out, g_ff = lax.optimization_barrier((moved, d_head, d_in, d_out, g_ff))
+        moved, d_head_a, d_in, d_out, g_ff = lax.optimization_barrier((moved, d_head_a, d_in, d_out, g_ff))
         g_in, g_out = (
             lax.psum_scatter(x, "ctx", scatter_dimension=0, tiled=True).astype(f32) for x in (d_in, d_out)
         )
-    g_head = lax.all_to_all(d_head.reshape(n_ctx, rows, part), "ctx", 0, 0, tiled=True)
+    g_head_a = lax.all_to_all(d_head_a, "ctx", 0, 0, tiled=True)
     moved = moved.reshape(n_ctx, own + 16, rows)
     gain_part = jnp.sum(moved[:, own:].astype(f32), axis=0).astype(bf16)
     moved = jnp.concatenate([moved[:, :own].reshape(n_ctx * own, rows), gain_part])
@@ -878,6 +907,8 @@
         squares = level[0]
     lane = lax.broadcasted_iota(jnp.int32, (8, 128), 1)
     totals = jnp.sum(lax.all_gather(jnp.where(lane == 0, squares, loss_part), "ctx"), axis=0)
+    totals, d_head_b = lax.optimization_barrier((totals, d_head_b))
+    g_head_b = lax.all_to_all(d_head_b, "ctx", 0, 0, tiled=True)
     loss = totals[0, 1]
     grad_norm = jnp.sqrt(totals[0, 0])
     factor = jnp.minimum(1.0, clip_level / grad_norm)
@@ -904,21 +935,26 @@
         wide,
         "layer_update",
     )
-    g_head, *layer = lax.optimization_barrier((g_head, *layer))
-    vocab = call_update(
-        functools.partial(vocab_update_kernel, part),
-        factor,
-        (g_head, g_embed),
-        [
-            pl.BlockSpec((n_ctx, wide // 2, part), lambda i: (0, i, 0)),
-            pl.BlockSpec((wide // 2, EMB_W), lambda i: (i, 0)),
-        ],
-        w_vocab,
-        mom_vocab,
-        avg_vocab,
-        wide // 2,
-        "vocab_update",
-    )
+    g_head_a, *layer = lax.optimization_barrier((g_head_a, *layer))
+    vocab = []
+    steps = rows // 2 // (wide // 2)
+    for first, g_head in ((0, g_head_a), (steps, g_head_b)):
+        vocab = call_update(
+            functools.partial(vocab_update_kernel, part),
+            factor,
+            (g_head, g_embed),
+            [
+                pl.BlockSpec((n_ctx, wide // 2, part), lambda i: (0, i, 0)),
+                pl.BlockSpec((wide // 2, EMB_W), lambda i, first=first: (first + i, 0)),
+            ],
+            w_vocab,
+            mom_vocab,
+            avg_vocab,
+            wide // 2,
+            "vocab_update",
+            (first, steps),
+            vocab,
+        )
     grad = factor * grad_gain
     gains_moment = momentum_rate * mom_gains + grad
     gains_new = gains - BASE * 0.1 * (grad + momentum_rate * gains_moment)

time: 720 us -> 718 us (level)
  starting transfers between devices: 130 us -> 110 us
  waiting for transfers between devices: 205 us -> 224 us
    ppermute x15, starting transfers between devices: 52.5 us -> 27.1 us  [head_gather(): lax.ppermute(x, 'head', [(i, (i - s) % n_head) for i in range(n_head)])]
    ppermute x18, waiting for transfers between devices: 69.3 us -> 87.7 us  [head_scatter(): lax.ppermute(x[:, s], 'head', [(i, (i + s) % n_head) for i in range(n_hea...]
    pallas_call x2 -> x3, Pallas kernels: 54.1 us -> 54.5 us  [call_update(): pl.pallas_call(inner, grid=(steps,), in_specs=[pl.BlockSpec(memory_space=...]
  transfers between devices with their start and end apart: 71 -> 72, of which waited for: 38 -> 41; matrix products, arithmetic and copies ran while one was open for 16% -> 17% of each run, Pallas kernels for 19% -> 21%
where the time goes in v6:
time: 718 us; the launch traced here: 707 us
  waiting for transfers between devices  224 us (31%)
  Pallas kernels  184 us (26%)
  starting transfers between devices  110 us (15%)
  matrix products  51.9 us (7%)
  other arithmetic  46.4 us (6%)
  local copies, waits for them, and re-layouts  34.9 us (5%)
  blocking collectives  33.9 us (5%)
  between operations  21.7 us (3%)
    ppermute x18, waiting for transfers between devices, head_scatter(): lax.ppermute(x[:, s], 'head', [(i, (i + s) % n_head) for i in range(n_hea...  87.7 us
    ppermute x15, waiting for transfers between devices, head_gather(): lax.ppermute(x, 'head', [(i, (i - s) % n_head) for i in range(n_head)])  60 us
    pallas_call x3, Pallas kernels, call_update(): pl.pallas_call(inner, grid=(steps,), in_specs=[pl.BlockSpec(memory_space=...  54.5 us
    ppermute x18, starting transfers between devices, head_scatter(): lax.ppermute(x[:, s], 'head', [(i, (i + s) % n_head) for i in range(n_hea...  32.1 us
    ppermute x20, waiting for transfers between devices, swap(): return lax.ppermute(x, 'ctx', [(i, i ^ bit) for i in range(n_ctx)])  31.9 us
    ppermute x15, starting transfers between devices, head_gather(): lax.ppermute(x, 'head', [(i, (i - s) % n_head) for i in range(n_head)])  27.1 us
    pallas_call x1, Pallas kernels, head_dlogits(): pl.pallas_call(functools.partial(dlogits_kernel, steps, len(pieces) // at...  22.8 us
    dot_general x4, matrix products, dot_nt(): lax.dot_general(a, b, (((1,), (1,)), ((), ())), preferred_element_type=f32)  18.7 us
  transfers between devices with their start and end apart: 72, of which 41 were waited for; matrix products, arithmetic and copies ran while one was open for 17% of the time, Pallas kernels for 21%

profile of v6, /device:TPU:0, one launch (start us, length us, event | category | flops | bytes accessed | tf_op | source)
XLA Modules:
  0.0 707.1 jit_solution(14127625687393827120)
XLA Ops:
  13.2 10.6 %all-gather.3 = f32[8,1,1280]{2,1,0:T(1,128)S(1)} all-gather(f32[1,1,1280]{2,1,0:T(1,128)S(1)} %reshape.829), channel_id=2, replica_groups=mesh['ctx'=8,'head'=4] {'ctx'}, dimensions={0}, use_global_device_ids=true | all-gather | bytes 46080 | tf_op jit(solution)/shard_map/all_gather | solution.py:719
  25.9 13.3 %embed_lookup.1 = bf16[2048,256]{1,0:T(8,128)(2,1)} custom-call(s32[2048,1]{1,0:T(8,128)} %copy.264.ids_ref, f32[256,16000]{1,0:T(8,128)} %refs_3_.3), custom_call_target="tpu_custom_call" | custom-call | flops 8455716864 | bytes 8257536 | tf_op jit(solution)/shard_map/embed_lookup/pallas_call | solution.py:88
  45.7 7.8 %head_cast.1 = (bf16[128,8192]{1,0:T(8,128)(2,1)}, bf16[128,8192]{1,0:T(8,128)(2,1)}) custom-call(f32[256,16000]{1,0:T(8,128)} %refs_3_.3), custom_call_target="tpu_custom_call" | custom-call | flops 2097152 | bytes 12582912 | tf_op jit(solution)/shard_map/head_cast/pallas_call | solution.py:356
  58.0 10.6 %collective-permute-done.1 = bf16[16,32,256]{2,1,0:T(8,128)(2,1)S(1)} collective-permute-done((bf16[16,32,256]{2,1,0:T(8,128)(2,1)S(1)}, bf16[16,32,256]{2,1,0:T(8,128)(2,1)S(1)}, u32[]{:S(2)}, u32[]{:S(2)}) %collective-permute-start.1) | collective-permute-done | bytes 262176 | tf_op jit(solution)/shard_map/ppermute | solution.py:689
  70.4 3.4 all-to-all-start
  75.1 8.8 %all-to-all-done = bf16[8,64,256]{2,1,0:T(8,128)(2,1)S(1)} async-done(((bf16[8,64,256]{2,1,0:T(8,128)(2,1)}), bf16[8,64,256]{2,1,0:T(8,128)(2,1)S(1)}, u32[]{:S(2)}, u32[]{:S(2)}) %all-to-all-start) | async-done | bytes 262176 | tf_op jit(solution)/shard_map/all_to_all | solution.py:733
  91.5 6.0 collective-permute-done.5
  97.5 7.6 %collective-permute-done.4 = bf16[2,32,2048]{2,1,0:T(8,128)(2,1)S(1)} collective-permute-done((bf16[2,32,2048]{2,1,0:T(8,128)(2,1)S(1)}, bf16[2,32,2048]{2,1,0:T(8,128)(2,1)S(1)}, u32[]{:S(2)}, u32[]{:S(2)}) %collective-permute-start.4) | collective-permute-done | bytes 262176 | tf_op jit(solution)/shard_map/ppermute | solution.py:696
  107.7 3.9 qkv.1
  111.6 13.7 %all-gather.1 = bf16[2048,128]{1,0:T(8,128)(2,1)} all-gather(bf16[256,128]{1,0:T(8,128)(2,1)} %get-tuple-element.86), channel_id=3, replica_groups=mesh['ctx'=8,'head'=4] {'ctx'}, dimensions={0}, use_global_device_ids=true | all-gather | bytes 589824 | tf_op jit(solution)/shard_map/all_gather | solution.py:759
  127.4 9.0 %attn_fwd.1 = (bf16[256,512]{1,0:T(8,128)(2,1)}, f32[2,4,8,128]{3,2,1,0:T(8,128)}) custom-call(bf16[256,512]{1,0:T(8,128)(2,1)} %get-tuple-element.85.q_ref, bf16[8,2,128,128]{3,2,1,0:T(8,128)(2,1)} %bitcast.406, s32[128,1]{1,0:T(8,128)} %fusion.56.qpos_ref, s32[1,1024]{1,0:T(1,128)} %bitcast.448), custom_call_target="tpu_custom_call" | custom-call | flops 1073741824 | bytes 524288 | tf_op jit(solution)/shard_map/attn_fwd/pallas_call | solution.py:228
  139.0 5.3 collective-permute-start.8
  146.7 4.3 collective-permute-done.8
  151.0 10.1 %collective-permute-done.9 = bf16[2,32,2048]{2,1,0:T(8,128)(2,1)S(1)} collective-permute-done((bf16[2,32,2048]{2,1,0:T(8,128)(2,1)S(1)}, bf16[2,32,2048]{2,1,0:T(8,128)(2,1)S(1)}, u32[]{:S(2)}, u32[]{:S(2)}) %collective-permute-start.9) | collective-permute-done | bytes 262176 | tf_op jit(solution)/shard_map/ppermute | solution.py:689
  162.2 5.1 collective-permute-start.12
  167.3 3.7 collective-permute-start.11
  172.1 8.0 %collective-permute-done.12 = bf16[2,32,2048]{2,1,0:T(8,128)(2,1)S(1)} collective-permute-done((bf16[2,32,2048]{2,1,0:T(8,128)(2,1)S(1)}, bf16[2,32,2048]{2,1,0:T(8,128)(2,1)S(1)}, u32[]{:S(2)}, u32[]{:S(2)}) %collective-permute-start.12) | collective-permute-done | bytes 262176 | tf_op jit(solution)/shard_map/ppermute | solution.py:696
  182.1 6.3 collective-permute-done.13
  188.6 5.9 collective-permute-done.14.refs_6_
  194.7 6.3 fusion.2
  201.4 5.3 fusion.17
  211.4 6.5 collective-permute-done.16
  217.9 3.7 collective-permute-done.18
  223.0 10.4 %collective-permute-done.17 = bf16[2,32,2048]{2,1,0:T(8,128)(2,1)S(1)} collective-permute-done((bf16[2,32,2048]{2,1,0:T(8,128)(2,1)S(1)}, bf16[2,32,2048]{2,1,0:T(8,128)(2,1)S(1)}, u32[]{:S(2)}, u32[]{:S(2)}) %collective-permute-start.17) | collective-permute-done | bytes 262176 | tf_op jit(solution)/shard_map/ppermute | solution.py:689
  235.1 4.5 collective-permute-done.19.refs_4_
  243.9 7.2 %collective-permute-done.23 = bf16[2,32,2048]{2,1,0:T(8,128)(2,1)S(1)} collective-permute-done((bf16[2,32,2048]{2,1,0:T(8,128)(2,1)S(1)}, bf16[2,32,2048]{2,1,0:T(8,128)(2,1)S(1)}, u32[]{:S(2)}, u32[]{:S(2)}) %collective-permute-start.23) | collective-permute-done | bytes 262176 | tf_op jit(solution)/shard_map/ppermute | solution.py:696
  252.3 8.9 %collective-permute-done.22 = bf16[2,32,2048]{2,1,0:T(8,128)(2,1)} collective-permute-done((bf16[2,32,2048]{2,1,0:T(8,128)(2,1)S(1)}, bf16[2,32,2048]{2,1,0:T(8,128)(2,1)}, u32[]{:S(2)}, u32[]{:S(2)}) %collective-permute-start.22) | collective-permute-done | bytes 262176 | tf_op jit(solution)/shard_map/ppermute | solution.py:696
  261.2 4.2 collective-permute-done.21
  267.6 13.6 %head_partial.1.refs_0_ = f32[256,8192]{1,0:T(8,128)} custom-call(s32[4]{0:T(128)} %pad_add_fusion.1.at_ref, bf16[256,2048]{1,0:T(8,128)(2,1)} %bitcast.352, bf16[128,8192]{1,0:T(8,128)(2,1)} %get-tuple-element.91.refs_0_, bf16[128,8192]{1,0:T(8,128)(2,1)} %get-tuple-element.92.refs_1_, bf16[128,8192]{1,0:T(8,128)(2,1)} %copy-done.2, ...), custom_call_target="tpu_custom_call" | custom-call | flops 4294967296 | bytes 25165824 | tf_op jit(solution)/shard_map/head_partial/pallas_call | solution.py:389
  281.2 3.1 collective-permute-done.25.refs_6_.refs_13_
  288.8 3.0 collective-permute-done.30.refs_7_.refs_14_
  294.8 17.0 %head_logits.1 = (f32[256,8192]{1,0:T(8,128)}, f32[8,256]{1,0:T(8,128)}) custom-call(s32[4]{0:T(128)} %pad_add_fusion.at_ref, bf16[256,2048]{1,0:T(8,128)(2,1)} %bitcast.353, s32[256,1]{1,0:T(8,128)} %and_select_fusion.slot_ref, f32[256,8192]{1,0:T(8,128)} %head_partial.1.refs_0_, bf16[128,8192]{1,0:T(8,128)(2,1)} %collective-permute-done.26.refs_1_.refs_8_, ...), custom_call_target="tpu_custom_call" | custom-call | flops 4294967296 | bytes 33554432 | tf_op jit(solution)/shard_map/head_logits/pallas_call | solution.py:446
  323.7 22.8 %head_dlogits.1 = (bf16[8,256,1024]{2,1,0:T(8,128)(2,1)}, bf16[256,2048]{1,0:T(8,128)(2,1)}) custom-call(s32[8]{0:T(128)} %stack.163.at_ref, f32[256,8192]{1,0:T(8,128)} %get-tuple-element.104.logits_ref, f32[256,8]{1,0:T(8,128)} %bitcast.405, s32[256,1]{1,0:T(8,128)} %and_select_fusion.slot_ref, bf16[128,8192]{1,0:T(8,128)(2,1)} %get-tuple-element.91.refs_0_, ...), custom_call_target="tpu_custom_call" | custom-call | flops 8589934592 | bytes 46137344 | tf_op jit(solution)/shard_map/head_dlogits/pallas_call | solution.py:504
  347.8 3.8 collective-permute-start.37
  351.8 6.9 collective-permute-done.35
  359.8 12.1 %collective-permute-done.36 = bf16[2,32,2048]{2,1,0:T(8,128)(2,1)S(1)} collective-permute-done((bf16[2,32,2048]{2,1,0:T(8,128)(2,1)S(1)}, bf16[2,32,2048]{2,1,0:T(8,128)(2,1)S(1)}, u32[]{:S(2)}, u32[]{:S(2)}) %collective-permute-start.36) | collective-permute-done | bytes 262176 | tf_op jit(solution)/shard_map/ppermute | solution.py:689
  377.3 4.6 all-to-all-start.1
  384.5 9.4 %collective-permute-done.39 = bf16[2,32,2048]{2,1,0:T(8,128)(2,1)S(1)} collective-permute-done((bf16[2,32,2048]{2,1,0:T(8,128)(2,1)S(1)}, bf16[2,32,2048]{2,1,0:T(8,128)(2,1)S(1)}, u32[]{:S(2)}, u32[]{:S(2)}) %collective-permute-start.39) | collective-permute-done | bytes 262176 | tf_op jit(solution)/shard_map/ppermute | solution.py:696
  395.7 5.9 fusion.47
  401.8 8.0 %fusion.11 = bf16[256,2048]{1,0:T(8,128)(2,1)S(1)} fusion(bf16[256,2816]{1,0:T(8,128)(2,1)S(1)} %add_convert_fusion.da_ref, bf16[2048,4224]{1,0:T(8,128)(2,1)} %all-gather.10.cloned.1.call-done), kind=kOutput, calls=%fused_computation.17 | convolution fusion | flops 2953314304 | bytes 14024704 | tf_op jit(solution)/shard_map/dot_general | solution.py:48
  410.6 5.3 collective-permute-start.41
  417.3 15.1 %ff_weight_grad.1 = bf16[2048,4224]{1,0:T(8,128)(2,1)} custom-call(bf16[256,2048]{1,0:T(8,128)(2,1)} %bitcast.369, bf16[256,2816]{1,0:T(8,128)(2,1)} %copy-done.7, bf16[256,2048]{1,0:T(8,128)(2,1)} %bitcast.371, bf16[256,1408]{1,0:T(8,128)(2,1)} %copy-done.12), custom_call_target="tpu_custom_call" | custom-call | flops 4429185024 | bytes 19398656 | tf_op jit(solution)/shard_map/ff_weight_grad/pallas_call | solution.py:545
  433.2 3.7 collective-permute-done.42
  443.8 3.5 collective-permute-start.45
  447.4 16.2 %multiply_reduce_fusion = (f32[]{:T(128)}, bf16[2048,1024]{1,0:T(8,128)(2,1)S(1)}) fusion(bf16[2048,2048]{1,0:T(8,128)(2,1)} %all-gather.12.cloned.1.call-done, bf16[2048,1024]{1,0:T(8,128)(2,1)} %bitcast.85), kind=kOutput, calls=%fused_computation.4 | convolution fusion | flops 8596226048 | bytes 16777220 | tf_op jit(solution)/shard_map/dot_general | solution.py:52
  466.6 3.1 fusion.28.do_ref
  469.7 12.0 %attn_bwd.1 = (bf16[256,512]{1,0:T(8,128)(2,1)}, bf16[8,2,128,128]{3,2,1,0:T(8,128)(2,1)}) custom-call(bf16[256,512]{1,0:T(8,128)(2,1)} %get-tuple-element.85.q_ref, bf16[256,512]{1,0:T(8,128)(2,1)} %fusion.28.do_ref, bf16[256,512]{1,0:T(8,128)(2,1)} %get-tuple-element.90.o_ref, f32[2,4,8,128]{3,2,1,0:T(8,128)} %get-tuple-element.115.lse_ref, ...), custom_call_target="tpu_custom_call" | custom-call | flops 2684354560 | bytes 1048576 | tf_op jit(solution)/shard_map/attn_bwd/pallas_call | solution.py:294
  481.7 4.2 all-to-all-start.2
  487.2 14.4 %all-to-all-done.2.parts_ref = bf16[8,256,128]{2,1,0:T(8,128)(2,1)} async-done(((bf16[8,256,128]{2,1,0:T(8,128)(2,1)}), bf16[8,256,128]{2,1,0:T(8,128)(2,1)}, u32[]{:S(2)}, u32[]{:S(2)}) %all-to-all-start.2) | async-done | bytes 524320 | tf_op jit(solution)/shard_map/all_to_all | solution.py:838
  512.0 5.7 collective-permute-done.47
  520.6 9.7 %collective-permute-done.48 = bf16[2,32,2048]{2,1,0:T(8,128)(2,1)S(1)} collective-permute-done((bf16[2,32,2048]{2,1,0:T(8,128)(2,1)S(1)}, bf16[2,32,2048]{2,1,0:T(8,128)(2,1)S(1)}, u32[]{:S(2)}, u32[]{:S(2)}) %collective-permute-start.48) | collective-permute-done | bytes 262176 | tf_op jit(solution)/shard_map/ppermute | solution.py:689
  533.5 4.3 all-to-all-start.3
  540.5 8.7 %all-to-all-done.3 = bf16[80,8,256]{2,0,1:T(8,128)(2,1)} async-done(((bf16[80,8,256]{2,0,1:T(8,128)(2,1)}), bf16[80,8,256]{2,0,1:T(8,128)(2,1)}, u32[]{:S(2)}, u32[]{:S(2)}) %all-to-all-start.3) | async-done | bytes 327712 | tf_op jit(solution)/shard_map/all_to_all | solution.py:861
  562.4 7.4 %collective-permute-done.57 = bf16[528,256]{1,0:T(8,128)(2,1)S(1)} collective-permute-done((bf16[528,256]{1,0:T(8,128)(2,1)S(1)}, bf16[528,256]{1,0:T(8,128)(2,1)S(1)}, u32[]{:S(2)}, u32[]{:S(2)}) %collective-permute-start.57) | collective-permute-done | bytes 270368 | tf_op jit(solution)/shard_map/ppermute | solution.py:883
  572.5 5.5 collective-permute-done.54
  586.6 4.2 collective-permute-done.53
  591.5 3.6 all-to-all-start.4
  595.1 12.7 %embed_grad.1 = (bf16[256,8064]{1,0:T(8,128)(2,1)}, f32[8,128]{1,0:T(8,128)}) custom-call(s32[2048,1]{1,0:T(8,128)} %copy.264.ids_ref, bf16[256,2048]{1,0:T(8,128)(2,1)} %bitcast.380), custom_call_target="tpu_custom_call" | custom-call | flops 8455716864 | bytes 4128768 | tf_op jit(solution)/shard_map/embed_grad/pallas_call | solution.py:125
  613.1 3.3 multiply_reduce_fusion.1
  626.7 9.5 %all-gather.2 = f32[64,128]{1,0:T(8,128)S(1)} all-gather(f32[8,128]{1,0:T(8,128)S(1)} %add_select_fusion.3), channel_id=4, replica_groups=mesh['ctx'=8,'head'=4] {'ctx'}, dimensions={0}, use_global_device_ids=true | all-gather | bytes 36864 | tf_op jit(solution)/shard_map/all_gather | solution.py:909
  637.5 4.3 all-to-all-start.5
  643.2 15.0 %layer_update.1 = (f32[256,5376]{1,0:T(8,128)}, f32[256,5376]{1,0:T(8,128)}, f32[256,5376]{1,0:T(8,128)}, bf16[256,5376]{1,0:T(8,128)(2,1)}) custom-call(f32[1,1]{1,0:T(1,128)} %bitcast.136.factor_ref.refs_0_, bf16[256,4224]{1,0:T(8,128)(2,1)} %reduce-scatter.2.cloned.1.call-done.refs_0_, f32[256,640]{1,0:T(8,128)} %get-tuple-element.165.refs_1_, ...), custom_call_target="tpu_custom_call" | custom-call | flops 13762560 | bytes 38535168 | tf_op jit(solution)/shard_map/layer_update/pallas_call | solution.py:621
  658.2 19.8 %vocab_update.2 = (f32[256,16000]{1,0:T(8,128)}, f32[256,16000]{1,0:T(8,128)}, f32[256,16000]{1,0:T(8,128)}, bf16[256,16000]{1,0:T(8,128)(2,1)}) custom-call(f32[1,1]{1,0:T(1,128)} %bitcast.136.factor_ref.refs_0_, bf16[8,128,1024]{2,1,0:T(8,128)(2,1)} %copy-done.4, bf16[256,8064]{1,0:T(8,128)(2,1)} %get-tuple-element.140.embed_ref.refs_2_, ...), custom_call_target="tpu_custom_call" | custom-call | flops 20480000 | bytes 57344000 | tf_op jit(solution)/shard_map/vocab_update/pallas_call | solution.py:621
  679.2 19.8 %vocab_update.3 = (f32[256,16000]{1,0:T(8,128)}, f32[256,16000]{1,0:T(8,128)}, f32[256,16000]{1,0:T(8,128)}, bf16[256,16000]{1,0:T(8,128)(2,1)}) custom-call(f32[1,1]{1,0:T(1,128)} %bitcast.136.factor_ref.refs_0_, bf16[8,128,1024]{2,1,0:T(8,128)(2,1)} %all-to-all-done.5.refs_1_, ...), custom_call_target="tpu_custom_call", output_to_operand_aliasing={{0}: (6, {}), {1}: (7, {}), {2}: (8, {}), {3}: (9, {})} | custom-call | flops 20480000 | bytes 57344000 | tf_op jit(solution)/shard_map/vocab_update/pallas_call | solution.py:621
  (354 shorter events, 163.7 us)
Async XLA Ops:
  7.2 99.2 %all-gather.8.cloned.1.call-start = ((), (), s32[]{:S(2)}) async-start(), calls=%async_computation.7 | async-start | bytes 5308416 | tf_op jit(solution)/shard_map/all_gather | solution.py:708
  10.9 183.7 %all-gather.10.cloned.1.call-start = ((), (), s32[]{:S(2)}) async-start(), calls=%async_computation.8 | async-start | bytes 19464192 | tf_op jit(solution)/shard_map/all_gather | solution.py:709
  41.1 16.9 %collective-permute-start = (bf16[16,32,256]{2,1,0:T(8,128)(2,1)}, bf16[16,32,256]{2,1,0:T(8,128)(2,1)S(1)}, u32[]{:S(2)}, u32[]{:S(2)}) collective-permute-start(bf16[16,32,256]{2,1,0:T(8,128)(2,1)} %get-tuple-element.199), channel_id=1, source_target_pairs={{0,1},{1,2},{2,3},{3,0},{4,5},{5,6},{6,7},{7,4},{8,9},{9,10},{10,1... | collective-permute-start | bytes 786440 | tf_op jit(solution)/shard_map/ppermute | solution.py:689
  42.6 15.3 %collective-permute-start.2 = (bf16[16,32,256]{2,1,0:T(8,128)(2,1)S(1)}, bf16[16,32,256]{2,1,0:T(8,128)(2,1)S(1)}, u32[]{:S(2)}, u32[]{:S(2)}) collective-permute-start(bf16[16,32,256]{2,1,0:T(8,128)(2,1)S(1)} %get-tuple-element.200), channel_id=1, source_target_pairs={{0,3},{1,0},{2,1},{3,2},{4,7},{5,4},{6,5},{7,6},{8,11},{9,8},{10,9... | collective-permute-start | bytes 786440 | tf_op jit(solution)/shard_map/ppermute | solution.py:689
  44.9 23.7 %collective-permute-start.1 = (bf16[16,32,256]{2,1,0:T(8,128)(2,1)S(1)}, bf16[16,32,256]{2,1,0:T(8,128)(2,1)S(1)}, u32[]{:S(2)}, u32[]{:S(2)}) collective-permute-start(bf16[16,32,256]{2,1,0:T(8,128)(2,1)S(1)} %get-tuple-element.201), channel_id=1, source_target_pairs={{0,2},{1,3},{2,0},{3,1},{4,6},{5,7},{6,4},{7,5},{8,10},{9,11},{10,... | collective-permute-start | bytes 786440 | tf_op jit(solution)/shard_map/ppermute | solution.py:689
  53.5 52.9 %collective-permute-start.6 = (bf16[128,8192]{1,0:T(8,128)(2,1)}, bf16[128,8192]{1,0:T(8,128)(2,1)S(1)}, u32[]{:S(2)}, u32[]{:S(2)}) collective-permute-start(bf16[128,8192]{1,0:T(8,128)(2,1)} %get-tuple-element.91.refs_0_), channel_id=1, source_target_pairs={{0,4},{4,0},{8,12},{12,8},{16,20},{20,16},{24,28},{28,24},{1,5},{5... | collective-permute-start | bytes 6291464 | tf_op jit(solution)/shard_map/ppermute | solution.py:715
  53.5 52.9 %collective-permute-start.7 = (bf16[128,8192]{1,0:T(8,128)(2,1)}, bf16[128,8192]{1,0:T(8,128)(2,1)}, u32[]{:S(2)}, u32[]{:S(2)}) collective-permute-start(bf16[128,8192]{1,0:T(8,128)(2,1)} %get-tuple-element.92.refs_1_), channel_id=1, source_target_pairs={{0,4},{4,0},{8,12},{12,8},{16,20},{20,16},{24,28},{28,24},{1,5},{5... | collective-permute-start | bytes 6291464 | tf_op jit(solution)/shard_map/ppermute | solution.py:715
  70.4 13.5 %all-to-all-start = ((bf16[8,64,256]{2,1,0:T(8,128)(2,1)}), bf16[8,64,256]{2,1,0:T(8,128)(2,1)S(1)}, u32[]{:S(2)}, u32[]{:S(2)}) async-start(bf16[8,64,256]{2,1,0:T(8,128)(2,1)} %bitcast.8), calls=%async_computation | async-start | bytes 524288 | tf_op jit(solution)/shard_map/all_to_all | solution.py:733
  73.8 364.2 %all-gather.12.cloned.1.call-start = ((), (), s32[]{:S(2)}) async-start(), calls=%async_computation.9 | async-start | bytes 9437184 | tf_op jit(solution)/shard_map/all_gather | solution.py:816
  86.4 11.1 %collective-permute-start.5 = (bf16[2,32,2048]{2,1,0:T(8,128)(2,1)S(1)}, bf16[2,32,2048]{2,1,0:T(8,128)(2,1)S(1)}, u32[]{:S(2)}, u32[]{:S(2)}) collective-permute-start(bf16[2,32,2048]{2,1,0:T(8,128)(2,1)S(1)} %multiply_convert_fusion.3), channel_id=1, source_target_pairs={{0,1},{1,2},{2,3},{3,0},{4,5},{5,6},{6,7},{7,4},{8,9},{9,10},{10,1... | collective-permute-start | bytes 786440 | tf_op jit(solution)/shard_map/ppermute | solution.py:696
  86.5 18.6 %collective-permute-start.4 = (bf16[2,32,2048]{2,1,0:T(8,128)(2,1)S(1)}, bf16[2,32,2048]{2,1,0:T(8,128)(2,1)S(1)}, u32[]{:S(2)}, u32[]{:S(2)}) collective-permute-start(bf16[2,32,2048]{2,1,0:T(8,128)(2,1)S(1)} %multiply_convert_fusion.3), channel_id=1, source_target_pairs={{0,2},{1,3},{2,0},{3,1},{4,6},{5,7},{6,4},{7,5},{8,10},{9,11},{10,... | collective-permute-start | bytes 786440 | tf_op jit(solution)/shard_map/ppermute | solution.py:696
  88.7 16.4 %collective-permute-start.3 = (bf16[2,32,2048]{2,1,0:T(8,128)(2,1)S(1)}, bf16[2,32,2048]{2,1,0:T(8,128)(2,1)S(1)}, u32[]{:S(2)}, u32[]{:S(2)}) collective-permute-start(bf16[2,32,2048]{2,1,0:T(8,128)(2,1)S(1)} %multiply_convert_fusion.3), channel_id=1, source_target_pairs={{0,3},{1,0},{2,1},{3,2},{4,7},{5,4},{6,5},{7,6},{8,11},{9,8},{10,9... | collective-permute-start | bytes 786440 | tf_op jit(solution)/shard_map/ppermute | solution.py:696
  125.4 69.2 %collective-permute-start.14 = (bf16[128,8192]{1,0:T(8,128)(2,1)S(1)}, bf16[128,8192]{1,0:T(8,128)(2,1)}, u32[]{:S(2)}, u32[]{:S(2)}) collective-permute-start(bf16[128,8192]{1,0:T(8,128)(2,1)S(1)} %copy-done.1), channel_id=1, source_target_pairs={{0,16},{4,20},{8,24},{12,28},{16,0},{20,4},{24,8},{28,12},{1,17},{... | collective-permute-start | bytes 6291464 | tf_op jit(solution)/shard_map/ppermute | solution.py:715
  126.2 68.5 %collective-permute-start.15 = (bf16[128,8192]{1,0:T(8,128)(2,1)}, bf16[128,8192]{1,0:T(8,128)(2,1)}, u32[]{:S(2)}, u32[]{:S(2)}) collective-permute-start(bf16[128,8192]{1,0:T(8,128)(2,1)} %get-tuple-element.92.refs_1_), channel_id=1, source_target_pairs={{0,8},{4,12},{8,0},{12,4},{16,24},{20,28},{24,16},{28,20},{1,9},{5... | collective-permute-start | bytes 6291464 | tf_op jit(solution)/shard_map/ppermute | solution.py:715
  139.0 12.0 %collective-permute-start.8 = (bf16[2,32,2048]{2,1,0:T(8,128)(2,1)S(1)}, bf16[2,32,2048]{2,1,0:T(8,128)(2,1)S(1)}, u32[]{:S(2)}, u32[]{:S(2)}) collective-permute-start(bf16[2,32,2048]{2,1,0:T(8,128)(2,1)S(1)} %get-tuple-element.196), channel_id=1, source_target_pairs={{0,1},{1,2},{2,3},{3,0},{4,5},{5,6},{6,7},{7,4},{8,9},{9,10},{10,1... | collective-permute-start | bytes 786440 | tf_op jit(solution)/shard_map/ppermute | solution.py:689
  144.3 16.8 %collective-permute-start.9 = (bf16[2,32,2048]{2,1,0:T(8,128)(2,1)S(1)}, bf16[2,32,2048]{2,1,0:T(8,128)(2,1)S(1)}, u32[]{:S(2)}, u32[]{:S(2)}) collective-permute-start(bf16[2,32,2048]{2,1,0:T(8,128)(2,1)S(1)} %get-tuple-element.197), channel_id=1, source_target_pairs={{0,2},{1,3},{2,0},{3,1},{4,6},{5,7},{6,4},{7,5},{8,10},{9,11},{10,... | collective-permute-start | bytes 786440 | tf_op jit(solution)/shard_map/ppermute | solution.py:689
  144.3 16.9 %collective-permute-start.10 = (bf16[2,32,2048]{2,1,0:T(8,128)(2,1)S(1)}, bf16[2,32,2048]{2,1,0:T(8,128)(2,1)S(1)}, u32[]{:S(2)}, u32[]{:S(2)}) collective-permute-start(bf16[2,32,2048]{2,1,0:T(8,128)(2,1)S(1)} %get-tuple-element.198), channel_id=1, source_target_pairs={{0,3},{1,0},{2,1},{3,2},{4,7},{5,4},{6,5},{7,6},{8,11},{9,8},{10,9... | collective-permute-start | bytes 786440 | tf_op jit(solution)/shard_map/ppermute | solution.py:689
  162.2 17.8 %collective-permute-start.12 = (bf16[2,32,2048]{2,1,0:T(8,128)(2,1)S(1)}, bf16[2,32,2048]{2,1,0:T(8,128)(2,1)S(1)}, u32[]{:S(2)}, u32[]{:S(2)}) collective-permute-start(bf16[2,32,2048]{2,1,0:T(8,128)(2,1)S(1)} %multiply_convert_fusion.2), channel_id=1, source_target_pairs={{0,2},{1,3},{2,0},{3,1},{4,6},{5,7},{6,4},{7,5},{8,10},{9,11},{10,... | collective-permute-start | bytes 786440 | tf_op jit(solution)/shard_map/ppermute | solution.py:696
  167.3 13.3 %collective-permute-start.11 = (bf16[2,32,2048]{2,1,0:T(8,128)(2,1)S(1)}, bf16[2,32,2048]{2,1,0:T(8,128)(2,1)S(1)}, u32[]{:S(2)}, u32[]{:S(2)}) collective-permute-start(bf16[2,32,2048]{2,1,0:T(8,128)(2,1)S(1)} %multiply_convert_fusion.2), channel_id=1, source_target_pairs={{0,3},{1,0},{2,1},{3,2},{4,7},{5,4},{6,5},{7,6},{8,11},{9,8},{10,9... | collective-permute-start | bytes 786440 | tf_op jit(solution)/shard_map/ppermute | solution.py:696
  171.1 17.3 %collective-permute-start.13 = (bf16[2,32,2048]{2,1,0:T(8,128)(2,1)S(1)}, bf16[2,32,2048]{2,1,0:T(8,128)(2,1)S(1)}, u32[]{:S(2)}, u32[]{:S(2)}) collective-permute-start(bf16[2,32,2048]{2,1,0:T(8,128)(2,1)S(1)} %multiply_convert_fusion.2), channel_id=1, source_target_pairs={{0,1},{1,2},{2,3},{3,0},{4,5},{5,6},{6,7},{7,4},{8,9},{9,10},{10,1... | collective-permute-start | bytes 786440 | tf_op jit(solution)/shard_map/ppermute | solution.py:696
  180.1 59.5 %collective-permute-start.19 = (bf16[128,8192]{1,0:T(8,128)(2,1)S(1)}, bf16[128,8192]{1,0:T(8,128)(2,1)}, u32[]{:S(2)}, u32[]{:S(2)}) collective-permute-start(bf16[128,8192]{1,0:T(8,128)(2,1)S(1)} %copy-done.1), channel_id=1, source_target_pairs={{0,8},{4,12},{8,0},{12,4},{16,24},{20,28},{24,16},{28,20},{1,9},{5... | collective-permute-start | bytes 6291464 | tf_op jit(solution)/shard_map/ppermute | solution.py:715
  180.7 59.0 %collective-permute-start.20 = (bf16[128,8192]{1,0:T(8,128)(2,1)}, bf16[128,8192]{1,0:T(8,128)(2,1)}, u32[]{:S(2)}, u32[]{:S(2)}) collective-permute-start(bf16[128,8192]{1,0:T(8,128)(2,1)} %get-tuple-element.92.refs_1_), channel_id=1, source_target_pairs={{0,16},{4,20},{8,24},{12,28},{16,0},{20,4},{24,8},{28,12},{1,17},{... | collective-permute-start | bytes 6291464 | tf_op jit(solution)/shard_map/ppermute | solution.py:715
  206.8 11.1 %collective-permute-start.16 = (bf16[2,32,2048]{2,1,0:T(8,128)(2,1)S(1)}, bf16[2,32,2048]{2,1,0:T(8,128)(2,1)S(1)}, u32[]{:S(2)}, u32[]{:S(2)}) collective-permute-start(bf16[2,32,2048]{2,1,0:T(8,128)(2,1)S(1)} %get-tuple-element.193), channel_id=1, source_target_pairs={{0,1},{1,2},{2,3},{3,0},{4,5},{5,6},{6,7},{7,4},{8,9},{9,10},{10,1... | collective-permute-start | bytes 786440 | tf_op jit(solution)/shard_map/ppermute | solution.py:689
  208.4 13.3 %collective-permute-start.18 = (bf16[2,32,2048]{2,1,0:T(8,128)(2,1)S(1)}, bf16[2,32,2048]{2,1,0:T(8,128)(2,1)S(1)}, u32[]{:S(2)}, u32[]{:S(2)}) collective-permute-start(bf16[2,32,2048]{2,1,0:T(8,128)(2,1)S(1)} %get-tuple-element.194), channel_id=1, source_target_pairs={{0,3},{1,0},{2,1},{3,2},{4,7},{5,4},{6,5},{7,6},{8,11},{9,8},{10,9... | collective-permute-start | bytes 786440 | tf_op jit(solution)/shard_map/ppermute | solution.py:689
  210.7 22.8 %collective-permute-start.17 = (bf16[2,32,2048]{2,1,0:T(8,128)(2,1)S(1)}, bf16[2,32,2048]{2,1,0:T(8,128)(2,1)S(1)}, u32[]{:S(2)}, u32[]{:S(2)}) collective-permute-start(bf16[2,32,2048]{2,1,0:T(8,128)(2,1)S(1)} %get-tuple-element.195), channel_id=1, source_target_pairs={{0,2},{1,3},{2,0},{3,1},{4,6},{5,7},{6,4},{7,5},{8,10},{9,11},{10,... | collective-permute-start | bytes 786440 | tf_op jit(solution)/shard_map/ppermute | solution.py:689
  217.9 66.9 %collective-permute-start.27 = (bf16[128,8192]{1,0:T(8,128)(2,1)}, bf16[128,8192]{1,0:T(8,128)(2,1)}, u32[]{:S(2)}, u32[]{:S(2)}) collective-permute-start(bf16[128,8192]{1,0:T(8,128)(2,1)} %collective-permute-done.15.refs_5_), channel_id=1, source_target_pairs={{0,4},{4,0},{8,12},{12,8},{16,20},{20,16},{24,28},{28,24},{1,5},{5... | collective-permute-start | bytes 6291464 | tf_op jit(solution)/shard_map/ppermute | solution.py:715
  221.6 62.7 %collective-permute-start.25 = (bf16[128,8192]{1,0:T(8,128)(2,1)}, bf16[128,8192]{1,0:T(8,128)(2,1)}, u32[]{:S(2)}, u32[]{:S(2)}) collective-permute-start(bf16[128,8192]{1,0:T(8,128)(2,1)} %collective-permute-done.15.refs_5_), channel_id=1, source_target_pairs={{0,16},{4,20},{8,24},{12,28},{16,0},{20,4},{24,8},{28,12},{1,17},{... | collective-permute-start | bytes 6291464 | tf_op jit(solution)/shard_map/ppermute | solution.py:715
  233.5 50.9 %collective-permute-start.24 = (bf16[128,8192]{1,0:T(8,128)(2,1)}, bf16[128,8192]{1,0:T(8,128)(2,1)}, u32[]{:S(2)}, u32[]{:S(2)}) collective-permute-start(bf16[128,8192]{1,0:T(8,128)(2,1)} %collective-permute-done.14.refs_6_), channel_id=1, source_target_pairs={{0,8},{4,12},{8,0},{12,4},{16,24},{20,28},{24,16},{28,20},{1,9},{5... | collective-permute-start | bytes 6291464 | tf_op jit(solution)/shard_map/ppermute | solution.py:715
  240.0 11.1 %collective-permute-start.23 = (bf16[2,32,2048]{2,1,0:T(8,128)(2,1)S(1)}, bf16[2,32,2048]{2,1,0:T(8,128)(2,1)S(1)}, u32[]{:S(2)}, u32[]{:S(2)}) collective-permute-start(bf16[2,32,2048]{2,1,0:T(8,128)(2,1)S(1)} %bitcast.397), channel_id=1, source_target_pairs={{0,1},{1,2},{2,3},{3,0},{4,5},{5,6},{6,7},{7,4},{8,9},{9,10},{10,1... | collective-permute-start | bytes 786440 | tf_op jit(solution)/shard_map/ppermute | solution.py:696
  241.5 19.7 %collective-permute-start.22 = (bf16[2,32,2048]{2,1,0:T(8,128)(2,1)S(1)}, bf16[2,32,2048]{2,1,0:T(8,128)(2,1)}, u32[]{:S(2)}, u32[]{:S(2)}) collective-permute-start(bf16[2,32,2048]{2,1,0:T(8,128)(2,1)S(1)} %bitcast.398), channel_id=1, source_target_pairs={{0,2},{1,3},{2,0},{3,1},{4,6},{5,7},{6,4},{7,5},{8,10},{9,11},{10,... | collective-permute-start | bytes 786440 | tf_op jit(solution)/shard_map/ppermute | solution.py:696
  251.1 14.3 %collective-permute-start.21 = (bf16[2,32,2048]{2,1,0:T(8,128)(2,1)S(1)}, bf16[2,32,2048]{2,1,0:T(8,128)(2,1)}, u32[]{:S(2)}, u32[]{:S(2)}) collective-permute-start(bf16[2,32,2048]{2,1,0:T(8,128)(2,1)S(1)} %bitcast.399), channel_id=1, source_target_pairs={{0,3},{1,0},{2,1},{3,2},{4,7},{5,4},{6,5},{7,6},{8,11},{9,8},{10,9... | collective-permute-start | bytes 786440 | tf_op jit(solution)/shard_map/ppermute | solution.py:696
  261.2 25.3 %collective-permute-start.28 = (bf16[128,8192]{1,0:T(8,128)(2,1)}, bf16[128,8192]{1,0:T(8,128)(2,1)S(1)}, u32[]{:S(2)}, u32[]{:S(2)}) collective-permute-start(bf16[128,8192]{1,0:T(8,128)(2,1)} %collective-permute-done.14.refs_6_), channel_id=1, source_target_pairs={{0,4},{4,0},{8,12},{12,8},{16,20},{20,16},{24,28},{28,24},{1,5},{5... | collective-permute-start | bytes 6291464 | tf_op jit(solution)/shard_map/ppermute | solution.py:715
  265.4 21.1 %collective-permute-start.26 = (bf16[128,8192]{1,0:T(8,128)(2,1)}, bf16[128,8192]{1,0:T(8,128)(2,1)}, u32[]{:S(2)}, u32[]{:S(2)}) collective-permute-start(bf16[128,8192]{1,0:T(8,128)(2,1)} %collective-permute-done.19.refs_4_), channel_id=1, source_target_pairs={{0,4},{4,0},{8,12},{12,8},{16,20},{20,16},{24,28},{28,24},{1,5},{5... | collective-permute-start | bytes 6291464 | tf_op jit(solution)/shard_map/ppermute | solution.py:715
  284.3 7.5 %collective-permute-start.30 = (bf16[128,8192]{1,0:T(8,128)(2,1)}, bf16[128,8192]{1,0:T(8,128)(2,1)}, u32[]{:S(2)}, u32[]{:S(2)}) collective-permute-start(bf16[128,8192]{1,0:T(8,128)(2,1)} %collective-permute-done.24.refs_5_.refs_12_), channel_id=1, source_target_pairs={{0,4},{4,0},{8,12},{12,8},{16,20},{20,16},{24,28},{28,24},{1,5},{5... | collective-permute-start | bytes 6291464 | tf_op jit(solution)/shard_map/ppermute | solution.py:715
  284.8 10.0 %collective-permute-start.31 = (bf16[128,8192]{1,0:T(8,128)(2,1)}, bf16[128,8192]{1,0:T(8,128)(2,1)}, u32[]{:S(2)}, u32[]{:S(2)}) collective-permute-start(bf16[128,8192]{1,0:T(8,128)(2,1)} %collective-permute-done.25.refs_6_.refs_13_), channel_id=1, source_target_pairs={{0,4},{4,0},{8,12},{12,8},{16,20},{20,16},{24,28},{28,24},{1,5},{5... | collective-permute-start | bytes 6291464 | tf_op jit(solution)/shard_map/ppermute | solution.py:715
  347.7 11.0 %collective-permute-start.35 = (bf16[2,32,2048]{2,1,0:T(8,128)(2,1)S(1)}, bf16[2,32,2048]{2,1,0:T(8,128)(2,1)S(1)}, u32[]{:S(2)}, u32[]{:S(2)}) collective-permute-start(bf16[2,32,2048]{2,1,0:T(8,128)(2,1)S(1)} %get-tuple-element.190), channel_id=1, source_target_pairs={{0,1},{1,2},{2,3},{3,0},{4,5},{5,6},{6,7},{7,4},{8,9},{9,10},{10,1... | collective-permute-start | bytes 786440 | tf_op jit(solution)/shard_map/ppermute | solution.py:689
  347.8 12.1 %collective-permute-start.37 = (bf16[2,32,2048]{2,1,0:T(8,128)(2,1)S(1)}, bf16[2,32,2048]{2,1,0:T(8,128)(2,1)S(1)}, u32[]{:S(2)}, u32[]{:S(2)}) collective-permute-start(bf16[2,32,2048]{2,1,0:T(8,128)(2,1)S(1)} %get-tuple-element.191), channel_id=1, source_target_pairs={{0,3},{1,0},{2,1},{3,2},{4,7},{5,4},{6,5},{7,6},{8,11},{9,8},{10,9... | collective-permute-start | bytes 786440 | tf_op jit(solution)/shard_map/ppermute | solution.py:689
  351.6 20.3 %collective-permute-start.36 = (bf16[2,32,2048]{2,1,0:T(8,128)(2,1)S(1)}, bf16[2,32,2048]{2,1,0:T(8,128)(2,1)S(1)}, u32[]{:S(2)}, u32[]{:S(2)}) collective-permute-start(bf16[2,32,2048]{2,1,0:T(8,128)(2,1)S(1)} %get-tuple-element.192), channel_id=1, source_target_pairs={{0,2},{1,3},{2,0},{3,1},{4,6},{5,7},{6,4},{7,5},{8,10},{9,11},{10,... | collective-permute-start | bytes 786440 | tf_op jit(solution)/shard_map/ppermute | solution.py:689
  373.4 11.1 %collective-permute-start.40 = (bf16[2,32,2048]{2,1,0:T(8,128)(2,1)S(1)}, bf16[2,32,2048]{2,1,0:T(8,128)(2,1)S(1)}, u32[]{:S(2)}, u32[]{:S(2)}) collective-permute-start(bf16[2,32,2048]{2,1,0:T(8,128)(2,1)S(1)} %bitcast.401), channel_id=1, source_target_pairs={{0,1},{1,2},{2,3},{3,0},{4,5},{5,6},{6,7},{7,4},{8,9},{9,10},{10,1... | collective-permute-start | bytes 786440 | tf_op jit(solution)/shard_map/ppermute | solution.py:696
  373.4 20.5 %collective-permute-start.39 = (bf16[2,32,2048]{2,1,0:T(8,128)(2,1)S(1)}, bf16[2,32,2048]{2,1,0:T(8,128)(2,1)S(1)}, u32[]{:S(2)}, u32[]{:S(2)}) collective-permute-start(bf16[2,32,2048]{2,1,0:T(8,128)(2,1)S(1)} %bitcast.402), channel_id=1, source_target_pairs={{0,2},{1,3},{2,0},{3,1},{4,6},{5,7},{6,4},{7,5},{8,10},{9,11},{10,... | collective-permute-start | bytes 786440 | tf_op jit(solution)/shard_map/ppermute | solution.py:696
  374.3 19.6 %collective-permute-start.38 = (bf16[2,32,2048]{2,1,0:T(8,128)(2,1)S(1)}, bf16[2,32,2048]{2,1,0:T(8,128)(2,1)S(1)}, u32[]{:S(2)}, u32[]{:S(2)}) collective-permute-start(bf16[2,32,2048]{2,1,0:T(8,128)(2,1)S(1)} %bitcast.403), channel_id=1, source_target_pairs={{0,3},{1,0},{2,1},{3,2},{4,7},{5,4},{6,5},{7,6},{8,11},{9,8},{10,9... | collective-permute-start | bytes 786440 | tf_op jit(solution)/shard_map/ppermute | solution.py:696
  377.3 60.8 %all-to-all-start.1 = ((bf16[8,256,1024]{2,1,0:T(8,128)(2,1)}), bf16[8,256,1024]{2,1,0:T(8,128)(2,1)}, u32[]{:S(2)}, u32[]{:S(2)}) async-start(bf16[8,256,1024]{2,1,0:T(8,128)(2,1)} %get-tuple-element.108), calls=%async_computation.1 | async-start | bytes 8388608 | tf_op jit(solution)/shard_map/all_to_all | solution.py:817
  381.8 231.3 %reduce-scatter.2.cloned.1.call-start = ((), (), s32[]{:S(2)}) async-start(), calls=%async_computation.10 | async-start | bytes 19464192 | tf_op jit(solution)/shard_map/reduce_scatter | solution.py:826
  410.6 21.8 %collective-permute-start.41 = (bf16[2,32,2048]{2,1,0:T(8,128)(2,1)}, bf16[2,32,2048]{2,1,0:T(8,128)(2,1)S(1)}, u32[]{:S(2)}, u32[]{:S(2)}) collective-permute-start(bf16[2,32,2048]{2,1,0:T(8,128)(2,1)} %get-tuple-element.187), channel_id=1, source_target_pairs={{0,1},{1,2},{2,3},{3,0},{4,5},{5,6},{6,7},{7,4},{8,9},{9,10},{10,1... | collective-permute-start | bytes 786440 | tf_op jit(solution)/shard_map/ppermute | solution.py:689
  415.9 16.6 %collective-permute-start.43 = (bf16[2,32,2048]{2,1,0:T(8,128)(2,1)}, bf16[2,32,2048]{2,1,0:T(8,128)(2,1)S(1)}, u32[]{:S(2)}, u32[]{:S(2)}) collective-permute-start(bf16[2,32,2048]{2,1,0:T(8,128)(2,1)} %get-tuple-element.188), channel_id=1, source_target_pairs={{0,3},{1,0},{2,1},{3,2},{4,7},{5,4},{6,5},{7,6},{8,11},{9,8},{10,9... | collective-permute-start | bytes 786440 | tf_op jit(solution)/shard_map/ppermute | solution.py:689
  415.9 21.0 %collective-permute-start.42 = (bf16[2,32,2048]{2,1,0:T(8,128)(2,1)S(1)}, bf16[2,32,2048]{2,1,0:T(8,128)(2,1)}, u32[]{:S(2)}, u32[]{:S(2)}) collective-permute-start(bf16[2,32,2048]{2,1,0:T(8,128)(2,1)S(1)} %get-tuple-element.189), channel_id=1, source_target_pairs={{0,2},{1,3},{2,0},{3,1},{4,6},{5,7},{6,4},{7,5},{8,10},{9,11},{10,... | collective-permute-start | bytes 786440 | tf_op jit(solution)/shard_map/ppermute | solution.py:689
  442.4 24.0 %collective-permute-start.46 = (bf16[2,32,2048]{2,1,0:T(8,128)(2,1)S(1)}, bf16[2,32,2048]{2,1,0:T(8,128)(2,1)S(1)}, u32[]{:S(2)}, u32[]{:S(2)}) collective-permute-start(bf16[2,32,2048]{2,1,0:T(8,128)(2,1)S(1)} %bitcast.390), channel_id=1, source_target_pairs={{0,1},{1,2},{2,3},{3,0},{4,5},{5,6},{6,7},{7,4},{8,9},{9,10},{10,1... | collective-permute-start | bytes 786440 | tf_op jit(solution)/shard_map/ppermute | solution.py:696
  443.8 22.6 %collective-permute-start.45 = (bf16[2,32,2048]{2,1,0:T(8,128)(2,1)S(1)}, bf16[2,32,2048]{2,1,0:T(8,128)(2,1)S(1)}, u32[]{:S(2)}, u32[]{:S(2)}) collective-permute-start(bf16[2,32,2048]{2,1,0:T(8,128)(2,1)S(1)} %bitcast.391), channel_id=1, source_target_pairs={{0,2},{1,3},{2,0},{3,1},{4,6},{5,7},{6,4},{7,5},{8,10},{9,11},{10,... | collective-permute-start | bytes 786440 | tf_op jit(solution)/shard_map/ppermute | solution.py:696
  447.2 19.2 %collective-permute-start.44 = (bf16[2,32,2048]{2,1,0:T(8,128)(2,1)S(1)}, bf16[2,32,2048]{2,1,0:T(8,128)(2,1)S(1)}, u32[]{:S(2)}, u32[]{:S(2)}) collective-permute-start(bf16[2,32,2048]{2,1,0:T(8,128)(2,1)S(1)} %bitcast.392), channel_id=1, source_target_pairs={{0,3},{1,0},{2,1},{3,2},{4,7},{5,4},{6,5},{7,6},{8,11},{9,8},{10,9... | collective-permute-start | bytes 786440 | tf_op jit(solution)/shard_map/ppermute | solution.py:696
  481.7 19.9 %all-to-all-start.2 = ((bf16[8,256,128]{2,1,0:T(8,128)(2,1)}), bf16[8,256,128]{2,1,0:T(8,128)(2,1)}, u32[]{:S(2)}, u32[]{:S(2)}) async-start(bf16[8,256,128]{2,1,0:T(8,128)(2,1)} %bitcast.408), calls=%async_computation.2 | async-start | bytes 1048576 | tf_op jit(solution)/shard_map/all_to_all | solution.py:838
  486.8 43.7 %collective-permute-start.50 = (bf16[2,2,256,512]{3,2,1,0:T(8,128)(2,1)S(1)}, bf16[2,2,256,512]{3,2,1,0:T(8,128)(2,1)}, u32[]{:S(2)}, u32[]{:S(2)}) collective-permute-start(bf16[2,2,256,512]{3,2,1,0:T(8,128)(2,1)S(1)} %dynamic-slice_bitcast_fusion), channel_id=1, source_target_pairs={{0,4},{4,0},{8,12},{12,8},{16,20},{20,16},{24,28},{28,24},{1,5},{5... | collective-permute-start | bytes 3145736 | tf_op jit(solution)/shard_map/ppermute | solution.py:715
  506.6 11.1 %collective-permute-start.47 = (bf16[2,32,2048]{2,1,0:T(8,128)(2,1)S(1)}, bf16[2,32,2048]{2,1,0:T(8,128)(2,1)S(1)}, u32[]{:S(2)}, u32[]{:S(2)}) collective-permute-start(bf16[2,32,2048]{2,1,0:T(8,128)(2,1)S(1)} %get-tuple-element.184), channel_id=1, source_target_pairs={{0,1},{1,2},{2,3},{3,0},{4,5},{5,6},{6,7},{7,4},{8,9},{9,10},{10,1... | collective-permute-start | bytes 786440 | tf_op jit(solution)/shard_map/ppermute | solution.py:689
  509.5 11.1 %collective-permute-start.49 = (bf16[2,32,2048]{2,1,0:T(8,128)(2,1)S(1)}, bf16[2,32,2048]{2,1,0:T(8,128)(2,1)S(1)}, u32[]{:S(2)}, u32[]{:S(2)}) collective-permute-start(bf16[2,32,2048]{2,1,0:T(8,128)(2,1)S(1)} %get-tuple-element.185), channel_id=1, source_target_pairs={{0,3},{1,0},{2,1},{3,2},{4,7},{5,4},{6,5},{7,6},{8,11},{9,8},{10,9... | collective-permute-start | bytes 786440 | tf_op jit(solution)/shard_map/ppermute | solution.py:689
  510.5 19.8 %collective-permute-start.48 = (bf16[2,32,2048]{2,1,0:T(8,128)(2,1)S(1)}, bf16[2,32,2048]{2,1,0:T(8,128)(2,1)S(1)}, u32[]{:S(2)}, u32[]{:S(2)}) collective-permute-start(bf16[2,32,2048]{2,1,0:T(8,128)(2,1)S(1)} %get-tuple-element.186), channel_id=1, source_target_pairs={{0,2},{1,3},{2,0},{3,1},{4,6},{5,7},{6,4},{7,5},{8,10},{9,11},{10,... | collective-permute-start | bytes 786440 | tf_op jit(solution)/shard_map/ppermute | solution.py:689
  531.9 17.3 %collective-permute-start.51 = (bf16[2,2,256,640]{3,2,0,1:T(8,128)(2,1)}, bf16[2,2,256,640]{3,2,0,1:T(8,128)(2,1)}, u32[]{:S(2)}, u32[]{:S(2)}) collective-permute-start(bf16[2,2,256,640]{3,2,0,1:T(8,128)(2,1)} %bitcast.346), channel_id=1, source_target_pairs={{0,4},{4,0},{8,12},{12,8},{16,20},{20,16},{24,28},{28,24},{1,5},{5... | collective-permute-start | bytes 3932168 | tf_op jit(solution)/shard_map/ppermute | solution.py:715
  533.5 15.7 %all-to-all-start.3 = ((bf16[80,8,256]{2,0,1:T(8,128)(2,1)}), bf16[80,8,256]{2,0,1:T(8,128)(2,1)}, u32[]{:S(2)}, u32[]{:S(2)}) async-start(bf16[80,8,256]{2,0,1:T(8,128)(2,1)} %copy.305), calls=%async_computation.3 | async-start | bytes 655360 | tf_op jit(solution)/shard_map/all_to_all | solution.py:861
  551.1 11.3 %collective-permute-start.58 = (bf16[528,256]{1,0:T(8,128)(2,1)S(1)}, bf16[528,256]{1,0:T(8,128)(2,1)S(1)}, u32[]{:S(2)}, u32[]{:S(2)}) collective-permute-start(bf16[528,256]{1,0:T(8,128)(2,1)S(1)} %pad_maximum_fusion.8), channel_id=1, source_target_pairs={{0,1},{1,2},{2,3},{3,0},{4,5},{5,6},{6,7},{7,4},{8,9},{9,10},{10,1... | collective-permute-start | bytes 811016 | tf_op jit(solution)/shard_map/ppermute | solution.py:883
  551.1 18.6 %collective-permute-start.57 = (bf16[528,256]{1,0:T(8,128)(2,1)S(1)}, bf16[528,256]{1,0:T(8,128)(2,1)S(1)}, u32[]{:S(2)}, u32[]{:S(2)}) collective-permute-start(bf16[528,256]{1,0:T(8,128)(2,1)S(1)} %pad_maximum_fusion.8), channel_id=1, source_target_pairs={{0,2},{1,3},{2,0},{3,1},{4,6},{5,7},{6,4},{7,5},{8,10},{9,11},{10,... | collective-permute-start | bytes 811016 | tf_op jit(solution)/shard_map/ppermute | solution.py:883
  553.0 16.7 %collective-permute-start.56 = (bf16[528,256]{1,0:T(8,128)(2,1)S(1)}, bf16[528,256]{1,0:T(8,128)(2,1)S(1)}, u32[]{:S(2)}, u32[]{:S(2)}) collective-permute-start(bf16[528,256]{1,0:T(8,128)(2,1)S(1)} %pad_maximum_fusion.8), channel_id=1, source_target_pairs={{0,3},{1,0},{2,1},{3,2},{4,7},{5,4},{6,5},{7,6},{8,11},{9,8},{10,9... | collective-permute-start | bytes 811016 | tf_op jit(solution)/shard_map/ppermute | solution.py:883
  556.8 21.2 %collective-permute-start.54 = (bf16[2,256,512]{2,1,0:T(8,128)(2,1)}, bf16[2,256,512]{2,1,0:T(8,128)(2,1)}, u32[]{:S(2)}, u32[]{:S(2)}) collective-permute-start(bf16[2,256,512]{2,1,0:T(8,128)(2,1)} %dynamic-slice_bitcast_fusion.2), channel_id=1, source_target_pairs={{0,16},{4,20},{8,24},{12,28},{16,0},{20,4},{24,8},{28,12},{1,17},{... | collective-permute-start | bytes 1572872 | tf_op jit(solution)/shard_map/ppermute | solution.py:715
  559.9 21.0 %collective-permute-start.52 = (bf16[2,256,640]{2,1,0:T(8,128)(2,1)}, bf16[2,256,640]{2,1,0:T(8,128)(2,1)}, u32[]{:S(2)}, u32[]{:S(2)}) collective-permute-start(bf16[2,256,640]{2,1,0:T(8,128)(2,1)} %dynamic-slice_bitcast_fusion.1), channel_id=1, source_target_pairs={{0,8},{4,12},{8,0},{12,4},{16,24},{20,28},{24,16},{28,20},{1,9},{5... | collective-permute-start | bytes 1966088 | tf_op jit(solution)/shard_map/ppermute | solution.py:715
  582.2 8.6 %collective-permute-start.53 = (bf16[256,640]{1,0:T(8,128)(2,1)S(1)}, bf16[256,640]{1,0:T(8,128)(2,1)S(1)}, u32[]{:S(2)}, u32[]{:S(2)}) collective-permute-start(bf16[256,640]{1,0:T(8,128)(2,1)S(1)} %dynamic-slice_bitcast_fusion.3), channel_id=1, source_target_pairs={{0,16},{4,20},{8,24},{12,28},{16,0},{20,4},{24,8},{28,12},{1,17},{... | collective-permute-start | bytes 983048 | tf_op jit(solution)/shard_map/ppermute | solution.py:715
  591.5 44.7 %all-to-all-start.4 = ((bf16[8,128,1024]{2,1,0:T(8,128)(2,1)}), bf16[8,128,1024]{2,1,0:T(8,128)(2,1)S(1)}, u32[]{:S(2)}, u32[]{:S(2)}) async-start(bf16[8,128,1024]{2,1,0:T(8,128)(2,1)} %get-tuple-element.123), calls=%async_computation.4 | async-start | bytes 4194304 | tf_op jit(solution)/shard_map/all_to_all | solution.py:877
  637.5 41.7 %all-to-all-start.5 = ((bf16[8,128,1024]{2,1,0:T(8,128)(2,1)}), bf16[8,128,1024]{2,1,0:T(8,128)(2,1)}, u32[]{:S(2)}, u32[]{:S(2)}) async-start(bf16[8,128,1024]{2,1,0:T(8,128)(2,1)} %get-tuple-element.139), calls=%async_computation.6 | async-start | bytes 4194304 | tf_op jit(solution)/shard_map/all_to_all | solution.py:911
  (50 other events, 464.3 us)
Sparse Core Ops, SparseCore 0:
  11.1 41.4 all-gather.7
  55.1 117.9 all-gather.9
  312.0 54.2 all-gather.11
  438.2 139.6 reduce-scatter.1
